TPU v7x, 32 devices: a whole 2x2x4 slice. The times are simulated.
32 devices in a mesh: groups: 2 (over y), ctx: 4 (over z), mp: 4 (over x, core).
Axes of the slice: x: 2, y: 2, z: 4, core: 2. Of those that a mesh axis runs over, the one named last changes fastest.
Arguments:
- queries: bfloat16 [2048, 4096], P(('groups', 'ctx'), 'mp'), parts along dimension 0, may hold values from -18 to 18
- keyvals: bfloat16 [2048, 512], P(('groups', 'ctx', 'mp')), parts along dimension 0, may hold values from -6 to 6
- segment_ids: int32 [2048], P('groups'), parts along dimension 0, may hold values from 0 to 2, never falling along the last dimension, each value on 1 to 512 neighbouring positions
- residual: bfloat16 [2048, 4096], P(('groups', 'ctx', 'mp')), parts along dimension 0, may hold values from -180 to 180
- out_weight: bfloat16 [4096, 4096], P('mp', 'ctx'), may hold values from -0.375 to 0.375
- lru_weight: bfloat16 [4096, 4096], P('ctx', 'mp'), may hold values from -0.09375 to 0.09375
- conv_weight: float32 [4, 4096], P(None, 'mp'), may hold values from -3 to 3
- gate_decay_w: bfloat16 [16, 256, 256], P('mp'), may hold values from -0.375 to 0.375
- gate_input_w: bfloat16 [16, 256, 256], P('mp'), may hold values from -0.375 to 0.375
- gate_decay_b: float32 [4096], P('mp'), may hold values from -3 to 3
- gate_input_b: float32 [4096], P('mp'), may hold values from -3 to 3
- decay_codes: int32 [4096], P('mp'), may hold values from 0 to 15
- norm_gain: float32 [4096], replicated, may hold values from 0.1 to 1.9
Outputs:
- resid_out: bfloat16 [2048, 4096], P(('groups', 'ctx', 'mp')), parts along dimension 0
- lru_out: bfloat16 [2048, 4096], P(('groups', 'ctx'), 'mp'), parts along dimension 0
There are 2 independent parts, one for each index of `groups`. A program takes and returns all parts, laid end to end along the dimension named above; an argument that names none is the same for every part. Nothing has to cross between parts.
All inputs are finite; a program needn't handle non-finite values.
Results may differ from a plain program's by a relative error of at most 0.017.
Values may be sent and summed in bfloat16 or wider, within the bound.
No kernel may reach another device: no remote copies, remote signals or barrier semaphores. Data moves between devices by JAX's collectives and lax.ppermute only.
A program may use at most 64 MiB of HBM per device.

v0:
```python
import math

import jax
import jax.numpy as jnp
from jax import lax
from jax.sharding import PartitionSpec as P

HD = 256
WIN = 2048
CONV = 4
LEVELS = 16
BW = 256


def shifted_2(value, axis, steps):
    count = lax.axis_size(axis)
    initial, last = (max(0, -steps), min(count, count - steps))
    return lax.ppermute(value, axis, [(source, source + steps) for source in range(initial, last)])


def decay_rates():
    levels = jnp.arange(LEVELS, dtype=jnp.float32)
    return 0.006 * jnp.exp(-levels * (math.log(3000.0) / (LEVELS - 1)))


def chain_link(former, latter):
    return (former[0] * latter[0], latter[0] * former[1] + latter[1])


def rms_scaled(values, norm_gain):
    value_f32 = values.astype(jnp.float32)
    inverse = lax.rsqrt(jnp.mean(value_f32 * value_f32, axis=-1, keepdims=True) + 1e-06)
    return (value_f32 * inverse * norm_gain).astype(jnp.bfloat16)


def attend_local(queries, keys_all, allowed):
    rows_here = queries.shape[0]
    heads_here = queries.shape[1] // HD
    query_heads = queries.reshape(rows_here, heads_here, HD)
    score_scale = 1.0 / math.sqrt(HD)
    scores = (
        jnp.einsum("thd,kd->htk", query_heads, keys_all[:, :HD], preferred_element_type=jnp.float32)
        * score_scale
    )
    scores = jnp.where(allowed[None], scores, -1e30)
    row_top = jnp.max(scores, axis=-1, keepdims=True)
    weights = jnp.exp(scores - row_top)
    probs = (weights / jnp.sum(weights, axis=-1, keepdims=True)).astype(jnp.bfloat16)
    gathered = jnp.einsum(
        "htk,kd->thd", probs, keys_all[:, HD:], preferred_element_type=jnp.float32
    )
    return gathered.reshape(rows_here, heads_here * HD).astype(jnp.bfloat16)


def local(
    queries,
    keyvals,
    segment_ids,
    residual,
    out_weight,
    lru_weight,
    conv_weight,
    gate_decay_w,
    gate_input_w,
    gate_decay_b,
    gate_input_b,
    decay_codes,
    norm_gain,
):
    rows_here = queries.shape[0]
    ctx_index = lax.axis_index("ctx")
    back_blocks = WIN // rows_here
    own_kv = lax.all_gather(keyvals, "mp", axis=0, tiled=True)
    earlier = []
    moving = own_kv
    for offset in range(back_blocks):
        moving = shifted_2(moving, "ctx", 1)
        earlier = [moving] + earlier
    keys_all = jnp.concatenate(earlier + [own_kv], axis=0)
    pad_seg = jnp.concatenate([jnp.full((WIN,), -1, jnp.int32), segment_ids])
    query_seg = lax.dynamic_slice_in_dim(segment_ids, ctx_index * rows_here, rows_here)
    key_seg = lax.dynamic_slice_in_dim(
        pad_seg, ctx_index * rows_here, (back_blocks + 1) * rows_here
    )
    query_pos = ctx_index * rows_here + jnp.arange(rows_here, dtype=jnp.int32)
    key_pos = (ctx_index - back_blocks) * rows_here + jnp.arange(
        (back_blocks + 1) * rows_here, dtype=jnp.int32
    )
    distance = query_pos[:, None] - key_pos[None, :]
    allowed = (distance >= 0) & (distance < WIN) & (query_seg[:, None] == key_seg[None, :])
    attended = attend_local(queries, keys_all, allowed)
    head_part = jnp.dot(
        attended,
        lax.all_gather(out_weight, "ctx", axis=1, tiled=True),
        preferred_element_type=jnp.float32,
    )
    summed = lax.psum_scatter(
        head_part.astype(jnp.bfloat16), "mp", scatter_dimension=0, tiled=True
    ).astype(jnp.float32)
    resid_out = (summed + residual.astype(jnp.float32)).astype(jnp.bfloat16)
    normed = lax.all_gather(rms_scaled(resid_out, norm_gain), "mp", axis=0, tiled=True)
    channels = lru_weight.shape[1]
    lru_in = jnp.dot(
        normed,
        lax.all_gather(lru_weight, "ctx", axis=0, tiled=True),
        preferred_element_type=jnp.float32,
    ).astype(jnp.bfloat16)
    rim_rows = shifted_2(lru_in[rows_here - (CONV - 1) :], "ctx", 1)
    extended = jnp.concatenate([rim_rows, lru_in], axis=0)
    ext_seg = lax.dynamic_slice_in_dim(
        pad_seg, ctx_index * rows_here + WIN - (CONV - 1), rows_here + CONV - 1
    )
    conv_acc = jnp.zeros((rows_here, channels), jnp.float32)
    for offset in range(CONV):
        lag_rows = CONV - 1 - offset
        shifted = extended[lag_rows : lag_rows + rows_here].astype(jnp.float32)
        same_doc = (ext_seg[lag_rows : lag_rows + rows_here] == query_seg)[:, None]
        conv_acc = conv_acc + jnp.where(same_doc, conv_weight[offset] * shifted, 0.0)
    conv_out = conv_acc.astype(jnp.bfloat16)
    blocks_here = channels // BW
    grouped = conv_out.reshape(rows_here, blocks_here, BW)
    decay_gate = jax.nn.sigmoid(
        jnp.einsum(
            "tbi,bij->tbj", grouped, gate_decay_w, preferred_element_type=jnp.float32
        ).reshape(rows_here, channels)
        + gate_decay_b
    )
    input_gate = jax.nn.sigmoid(
        jnp.einsum(
            "tbi,bij->tbj", grouped, gate_input_w, preferred_element_type=jnp.float32
        ).reshape(rows_here, channels)
        + gate_input_b
    )
    levels = jnp.arange(LEVELS, dtype=jnp.int32)
    decay_rate = jnp.sum(
        jnp.where(decay_codes[:, None] == levels[None, :], decay_rates()[None, :], 0.0), axis=1
    )
    log_decay = -8.0 * decay_gate * decay_rate
    restart = (query_seg != ext_seg[CONV - 2 : CONV - 2 + rows_here])[:, None]
    keep_factor = jnp.where(restart, 0.0, jnp.exp(log_decay))
    input_scale = jnp.where(restart, 1.0, jnp.sqrt(-jnp.expm1(2.0 * log_decay)))
    driven = input_scale * input_gate * conv_out.astype(jnp.float32)
    cum_keep, local_state = lax.associative_scan(chain_link, (keep_factor, driven), axis=0)
    block_keep = cum_keep[rows_here - 1]
    block_state = local_state[rows_here - 1]

    def relay_turn(turn_index, state_in):
        return shifted_2(block_keep * state_in + block_state, "ctx", 1)

    incoming = lax.fori_loop(0, lax.axis_size("ctx") - 1, relay_turn, jnp.zeros_like(block_state))
    states = local_state + cum_keep * incoming[None, :]
    return (resid_out, states.astype(jnp.bfloat16))


def solution(mesh):
    in_specs = (
        P(("groups", "ctx"), "mp"),
        P(("groups", "ctx", "mp"), None),
        P("groups"),
        P(("groups", "ctx", "mp"), None),
        P("mp", "ctx"),
        P("ctx", "mp"),
        P(None, "mp"),
        P("mp", None, None),
        P("mp", None, None),
        P("mp"),
        P("mp"),
        P("mp"),
        P(),
    )
    out_specs = (P(("groups", "ctx", "mp"), None), P(("groups", "ctx"), "mp"))
    return jax.shard_map(local, mesh=mesh, in_specs=in_specs, out_specs=out_specs, check_vma=False)
```

profile of v0, /device:TPU:0, one launch (start us, length us, event | category | flops | bytes accessed | tf_op | source)
XLA Modules:
  0.0 554.3 jit_solution(5232723126797398906)
XLA Ops:
  8.0 7.4 %all_gather.12 = bf16[256,512]{1,0:T(8,128)(2,1)S(1)} all-gather(bf16[64,512]{1,0:T(8,128)(2,1)} %param.16), channel_id=1, replica_groups=mesh['groups'=2,'ctx'=4,'mp'=4] {'mp'}, dimensions={0}, use_global_device_ids=true | all-gather | bytes 327680 | tf_op jit(solution)/shard_map/all_gather | solution.py:73
  15.4 3.5 collective-permute-start.1
  18.9 9.3 %collective-permute-done.1 = bf16[256,512]{1,0:T(8,128)(2,1)S(1)} collective-permute-done((bf16[256,512]{1,0:T(8,128)(2,1)S(1)}, bf16[256,512]{1,0:T(8,128)(2,1)S(1)}, u32[]{:S(2)}, u32[]{:S(2)}) %collective-permute-start.1) | collective-permute-done | bytes 262176 | tf_op jit(solution)/shard_map/ppermute | solution.py:18
  28.3 8.5 %collective-permute-start.2 = (bf16[256,512]{1,0:T(8,128)(2,1)S(1)}, bf16[256,512]{1,0:T(8,128)(2,1)S(1)}, u32[]{:S(2)}, u32[]{:S(2)}) collective-permute-start(bf16[256,512]{1,0:T(8,128)(2,1)S(1)} %collective-permute-done.1), channel_id=1, source_target_pairs={{0,4},{4,8},{8,12},{1,5},{5,9},{9,13},{2,6},{6,10},{10,14},{3,7},{... | collective-permute-start | bytes 786440 | tf_op jit(solution)/shard_map/ppermute | solution.py:18
  36.8 11.2 %collective-permute-done.2 = bf16[256,512]{1,0:T(8,128)(2,1)S(1)} collective-permute-done((bf16[256,512]{1,0:T(8,128)(2,1)S(1)}, bf16[256,512]{1,0:T(8,128)(2,1)S(1)}, u32[]{:S(2)}, u32[]{:S(2)}) %collective-permute-start.2) | collective-permute-done | bytes 262176 | tf_op jit(solution)/shard_map/ppermute | solution.py:18
  48.0 13.6 %collective-permute-start.3 = (bf16[256,512]{1,0:T(8,128)(2,1)S(1)}, bf16[256,512]{1,0:T(8,128)(2,1)S(1)}, u32[]{:S(2)}, u32[]{:S(2)}) collective-permute-start(bf16[256,512]{1,0:T(8,128)(2,1)S(1)} %collective-permute-done.2), channel_id=1, source_target_pairs={{0,4},{4,8},{8,12},{1,5},{5,9},{9,13},{2,6},{6,10},{10,14},{3,7},{... | collective-permute-start | bytes 786440 | tf_op jit(solution)/shard_map/ppermute | solution.py:18
  61.6 10.2 %collective-permute-done.3 = bf16[256,512]{1,0:T(8,128)(2,1)S(1)} collective-permute-done((bf16[256,512]{1,0:T(8,128)(2,1)S(1)}, bf16[256,512]{1,0:T(8,128)(2,1)S(1)}, u32[]{:S(2)}, u32[]{:S(2)}) %collective-permute-start.3) | collective-permute-done | bytes 262176 | tf_op jit(solution)/shard_map/ppermute | solution.py:18
  71.8 12.3 %collective-permute-start.4 = (bf16[256,512]{1,0:T(8,128)(2,1)S(1)}, bf16[256,512]{1,0:T(8,128)(2,1)S(1)}, u32[]{:S(2)}, u32[]{:S(2)}) collective-permute-start(bf16[256,512]{1,0:T(8,128)(2,1)S(1)} %collective-permute-done.3), channel_id=1, source_target_pairs={{0,4},{4,8},{8,12},{1,5},{5,9},{9,13},{2,6},{6,10},{10,14},{3,7},{... | collective-permute-start | bytes 786440 | tf_op jit(solution)/shard_map/ppermute | solution.py:18
  84.1 9.6 %collective-permute-done.4 = bf16[256,512]{1,0:T(8,128)(2,1)S(1)} collective-permute-done((bf16[256,512]{1,0:T(8,128)(2,1)S(1)}, bf16[256,512]{1,0:T(8,128)(2,1)S(1)}, u32[]{:S(2)}, u32[]{:S(2)}) %collective-permute-start.4) | collective-permute-done | bytes 262176 | tf_op jit(solution)/shard_map/ppermute | solution.py:18
  93.7 11.3 %collective-permute-start.5 = (bf16[256,512]{1,0:T(8,128)(2,1)S(1)}, bf16[256,512]{1,0:T(8,128)(2,1)S(1)}, u32[]{:S(2)}, u32[]{:S(2)}) collective-permute-start(bf16[256,512]{1,0:T(8,128)(2,1)S(1)} %collective-permute-done.4), channel_id=1, source_target_pairs={{0,4},{4,8},{8,12},{1,5},{5,9},{9,13},{2,6},{6,10},{10,14},{3,7},{... | collective-permute-start | bytes 786440 | tf_op jit(solution)/shard_map/ppermute | solution.py:18
  105.0 9.7 %collective-permute-done.5 = bf16[256,512]{1,0:T(8,128)(2,1)S(1)} collective-permute-done((bf16[256,512]{1,0:T(8,128)(2,1)S(1)}, bf16[256,512]{1,0:T(8,128)(2,1)S(1)}, u32[]{:S(2)}, u32[]{:S(2)}) %collective-permute-start.5) | collective-permute-done | bytes 262176 | tf_op jit(solution)/shard_map/ppermute | solution.py:18
  114.6 13.8 %collective-permute-start.6 = (bf16[256,512]{1,0:T(8,128)(2,1)S(1)}, bf16[256,512]{1,0:T(8,128)(2,1)S(1)}, u32[]{:S(2)}, u32[]{:S(2)}) collective-permute-start(bf16[256,512]{1,0:T(8,128)(2,1)S(1)} %collective-permute-done.5), channel_id=1, source_target_pairs={{0,4},{4,8},{8,12},{1,5},{5,9},{9,13},{2,6},{6,10},{10,14},{3,7},{... | collective-permute-start | bytes 786440 | tf_op jit(solution)/shard_map/ppermute | solution.py:18
  128.7 9.4 %collective-permute-done.6 = bf16[256,512]{1,0:T(8,128)(2,1)S(1)} collective-permute-done((bf16[256,512]{1,0:T(8,128)(2,1)S(1)}, bf16[256,512]{1,0:T(8,128)(2,1)S(1)}, u32[]{:S(2)}, u32[]{:S(2)}) %collective-permute-start.6) | collective-permute-done | bytes 262176 | tf_op jit(solution)/shard_map/ppermute | solution.py:18
  138.1 9.9 %collective-permute-start.7 = (bf16[256,512]{1,0:T(8,128)(2,1)S(1)}, bf16[256,512]{1,0:T(8,128)(2,1)S(1)}, u32[]{:S(2)}, u32[]{:S(2)}) collective-permute-start(bf16[256,512]{1,0:T(8,128)(2,1)S(1)} %collective-permute-done.6), channel_id=1, source_target_pairs={{0,4},{4,8},{8,12},{1,5},{5,9},{9,13},{2,6},{6,10},{10,14},{3,7},{... | collective-permute-start | bytes 786440 | tf_op jit(solution)/shard_map/ppermute | solution.py:18
  148.1 9.5 %collective-permute-done.7 = bf16[256,512]{1,0:T(8,128)(2,1)S(1)} collective-permute-done((bf16[256,512]{1,0:T(8,128)(2,1)S(1)}, bf16[256,512]{1,0:T(8,128)(2,1)S(1)}, u32[]{:S(2)}, u32[]{:S(2)}) %collective-permute-start.7) | collective-permute-done | bytes 262176 | tf_op jit(solution)/shard_map/ppermute | solution.py:18
  157.6 13.0 %collective-permute-start.8 = (bf16[256,512]{1,0:T(8,128)(2,1)S(1)}, bf16[256,512]{1,0:T(8,128)(2,1)S(1)}, u32[]{:S(2)}, u32[]{:S(2)}) collective-permute-start(bf16[256,512]{1,0:T(8,128)(2,1)S(1)} %collective-permute-done.7), channel_id=1, source_target_pairs={{0,4},{4,8},{8,12},{1,5},{5,9},{9,13},{2,6},{6,10},{10,14},{3,7},{... | collective-permute-start | bytes 786440 | tf_op jit(solution)/shard_map/ppermute | solution.py:18
  170.6 1.6 fusion.7
  172.2 8.0 %collective-permute-done.8 = bf16[256,512]{1,0:T(8,128)(2,1)S(1)} collective-permute-done((bf16[256,512]{1,0:T(8,128)(2,1)S(1)}, bf16[256,512]{1,0:T(8,128)(2,1)S(1)}, u32[]{:S(2)}, u32[]{:S(2)}) %collective-permute-start.8) | collective-permute-done | bytes 262176 | tf_op jit(solution)/shard_map/ppermute | solution.py:18
  180.4 1.4 copy-done.12
  181.8 4.7 fusion.53
  186.5 6.0 %fusion.8 = bf16[256,4,256]{2,0,1:T(8,128)(2,1)S(1)} fusion(f32[4,256]{1,0:T(4,128)S(1)} %fusion.53, bf16[2304,512]{1,0:T(8,128)(2,1)} %copy-done.12, pred[256,2304]{0,1:T(8,128)(4,1)S(1)} %fusion.7, bf16[32,4,8,256]{3,2,1,0:T(8,128)(2,1)S(1)} %bitcast.79), kind=kOutput, calls=%fused_computation.17 | convolution fusion | flops 2427981056 | bytes 4001792 | tf_op jit(solution)/shard_map/htk,kd->thd/dot_general | solution.py:49
  192.5 6.9 %all-gather.4.cloned.1.call-done = bf16[1024,4096]{1,0:T(8,128)(2,1)} async-done(((bf16[1024,1024]{1,0:T(8,128)(2,1)}), bf16[1024,4096]{1,0:T(8,128)(2,1)}) %all-gather.4.cloned.1.call-update) | async-done | bytes 8388624 | tf_op jit(solution)/shard_map/all_gather | solution.py:94
  199.5 7.1 %convolution_convert_fusion = bf16[256,4096]{1,0:T(8,128)(2,1)} fusion(bf16[256,1024]{0,1:T(8,128)(2,1)S(1)} %bitcast.71, bf16[1024,4096]{1,0:T(8,128)(2,1)} %all-gather.4.cloned.1.call-done), kind=kOutput, calls=%fused_computation.6 | convolution fusion | flops 2148532224 | bytes 11010048 | tf_op jit(solution)/shard_map/dot_general | solution.py:92
  207.6 33.9 %reduce-scatter.2.cloned.1.call-done = bf16[64,4096]{1,0:T(8,128)(2,1)} async-done(((bf16[256,4096]{1,0:T(8,128)(2,1)}), bf16[64,4096]{1,0:T(8,128)(2,1)}) %reduce-scatter.2.cloned.1.call-update) | async-done | bytes 524304 | tf_op jit(solution)/shard_map/reduce_scatter | solution.py:97
  244.8 147.9 %all-gather.8.cloned.1.call-done = bf16[4096,1024]{1,0:T(8,128)(2,1)} async-done(((bf16[1024,1024]{1,0:T(8,128)(2,1)}), bf16[4096,1024]{1,0:T(8,128)(2,1)}) %all-gather.8.cloned.1.call-update) | async-done | bytes 8388624 | tf_op jit(solution)/shard_map/all_gather | solution.py:105
  392.8 22.8 %all-gather.6.cloned.1.call-done = bf16[256,4096]{1,0:T(8,128)(2,1)} async-done(((bf16[64,4096]{1,0:T(8,128)(2,1)}), bf16[256,4096]{1,0:T(8,128)(2,1)}) %all-gather.6.cloned.1.call-update) | async-done | bytes 2097168 | tf_op jit(solution)/shard_map/all_gather | solution.py:101
  415.5 6.3 %convolution_convert_fusion.1 = bf16[256,1024]{1,0:T(8,128)(2,1)S(1)} fusion(bf16[256,4096]{1,0:T(8,128)(2,1)} %all-gather.6.cloned.1.call-done, bf16[4096,1024]{1,0:T(8,128)(2,1)} %all-gather.8.cloned.1.call-done), kind=kOutput, calls=%fused_computation.18 | convolution fusion | flops 2147745792 | bytes 11010048 | tf_op jit(solution)/shard_map/dot_general | solution.py:103
  421.9 3.4 collective-permute-start.9
  430.8 2.8 convert_multiply_fusion.2
  433.6 1.4 slice.296
  435.0 1.5 slice.297
  436.5 1.5 slice.295
  438.0 1.5 slice.299
  439.4 2.5 multiply_add_fusion.1
  441.9 1.7 slice.302
  443.6 1.7 slice.303
  446.8 1.9 multiply_add_fusion.2
  450.1 1.6 slice.307
  451.7 1.6 slice.311
  453.4 1.8 multiply_add_fusion.3
  456.4 1.5 slice.313
  457.9 1.5 slice.317
  459.5 1.6 multiply_add_fusion.4
  461.0 1.4 slice.320
  462.5 1.4 slice.321
  463.9 1.4 slice.319
  465.4 1.5 slice.323
  466.8 1.4 multiply_add_fusion.5
  480.4 1.4 fusion.50
  487.2 1.5 slice.318
  488.7 1.4 slice.343
  492.8 1.5 slice.312
  500.8 1.7 slice.349
  504.5 1.5 slice.294
  506.0 1.5 slice.351
  515.7 2.7 pad.114
  518.6 2.3 fusion.24
  521.1 2.7 pad.130
  525.0 2.7 pad.129
  528.5 16.5 %while.10 = (s32[]{:T(128)}, f32[1024]{0:T(1024)S(1)}, f32[1024]{0:T(1024)S(1)}, f32[1024]{0:T(1024)S(1)}, s32[]{:T(128)}) while((s32[]{:T(128)}, f32[1024]{0:T(1024)S(1)}, f32[1024]{0:T(1024)S(1)}, f32[1024]{0:T(1024)S(1)}, s32[]{:T(128)}) %tuple.63), condition=%wide.region_6.7_spmd, body=%wide.region_5.6_spmd.sunk | while | flops 2050 | bytes 32869 | solution.py:150
  528.5 4.2 collective-permute-start
  534.0 4.2 collective-permute-start
  539.5 4.2 collective-permute-start
  545.0 2.8 add_convert_fusion
  (195 shorter events, 57.5 us)
Async XLA Ops:
  7.2 420.2 %copy-start = (bf16[4,256,256]{2,1,0:T(8,128)(2,1)S(1)}, bf16[4,256,256]{2,1,0:T(8,128)(2,1)}, u32[]{:S(2)}) copy-start(bf16[4,256,256]{2,1,0:T(8,128)(2,1)} %param.22) | copy-start | bytes 1572868
  7.2 121.3 %copy-start.13 = (s32[1024]{0:T(1024)S(1)}, s32[1024]{0:T(1024)}, u32[]{:S(2)}) copy-start(s32[1024]{0:T(1024)} %param.17) | copy-start | bytes 12292
  7.2 192.3 %all-gather.4.cloned.1.call-start = ((), (), s32[]{:S(2)}) async-start(), calls=%async_computation.1 | async-start | bytes 10485760 | tf_op jit(solution)/shard_map/all_gather | solution.py:94
  7.9 233.6 %reduce-scatter.2.cloned.1.call-start = ((), (), s32[]{:S(2)}) async-start(), calls=%async_computation.2 | async-start | bytes 2621440 | tf_op jit(solution)/shard_map/reduce_scatter | solution.py:97
  15.4 12.9 %collective-permute-start.1 = (bf16[256,512]{1,0:T(8,128)(2,1)S(1)}, bf16[256,512]{1,0:T(8,128)(2,1)S(1)}, u32[]{:S(2)}, u32[]{:S(2)}) collective-permute-start(bf16[256,512]{1,0:T(8,128)(2,1)S(1)} %all_gather.12), channel_id=1, source_target_pairs={{0,4},{4,8},{8,12},{1,5},{5,9},{9,13},{2,6},{6,10},{10,14},{3,7},{... | collective-permute-start | bytes 786440 | tf_op jit(solution)/shard_map/ppermute | solution.py:18
  28.3 19.7 %collective-permute-start.2 = (bf16[256,512]{1,0:T(8,128)(2,1)S(1)}, bf16[256,512]{1,0:T(8,128)(2,1)S(1)}, u32[]{:S(2)}, u32[]{:S(2)}) collective-permute-start(bf16[256,512]{1,0:T(8,128)(2,1)S(1)} %collective-permute-done.1), channel_id=1, source_target_pairs={{0,4},{4,8},{8,12},{1,5},{5,9},{9,13},{2,6},{6,10},{10,14},{3,7},{... | collective-permute-start | bytes 786440 | tf_op jit(solution)/shard_map/ppermute | solution.py:18
  48.0 23.8 %collective-permute-start.3 = (bf16[256,512]{1,0:T(8,128)(2,1)S(1)}, bf16[256,512]{1,0:T(8,128)(2,1)S(1)}, u32[]{:S(2)}, u32[]{:S(2)}) collective-permute-start(bf16[256,512]{1,0:T(8,128)(2,1)S(1)} %collective-permute-done.2), channel_id=1, source_target_pairs={{0,4},{4,8},{8,12},{1,5},{5,9},{9,13},{2,6},{6,10},{10,14},{3,7},{... | collective-permute-start | bytes 786440 | tf_op jit(solution)/shard_map/ppermute | solution.py:18
  71.8 21.9 %collective-permute-start.4 = (bf16[256,512]{1,0:T(8,128)(2,1)S(1)}, bf16[256,512]{1,0:T(8,128)(2,1)S(1)}, u32[]{:S(2)}, u32[]{:S(2)}) collective-permute-start(bf16[256,512]{1,0:T(8,128)(2,1)S(1)} %collective-permute-done.3), channel_id=1, source_target_pairs={{0,4},{4,8},{8,12},{1,5},{5,9},{9,13},{2,6},{6,10},{10,14},{3,7},{... | collective-permute-start | bytes 786440 | tf_op jit(solution)/shard_map/ppermute | solution.py:18
  93.7 21.0 %collective-permute-start.5 = (bf16[256,512]{1,0:T(8,128)(2,1)S(1)}, bf16[256,512]{1,0:T(8,128)(2,1)S(1)}, u32[]{:S(2)}, u32[]{:S(2)}) collective-permute-start(bf16[256,512]{1,0:T(8,128)(2,1)S(1)} %collective-permute-done.4), channel_id=1, source_target_pairs={{0,4},{4,8},{8,12},{1,5},{5,9},{9,13},{2,6},{6,10},{10,14},{3,7},{... | collective-permute-start | bytes 786440 | tf_op jit(solution)/shard_map/ppermute | solution.py:18
  114.6 23.4 %collective-permute-start.6 = (bf16[256,512]{1,0:T(8,128)(2,1)S(1)}, bf16[256,512]{1,0:T(8,128)(2,1)S(1)}, u32[]{:S(2)}, u32[]{:S(2)}) collective-permute-start(bf16[256,512]{1,0:T(8,128)(2,1)S(1)} %collective-permute-done.5), channel_id=1, source_target_pairs={{0,4},{4,8},{8,12},{1,5},{5,9},{9,13},{2,6},{6,10},{10,14},{3,7},{... | collective-permute-start | bytes 786440 | tf_op jit(solution)/shard_map/ppermute | solution.py:18
  138.1 19.5 %collective-permute-start.7 = (bf16[256,512]{1,0:T(8,128)(2,1)S(1)}, bf16[256,512]{1,0:T(8,128)(2,1)S(1)}, u32[]{:S(2)}, u32[]{:S(2)}) collective-permute-start(bf16[256,512]{1,0:T(8,128)(2,1)S(1)} %collective-permute-done.6), channel_id=1, source_target_pairs={{0,4},{4,8},{8,12},{1,5},{5,9},{9,13},{2,6},{6,10},{10,14},{3,7},{... | collective-permute-start | bytes 786440 | tf_op jit(solution)/shard_map/ppermute | solution.py:18
  157.6 22.6 %collective-permute-start.8 = (bf16[256,512]{1,0:T(8,128)(2,1)S(1)}, bf16[256,512]{1,0:T(8,128)(2,1)S(1)}, u32[]{:S(2)}, u32[]{:S(2)}) collective-permute-start(bf16[256,512]{1,0:T(8,128)(2,1)S(1)} %collective-permute-done.7), channel_id=1, source_target_pairs={{0,4},{4,8},{8,12},{1,5},{5,9},{9,13},{2,6},{6,10},{10,14},{3,7},{... | collective-permute-start | bytes 786440 | tf_op jit(solution)/shard_map/ppermute | solution.py:18
  180.4 1.4 copy-start.12
  181.8 4.7 copy-start.28
  206.5 35.0 %copy-start.4 = (bf16[64,4096]{1,0:T(8,128)(2,1)S(1)}, bf16[64,4096]{1,0:T(8,128)(2,1)}, u32[]{:S(2)}) copy-start(bf16[64,4096]{1,0:T(8,128)(2,1)} %param.18) | copy-start | bytes 1572868
  206.6 37.1 %copy-start.14 = (f32[4096]{0:T(1024)S(1)}, f32[4096]{0:T(1024)}, u32[]{:S(2)}) copy-start(f32[4096]{0:T(1024)} %param.27) | copy-start | bytes 49156
  206.6 38.1 %copy-start.25 = (s32[1024]{0:T(1024)S(1)}, s32[1024]{0:T(1024)}, u32[]{:S(2)}) copy-start(s32[1024]{0:T(1024)} %param.26) | copy-start | bytes 12292
  206.6 38.2 %copy-start.24 = (f32[4,1024]{1,0:T(4,128)S(1)}, f32[4,1024]{1,0:T(4,128)}, u32[]{:S(2)}) copy-start(f32[4,1024]{1,0:T(4,128)} %param.21) | copy-start | bytes 49156
  206.6 186.1 %all-gather.8.cloned.1.call-start = ((), (), s32[]{:S(2)}) async-start(), calls=%async_computation.4 | async-start | bytes 10485760 | tf_op jit(solution)/shard_map/all_gather | solution.py:105
  207.3 208.2 %all-gather.6.cloned.1.call-start = ((), (), s32[]{:S(2)}) async-start(), calls=%async_computation.3 | async-start | bytes 2621440 | tf_op jit(solution)/shard_map/all_gather | solution.py:101
  242.9 0.8 copy-start.2
  421.9 4.7 collective-permute-start.9
  427.4 1.7 copy-start.5
  429.1 1.7 copy-start.26
  429.1 1.7 copy-start.27
  504.4 7.2 %copy-start.11 = (f32[3,1024]{1,0:T(4,128)S(1)}, f32[3,1024]{1,0:T(4,128)}, u32[]{:S(2)}) copy-start(f32[3,1024]{1,0:T(4,128)} %slice.341) | copy-start | bytes 36868
  504.4 7.2 %copy-start.23 = (f32[1,1024]{1,0:T(1,128)S(1)}, f32[1,1024]{1,0:T(1,128)}, u32[]{:S(2)}) copy-start(f32[1,1024]{1,0:T(1,128)} %slice.407) | copy-start | bytes 12292
  504.4 7.3 %copy-start.22 = (f32[1,1024]{1,0:T(1,128)S(1)}, f32[1,1024]{1,0:T(1,128)}, u32[]{:S(2)}) copy-start(f32[1,1024]{1,0:T(1,128)} %slice.381) | copy-start | bytes 12292
  504.4 7.4 %copy-start.9 = (f32[7,1024]{1,0:T(8,128)S(1)}, f32[7,1024]{1,0:T(8,128)}, u32[]{:S(2)}) copy-start(f32[7,1024]{1,0:T(8,128)} %slice.318) | copy-start | bytes 86020
  504.4 7.4 %copy-start.10 = (f32[7,1024]{1,0:T(8,128)S(1)}, f32[7,1024]{1,0:T(8,128)}, u32[]{:S(2)}) copy-start(f32[7,1024]{1,0:T(8,128)} %slice.343) | copy-start | bytes 86020
  504.4 8.9 %copy-start.7 = (f32[15,1024]{1,0:T(8,128)S(1)}, f32[15,1024]{1,0:T(8,128)}, u32[]{:S(2)}) copy-start(f32[15,1024]{1,0:T(8,128)} %slice.312) | copy-start | bytes 184324
  504.4 8.9 %copy-start.8 = (f32[15,1024]{1,0:T(8,128)S(1)}, f32[15,1024]{1,0:T(8,128)}, u32[]{:S(2)}) copy-start(f32[15,1024]{1,0:T(8,128)} %slice.345) | copy-start | bytes 184324
  507.5 6.8 %copy-start.6 = (f32[31,1024]{1,0:T(8,128)S(1)}, f32[31,1024]{1,0:T(8,128)}, u32[]{:S(2)}) copy-start(f32[31,1024]{1,0:T(8,128)} %slice.347) | copy-start | bytes 380932
  508.1 5.3 copy-start.21
  511.8 2.6 copy-start.20
  513.4 1.2 copy-start.19
  514.3 1.0 copy-start.3
  514.5 0.9 copy-start.18
  515.4 2.9 copy-start.17
  518.6 2.3 copy-start.16
  520.9 3.0 copy-start.15
  521.1 6.6 %copy-start.1 = (f32[256,1024]{1,0:T(8,128)S(1)}, f32[256,1024]{1,0:T(8,128)}, u32[]{:S(2)}) copy-start(f32[256,1024]{1,0:T(8,128)} %pad.114) | copy-start | bytes 3145732
  528.5 5.5 collective-permute-start
  534.0 5.5 collective-permute-start
  539.5 5.5 collective-permute-start
Sparse Core Ops, SparseCore 0:
  9.6 189.8 all-gather.3
  206.7 34.7 reduce-scatter.1
  243.1 149.6 all-gather.7
  394.7 20.7 all-gather.5
where the time goes:
time: 557 us; the launch traced here: 554 us
  waiting for transfers between devices  295 us (53%)
  starting transfers between devices  102 us (18%)
  local copies, waits for them, and re-layouts  77.2 us (14%)
  other arithmetic  32.9 us (6%)
  matrix products  24.8 us (4%)
  between operations  14.7 us (3%)
  blocking collectives  7.43 us (1%)
    all_gather x1, waiting for transfers between devices, local(): lax.all_gather(lru_weight, 'ctx', axis=0, tiled=True)  148 us
    ppermute x12, starting transfers between devices, shifted_2(): lax.ppermute(value, axis, [(source, source + steps) for source in range(i...  102 us
    ppermute x12, waiting for transfers between devices, shifted_2(): lax.ppermute(value, axis, [(source, source + steps) for source in range(i...  82.1 us
    slice x52, local copies, waits for them, and re-layouts, local(): lax.associative_scan(chain_link, (keep_factor, driven), axis=0)  61 us
    reduce_scatter x1, waiting for transfers between devices, local(): lax.psum_scatter(head_part.astype(jnp.bfloat16), 'mp', scatter_dimension=...  33.9 us
    all_gather x1, waiting for transfers between devices, local(): lax.all_gather(rms_scaled(resid_out, norm_gain), 'mp', axis=0, tiled=True)  22.8 us
    add x13, other arithmetic, chain_link(): return (former[0] * latter[0], latter[0] * former[1] + latter[1])  13.8 us
  transfers between devices with their start and end apart: 16, of which 16 were waited for; matrix products, arithmetic and copies ran while one was open for 3% of the time, Pallas kernels for 0%

commit v1 on v0

--- a/solution.py
+++ b/solution.py
@@ -1,8 +1,11 @@
+import functools
 import math
 
 import jax
 import jax.numpy as jnp
 from jax import lax
+from jax.experimental import pallas as pl
+from jax.experimental.pallas import tpu as pltpu
 from jax.sharding import PartitionSpec as P
 
 HD = 256
@@ -52,7 +55,7 @@
     return gathered.reshape(rows_here, heads_here * HD).astype(jnp.bfloat16)
 
 
-def local(
+def local_wide(
     queries,
     keyvals,
     segment_ids,
@@ -152,6 +155,413 @@
     return (resid_out, states.astype(jnp.bfloat16))
 
 
+F32 = jnp.float32
+BF16 = jnp.bfloat16
+VMEM = pl.BlockSpec(memory_space=pltpu.VMEM)
+SMEM = pl.BlockSpec(memory_space=pltpu.SMEM)
+TILE = 16
+SUB = 8
+LANES = 128
+
+
+def rotated(value, axis, steps):
+    count = lax.axis_size(axis)
+    return lax.ppermute(value, axis, [(s, (s - steps) % count) for s in range(count)])
+
+
+def swapped(value, axis, flip):
+    count = lax.axis_size(axis)
+    return lax.ppermute(value, axis, [(s, s ^ flip) for s in range(count)])
+
+
+def segment_start(pos, low, high):
+    return jnp.where(pos >= high, high, jnp.where(pos >= low, low, 0))
+
+
+def assemble_kernel(rows, shard, nctx, scal, *refs):
+    out = refs[-1]
+    ctx_index, mp_index = scal[0], scal[1]
+    for flip, piece in enumerate(refs[:-1]):
+        member = jnp.bitwise_xor(mp_index, flip)
+        for step in range(nctx):
+            block = lax.rem(ctx_index + step, nctx)
+            first = pl.multiple_of(block * rows + member * shard, shard)
+            out[pl.ds(first, shard), :] = piece[step * shard : (step + 1) * shard, :]
+
+
+def assemble(scal, pieces, rows, shard, nctx):
+    tokens = nctx * rows
+    width = pieces[0].shape[1]
+    return pl.pallas_call(
+        functools.partial(assemble_kernel, rows, shard, nctx),
+        out_shape=jax.ShapeDtypeStruct((tokens, width), BF16),
+        in_specs=[SMEM] + [VMEM] * len(pieces),
+        out_specs=VMEM,
+        name="assemble",
+    )(scal, *pieces)
+
+
+def attend_kernel(nctx, back, steps, shard, scal, *refs):
+    count = len(steps)
+    q_refs, resid_refs = refs[:count], refs[count : 2 * count]
+    kv, weight, keep, send, att, acc = refs[2 * count :]
+    rows, width = q_refs[0].shape
+    heads = width // HD
+    half = weight.shape[1] // 2
+    ctx_index, mp_index, low, high = scal[0], scal[1], scal[2], scal[3]
+    side = jnp.bitwise_and(mp_index, 1)
+    window = min(back + 1, nctx) * rows
+    scale = 1.0 / math.sqrt(HD)
+    for j, step in enumerate(steps):
+        block = lax.rem(ctx_index + step, nctx)
+        first_key = pl.multiple_of(
+            jnp.minimum(jnp.maximum(block - back, 0), nctx - window // rows) * rows, rows
+        )
+        qpos = block * rows + lax.broadcasted_iota(jnp.int32, (rows, 1), 0)
+        start = segment_start(qpos, low, high)
+        kpos = first_key + lax.broadcasted_iota(jnp.int32, (1, window), 1)
+        allowed = (kpos <= qpos) & (kpos >= start) & (qpos - kpos < WIN)
+        for h in range(heads):
+            query = q_refs[j][:, h * HD : (h + 1) * HD]
+            keys = kv[pl.ds(first_key, window), :HD]
+            scores = lax.dot_general(
+                query, keys, (((1,), (1,)), ((), ())), preferred_element_type=F32
+            )
+            scores = jnp.where(allowed, scores * scale, -1e30)
+            top = jnp.max(scores, axis=1, keepdims=True)
+            weights = jnp.exp(scores - top)
+            total = jnp.sum(weights, axis=1, keepdims=True)
+            values = kv[pl.ds(first_key, window), HD:]
+            gathered = jnp.dot(weights.astype(BF16), values, preferred_element_type=F32)
+            att[:, h * HD : (h + 1) * HD] = (gathered / total).astype(BF16)
+        own = pl.ds(pl.multiple_of(mp_index * shard, shard), shard)
+        for out, which in ((send, 1 - side), (keep, side)):
+            cols = pl.ds(pl.multiple_of(which * half, half), half)
+            acc[...] = jnp.dot(att[...], weight[:, cols], preferred_element_type=F32)
+            acc[own, :] += resid_refs[j][:, cols].astype(F32)
+            out[j * rows : (j + 1) * rows, :] = acc[...].astype(BF16)
+
+
+def attend(scal, queries, residuals, kv, weight, nctx, back, steps, shard):
+    rows, width = queries[0].shape
+    count = len(steps)
+    half = weight.shape[1] // 2
+    shape = jax.ShapeDtypeStruct((count * rows, half), BF16)
+    return pl.pallas_call(
+        functools.partial(attend_kernel, nctx, back, steps, shard),
+        out_shape=(shape, shape),
+        in_specs=[SMEM] + [VMEM] * (2 * count + 2),
+        out_specs=(VMEM, VMEM),
+        scratch_shapes=[pltpu.VMEM((rows, width), BF16), pltpu.VMEM((rows, half), F32)],
+        name="attend",
+    )(scal, *queries, *residuals, kv, weight)
+
+
+def project_kernel(jobs, nhalves, shard, scal, *refs):
+    halves, (gain, weight), outs = refs[:nhalves], refs[nhalves : nhalves + 2], refs[nhalves + 2 :]
+    ctx_index, mp_index = scal[0], scal[1]
+    side = jnp.bitwise_and(mp_index, 1)
+    channels = weight.shape[1]
+    half = weight.shape[0] // 2
+    gains, weights = [], []
+    for which in (side, 1 - side):
+        span = pl.multiple_of(which * half, half)
+        gains.append(gain[:, pl.ds(pl.multiple_of(ctx_index * 2 * half + span, half), half)])
+        weights.append(weight[pl.ds(span, half), :])
+    ones = jnp.ones((SUB, half), BF16)
+
+    def parts_of(source, last):
+        (own_ref, other_ref), first, rows = source
+        begin = first + rows - last if last else first
+        stop = first + rows
+        return own_ref[begin:stop, :].astype(F32), other_ref[begin:stop, :].astype(F32)
+
+    def projected(parts):
+        total = None
+        for part, scale, matrix in zip(parts, gains, weights):
+            term = jnp.dot((part * scale).astype(BF16), matrix, preferred_element_type=F32)
+            total = term if total is None else total + term
+        return total
+
+    def squares(parts):
+        total = None
+        for part in parts:
+            term = lax.dot_general(
+                ones, (part * part).astype(BF16), (((1,), (1,)), ((), ())), preferred_element_type=F32
+            )
+            total = term if total is None else total + term
+        return total
+
+    at = 0
+    for main, prior in jobs:
+        sums = []
+        if main is not None:
+            source = ((halves[main[0]], halves[main[0] + 1]), main[1], main[2])
+            rows = main[2]
+            parts = parts_of(source, 0)
+            outs[at][0:rows, :] = projected(parts).astype(BF16)
+            sums = squares(parts)
+            mine = pl.ds(pl.multiple_of(main[1] + mp_index * shard, TILE), shard)
+            for which, ref in ((side, source[0][0]), (1 - side, source[0][1])):
+                outs[at + 1][:, pl.ds(pl.multiple_of(which * half, half), half)] = ref[mine, :]
+        if prior is not None:
+            source = ((halves[prior[0]], halves[prior[0] + 1]), prior[1], prior[2])
+            tail = projected(parts_of(source, TILE))[TILE - SUB :, :]
+            tail_sums = squares(parts_of(source, LANES))
+            line = outs[at]
+            base = rows if main is not None else 0
+            if main is None:
+                own = ((halves[prior[3]], halves[prior[3] + 1]), prior[4], prior[5])
+                sums = squares(parts_of(own, 0))
+            spare = channels - sums.shape[1] - LANES
+            pieces = [sums, tail_sums] + ([jnp.zeros((SUB, spare), F32)] if spare else [])
+            sums = jnp.concatenate(pieces, axis=1)
+            coarse = sums.astype(BF16).astype(F32)
+            index = lax.broadcasted_iota(jnp.int32, sums.shape, 0)
+            sums = jnp.where(index == 0, coarse, sums - coarse)
+            line[base : base + TILE, :] = jnp.concatenate([sums, tail], axis=0).astype(BF16)
+        at += 1 if main is None else 2
+
+
+def project(scal, halves, gain, weight, jobs, shard):
+    channels = weight.shape[1]
+    shapes = []
+    for main, prior in jobs:
+        extra = TILE if prior is not None else 0
+        shapes.append(jax.ShapeDtypeStruct(((main[2] if main else 0) + extra, channels), BF16))
+        if main is not None:
+            shapes.append(jax.ShapeDtypeStruct((shard, weight.shape[0]), BF16))
+    return pl.pallas_call(
+        functools.partial(project_kernel, jobs, len(halves), shard),
+        out_shape=tuple(shapes),
+        in_specs=[SMEM] + [VMEM] * (len(halves) + 2),
+        out_specs=tuple([VMEM] * len(shapes)),
+        name="project",
+    )(scal, *halves, gain, weight)
+
+
+def minus_expm1(x):
+    series = jnp.full_like(x, 1.0 / 5040.0)
+    for divisor in (720.0, 120.0, 24.0, 6.0, 2.0, 1.0):
+        series = series * x + 1.0 / divisor
+    return jnp.where(x > -0.3, -x * series, 1.0 - jnp.exp(x))
+
+
+def recur_kernel(features, scal, *refs):
+    count = (len(refs) - 12) // 2
+    mains, lines = refs[:count], refs[count : 2 * count]
+    conv_w, decay_w, input_w, decay_b, input_b, codes = refs[2 * count : 2 * count + 6]
+    local_ref, cum_ref, last_ref, ext, keep_s, state_s = refs[2 * count + 6 :]
+    rows = mains[0].shape[0]
+    width = mains[0].shape[1]
+    ctx_index, low, high = scal[0], scal[2], scal[3]
+    stats = None
+    for line in lines:
+        both = line[:, : rows + LANES].astype(F32)
+        term = both[0:1, :] + both[1:2, :]
+        stats = term if stats is None else stats + term
+    inverse = lax.rsqrt(stats * (1.0 / features) + 1e-06)
+    inverse = jnp.transpose(jnp.broadcast_to(inverse, (LANES, rows + LANES)))[:, 0:1]
+    lanes = pl.ds(pl.multiple_of(pl.program_id(0) * width, width), width)
+    main = tail = None
+    for piece, line in zip(mains, lines):
+        term, tail_term = piece[...].astype(F32), line[:, lanes].astype(F32)[SUB:, :]
+        main = term if main is None else main + term
+        tail = tail_term if tail is None else tail + tail_term
+    ext[0:SUB, :] = (tail * inverse[rows + LANES - SUB :, :]).astype(BF16).astype(F32)
+    ext[SUB : SUB + rows, :] = (main * inverse[:rows, :]).astype(BF16).astype(F32)
+    pos = ctx_index * rows + lax.broadcasted_iota(jnp.int32, (rows, 1), 0)
+    start = segment_start(pos, low, high)
+    conv = None
+    for lag in range(CONV):
+        shifted = ext[SUB - lag : SUB - lag + rows, :]
+        term = jnp.where(pos - lag >= start, conv_w[lag : lag + 1, :] * shifted, 0.0)
+        conv = term if conv is None else conv + term
+    conv = conv.astype(BF16)
+    gate_d = jax.nn.sigmoid(
+        jnp.dot(conv, decay_w[0], preferred_element_type=F32) + decay_b[...]
+    )
+    gate_i = jax.nn.sigmoid(
+        jnp.dot(conv, input_w[0], preferred_element_type=F32) + input_b[...]
+    )
+    rate = 0.006 * jnp.exp(-codes[...].astype(F32) * (math.log(3000.0) / (LEVELS - 1)))
+    log_decay = -8.0 * gate_d * rate
+    restart = pos == start
+    keep = jnp.where(restart, 0.0, jnp.exp(log_decay))
+    scale = jnp.where(restart, 1.0, jnp.sqrt(minus_expm1(2.0 * log_decay)))
+    state = scale * gate_i * conv.astype(F32)
+    tiles = rows // SUB
+    keep = keep.reshape(tiles, SUB, width)
+    state = state.reshape(tiles, SUB, width)
+    index = lax.broadcasted_iota(jnp.int32, (tiles, SUB, width), 1)
+    shift = 1
+    while shift < SUB:
+        inside = index >= shift
+        prior_keep = jnp.where(inside, pltpu.roll(keep, shift, 1), 1.0)
+        prior_state = jnp.where(inside, pltpu.roll(state, shift, 1), 0.0)
+        state = keep * prior_state + state
+        keep = keep * prior_keep
+        shift *= 2
+    keep_s[...] = keep
+    state_s[...] = state
+    run_keep = jnp.ones((1, width), F32)
+    run_state = jnp.zeros((1, width), F32)
+    for t in range(tiles):
+        keep_t, state_t = keep_s[t], state_s[t]
+        new_state = state_t + keep_t * run_state
+        new_keep = keep_t * run_keep
+        local_ref[t * SUB : (t + 1) * SUB, :] = new_state
+        cum_ref[t * SUB : (t + 1) * SUB, :] = new_keep
+        run_state, run_keep = new_state[SUB - 1 :, :], new_keep[SUB - 1 :, :]
+    line = lax.broadcasted_iota(jnp.int32, (SUB, width), 0)
+    last_ref[...] = jnp.where(line == 0, run_keep, run_state)
+
+
+def recur(scal, mains, lines, conv_w, decay_w, input_w, decay_b, input_b, codes, rows, features):
+    channels = conv_w.shape[1]
+    tiles = rows // SUB
+    by_block = pl.BlockSpec((rows, BW), lambda j: (0, j))
+    row_spec = pl.BlockSpec((1, BW), lambda j: (0, j))
+    gate_spec = pl.BlockSpec((1, BW, BW), lambda j: (j, 0, 0))
+    line_specs = [
+        pl.BlockSpec((TILE, channels), functools.partial(lambda at, j: (at, 0), at))
+        for _, at in lines
+    ]
+    full = jax.ShapeDtypeStruct((rows, channels), F32)
+    return pl.pallas_call(
+        functools.partial(recur_kernel, features),
+        grid=(channels // BW,),
+        out_shape=(full, full, jax.ShapeDtypeStruct((SUB, channels), F32)),
+        in_specs=[SMEM]
+        + [by_block] * len(mains)
+        + line_specs
+        + [pl.BlockSpec((CONV, BW), lambda j: (0, j)), gate_spec, gate_spec]
+        + [row_spec] * 3,
+        out_specs=(by_block, by_block, pl.BlockSpec((SUB, BW), lambda j: (0, j))),
+        scratch_shapes=[
+            pltpu.VMEM((rows + SUB, BW), F32),
+            pltpu.VMEM((tiles, SUB, BW), F32),
+            pltpu.VMEM((tiles, SUB, BW), F32),
+        ],
+        name="recur",
+    )(scal, *mains, *[line for line, _ in lines], conv_w, decay_w, input_w, decay_b, input_b, codes)
+
+
+def local_near(
+    queries,
+    keyvals,
+    segment_ids,
+    residual,
+    out_weight,
+    lru_weight,
+    conv_weight,
+    gate_decay_w,
+    gate_input_w,
+    gate_decay_b,
+    gate_input_b,
+    decay_codes,
+    norm_gain,
+):
+    rows = queries.shape[0]
+    shard = keyvals.shape[0]
+    tokens = segment_ids.shape[0]
+    nctx, nmp = lax.axis_size("ctx"), lax.axis_size("mp")
+    ctx_index, mp_index = lax.axis_index("ctx"), lax.axis_index("mp")
+    features = residual.shape[1]
+    cols = out_weight.shape[1]
+    longest = tokens // 2
+    back = -(-(min(WIN, longest) - 1) // rows)
+    reach = min(nctx - 1, -(-longest // rows))
+    low = jnp.sum((segment_ids < 1).astype(jnp.int32))
+    high = jnp.sum((segment_ids < 2).astype(jnp.int32))
+    scal = jnp.stack([ctx_index, mp_index, low, high]).astype(jnp.int32)
+
+    own_kv = jnp.concatenate(
+        [keyvals] + [rotated(keyvals, "ctx", step) for step in range(1, nctx)], axis=0
+    )
+    pieces = {0: own_kv}
+    flip = nmp // 2
+    while flip >= 1:
+        for done in sorted(pieces):
+            pieces[done | flip] = swapped(pieces[done], "mp", flip)
+        flip //= 2
+    kv = assemble(scal, [pieces[e] for e in range(nmp)], rows, shard, nctx)
+
+    visiting = [queries] + [rotated(queries, "ctx", step) for step in range(1, nctx)]
+    resid_parts = []
+    for step in range(nctx):
+        first = lax.rem(ctx_index + nctx - step, nctx) * cols
+        part = lax.dynamic_slice_in_dim(residual, first, cols, axis=1)
+        resid_parts.append(rotated(part, "ctx", step) if step else part)
+
+    chunks = [tuple(range(i, min(i + 2, nctx))) for i in range(0, nctx, 2)]
+    gain = norm_gain.reshape(1, features)
+    where_is, halves = {}, []
+    messages, lines, resid_rows = {}, {}, {}
+    for steps in chunks:
+        keep, send = attend(
+            scal,
+            [visiting[s] for s in steps],
+            [resid_parts[s] for s in steps],
+            kv,
+            out_weight,
+            nctx,
+            back,
+            steps,
+            shard,
+        )
+        mine = (keep.astype(F32) + swapped(send, "mp", 1).astype(F32)).astype(BF16)
+        flip = 2
+        while flip < nmp:
+            mine = (mine.astype(F32) + swapped(mine, "mp", flip).astype(F32)).astype(BF16)
+            flip *= 2
+        for j, s in enumerate(steps):
+            where_is[s] = (len(halves), j * rows, rows)
+        halves = halves + [mine, swapped(mine, "mp", 1)]
+        jobs = [(where_is[s], where_is[s - 1] if s else None) for s in steps]
+        if steps[-1] == nctx - 1:
+            jobs.append((None, where_is[nctx - 1] + where_is[0]))
+        outs = project(scal, halves, gain, lru_weight, jobs, shard)
+        for j, s in enumerate(steps):
+            messages[s], resid_rows[s] = outs[2 * j], outs[2 * j + 1]
+        if steps[-1] == nctx - 1:
+            own_line = outs[2 * len(steps)]
+    mains, lines = [messages[0]], [(own_line, 0)]
+    for step in range(1, nctx):
+        got = rotated(messages[step], "ctx", -step)
+        mains.append(got)
+        lines.append((got, rows // TILE))
+    local_state, cum_keep, last = recur(
+        scal,
+        mains,
+        lines,
+        conv_weight,
+        gate_decay_w,
+        gate_input_w,
+        gate_decay_b.reshape(1, -1),
+        gate_input_b.reshape(1, -1),
+        decay_codes.reshape(1, -1),
+        rows,
+        features,
+    )
+    incoming = jnp.zeros_like(last[0])
+    for step in range(reach, 0, -1):
+        before = rotated(last, "ctx", -step)
+        incoming = jnp.where(ctx_index >= step, before[0] * incoming + before[1], 0.0)
+    states = local_state + cum_keep * incoming[None, :]
+    resid_out = jnp.zeros(residual.shape, BF16)
+    for step in range(nctx):
+        part = rotated(resid_rows[step], "ctx", -step) if step else resid_rows[step]
+        first = lax.rem(ctx_index + nctx - step, nctx) * cols
+        resid_out = lax.dynamic_update_slice_in_dim(resid_out, part, first, axis=1)
+    return (resid_out, states.astype(BF16))
+
+
+def local(queries, keyvals, segment_ids, *rest):
+    near = segment_ids.shape[0] <= WIN and lax.axis_size("mp") % 2 == 0
+    return (local_near if near else local_wide)(queries, keyvals, segment_ids, *rest)
+
+
 def solution(mesh):
     in_specs = (
         P(("groups", "ctx"), "mp"),

time: 557 us -> 207 us (0.37)
  waiting for transfers between devices: 295 us -> 121 us
  local copies, waits for them, and re-layouts: 77.2 us -> 8.13 us
  starting transfers between devices: 102 us -> 33.9 us
  Pallas kernels: 0 us -> 35.3 us
  other arithmetic: 32.9 us -> 7.19 us
  matrix products: 24.8 us -> 0 us
  between operations: 14.7 us -> 0.89 us
  blocking collectives: 7.43 us -> 0 us
    all_gather x3 -> x0, waiting for transfers between devices: 178 us -> none  [the longest x1 148 us: local(): lax.all_gather(lru_weight, 'ctx', axis=0, tiled=True)]
    ppermute x12 -> x26, starting transfers between devices: 102 us -> 33.9 us  [the longest x17 31 us: rotated(): lax.ppermute(value, axis, [(s, (s - steps) % count) for s in range(count)])]
    slice x54 -> x0, local copies, waits for them, and re-layouts: 61 us -> none  [the longest x52 61 us: local(): lax.associative_scan(chain_link, (keep_factor, driven), axis=0)]
    ppermute x12 -> x26, waiting for transfers between devices: 82.1 us -> 121 us  [the longest x17 92.1 us: rotated(): lax.ppermute(value, axis, [(s, (s - steps) % count) for s in range(count)])]
    pallas_call x0 -> x6, Pallas kernels: none -> 35.3 us  [the longest x2 16 us: attend(): pl.pallas_call(functools.partial(attend_kernel, nctx, back, steps, shard)...]
    reduce_scatter x1 -> x0, waiting for transfers between devices: 33.9 us -> none  [local(): lax.psum_scatter(head_part.astype(jnp.bfloat16), 'mp', scatter_dimension=...]
    dot_general x5 -> x0, matrix products: 20.1 us -> none  [the longest x1 7.07 us: local(): jnp.dot(attended, lax.all_gather(out_weight, 'ctx', axis=1, tiled=True),...]
    add x33 -> x0, other arithmetic: 16.1 us -> none  [the longest x13 13.8 us: chain_link(): return (former[0] * latter[0], latter[0] * former[1] + latter[1])]
  transfers between devices with their start and end apart: 16 -> 26, of which waited for: 16 -> 13; matrix products, arithmetic and copies ran while one was open for 3% -> 4% of each run, Pallas kernels for 0% -> 14%
where the time goes in v1:
time: 207 us; the launch traced here: 206 us
  waiting for transfers between devices  121 us (58%)
  Pallas kernels  35.3 us (17%)
  starting transfers between devices  33.9 us (16%)
  local copies, waits for them, and re-layouts  8.13 us (4%)
  other arithmetic  7.19 us (3%)
    ppermute x17, waiting for transfers between devices, rotated(): lax.ppermute(value, axis, [(s, (s - steps) % count) for s in range(count)])  92.1 us
    ppermute x17, starting transfers between devices, rotated(): lax.ppermute(value, axis, [(s, (s - steps) % count) for s in range(count)])  31 us
    ppermute x9, waiting for transfers between devices, swapped(): return lax.ppermute(value, axis, [(s, s ^ flip) for s in range(count)])  29 us
    pallas_call x2, Pallas kernels, attend(): pl.pallas_call(functools.partial(attend_kernel, nctx, back, steps, shard)...  16 us
    pallas_call x2, Pallas kernels, project(): pl.pallas_call(functools.partial(project_kernel, jobs, len(halves), shard...  10.2 us
    pallas_call x1, Pallas kernels, recur(): pl.pallas_call(functools.partial(recur_kernel, features), grid=(channels...  6.79 us
    unnamed x45, local copies, waits for them, and re-layouts  5.32 us
  transfers between devices with their start and end apart: 26, of which 13 were waited for; matrix products, arithmetic and copies ran while one was open for 4% of the time, Pallas kernels for 14%

profile of v1, /device:TPU:0, one launch (start us, length us, event | category | flops | bytes accessed | tf_op | source)
XLA Modules:
  0.0 206.4 jit_solution(6363002107223623511)
XLA Ops:
  0.6 5.1 %collective-permute-start.2 = (bf16[64,512]{1,0:T(8,128)(2,1)}, bf16[64,512]{1,0:T(8,128)(2,1)S(1)}, u32[]{:S(2)}, u32[]{:S(2)}) collective-permute-start(bf16[64,512]{1,0:T(8,128)(2,1)} %param.14), channel_id=1, source_target_pairs={{0,12},{4,0},{8,4},{12,8},{1,13},{5,1},{9,5},{13,9},{2,14},{6,2},{... | collective-permute-start | bytes 196616 | tf_op jit(solution)/shard_map/ppermute | solution.py:169
  5.8 1.0 collective-permute-start.4
  6.8 0.9 constant_dynamic-update-slice_fusion.3
  7.7 0.9 collective-permute-done.2
  8.6 3.9 %collective-permute-done.3 = bf16[64,512]{1,0:T(8,128)(2,1)S(1)} collective-permute-done((bf16[64,512]{1,0:T(8,128)(2,1)}, bf16[64,512]{1,0:T(8,128)(2,1)S(1)}, u32[]{:S(2)}, u32[]{:S(2)}) %collective-permute-start.3) | collective-permute-done | bytes 65568 | tf_op jit(solution)/shard_map/ppermute | solution.py:169
  12.5 0.0 copy-start.12
  12.5 1.6 collective-permute-start.6
  14.0 1.7 collective-permute-start.12
  15.8 0.7 collective-permute-start.13
  16.5 4.1 %collective-permute-done.6.refs_2_ = bf16[256,512]{1,0:T(8,128)(2,1)S(1)} collective-permute-done((bf16[256,512]{1,0:T(8,128)(2,1)S(1)}, bf16[256,512]{1,0:T(8,128)(2,1)S(1)}, u32[]{:S(2)}, u32[]{:S(2)}) %collective-permute-start.6) | collective-permute-done | bytes 262176 | tf_op jit(solution)/shard_map/ppermute | solution.py:174
  20.6 0.2 collective-permute-start
  20.8 1.8 constant_dynamic-slice_fusion
  22.6 1.3 collective-permute-start.14
  23.9 1.9 collective-permute-start.15
  25.8 1.3 convert_reduce_fusion.1
  27.1 1.8 pad_add_fusion.scal
  28.9 2.3 %assemble.1.refs_4_ = bf16[1024,512]{1,0:T(8,128)(2,1)} custom-call(s32[4]{0:T(128)} %pad_add_fusion.scal, bf16[256,512]{1,0:T(8,128)(2,1)} %copy-done.12, bf16[256,512]{1,0:T(8,128)(2,1)} %copy-done.14, bf16[256,512]{1,0:T(8,128)(2,1)} %copy-done.13, bf16[256,512]{1,0:T(8,128)(2,1)} %copy-done.15), custom_call_target="tpu_custom_call" | custom-call | tf_op jit(solution)/shard_map/assemble/pallas_call | solution.py:195
  31.2 38.5 %collective-permute-done.14.refs_2_ = bf16[64,1024]{1,0:T(8,128)(2,1)S(1)} collective-permute-done((bf16[64,1024]{1,0:T(8,128)(2,1)S(1)}, bf16[64,1024]{1,0:T(8,128)(2,1)S(1)}, u32[]{:S(2)}, u32[]{:S(2)}) %collective-permute-start.14) | collective-permute-done | bytes 131104 | tf_op jit(solution)/shard_map/ppermute | solution.py:169
  69.7 0.0 copy-start.7
  69.7 0.6 copy-done.16
  70.3 0.1 copy-done.17
  70.4 0.1 copy-done.7
  70.5 0.8 copy-done.8
  71.3 8.0 %attend.3 = (bf16[512,512]{1,0:T(8,128)(2,1)}, bf16[512,512]{1,0:T(8,128)(2,1)}) custom-call(s32[4]{0:T(128)} %pad_add_fusion.scal, bf16[256,1024]{1,0:T(8,128)(2,1)} %copy-done.7, bf16[256,1024]{1,0:T(8,128)(2,1)} %copy-done.8, bf16[64,1024]{1,0:T(8,128)(2,1)} %copy-done.16, bf16[64,1024]{1,0:T(8,128)(2,1)} %copy-done.17, ...), custom_call_target="tpu_custom_call" | custom-call | tf_op jit(solution)/shard_map/attend/pallas_call | solution.py:250
  79.3 0.0 collective-permute-start.1
  79.3 5.9 %collective-permute-done.1.refs_3_ = bf16[64,1024]{1,0:T(8,128)(2,1)S(1)} collective-permute-done((bf16[64,1024]{1,0:T(8,128)(2,1)S(1)}, bf16[64,1024]{1,0:T(8,128)(2,1)S(1)}, u32[]{:S(2)}, u32[]{:S(2)}) %collective-permute-start.1) | collective-permute-done | bytes 131104 | tf_op jit(solution)/shard_map/ppermute | solution.py:169
  85.2 0.6 copy-done.18
  85.9 0.2 copy-done.6
  86.0 8.0 %attend.2 = (bf16[512,512]{1,0:T(8,128)(2,1)}, bf16[512,512]{1,0:T(8,128)(2,1)}) custom-call(s32[4]{0:T(128)} %pad_add_fusion.scal, bf16[256,1024]{1,0:T(8,128)(2,1)} %refs_0_.1, bf16[256,1024]{1,0:T(8,128)(2,1)} %copy-done.6, bf16[64,1024]{1,0:T(8,128)(2,1)} %get-tuple-element.38.refs_2_, bf16[64,1024]{1,0:T(8,128)(2,1)} %copy-done.18, ...), custom_call_target="tpu_custom_call" | custom-call | tf_op jit(solution)/shard_map/attend/pallas_call | solution.py:250
  94.1 0.1 add_convert_fusion.2
  94.2 0.6 collective-permute-start.17
  94.8 1.4 collective-permute-done.8
  96.2 1.2 add_convert_fusion.4
  97.3 0.6 collective-permute-start.9
  97.9 11.1 %collective-permute-done.17 = bf16[512,512]{1,0:T(8,128)(2,1)S(1)} collective-permute-done((bf16[512,512]{1,0:T(8,128)(2,1)S(1)}, bf16[512,512]{1,0:T(8,128)(2,1)S(1)}, u32[]{:S(2)}, u32[]{:S(2)}) %collective-permute-start.17) | collective-permute-done | bytes 524320 | tf_op jit(solution)/shard_map/ppermute | solution.py:174
  109.1 0.1 add_convert_fusion.1.refs_2_
  109.2 0.1 collective-permute-start.18
  109.3 10.5 %collective-permute-done.9 = bf16[512,512]{1,0:T(8,128)(2,1)S(1)} collective-permute-done((bf16[512,512]{1,0:T(8,128)(2,1)S(1)}, bf16[512,512]{1,0:T(8,128)(2,1)S(1)}, u32[]{:S(2)}, u32[]{:S(2)}) %collective-permute-start.9) | collective-permute-done | bytes 524320 | tf_op jit(solution)/shard_map/ppermute | solution.py:174
  119.8 0.1 add_convert_fusion.3.refs_0_
  120.0 0.0 copy-start
  120.0 0.1 collective-permute-start.10
  120.1 1.9 collective-permute-done.10.refs_1_
  122.0 0.8 copy-done.5
  122.7 5.7 %project.3 = (bf16[272,1024]{1,0:T(8,128)(2,1)}, bf16[64,1024]{1,0:T(8,128)(2,1)}, bf16[272,1024]{1,0:T(8,128)(2,1)}, bf16[64,1024]{1,0:T(8,128)(2,1)}, bf16[16,1024]{1,0:T(8,128)(2,1)}) custom-call(s32[4]{0:T(128)} %pad_add_fusion.scal, bf16[512,512]{1,0:T(8,128)(2,1)} %copy-done, bf16[512,512]{1,0:T(8,128)(2,1)} %copy-done.5, bf16[512,512]{1,0:T(8,128)(2,1)} %copy-done.4, ...), custom_call_target="tpu_custom_call" | custom-call | tf_op jit(solution)/shard_map/project/pallas_call | solution.py:334
  128.5 0.1 collective-permute-start.22
  128.6 2.1 %collective-permute-start.23 = (bf16[272,1024]{1,0:T(8,128)(2,1)}, bf16[272,1024]{1,0:T(8,128)(2,1)S(1)}, u32[]{:S(2)}, u32[]{:S(2)}) collective-permute-start(bf16[272,1024]{1,0:T(8,128)(2,1)} %get-tuple-element.29), channel_id=1, source_target_pairs={{0,12},{4,0},{8,4},{12,8},{1,13},{5,1},{9,5},{13,9},{2,14},{6,2},{... | collective-permute-start | bytes 1671176 | tf_op jit(solution)/shard_map/ppermute | solution.py:169
  130.7 4.5 %project.2 = (bf16[256,1024]{1,0:T(8,128)(2,1)}, bf16[64,1024]{1,0:T(8,128)(2,1)}, bf16[272,1024]{1,0:T(8,128)(2,1)}, bf16[64,1024]{1,0:T(8,128)(2,1)}) custom-call(s32[4]{0:T(128)} %pad_add_fusion.scal, bf16[512,512]{1,0:T(8,128)(2,1)} %copy-done, bf16[512,512]{1,0:T(8,128)(2,1)} %copy-done.5, f32[1,4096]{1,0:T(1,128)} %bitcast.10, bf16[1024,1024]{1,0:T(8,128)(2,1)} %refs_5_.5), custom_call_target="tpu_custom_call" | custom-call | tf_op jit(solution)/shard_map/project/pallas_call | solution.py:334
  135.2 0.5 collective-permute-start.21
  135.7 2.0 collective-permute-start.11
  137.7 1.9 collective-permute-start.19
  139.6 0.9 constant_dynamic-update-slice_fusion.7
  140.5 30.6 %collective-permute-done.11 = bf16[64,1024]{1,0:T(8,128)(2,1)S(1)} collective-permute-done((bf16[64,1024]{1,0:T(8,128)(2,1)}, bf16[64,1024]{1,0:T(8,128)(2,1)S(1)}, u32[]{:S(2)}, u32[]{:S(2)}) %collective-permute-start.11) | collective-permute-done | bytes 131104 | tf_op jit(solution)/shard_map/ppermute | solution.py:169
  171.1 7.2 %collective-permute-start.20 = (bf16[64,1024]{1,0:T(8,128)(2,1)S(1)}, bf16[64,1024]{1,0:T(8,128)(2,1)S(1)}, u32[]{:S(2)}, u32[]{:S(2)}) collective-permute-start(bf16[64,1024]{1,0:T(8,128)(2,1)S(1)} %copy-done.19), channel_id=1, source_target_pairs={{0,12},{4,0},{8,4},{12,8},{1,13},{5,1},{9,5},{13,9},{2,14},{6,2},{... | collective-permute-start | bytes 393224 | tf_op jit(solution)/shard_map/ppermute | solution.py:169
  178.3 9.7 %collective-permute-done.19 = bf16[64,1024]{1,0:T(8,128)(2,1)S(1)} collective-permute-done((bf16[64,1024]{1,0:T(8,128)(2,1)S(1)}, bf16[64,1024]{1,0:T(8,128)(2,1)S(1)}, u32[]{:S(2)}, u32[]{:S(2)}) %collective-permute-start.19) | collective-permute-done | bytes 131104 | tf_op jit(solution)/shard_map/ppermute | solution.py:169
  188.1 0.8 copy-done.1
  188.9 0.2 copy-done.2
  189.1 0.2 copy-done.3
  189.3 6.8 %recur.1 = (f32[256,1024]{1,0:T(8,128)}, f32[256,1024]{1,0:T(8,128)}, f32[8,1024]{1,0:T(8,128)}) custom-call(s32[4]{0:T(128)} %pad_add_fusion.scal, bf16[256,1024]{1,0:T(8,128)(2,1)} %get-tuple-element.26.refs_0_, bf16[272,1024]{1,0:T(8,128)(2,1)} %copy-done.3, bf16[272,1024]{1,0:T(8,128)(2,1)} %copy-done.1, bf16[272,1024]{1,0:T(8,128)(2,1)} %copy-done.2, ...), custom_call_target="tpu_custom_call" | custom-call | tf_op jit(solution)/shard_map/recur/pallas_call | solution.py:431
  196.0 1.8 collective-permute-start.24
  197.8 3.4 %collective-permute-start.25 = (f32[8,1024]{1,0:T(8,128)}, f32[8,1024]{1,0:T(8,128)S(1)}, u32[]{:S(2)}, u32[]{:S(2)}) collective-permute-start(f32[8,1024]{1,0:T(8,128)} %get-tuple-element.33), channel_id=1, source_target_pairs={{0,8},{4,12},{8,0},{12,4},{1,9},{5,13},{9,1},{13,5},{2,10},{6,14},... | collective-permute-start | bytes 98312 | tf_op jit(solution)/shard_map/ppermute | solution.py:169
  201.2 0.0 copy-start.11
  201.2 1.6 collective-permute-done.24
  202.9 1.0 collective-permute-done.25
  203.9 2.5 %add_convert_fusion = bf16[256,1024]{1,0:T(8,128)(2,1)} fusion(f32[256,1024]{1,0:T(8,128)} %get-tuple-element.31, f32[256,1024]{1,0:T(8,128)} %get-tuple-element.32, f32[1024]{0:T(1024)S(1)} %bitcast.11), kind=kLoop, calls=%fused_computation | loop fusion | flops 786432 | bytes 2625536 | tf_op jit(solution)/shard_map/convert_element_type | solution.py:557
  (54 shorter events, 0.2 us)
Async XLA Ops:
  0.6 7.9 %collective-permute-start.2 = (bf16[64,512]{1,0:T(8,128)(2,1)}, bf16[64,512]{1,0:T(8,128)(2,1)S(1)}, u32[]{:S(2)}, u32[]{:S(2)}) collective-permute-start(bf16[64,512]{1,0:T(8,128)(2,1)} %param.14), channel_id=1, source_target_pairs={{0,12},{4,0},{8,4},{12,8},{1,13},{5,1},{9,5},{13,9},{2,14},{6,2},{... | collective-permute-start | bytes 196616 | tf_op jit(solution)/shard_map/ppermute | solution.py:169
  5.8 6.7 %collective-permute-start.3 = (bf16[64,512]{1,0:T(8,128)(2,1)}, bf16[64,512]{1,0:T(8,128)(2,1)S(1)}, u32[]{:S(2)}, u32[]{:S(2)}) collective-permute-start(bf16[64,512]{1,0:T(8,128)(2,1)} %param.14), channel_id=1, source_target_pairs={{0,8},{4,12},{8,0},{12,4},{1,9},{5,13},{9,1},{13,5},{2,10},{6,14},... | collective-permute-start | bytes 196616 | tf_op jit(solution)/shard_map/ppermute | solution.py:169
  5.8 6.7 %collective-permute-start.4 = (bf16[64,512]{1,0:T(8,128)(2,1)}, bf16[64,512]{1,0:T(8,128)(2,1)S(1)}, u32[]{:S(2)}, u32[]{:S(2)}) collective-permute-start(bf16[64,512]{1,0:T(8,128)(2,1)} %param.14), channel_id=1, source_target_pairs={{0,4},{4,8},{8,12},{12,0},{1,5},{5,9},{9,13},{13,1},{2,6},{6,10},{... | collective-permute-start | bytes 196616 | tf_op jit(solution)/shard_map/ppermute | solution.py:169
  12.5 16.4 %copy-start.12 = (bf16[256,512]{1,0:T(8,128)(2,1)}, bf16[256,512]{1,0:T(8,128)(2,1)S(1)}, u32[]{:S(2)}) copy-start(bf16[256,512]{1,0:T(8,128)(2,1)S(1)} %constant_dynamic-update-slice_fusion.refs_0_) | copy-start | bytes 786436
  12.5 8.1 %collective-permute-start.6 = (bf16[256,512]{1,0:T(8,128)(2,1)S(1)}, bf16[256,512]{1,0:T(8,128)(2,1)S(1)}, u32[]{:S(2)}, u32[]{:S(2)}) collective-permute-start(bf16[256,512]{1,0:T(8,128)(2,1)S(1)} %constant_dynamic-update-slice_fusion.refs_0_), channel_id=1, source_target_pairs={{0,2},{1,3},{2,0},{3,1},{4,6},{5,7},{6,4},{7,5},{8,10},{9,11},{10,... | collective-permute-start | bytes 786440 | tf_op jit(solution)/shard_map/ppermute | solution.py:174
  14.0 55.6 %collective-permute-start.12 = (bf16[256,1024]{1,0:T(8,128)(2,1)}, bf16[256,1024]{1,0:T(8,128)(2,1)S(1)}, u32[]{:S(2)}, u32[]{:S(2)}) collective-permute-start(bf16[256,1024]{1,0:T(8,128)(2,1)} %refs_0_.1), channel_id=1, source_target_pairs={{0,8},{4,12},{8,0},{12,4},{1,9},{5,13},{9,1},{13,5},{2,10},{6,14},... | collective-permute-start | bytes 1572872 | tf_op jit(solution)/shard_map/ppermute | solution.py:169
  15.8 53.9 %collective-permute-start.13 = (bf16[256,1024]{1,0:T(8,128)(2,1)}, bf16[256,1024]{1,0:T(8,128)(2,1)S(1)}, u32[]{:S(2)}, u32[]{:S(2)}) collective-permute-start(bf16[256,1024]{1,0:T(8,128)(2,1)} %refs_0_.1), channel_id=1, source_target_pairs={{0,4},{4,8},{8,12},{12,0},{1,5},{5,9},{9,13},{13,1},{2,6},{6,10},{... | collective-permute-start | bytes 1572872 | tf_op jit(solution)/shard_map/ppermute | solution.py:169
  16.5 6.1 %collective-permute-start.5 = (bf16[256,512]{1,0:T(8,128)(2,1)S(1)}, bf16[256,512]{1,0:T(8,128)(2,1)S(1)}, u32[]{:S(2)}, u32[]{:S(2)}) collective-permute-start(bf16[256,512]{1,0:T(8,128)(2,1)S(1)} %constant_dynamic-update-slice_fusion.refs_0_), channel_id=1, source_target_pairs={{0,1},{1,0},{2,3},{3,2},{4,5},{5,4},{6,7},{7,6},{8,9},{9,8},{10,11... | collective-permute-start | bytes 786440 | tf_op jit(solution)/shard_map/ppermute | solution.py:174
  20.6 8.3 %copy-start.13 = (bf16[256,512]{1,0:T(8,128)(2,1)}, bf16[256,512]{1,0:T(8,128)(2,1)S(1)}, u32[]{:S(2)}) copy-start(bf16[256,512]{1,0:T(8,128)(2,1)S(1)} %collective-permute-done.6.refs_2_) | copy-start | bytes 786436
  20.6 3.3 %collective-permute-start.7 = (bf16[256,512]{1,0:T(8,128)(2,1)S(1)}, bf16[256,512]{1,0:T(8,128)(2,1)S(1)}, u32[]{:S(2)}, u32[]{:S(2)}) collective-permute-start(bf16[256,512]{1,0:T(8,128)(2,1)S(1)} %collective-permute-done.6.refs_2_), channel_id=1, source_target_pairs={{0,1},{1,0},{2,3},{3,2},{4,5},{5,4},{6,7},{7,6},{8,9},{9,8},{10,11... | collective-permute-start | bytes 786440 | tf_op jit(solution)/shard_map/ppermute | solution.py:174
  20.6 64.6 %collective-permute-start = (bf16[256,1024]{1,0:T(8,128)(2,1)}, bf16[256,1024]{1,0:T(8,128)(2,1)S(1)}, u32[]{:S(2)}, u32[]{:S(2)}) collective-permute-start(bf16[256,1024]{1,0:T(8,128)(2,1)} %refs_0_.1), channel_id=1, source_target_pairs={{0,12},{4,0},{8,4},{12,8},{1,13},{5,1},{9,5},{13,9},{2,14},{6,2},{... | collective-permute-start | bytes 1572872 | tf_op jit(solution)/shard_map/ppermute | solution.py:169
  22.6 6.3 %copy-start.14 = (bf16[256,512]{1,0:T(8,128)(2,1)}, bf16[256,512]{1,0:T(8,128)(2,1)S(1)}, u32[]{:S(2)}) copy-start(bf16[256,512]{1,0:T(8,128)(2,1)S(1)} %collective-permute-done.5.refs_1_) | copy-start | bytes 786436
  22.6 47.0 %collective-permute-start.14 = (bf16[64,1024]{1,0:T(8,128)(2,1)S(1)}, bf16[64,1024]{1,0:T(8,128)(2,1)S(1)}, u32[]{:S(2)}, u32[]{:S(2)}) collective-permute-start(bf16[64,1024]{1,0:T(8,128)(2,1)S(1)} %get-tuple-element.39), channel_id=1, source_target_pairs={{0,8},{4,12},{8,0},{12,4},{1,9},{5,13},{9,1},{13,5},{2,10},{6,14},... | collective-permute-start | bytes 393224 | tf_op jit(solution)/shard_map/ppermute | solution.py:169
  23.9 5.0 %copy-start.15 = (bf16[256,512]{1,0:T(8,128)(2,1)}, bf16[256,512]{1,0:T(8,128)(2,1)S(1)}, u32[]{:S(2)}) copy-start(bf16[256,512]{1,0:T(8,128)(2,1)S(1)} %collective-permute-done.7.refs_3_) | copy-start | bytes 786436
  23.9 45.8 %collective-permute-start.15 = (bf16[64,1024]{1,0:T(8,128)(2,1)S(1)}, bf16[64,1024]{1,0:T(8,128)(2,1)S(1)}, u32[]{:S(2)}, u32[]{:S(2)}) collective-permute-start(bf16[64,1024]{1,0:T(8,128)(2,1)S(1)} %get-tuple-element.36), channel_id=1, source_target_pairs={{0,4},{4,8},{8,12},{12,0},{1,5},{5,9},{9,13},{13,1},{2,6},{6,10},{... | collective-permute-start | bytes 393224 | tf_op jit(solution)/shard_map/ppermute | solution.py:169
  69.7 0.6 copy-start.16
  69.7 0.7 copy-start.17
  69.7 0.9 copy-start.7
  70.5 0.8 copy-start.8
  79.3 14.7 %collective-permute-start.16 = (bf16[512,512]{1,0:T(8,128)(2,1)}, bf16[512,512]{1,0:T(8,128)(2,1)S(1)}, u32[]{:S(2)}, u32[]{:S(2)}) collective-permute-start(bf16[512,512]{1,0:T(8,128)(2,1)} %get-tuple-element.23), channel_id=1, source_target_pairs={{0,1},{1,0},{2,3},{3,2},{4,5},{5,4},{6,7},{7,6},{8,9},{9,8},{10,11... | collective-permute-start | bytes 1572872 | tf_op jit(solution)/shard_map/ppermute | solution.py:174
  79.3 5.9 %collective-permute-start.1 = (bf16[64,1024]{1,0:T(8,128)(2,1)S(1)}, bf16[64,1024]{1,0:T(8,128)(2,1)S(1)}, u32[]{:S(2)}, u32[]{:S(2)}) collective-permute-start(bf16[64,1024]{1,0:T(8,128)(2,1)S(1)} %get-tuple-element.37), channel_id=1, source_target_pairs={{0,12},{4,0},{8,4},{12,8},{1,13},{5,1},{9,5},{13,9},{2,14},{6,2},{... | collective-permute-start | bytes 393224 | tf_op jit(solution)/shard_map/ppermute | solution.py:169
  85.2 0.7 copy-start.18
  85.2 0.8 copy-start.6
  86.0 8.0 %copy-start.9 = (bf16[512,512]{1,0:T(8,128)(2,1)S(1)}, bf16[512,512]{1,0:T(8,128)(2,1)}, u32[]{:S(2)}) copy-start(bf16[512,512]{1,0:T(8,128)(2,1)} %get-tuple-element.22) | copy-start | bytes 1572868
  94.0 2.1 %collective-permute-start.8 = (bf16[512,512]{1,0:T(8,128)(2,1)}, bf16[512,512]{1,0:T(8,128)(2,1)S(1)}, u32[]{:S(2)}, u32[]{:S(2)}) collective-permute-start(bf16[512,512]{1,0:T(8,128)(2,1)} %get-tuple-element.19), channel_id=1, source_target_pairs={{0,1},{1,0},{2,3},{3,2},{4,5},{5,4},{6,7},{7,6},{8,9},{9,8},{10,11... | collective-permute-start | bytes 1572872 | tf_op jit(solution)/shard_map/ppermute | solution.py:174
  94.2 14.9 %collective-permute-start.17 = (bf16[512,512]{1,0:T(8,128)(2,1)S(1)}, bf16[512,512]{1,0:T(8,128)(2,1)S(1)}, u32[]{:S(2)}, u32[]{:S(2)}) collective-permute-start(bf16[512,512]{1,0:T(8,128)(2,1)S(1)} %add_convert_fusion.2), channel_id=1, source_target_pairs={{0,2},{1,3},{2,0},{3,1},{4,6},{5,7},{6,4},{7,5},{8,10},{9,11},{10,... | collective-permute-start | bytes 1572872 | tf_op jit(solution)/shard_map/ppermute | solution.py:174
  97.3 22.5 %collective-permute-start.9 = (bf16[512,512]{1,0:T(8,128)(2,1)S(1)}, bf16[512,512]{1,0:T(8,128)(2,1)S(1)}, u32[]{:S(2)}, u32[]{:S(2)}) collective-permute-start(bf16[512,512]{1,0:T(8,128)(2,1)S(1)} %add_convert_fusion.4), channel_id=1, source_target_pairs={{0,2},{1,3},{2,0},{3,1},{4,6},{5,7},{6,4},{7,5},{8,10},{9,11},{10,... | collective-permute-start | bytes 1572872 | tf_op jit(solution)/shard_map/ppermute | solution.py:174
  109.2 12.8 %copy-start.4 = (bf16[512,512]{1,0:T(8,128)(2,1)}, bf16[512,512]{1,0:T(8,128)(2,1)S(1)}, u32[]{:S(2)}) copy-start(bf16[512,512]{1,0:T(8,128)(2,1)S(1)} %add_convert_fusion.1.refs_2_) | copy-start | bytes 1572868
  109.2 10.8 %collective-permute-start.18 = (bf16[512,512]{1,0:T(8,128)(2,1)S(1)}, bf16[512,512]{1,0:T(8,128)(2,1)S(1)}, u32[]{:S(2)}, u32[]{:S(2)}) collective-permute-start(bf16[512,512]{1,0:T(8,128)(2,1)S(1)} %add_convert_fusion.1.refs_2_), channel_id=1, source_target_pairs={{0,1},{1,0},{2,3},{3,2},{4,5},{5,4},{6,7},{7,6},{8,9},{9,8},{10,11... | collective-permute-start | bytes 1572872 | tf_op jit(solution)/shard_map/ppermute | solution.py:174
  120.0 2.0 copy-start
  120.0 2.0 collective-permute-start.10
  120.1 1.9 copy-start.10
  121.9 0.8 copy-start.5
  128.5 9.2 %copy-start.20 = (bf16[64,1024]{1,0:T(8,128)(2,1)S(1)}, bf16[64,1024]{1,0:T(8,128)(2,1)}, u32[]{:S(2)}) copy-start(bf16[64,1024]{1,0:T(8,128)(2,1)} %get-tuple-element.24) | copy-start | bytes 393220
  128.5 42.7 %copy-start.19 = (bf16[64,1024]{1,0:T(8,128)(2,1)S(1)}, bf16[64,1024]{1,0:T(8,128)(2,1)}, u32[]{:S(2)}) copy-start(bf16[64,1024]{1,0:T(8,128)(2,1)} %get-tuple-element.25) | copy-start | bytes 393220
  128.5 59.6 %collective-permute-start.22 = (bf16[272,1024]{1,0:T(8,128)(2,1)}, bf16[272,1024]{1,0:T(8,128)(2,1)S(1)}, u32[]{:S(2)}, u32[]{:S(2)}) collective-permute-start(bf16[272,1024]{1,0:T(8,128)(2,1)} %get-tuple-element.28), channel_id=1, source_target_pairs={{0,8},{4,12},{8,0},{12,4},{1,9},{5,13},{9,1},{13,5},{2,10},{6,14},... | collective-permute-start | bytes 1671176 | tf_op jit(solution)/shard_map/ppermute | solution.py:169
  128.6 59.5 %collective-permute-start.23 = (bf16[272,1024]{1,0:T(8,128)(2,1)}, bf16[272,1024]{1,0:T(8,128)(2,1)S(1)}, u32[]{:S(2)}, u32[]{:S(2)}) collective-permute-start(bf16[272,1024]{1,0:T(8,128)(2,1)} %get-tuple-element.29), channel_id=1, source_target_pairs={{0,12},{4,0},{8,4},{12,8},{1,13},{5,1},{9,5},{13,9},{2,14},{6,2},{... | collective-permute-start | bytes 1671176 | tf_op jit(solution)/shard_map/ppermute | solution.py:169
  135.2 52.9 %collective-permute-start.21 = (bf16[272,1024]{1,0:T(8,128)(2,1)}, bf16[272,1024]{1,0:T(8,128)(2,1)S(1)}, u32[]{:S(2)}, u32[]{:S(2)}) collective-permute-start(bf16[272,1024]{1,0:T(8,128)(2,1)} %get-tuple-element.27), channel_id=1, source_target_pairs={{0,4},{4,8},{8,12},{12,0},{1,5},{5,9},{9,13},{13,1},{2,6},{6,10},{... | collective-permute-start | bytes 1671176 | tf_op jit(solution)/shard_map/ppermute | solution.py:169
  135.7 35.5 %collective-permute-start.11 = (bf16[64,1024]{1,0:T(8,128)(2,1)}, bf16[64,1024]{1,0:T(8,128)(2,1)S(1)}, u32[]{:S(2)}, u32[]{:S(2)}) collective-permute-start(bf16[64,1024]{1,0:T(8,128)(2,1)} %get-tuple-element.21), channel_id=1, source_target_pairs={{0,4},{4,8},{8,12},{12,0},{1,5},{5,9},{9,13},{13,1},{2,6},{6,10},{... | collective-permute-start | bytes 393224 | tf_op jit(solution)/shard_map/ppermute | solution.py:169
  137.7 50.3 %collective-permute-start.19 = (bf16[64,1024]{1,0:T(8,128)(2,1)S(1)}, bf16[64,1024]{1,0:T(8,128)(2,1)S(1)}, u32[]{:S(2)}, u32[]{:S(2)}) collective-permute-start(bf16[64,1024]{1,0:T(8,128)(2,1)S(1)} %copy-done.20), channel_id=1, source_target_pairs={{0,8},{4,12},{8,0},{12,4},{1,9},{5,13},{9,1},{13,5},{2,10},{6,14},... | collective-permute-start | bytes 393224 | tf_op jit(solution)/shard_map/ppermute | solution.py:169
  171.1 30.1 %collective-permute-start.20 = (bf16[64,1024]{1,0:T(8,128)(2,1)S(1)}, bf16[64,1024]{1,0:T(8,128)(2,1)S(1)}, u32[]{:S(2)}, u32[]{:S(2)}) collective-permute-start(bf16[64,1024]{1,0:T(8,128)(2,1)S(1)} %copy-done.19), channel_id=1, source_target_pairs={{0,12},{4,0},{8,4},{12,8},{1,13},{5,1},{9,5},{13,9},{2,14},{6,2},{... | collective-permute-start | bytes 393224 | tf_op jit(solution)/shard_map/ppermute | solution.py:169
  188.1 0.8 copy-start.1
  188.1 1.0 copy-start.2
  188.1 1.1 copy-start.3
  196.0 6.8 %collective-permute-start.24 = (f32[8,1024]{1,0:T(8,128)}, f32[8,1024]{1,0:T(8,128)S(1)}, u32[]{:S(2)}, u32[]{:S(2)}) collective-permute-start(f32[8,1024]{1,0:T(8,128)} %get-tuple-element.33), channel_id=1, source_target_pairs={{0,4},{4,8},{8,12},{12,0},{1,5},{5,9},{9,13},{13,1},{2,6},{6,10},{... | collective-permute-start | bytes 98312 | tf_op jit(solution)/shard_map/ppermute | solution.py:169
  197.8 6.0 %collective-permute-start.25 = (f32[8,1024]{1,0:T(8,128)}, f32[8,1024]{1,0:T(8,128)S(1)}, u32[]{:S(2)}, u32[]{:S(2)}) collective-permute-start(f32[8,1024]{1,0:T(8,128)} %get-tuple-element.33), channel_id=1, source_target_pairs={{0,8},{4,12},{8,0},{12,4},{1,9},{5,13},{9,1},{13,5},{2,10},{6,14},... | collective-permute-start | bytes 98312 | tf_op jit(solution)/shard_map/ppermute | solution.py:169
  201.2 5.2 %copy-start.11 = (bf16[64,4096]{1,0:T(8,128)(2,1)}, bf16[64,4096]{1,0:T(8,128)(2,1)S(1)}, u32[]{:S(2)}) copy-start(bf16[64,4096]{1,0:T(8,128)(2,1)S(1)} %constant_dynamic-update-slice_fusion.4) | copy-start | bytes 1572868

commit v2 on v1

--- a/solution.py
+++ b/solution.py
@@ -76,7 +76,7 @@
     own_kv = lax.all_gather(keyvals, "mp", axis=0, tiled=True)
     earlier = []
     moving = own_kv
-    for offset in range(back_blocks):
+    for _ in range(back_blocks):
         moving = shifted_2(moving, "ctx", 1)
         earlier = [moving] + earlier
     keys_all = jnp.concatenate(earlier + [own_kv], axis=0)
@@ -178,6 +178,52 @@
     return jnp.where(pos >= high, high, jnp.where(pos >= low, low, 0))
 
 
+def pack_kernel(nctx, scal, queries, residual, own, *outs):
+    rows = queries.shape[0]
+    cols = own.shape[1]
+    for step in range(nctx):
+        block = lax.rem(scal[0] + nctx - step, nctx)
+        part = residual[:, pl.ds(pl.multiple_of(block * cols, cols), cols)]
+        if step:
+            outs[step - 1][0:rows, :] = queries[...]
+            outs[step - 1][rows:, :] = part
+        else:
+            own[...] = part
+
+
+def pack(scal, queries, residual, nctx):
+    rows, width = queries.shape
+    shard = residual.shape[0]
+    message = jax.ShapeDtypeStruct((rows + shard, width), BF16)
+    return pl.pallas_call(
+        functools.partial(pack_kernel, nctx),
+        out_shape=(jax.ShapeDtypeStruct((shard, width), BF16),) + (message,) * (nctx - 1),
+        in_specs=[SMEM, VMEM, VMEM],
+        out_specs=(VMEM,) * nctx,
+        name="pack",
+    )(scal, queries, residual)
+
+
+def join_kernel(nctx, scal, *refs):
+    out = refs[-1]
+    cols = refs[0].shape[1]
+    for step, part in enumerate(refs[:-1]):
+        block = lax.rem(scal[0] + nctx - step, nctx)
+        out[:, pl.ds(pl.multiple_of(block * cols, cols), cols)] = part[...]
+
+
+def join(scal, parts):
+    nctx = len(parts)
+    shard, cols = parts[0].shape
+    return pl.pallas_call(
+        functools.partial(join_kernel, nctx),
+        out_shape=jax.ShapeDtypeStruct((shard, nctx * cols), BF16),
+        in_specs=[SMEM] + [VMEM] * nctx,
+        out_specs=VMEM,
+        name="join",
+    )(scal, *parts)
+
+
 def assemble_kernel(rows, shard, nctx, scal, *refs):
     out = refs[-1]
     ctx_index, mp_index = scal[0], scal[1]
@@ -205,7 +251,7 @@
     count = len(steps)
     q_refs, resid_refs = refs[:count], refs[count : 2 * count]
     kv, weight, keep, send, att, acc = refs[2 * count :]
-    rows, width = q_refs[0].shape
+    rows, width = att.shape
     heads = width // HD
     half = weight.shape[1] // 2
     ctx_index, mp_index, low, high = scal[0], scal[1], scal[2], scal[3]
@@ -222,7 +268,7 @@
         kpos = first_key + lax.broadcasted_iota(jnp.int32, (1, window), 1)
         allowed = (kpos <= qpos) & (kpos >= start) & (qpos - kpos < WIN)
         for h in range(heads):
-            query = q_refs[j][:, h * HD : (h + 1) * HD]
+            query = q_refs[j][0:rows, h * HD : (h + 1) * HD]
             keys = kv[pl.ds(first_key, window), :HD]
             scores = lax.dot_general(
                 query, keys, (((1,), (1,)), ((), ())), preferred_element_type=F32
@@ -238,12 +284,13 @@
         for out, which in ((send, 1 - side), (keep, side)):
             cols = pl.ds(pl.multiple_of(which * half, half), half)
             acc[...] = jnp.dot(att[...], weight[:, cols], preferred_element_type=F32)
-            acc[own, :] += resid_refs[j][:, cols].astype(F32)
+            mine = resid_refs[j][resid_refs[j].shape[0] - shard :, cols]
+            acc[own, :] += mine.astype(F32)
             out[j * rows : (j + 1) * rows, :] = acc[...].astype(BF16)
 
 
 def attend(scal, queries, residuals, kv, weight, nctx, back, steps, shard):
-    rows, width = queries[0].shape
+    rows, width = kv.shape[0] // nctx, queries[0].shape[1]
     count = len(steps)
     half = weight.shape[1] // 2
     shape = jax.ShapeDtypeStruct((count * rows, half), BF16)
@@ -468,41 +515,38 @@
     nctx, nmp = lax.axis_size("ctx"), lax.axis_size("mp")
     ctx_index, mp_index = lax.axis_index("ctx"), lax.axis_index("mp")
     features = residual.shape[1]
-    cols = out_weight.shape[1]
     longest = tokens // 2
     back = -(-(min(WIN, longest) - 1) // rows)
     reach = min(nctx - 1, -(-longest // rows))
-    low = jnp.sum((segment_ids < 1).astype(jnp.int32))
-    high = jnp.sum((segment_ids < 2).astype(jnp.int32))
-    scal = jnp.stack([ctx_index, mp_index, low, high]).astype(jnp.int32)
-
-    own_kv = jnp.concatenate(
-        [keyvals] + [rotated(keyvals, "ctx", step) for step in range(1, nctx)], axis=0
-    )
-    pieces = {0: own_kv}
+    place = jnp.stack([ctx_index, mp_index]).astype(jnp.int32)
+
+    kv_parts = [keyvals]
+    for step in range(1, nctx):
+        kv_parts.append(rotated(keyvals, "ctx", step))
+    own_resid, *messages_out = pack(place, queries, residual, nctx)
+    visiting = [queries]
+    for step in range(1, nctx):
+        visiting.append(rotated(messages_out[step - 1], "ctx", step))
+    pieces = {0: jnp.concatenate(kv_parts, axis=0)}
     flip = nmp // 2
     while flip >= 1:
         for done in sorted(pieces):
             pieces[done | flip] = swapped(pieces[done], "mp", flip)
         flip //= 2
-    kv = assemble(scal, [pieces[e] for e in range(nmp)], rows, shard, nctx)
-
-    visiting = [queries] + [rotated(queries, "ctx", step) for step in range(1, nctx)]
-    resid_parts = []
-    for step in range(nctx):
-        first = lax.rem(ctx_index + nctx - step, nctx) * cols
-        part = lax.dynamic_slice_in_dim(residual, first, cols, axis=1)
-        resid_parts.append(rotated(part, "ctx", step) if step else part)
-
-    chunks = [tuple(range(i, min(i + 2, nctx))) for i in range(0, nctx, 2)]
+    kv = assemble(place, [pieces[e] for e in range(nmp)], rows, shard, nctx)
+    low = jnp.sum((segment_ids < 1).astype(jnp.int32))
+    high = jnp.sum((segment_ids < 2).astype(jnp.int32))
+    scal = jnp.stack([ctx_index, mp_index, low, high]).astype(jnp.int32)
+
+    chunks = [tuple(range(min(2, nctx)))] + [(step,) for step in range(2, nctx)]
     gain = norm_gain.reshape(1, features)
-    where_is, halves = {}, []
-    messages, lines, resid_rows = {}, {}, {}
-    for steps in chunks:
+    where_is, chunk_halves = {}, []
+    messages, resid_rows = {}, {}
+    for at, steps in enumerate(chunks):
         keep, send = attend(
             scal,
             [visiting[s] for s in steps],
-            [resid_parts[s] for s in steps],
+            [visiting[s] if s else own_resid for s in steps],
             kv,
             out_weight,
             nctx,
@@ -510,27 +554,42 @@
             steps,
             shard,
         )
-        mine = (keep.astype(F32) + swapped(send, "mp", 1).astype(F32)).astype(BF16)
+        other = swapped(send, "mp", 1)
+        mine = (keep.astype(F32) + other.astype(F32)).astype(BF16)
         flip = 2
         while flip < nmp:
-            mine = (mine.astype(F32) + swapped(mine, "mp", flip).astype(F32)).astype(BF16)
+            other = swapped(mine, "mp", flip)
+            mine = (mine.astype(F32) + other.astype(F32)).astype(BF16)
             flip *= 2
+        other = swapped(mine, "mp", 1)
         for j, s in enumerate(steps):
-            where_is[s] = (len(halves), j * rows, rows)
-        halves = halves + [mine, swapped(mine, "mp", 1)]
-        jobs = [(where_is[s], where_is[s - 1] if s else None) for s in steps]
-        if steps[-1] == nctx - 1:
-            jobs.append((None, where_is[nctx - 1] + where_is[0]))
-        outs = project(scal, halves, gain, lru_weight, jobs, shard)
+            where_is[s] = (at, j * rows, rows)
+        chunk_halves.append((mine, other))
+        ends = steps[-1] == nctx - 1
+        used = sorted({where_is[s][0] for s in steps} | {where_is[s - 1][0] for s in steps if s} | ({0} if ends else set()))
+        slot = {c: 2 * i for i, c in enumerate(used)}
+        held = [piece for c in used for piece in chunk_halves[c]]
+
+        def found(s):
+            c, first, length = where_is[s]
+            return (slot[c], first, length)
+
+        jobs = [(found(s), found(s - 1) if s else None) for s in steps]
+        if ends:
+            jobs.append((None, found(nctx - 1) + found(0)))
+        outs = project(scal, held, gain, lru_weight, jobs, shard)
         for j, s in enumerate(steps):
             messages[s], resid_rows[s] = outs[2 * j], outs[2 * j + 1]
-        if steps[-1] == nctx - 1:
+        if ends:
             own_line = outs[2 * len(steps)]
     mains, lines = [messages[0]], [(own_line, 0)]
     for step in range(1, nctx):
         got = rotated(messages[step], "ctx", -step)
         mains.append(got)
         lines.append((got, rows // TILE))
+    resid_parts = [resid_rows[0]]
+    for step in range(1, nctx):
+        resid_parts.append(rotated(resid_rows[step], "ctx", -step))
     local_state, cum_keep, last = recur(
         scal,
         mains,
@@ -544,22 +603,26 @@
         rows,
         features,
     )
+    before = []
+    for step in range(1, reach + 1):
+        before.append(rotated(last, "ctx", -step))
+    resid_out = join(place, resid_parts)
     incoming = jnp.zeros_like(last[0])
     for step in range(reach, 0, -1):
-        before = rotated(last, "ctx", -step)
-        incoming = jnp.where(ctx_index >= step, before[0] * incoming + before[1], 0.0)
+        piece = before[step - 1]
+        incoming = jnp.where(ctx_index >= step, piece[0] * incoming + piece[1], 0.0)
     states = local_state + cum_keep * incoming[None, :]
-    resid_out = jnp.zeros(residual.shape, BF16)
-    for step in range(nctx):
-        part = rotated(resid_rows[step], "ctx", -step) if step else resid_rows[step]
-        first = lax.rem(ctx_index + nctx - step, nctx) * cols
-        resid_out = lax.dynamic_update_slice_in_dim(resid_out, part, first, axis=1)
     return (resid_out, states.astype(BF16))
 
 
-def local(queries, keyvals, segment_ids, *rest):
-    near = segment_ids.shape[0] <= WIN and lax.axis_size("mp") % 2 == 0
-    return (local_near if near else local_wide)(queries, keyvals, segment_ids, *rest)
+def local(queries, keyvals, segment_ids, residual, out_weight, *rest):
+    near = (
+        segment_ids.shape[0] <= WIN
+        and lax.axis_size("mp") % 2 == 0
+        and queries.shape[1] == out_weight.shape[1]
+    )
+    form = local_near if near else local_wide
+    return form(queries, keyvals, segment_ids, residual, out_weight, *rest)
 
 
 def solution(mesh):

time: 207 us -> 181 us (0.87)
  waiting for transfers between devices: 121 us -> 63.7 us
  starting transfers between devices: 33.9 us -> 53.9 us
  Pallas kernels: 35.3 us -> 45.9 us
    ppermute x17 -> x14, waiting for transfers between devices: 92.1 us -> 43.5 us  [rotated(): lax.ppermute(value, axis, [(s, (s - steps) % count) for s in range(count)])]
    ppermute x17 -> x14, starting transfers between devices: 31 us -> 48.9 us  [rotated(): lax.ppermute(value, axis, [(s, (s - steps) % count) for s in range(count)])]
    ppermute x9 -> x12, waiting for transfers between devices: 29 us -> 20.2 us  [swapped(): return lax.ppermute(value, axis, [(s, s ^ flip) for s in range(count)])]
    pallas_call x0 -> x2, Pallas kernels: none -> 4.53 us  [the longest x1 2.59 us: pack(): pl.pallas_call(functools.partial(pack_kernel, nctx), out_shape=(jax.Shape...]
    unnamed x45 -> x51, local copies, waits for them, and re-layouts: 5.32 us -> 8.65 us
    pallas_call x2 -> x3, Pallas kernels: 16 us -> 19.3 us  [attend(): pl.pallas_call(functools.partial(attend_kernel, nctx, back, steps, shard)...]
    pallas_call x2 -> x3, Pallas kernels: 10.2 us -> 13.1 us  [project(): pl.pallas_call(functools.partial(project_kernel, jobs, len(halves), shard...]
    ppermute x9 -> x12, starting transfers between devices: 2.9 us -> 4.99 us  [swapped(): return lax.ppermute(value, axis, [(s, s ^ flip) for s in range(count)])]
  transfers between devices with their start and end apart: 26 -> 26, of which waited for: 13 -> 9; matrix products, arithmetic and copies ran while one was open for 4% -> 3% of each run, Pallas kernels for 14% -> 25%
where the time goes in v2:
time: 181 us
  waiting for transfers between devices  63.7 us (35%)
  starting transfers between devices  53.9 us (30%)
  Pallas kernels  45.9 us (25%)
  local copies, waits for them, and re-layouts  8.66 us (5%)
  other arithmetic  7.72 us (4%)
    ppermute x14, starting transfers between devices, rotated(): lax.ppermute(value, axis, [(s, (s - steps) % count) for s in range(count)])  48.9 us
    ppermute x14, waiting for transfers between devices, rotated(): lax.ppermute(value, axis, [(s, (s - steps) % count) for s in range(count)])  43.5 us
    ppermute x12, waiting for transfers between devices, swapped(): return lax.ppermute(value, axis, [(s, s ^ flip) for s in range(count)])  20.2 us
    pallas_call x3, Pallas kernels, attend(): pl.pallas_call(functools.partial(attend_kernel, nctx, back, steps, shard)...  19.3 us
    pallas_call x3, Pallas kernels, project(): pl.pallas_call(functools.partial(project_kernel, jobs, len(halves), shard...  13.1 us
    unnamed x51, local copies, waits for them, and re-layouts  8.65 us
    pallas_call x1, Pallas kernels, recur(): pl.pallas_call(functools.partial(recur_kernel, features), grid=(channels...  6.77 us
    ppermute x12, starting transfers between devices, swapped(): return lax.ppermute(value, axis, [(s, s ^ flip) for s in range(count)])  4.99 us
  transfers between devices with their start and end apart: 26, of which 9 were waited for; matrix products, arithmetic and copies ran while one was open for 3% of the time, Pallas kernels for 25%

profile of v2, /device:TPU:0, one launch (start us, length us, event | category | flops | bytes accessed | tf_op | source)
XLA Modules:
  0.0 180.8 jit_solution(1247060691578312290)
XLA Ops:
  0.6 4.1 %collective-permute-start.2 = (bf16[64,512]{1,0:T(8,128)(2,1)}, bf16[64,512]{1,0:T(8,128)(2,1)S(1)}, u32[]{:S(2)}, u32[]{:S(2)}) collective-permute-start(bf16[64,512]{1,0:T(8,128)(2,1)} %param.14), channel_id=1, source_target_pairs={{0,8},{4,12},{8,0},{12,4},{1,9},{5,13},{9,1},{13,5},{2,10},{6,14},... | collective-permute-start | bytes 196616 | tf_op jit(solution)/shard_map/ppermute | solution.py:169
  4.8 1.3 collective-permute-start.1
  6.1 0.7 collective-permute-start.3
  6.8 0.6 pad_add_fusion.scal
  7.3 2.6 %pack.1 = (bf16[64,1024]{1,0:T(8,128)(2,1)}, bf16[320,1024]{1,0:T(8,128)(2,1)}, bf16[320,1024]{1,0:T(8,128)(2,1)}, bf16[320,1024]{1,0:T(8,128)(2,1)}) custom-call(s32[2]{0:T(128)} %pad_add_fusion.scal, bf16[256,1024]{1,0:T(8,128)(2,1)} %refs_0_.1, bf16[64,4096]{1,0:T(8,128)(2,1)} %residual.1), custom_call_target="tpu_custom_call" | custom-call | tf_op jit(solution)/shard_map/pack/pallas_call | solution.py:198
  9.9 3.1 %collective-permute-start = (bf16[320,1024]{1,0:T(8,128)(2,1)}, bf16[320,1024]{1,0:T(8,128)(2,1)S(1)}, u32[]{:S(2)}, u32[]{:S(2)}) collective-permute-start(bf16[320,1024]{1,0:T(8,128)(2,1)} %get-tuple-element.24), channel_id=1, source_target_pairs={{0,12},{4,0},{8,4},{12,8},{1,13},{5,1},{9,5},{13,9},{2,14},{6,2},{... | collective-permute-start | bytes 1966088 | tf_op jit(solution)/shard_map/ppermute | solution.py:169
  13.1 0.8 constant_dynamic-update-slice_fusion.3
  14.0 1.6 collective-permute-start.5
  15.6 5.4 %collective-permute-done.5.refs_2_ = bf16[256,512]{1,0:T(8,128)(2,1)S(1)} collective-permute-done((bf16[256,512]{1,0:T(8,128)(2,1)S(1)}, bf16[256,512]{1,0:T(8,128)(2,1)S(1)}, u32[]{:S(2)}, u32[]{:S(2)}) %collective-permute-start.5) | collective-permute-done | bytes 262176 | tf_op jit(solution)/shard_map/ppermute | solution.py:174
  21.0 0.9 collective-permute-start.11
  21.9 1.3 convert_reduce_fusion.1
  23.3 1.8 pad_add_fusion.1.scal
  25.1 0.7 copy-done.16
  25.8 0.7 copy-done.17
  26.5 2.3 %assemble.1.refs_4_.refs_2_ = bf16[1024,512]{1,0:T(8,128)(2,1)} custom-call(s32[2]{0:T(128)} %pad_add_fusion.scal, bf16[256,512]{1,0:T(8,128)(2,1)} %copy-done.12, bf16[256,512]{1,0:T(8,128)(2,1)} %copy-done.16, bf16[256,512]{1,0:T(8,128)(2,1)} %copy-done.15, bf16[256,512]{1,0:T(8,128)(2,1)} %copy-done.17), custom_call_target="tpu_custom_call" | custom-call | tf_op jit(solution)/shard_map/assemble/pallas_call | solution.py:241
  28.7 0.8 copy-done.4
  29.6 8.2 %attend.3 = (bf16[512,512]{1,0:T(8,128)(2,1)}, bf16[512,512]{1,0:T(8,128)(2,1)}) custom-call(s32[4]{0:T(128)} %pad_add_fusion.1.scal, bf16[256,1024]{1,0:T(8,128)(2,1)} %refs_0_.1, bf16[320,1024]{1,0:T(8,128)(2,1)} %copy-done.4, bf16[64,1024]{1,0:T(8,128)(2,1)} %get-tuple-element.25.refs_2_, bf16[320,1024]{1,0:T(8,128)(2,1)} %copy-done.4, ...), custom_call_target="tpu_custom_call" | custom-call | tf_op jit(solution)/shard_map/attend/pallas_call | solution.py:297
  37.8 0.2 collective-permute-start.7
  38.0 14.3 %collective-permute-start.16 = (bf16[320,1024]{1,0:T(8,128)(2,1)S(1)}, bf16[320,1024]{1,0:T(8,128)(2,1)S(1)}, u32[]{:S(2)}, u32[]{:S(2)}) collective-permute-start(bf16[320,1024]{1,0:T(8,128)(2,1)S(1)} %copy-done.21), channel_id=1, source_target_pairs={{0,4},{4,8},{8,12},{12,0},{1,5},{5,9},{9,13},{13,1},{2,6},{6,10},{... | collective-permute-start | bytes 1966088 | tf_op jit(solution)/shard_map/ppermute | solution.py:169
  52.3 16.6 %collective-permute-done.11.refs_0_.refs_1_ = bf16[320,1024]{1,0:T(8,128)(2,1)S(1)} collective-permute-done((bf16[320,1024]{1,0:T(8,128)(2,1)}, bf16[320,1024]{1,0:T(8,128)(2,1)S(1)}, u32[]{:S(2)}, u32[]{:S(2)}) %collective-permute-start.11) | collective-permute-done | bytes 655392 | tf_op jit(solution)/shard_map/ppermute | solution.py:169
  68.9 0.8 copy-done.2
  69.8 5.5 %attend.4 = (bf16[256,512]{1,0:T(8,128)(2,1)}, bf16[256,512]{1,0:T(8,128)(2,1)}) custom-call(s32[4]{0:T(128)} %pad_add_fusion.1.scal, bf16[320,1024]{1,0:T(8,128)(2,1)} %copy-done.2, bf16[320,1024]{1,0:T(8,128)(2,1)} %copy-done.2, bf16[1024,512]{1,0:T(8,128)(2,1)} %assemble.1.refs_4_.refs_2_, bf16[1024,1024]{1,0:T(8,128)(2,1)} %refs_3_.5), custom_call_target="tpu_custom_call" | custom-call | tf_op jit(solution)/shard_map/attend/pallas_call | solution.py:297
  75.3 0.1 add_convert_fusion.2
  75.5 1.6 collective-permute-start.8
  77.0 0.8 copy-done.3
  77.9 5.5 %attend.5 = (bf16[256,512]{1,0:T(8,128)(2,1)}, bf16[256,512]{1,0:T(8,128)(2,1)}) custom-call(s32[4]{0:T(128)} %pad_add_fusion.1.scal, bf16[320,1024]{1,0:T(8,128)(2,1)} %copy-done.3, bf16[320,1024]{1,0:T(8,128)(2,1)} %copy-done.3, bf16[1024,512]{1,0:T(8,128)(2,1)} %assemble.1.refs_4_.refs_2_, bf16[1024,1024]{1,0:T(8,128)(2,1)} %refs_3_.5), custom_call_target="tpu_custom_call" | custom-call | tf_op jit(solution)/shard_map/attend/pallas_call | solution.py:297
  83.4 0.2 collective-permute-start.17
  83.6 0.1 add_convert_fusion.6
  83.7 0.6 collective-permute-start.13
  84.3 0.9 collective-permute-done.17
  85.1 1.0 add_convert_fusion.4
  86.2 0.7 collective-permute-start.18
  86.9 3.5 %collective-permute-done.8 = bf16[512,512]{1,0:T(8,128)(2,1)S(1)} collective-permute-done((bf16[512,512]{1,0:T(8,128)(2,1)S(1)}, bf16[512,512]{1,0:T(8,128)(2,1)S(1)}, u32[]{:S(2)}, u32[]{:S(2)}) %collective-permute-start.8) | collective-permute-done | bytes 524320 | tf_op jit(solution)/shard_map/ppermute | solution.py:174
  90.3 0.1 add_convert_fusion.1.refs_0_
  90.5 0.1 collective-permute-start.9
  90.6 5.4 %collective-permute-done.13 = bf16[256,512]{1,0:T(8,128)(2,1)S(1)} collective-permute-done((bf16[256,512]{1,0:T(8,128)(2,1)S(1)}, bf16[256,512]{1,0:T(8,128)(2,1)S(1)}, u32[]{:S(2)}, u32[]{:S(2)}) %collective-permute-start.13) | collective-permute-done | bytes 262176 | tf_op jit(solution)/shard_map/ppermute | solution.py:174
  95.9 0.1 add_convert_fusion.5.refs_2_
  96.0 0.1 collective-permute-start.14
  96.1 5.0 %collective-permute-done.18 = bf16[256,512]{1,0:T(8,128)(2,1)S(1)} collective-permute-done((bf16[256,512]{1,0:T(8,128)(2,1)S(1)}, bf16[256,512]{1,0:T(8,128)(2,1)S(1)}, u32[]{:S(2)}, u32[]{:S(2)}) %collective-permute-start.18) | collective-permute-done | bytes 262176 | tf_op jit(solution)/shard_map/ppermute | solution.py:174
  101.1 0.1 add_convert_fusion.3.refs_4_
  101.2 0.1 collective-permute-start.19
  101.3 0.8 copy-done.1
  102.0 4.5 %project.3 = (bf16[256,1024]{1,0:T(8,128)(2,1)}, bf16[64,1024]{1,0:T(8,128)(2,1)}, bf16[272,1024]{1,0:T(8,128)(2,1)}, bf16[64,1024]{1,0:T(8,128)(2,1)}) custom-call(s32[4]{0:T(128)} %pad_add_fusion.1.scal, bf16[512,512]{1,0:T(8,128)(2,1)} %copy-done, bf16[512,512]{1,0:T(8,128)(2,1)} %copy-done.1, f32[1,4096]{1,0:T(1,128)} %bitcast.9, bf16[1024,1024]{1,0:T(8,128)(2,1)} %refs_7_.1), custom_call_target="tpu_custom_call" | custom-call | tf_op jit(solution)/shard_map/project/pallas_call | solution.py:381
  106.5 0.7 copy-done.10
  107.3 4.1 %project.4 = (bf16[272,1024]{1,0:T(8,128)(2,1)}, bf16[64,1024]{1,0:T(8,128)(2,1)}) custom-call(s32[4]{0:T(128)} %pad_add_fusion.1.scal, bf16[512,512]{1,0:T(8,128)(2,1)} %copy-done, bf16[512,512]{1,0:T(8,128)(2,1)} %copy-done.1, bf16[256,512]{1,0:T(8,128)(2,1)} %copy-done.5, bf16[256,512]{1,0:T(8,128)(2,1)} %copy-done.10, f32[1,4096]{1,0:T(1,128)} %bitcast.10, ...), custom_call_target="tpu_custom_call" | custom-call | tf_op jit(solution)/shard_map/project/pallas_call | solution.py:381
  111.4 0.1 collective-permute-start.22
  111.5 0.7 copy-done.14
  112.2 4.5 %project.5 = (bf16[272,1024]{1,0:T(8,128)(2,1)}, bf16[64,1024]{1,0:T(8,128)(2,1)}, bf16[16,1024]{1,0:T(8,128)(2,1)}) custom-call(s32[4]{0:T(128)} %pad_add_fusion.1.scal, bf16[512,512]{1,0:T(8,128)(2,1)} %copy-done, bf16[512,512]{1,0:T(8,128)(2,1)} %copy-done.1, bf16[256,512]{1,0:T(8,128)(2,1)} %copy-done.5, bf16[256,512]{1,0:T(8,128)(2,1)} %copy-done.10, ...), custom_call_target="tpu_custom_call" | custom-call | tf_op jit(solution)/shard_map/project/pallas_call | solution.py:381
  116.7 3.8 %collective-permute-start.23 = (bf16[272,1024]{1,0:T(8,128)(2,1)}, bf16[272,1024]{1,0:T(8,128)(2,1)S(1)}, u32[]{:S(2)}, u32[]{:S(2)}) collective-permute-start(bf16[272,1024]{1,0:T(8,128)(2,1)} %get-tuple-element.41), channel_id=1, source_target_pairs={{0,12},{4,0},{8,4},{12,8},{1,13},{5,1},{9,5},{13,9},{2,14},{6,2},{... | collective-permute-start | bytes 1671176 | tf_op jit(solution)/shard_map/ppermute | solution.py:169
  120.5 0.6 collective-permute-start.20
  121.0 1.5 collective-permute-start.15
  122.5 1.6 collective-permute-done.21.refs_1_.refs_5_
  124.1 0.4 collective-permute-start.10
  124.6 22.9 %collective-permute-done.22.refs_2_.refs_6_ = bf16[272,1024]{1,0:T(8,128)(2,1)S(1)} collective-permute-done((bf16[272,1024]{1,0:T(8,128)(2,1)}, bf16[272,1024]{1,0:T(8,128)(2,1)S(1)}, u32[]{:S(2)}, u32[]{:S(2)}) %collective-permute-start.22) | collective-permute-done | bytes 557088 | tf_op jit(solution)/shard_map/ppermute | solution.py:169
  147.5 0.8 copy-done.7
  148.3 0.2 copy-done.8
  148.5 6.8 %recur.1 = (f32[256,1024]{1,0:T(8,128)}, f32[256,1024]{1,0:T(8,128)}, f32[8,1024]{1,0:T(8,128)}) custom-call(s32[4]{0:T(128)} %pad_add_fusion.1.scal, bf16[256,1024]{1,0:T(8,128)(2,1)} %get-tuple-element.38.refs_0_, bf16[272,1024]{1,0:T(8,128)(2,1)} %copy-done.6, bf16[272,1024]{1,0:T(8,128)(2,1)} %copy-done.7, bf16[272,1024]{1,0:T(8,128)(2,1)} %copy-done.8, ...), custom_call_target="tpu_custom_call" | custom-call | tf_op jit(solution)/shard_map/recur/pallas_call | solution.py:478
  155.3 17.1 %collective-permute-start.25 = (f32[8,1024]{1,0:T(8,128)}, f32[8,1024]{1,0:T(8,128)S(1)}, u32[]{:S(2)}, u32[]{:S(2)}) collective-permute-start(f32[8,1024]{1,0:T(8,128)} %get-tuple-element.45), channel_id=1, source_target_pairs={{0,8},{4,12},{8,0},{12,4},{1,9},{5,13},{9,1},{13,5},{2,10},{6,14},... | collective-permute-start | bytes 98312 | tf_op jit(solution)/shard_map/ppermute | solution.py:169
  172.3 1.0 collective-permute-start.24
  173.4 0.6 copy-done.18
  174.0 0.1 copy-done.19
  174.1 1.9 %join.1 = bf16[64,4096]{1,0:T(8,128)(2,1)} custom-call(s32[2]{0:T(128)} %pad_add_fusion.scal, bf16[64,1024]{1,0:T(8,128)(2,1)} %get-tuple-element.28.refs_0_, bf16[64,1024]{1,0:T(8,128)(2,1)} %copy-done.20, bf16[64,1024]{1,0:T(8,128)(2,1)} %copy-done.19, bf16[64,1024]{1,0:T(8,128)(2,1)} %copy-done.18), custom_call_target="tpu_custom_call" | custom-call | tf_op jit(solution)/shard_map/join/pallas_call | solution.py:218
  176.0 2.3 %collective-permute-done.24 = f32[8,1024]{1,0:T(8,128)S(1)} collective-permute-done((f32[8,1024]{1,0:T(8,128)}, f32[8,1024]{1,0:T(8,128)S(1)}, u32[]{:S(2)}, u32[]{:S(2)}) %collective-permute-start.24) | collective-permute-done | bytes 32800 | tf_op jit(solution)/shard_map/ppermute | solution.py:169
  178.3 2.5 %add_convert_fusion = bf16[256,1024]{1,0:T(8,128)(2,1)} fusion(f32[256,1024]{1,0:T(8,128)} %get-tuple-element.43, f32[256,1024]{1,0:T(8,128)} %get-tuple-element.44, f32[1024]{0:T(1024)S(1)} %bitcast.12), kind=kLoop, calls=%fused_computation | loop fusion | flops 786432 | bytes 2625536 | tf_op jit(solution)/shard_map/convert_element_type | solution.py:615
  (61 shorter events, 0.2 us)
Async XLA Ops:
  0.6 13.3 %collective-permute-start.2 = (bf16[64,512]{1,0:T(8,128)(2,1)}, bf16[64,512]{1,0:T(8,128)(2,1)S(1)}, u32[]{:S(2)}, u32[]{:S(2)}) collective-permute-start(bf16[64,512]{1,0:T(8,128)(2,1)} %param.14), channel_id=1, source_target_pairs={{0,8},{4,12},{8,0},{12,4},{1,9},{5,13},{9,1},{13,5},{2,10},{6,14},... | collective-permute-start | bytes 196616 | tf_op jit(solution)/shard_map/ppermute | solution.py:169
  4.8 9.2 %collective-permute-start.1 = (bf16[64,512]{1,0:T(8,128)(2,1)}, bf16[64,512]{1,0:T(8,128)(2,1)S(1)}, u32[]{:S(2)}, u32[]{:S(2)}) collective-permute-start(bf16[64,512]{1,0:T(8,128)(2,1)} %param.14), channel_id=1, source_target_pairs={{0,12},{4,0},{8,4},{12,8},{1,13},{5,1},{9,5},{13,9},{2,14},{6,2},{... | collective-permute-start | bytes 196616 | tf_op jit(solution)/shard_map/ppermute | solution.py:169
  6.1 7.9 %collective-permute-start.3 = (bf16[64,512]{1,0:T(8,128)(2,1)}, bf16[64,512]{1,0:T(8,128)(2,1)S(1)}, u32[]{:S(2)}, u32[]{:S(2)}) collective-permute-start(bf16[64,512]{1,0:T(8,128)(2,1)} %param.14), channel_id=1, source_target_pairs={{0,4},{4,8},{8,12},{12,0},{1,5},{5,9},{9,13},{13,1},{2,6},{6,10},{... | collective-permute-start | bytes 196616 | tf_op jit(solution)/shard_map/ppermute | solution.py:169
  9.9 18.8 %collective-permute-start = (bf16[320,1024]{1,0:T(8,128)(2,1)}, bf16[320,1024]{1,0:T(8,128)(2,1)S(1)}, u32[]{:S(2)}, u32[]{:S(2)}) collective-permute-start(bf16[320,1024]{1,0:T(8,128)(2,1)} %get-tuple-element.24), channel_id=1, source_target_pairs={{0,12},{4,0},{8,4},{12,8},{1,13},{5,1},{9,5},{13,9},{2,14},{6,2},{... | collective-permute-start | bytes 1966088 | tf_op jit(solution)/shard_map/ppermute | solution.py:169
  14.0 11.1 %copy-start.12 = (bf16[256,512]{1,0:T(8,128)(2,1)}, bf16[256,512]{1,0:T(8,128)(2,1)S(1)}, u32[]{:S(2)}) copy-start(bf16[256,512]{1,0:T(8,128)(2,1)S(1)} %constant_dynamic-update-slice_fusion.refs_0_) | copy-start | bytes 786436
  14.0 7.0 %collective-permute-start.5 = (bf16[256,512]{1,0:T(8,128)(2,1)S(1)}, bf16[256,512]{1,0:T(8,128)(2,1)S(1)}, u32[]{:S(2)}, u32[]{:S(2)}) collective-permute-start(bf16[256,512]{1,0:T(8,128)(2,1)S(1)} %constant_dynamic-update-slice_fusion.refs_0_), channel_id=1, source_target_pairs={{0,2},{1,3},{2,0},{3,1},{4,6},{5,7},{6,4},{7,5},{8,10},{9,11},{10,... | collective-permute-start | bytes 786440 | tf_op jit(solution)/shard_map/ppermute | solution.py:174
  15.6 9.5 %collective-permute-start.4 = (bf16[256,512]{1,0:T(8,128)(2,1)S(1)}, bf16[256,512]{1,0:T(8,128)(2,1)S(1)}, u32[]{:S(2)}, u32[]{:S(2)}) collective-permute-start(bf16[256,512]{1,0:T(8,128)(2,1)S(1)} %constant_dynamic-update-slice_fusion.refs_0_), channel_id=1, source_target_pairs={{0,1},{1,0},{2,3},{3,2},{4,5},{5,4},{6,7},{7,6},{8,9},{9,8},{10,11... | collective-permute-start | bytes 786440 | tf_op jit(solution)/shard_map/ppermute | solution.py:174
  21.0 4.1 %copy-start.15 = (bf16[256,512]{1,0:T(8,128)(2,1)}, bf16[256,512]{1,0:T(8,128)(2,1)S(1)}, u32[]{:S(2)}) copy-start(bf16[256,512]{1,0:T(8,128)(2,1)S(1)} %collective-permute-done.5.refs_2_) | copy-start | bytes 786436
  21.0 4.1 %collective-permute-start.6 = (bf16[256,512]{1,0:T(8,128)(2,1)S(1)}, bf16[256,512]{1,0:T(8,128)(2,1)S(1)}, u32[]{:S(2)}, u32[]{:S(2)}) collective-permute-start(bf16[256,512]{1,0:T(8,128)(2,1)S(1)} %collective-permute-done.5.refs_2_), channel_id=1, source_target_pairs={{0,1},{1,0},{2,3},{3,2},{4,5},{5,4},{6,7},{7,6},{8,9},{9,8},{10,11... | collective-permute-start | bytes 786440 | tf_op jit(solution)/shard_map/ppermute | solution.py:174
  21.0 47.9 %collective-permute-start.11 = (bf16[320,1024]{1,0:T(8,128)(2,1)}, bf16[320,1024]{1,0:T(8,128)(2,1)S(1)}, u32[]{:S(2)}, u32[]{:S(2)}) collective-permute-start(bf16[320,1024]{1,0:T(8,128)(2,1)} %get-tuple-element.30), channel_id=1, source_target_pairs={{0,8},{4,12},{8,0},{12,4},{1,9},{5,13},{9,1},{13,5},{2,10},{6,14},... | collective-permute-start | bytes 1966088 | tf_op jit(solution)/shard_map/ppermute | solution.py:169
  25.1 0.7 copy-start.16
  25.8 0.7 copy-start.17
  28.7 0.9 copy-start.4
  29.6 8.4 %copy-start.21 = (bf16[320,1024]{1,0:T(8,128)(2,1)S(1)}, bf16[320,1024]{1,0:T(8,128)(2,1)}, u32[]{:S(2)}) copy-start(bf16[320,1024]{1,0:T(8,128)(2,1)} %get-tuple-element.34) | copy-start | bytes 1966084
  37.8 37.5 %collective-permute-start.7 = (bf16[512,512]{1,0:T(8,128)(2,1)}, bf16[512,512]{1,0:T(8,128)(2,1)S(1)}, u32[]{:S(2)}, u32[]{:S(2)}) collective-permute-start(bf16[512,512]{1,0:T(8,128)(2,1)} %get-tuple-element.27), channel_id=1, source_target_pairs={{0,1},{1,0},{2,3},{3,2},{4,5},{5,4},{6,7},{7,6},{8,9},{9,8},{10,11... | collective-permute-start | bytes 1572872 | tf_op jit(solution)/shard_map/ppermute | solution.py:174
  38.0 37.3 %copy-start.11 = (bf16[512,512]{1,0:T(8,128)(2,1)S(1)}, bf16[512,512]{1,0:T(8,128)(2,1)}, u32[]{:S(2)}) copy-start(bf16[512,512]{1,0:T(8,128)(2,1)} %get-tuple-element.26) | copy-start | bytes 1572868
  38.0 39.0 %collective-permute-start.16 = (bf16[320,1024]{1,0:T(8,128)(2,1)S(1)}, bf16[320,1024]{1,0:T(8,128)(2,1)S(1)}, u32[]{:S(2)}, u32[]{:S(2)}) collective-permute-start(bf16[320,1024]{1,0:T(8,128)(2,1)S(1)} %copy-done.21), channel_id=1, source_target_pairs={{0,4},{4,8},{8,12},{12,0},{1,5},{5,9},{9,13},{13,1},{2,6},{6,10},{... | collective-permute-start | bytes 1966088 | tf_op jit(solution)/shard_map/ppermute | solution.py:169
  68.9 0.8 copy-start.2
  75.3 8.3 %collective-permute-start.12 = (bf16[256,512]{1,0:T(8,128)(2,1)}, bf16[256,512]{1,0:T(8,128)(2,1)S(1)}, u32[]{:S(2)}, u32[]{:S(2)}) collective-permute-start(bf16[256,512]{1,0:T(8,128)(2,1)} %get-tuple-element.32), channel_id=1, source_target_pairs={{0,1},{1,0},{2,3},{3,2},{4,5},{5,4},{6,7},{7,6},{8,9},{9,8},{10,11... | collective-permute-start | bytes 786440 | tf_op jit(solution)/shard_map/ppermute | solution.py:174
  75.5 8.2 %copy-start.13 = (bf16[256,512]{1,0:T(8,128)(2,1)S(1)}, bf16[256,512]{1,0:T(8,128)(2,1)}, u32[]{:S(2)}) copy-start(bf16[256,512]{1,0:T(8,128)(2,1)} %get-tuple-element.31) | copy-start | bytes 786436
  75.5 14.9 %collective-permute-start.8 = (bf16[512,512]{1,0:T(8,128)(2,1)S(1)}, bf16[512,512]{1,0:T(8,128)(2,1)S(1)}, u32[]{:S(2)}, u32[]{:S(2)}) collective-permute-start(bf16[512,512]{1,0:T(8,128)(2,1)S(1)} %add_convert_fusion.2), channel_id=1, source_target_pairs={{0,2},{1,3},{2,0},{3,1},{4,6},{5,7},{6,4},{7,5},{8,10},{9,11},{10,... | collective-permute-start | bytes 1572872 | tf_op jit(solution)/shard_map/ppermute | solution.py:174
  77.0 0.8 copy-start.3
  83.4 1.7 collective-permute-start.17
  83.7 12.3 %collective-permute-start.13 = (bf16[256,512]{1,0:T(8,128)(2,1)S(1)}, bf16[256,512]{1,0:T(8,128)(2,1)S(1)}, u32[]{:S(2)}, u32[]{:S(2)}) collective-permute-start(bf16[256,512]{1,0:T(8,128)(2,1)S(1)} %add_convert_fusion.6), channel_id=1, source_target_pairs={{0,2},{1,3},{2,0},{3,1},{4,6},{5,7},{6,4},{7,5},{8,10},{9,11},{10,... | collective-permute-start | bytes 786440 | tf_op jit(solution)/shard_map/ppermute | solution.py:174
  86.2 14.9 %collective-permute-start.18 = (bf16[256,512]{1,0:T(8,128)(2,1)S(1)}, bf16[256,512]{1,0:T(8,128)(2,1)S(1)}, u32[]{:S(2)}, u32[]{:S(2)}) collective-permute-start(bf16[256,512]{1,0:T(8,128)(2,1)S(1)} %add_convert_fusion.4), channel_id=1, source_target_pairs={{0,2},{1,3},{2,0},{3,1},{4,6},{5,7},{6,4},{7,5},{8,10},{9,11},{10,... | collective-permute-start | bytes 786440 | tf_op jit(solution)/shard_map/ppermute | solution.py:174
  90.5 10.8 %copy-start = (bf16[512,512]{1,0:T(8,128)(2,1)}, bf16[512,512]{1,0:T(8,128)(2,1)S(1)}, u32[]{:S(2)}) copy-start(bf16[512,512]{1,0:T(8,128)(2,1)S(1)} %add_convert_fusion.1.refs_0_) | copy-start | bytes 1572868
  90.5 10.8 %collective-permute-start.9 = (bf16[512,512]{1,0:T(8,128)(2,1)S(1)}, bf16[512,512]{1,0:T(8,128)(2,1)S(1)}, u32[]{:S(2)}, u32[]{:S(2)}) collective-permute-start(bf16[512,512]{1,0:T(8,128)(2,1)S(1)} %add_convert_fusion.1.refs_0_), channel_id=1, source_target_pairs={{0,1},{1,0},{2,3},{3,2},{4,5},{5,4},{6,7},{7,6},{8,9},{9,8},{10,11... | collective-permute-start | bytes 1572872 | tf_op jit(solution)/shard_map/ppermute | solution.py:174
  96.0 10.5 %copy-start.5 = (bf16[256,512]{1,0:T(8,128)(2,1)}, bf16[256,512]{1,0:T(8,128)(2,1)S(1)}, u32[]{:S(2)}) copy-start(bf16[256,512]{1,0:T(8,128)(2,1)S(1)} %add_convert_fusion.5.refs_2_) | copy-start | bytes 786436
  96.0 10.5 %collective-permute-start.14 = (bf16[256,512]{1,0:T(8,128)(2,1)S(1)}, bf16[256,512]{1,0:T(8,128)(2,1)S(1)}, u32[]{:S(2)}, u32[]{:S(2)}) collective-permute-start(bf16[256,512]{1,0:T(8,128)(2,1)S(1)} %add_convert_fusion.5.refs_2_), channel_id=1, source_target_pairs={{0,1},{1,0},{2,3},{3,2},{4,5},{5,4},{6,7},{7,6},{8,9},{9,8},{10,11... | collective-permute-start | bytes 786440 | tf_op jit(solution)/shard_map/ppermute | solution.py:174
  101.2 10.3 %copy-start.9 = (bf16[256,512]{1,0:T(8,128)(2,1)}, bf16[256,512]{1,0:T(8,128)(2,1)S(1)}, u32[]{:S(2)}) copy-start(bf16[256,512]{1,0:T(8,128)(2,1)S(1)} %add_convert_fusion.3.refs_4_) | copy-start | bytes 786436
  101.2 10.3 %collective-permute-start.19 = (bf16[256,512]{1,0:T(8,128)(2,1)S(1)}, bf16[256,512]{1,0:T(8,128)(2,1)S(1)}, u32[]{:S(2)}, u32[]{:S(2)}) collective-permute-start(bf16[256,512]{1,0:T(8,128)(2,1)S(1)} %add_convert_fusion.3.refs_4_), channel_id=1, source_target_pairs={{0,1},{1,0},{2,3},{3,2},{4,5},{5,4},{6,7},{7,6},{8,9},{9,8},{10,11... | collective-permute-start | bytes 786440 | tf_op jit(solution)/shard_map/ppermute | solution.py:174
  101.3 0.8 copy-start.1
  106.5 17.6 %collective-permute-start.21 = (bf16[272,1024]{1,0:T(8,128)(2,1)}, bf16[272,1024]{1,0:T(8,128)(2,1)S(1)}, u32[]{:S(2)}, u32[]{:S(2)}) collective-permute-start(bf16[272,1024]{1,0:T(8,128)(2,1)} %get-tuple-element.39), channel_id=1, source_target_pairs={{0,4},{4,8},{8,12},{12,0},{1,5},{5,9},{9,13},{13,1},{2,6},{6,10},{... | collective-permute-start | bytes 1671176 | tf_op jit(solution)/shard_map/ppermute | solution.py:169
  106.5 0.7 copy-start.10
  111.4 9.7 %copy-start.23 = (bf16[64,1024]{1,0:T(8,128)(2,1)S(1)}, bf16[64,1024]{1,0:T(8,128)(2,1)}, u32[]{:S(2)}) copy-start(bf16[64,1024]{1,0:T(8,128)(2,1)} %get-tuple-element.33) | copy-start | bytes 393220
  111.4 12.8 %copy-start.22 = (bf16[64,1024]{1,0:T(8,128)(2,1)S(1)}, bf16[64,1024]{1,0:T(8,128)(2,1)}, u32[]{:S(2)}) copy-start(bf16[64,1024]{1,0:T(8,128)(2,1)} %get-tuple-element.29) | copy-start | bytes 393220
  111.4 36.1 %collective-permute-start.22 = (bf16[272,1024]{1,0:T(8,128)(2,1)}, bf16[272,1024]{1,0:T(8,128)(2,1)S(1)}, u32[]{:S(2)}, u32[]{:S(2)}) collective-permute-start(bf16[272,1024]{1,0:T(8,128)(2,1)} %get-tuple-element.40), channel_id=1, source_target_pairs={{0,8},{4,12},{8,0},{12,4},{1,9},{5,13},{9,1},{13,5},{2,10},{6,14},... | collective-permute-start | bytes 1671176 | tf_op jit(solution)/shard_map/ppermute | solution.py:169
  111.5 0.7 copy-start.14
  116.7 30.8 %collective-permute-start.23 = (bf16[272,1024]{1,0:T(8,128)(2,1)}, bf16[272,1024]{1,0:T(8,128)(2,1)S(1)}, u32[]{:S(2)}, u32[]{:S(2)}) collective-permute-start(bf16[272,1024]{1,0:T(8,128)(2,1)} %get-tuple-element.41), channel_id=1, source_target_pairs={{0,12},{4,0},{8,4},{12,8},{1,13},{5,1},{9,5},{13,9},{2,14},{6,2},{... | collective-permute-start | bytes 1671176 | tf_op jit(solution)/shard_map/ppermute | solution.py:169
  120.5 52.8 %collective-permute-start.20 = (bf16[64,1024]{1,0:T(8,128)(2,1)}, bf16[64,1024]{1,0:T(8,128)(2,1)S(1)}, u32[]{:S(2)}, u32[]{:S(2)}) collective-permute-start(bf16[64,1024]{1,0:T(8,128)(2,1)} %get-tuple-element.37), channel_id=1, source_target_pairs={{0,12},{4,0},{8,4},{12,8},{1,13},{5,1},{9,5},{13,9},{2,14},{6,2},{... | collective-permute-start | bytes 393224 | tf_op jit(solution)/shard_map/ppermute | solution.py:169
  121.0 52.3 %collective-permute-start.15 = (bf16[64,1024]{1,0:T(8,128)(2,1)S(1)}, bf16[64,1024]{1,0:T(8,128)(2,1)S(1)}, u32[]{:S(2)}, u32[]{:S(2)}) collective-permute-start(bf16[64,1024]{1,0:T(8,128)(2,1)S(1)} %copy-done.23), channel_id=1, source_target_pairs={{0,8},{4,12},{8,0},{12,4},{1,9},{5,13},{9,1},{13,5},{2,10},{6,14},... | collective-permute-start | bytes 393224 | tf_op jit(solution)/shard_map/ppermute | solution.py:169
  124.1 23.4 %copy-start.6 = (bf16[272,1024]{1,0:T(8,128)(2,1)}, bf16[272,1024]{1,0:T(8,128)(2,1)S(1)}, u32[]{:S(2)}) copy-start(bf16[272,1024]{1,0:T(8,128)(2,1)S(1)} %collective-permute-done.21.refs_1_.refs_5_) | copy-start | bytes 1671172
  124.1 49.2 %collective-permute-start.10 = (bf16[64,1024]{1,0:T(8,128)(2,1)S(1)}, bf16[64,1024]{1,0:T(8,128)(2,1)S(1)}, u32[]{:S(2)}, u32[]{:S(2)}) collective-permute-start(bf16[64,1024]{1,0:T(8,128)(2,1)S(1)} %copy-done.22), channel_id=1, source_target_pairs={{0,4},{4,8},{8,12},{12,0},{1,5},{5,9},{9,13},{13,1},{2,6},{6,10},{... | collective-permute-start | bytes 393224 | tf_op jit(solution)/shard_map/ppermute | solution.py:169
  147.5 0.8 copy-start.7
  147.5 1.0 copy-start.8
  155.3 20.7 %collective-permute-start.25 = (f32[8,1024]{1,0:T(8,128)}, f32[8,1024]{1,0:T(8,128)S(1)}, u32[]{:S(2)}, u32[]{:S(2)}) collective-permute-start(f32[8,1024]{1,0:T(8,128)} %get-tuple-element.45), channel_id=1, source_target_pairs={{0,8},{4,12},{8,0},{12,4},{1,9},{5,13},{9,1},{13,5},{2,10},{6,14},... | collective-permute-start | bytes 98312 | tf_op jit(solution)/shard_map/ppermute | solution.py:169
  172.3 5.9 %collective-permute-start.24 = (f32[8,1024]{1,0:T(8,128)}, f32[8,1024]{1,0:T(8,128)S(1)}, u32[]{:S(2)}, u32[]{:S(2)}) collective-permute-start(f32[8,1024]{1,0:T(8,128)} %get-tuple-element.45), channel_id=1, source_target_pairs={{0,4},{4,8},{8,12},{12,0},{1,5},{5,9},{9,13},{13,1},{2,6},{6,10},{... | collective-permute-start | bytes 98312 | tf_op jit(solution)/shard_map/ppermute | solution.py:169
  173.3 0.6 copy-start.18
  173.3 0.7 copy-start.19
  173.4 0.7 copy-start.20

commit v3 on v2

--- a/solution.py
+++ b/solution.py
@@ -162,6 +162,7 @@
 TILE = 16
 SUB = 8
 LANES = 128
+GRANT = 20 << 20
 
 
 def rotated(value, axis, steps):
@@ -178,37 +179,31 @@
     return jnp.where(pos >= high, high, jnp.where(pos >= low, low, 0))
 
 
-def pack_kernel(nctx, scal, queries, residual, own, *outs):
-    rows = queries.shape[0]
-    cols = own.shape[1]
-    for step in range(nctx):
-        block = lax.rem(scal[0] + nctx - step, nctx)
-        part = residual[:, pl.ds(pl.multiple_of(block * cols, cols), cols)]
-        if step:
-            outs[step - 1][0:rows, :] = queries[...]
-            outs[step - 1][rows:, :] = part
-        else:
-            own[...] = part
-
-
-def pack(scal, queries, residual, nctx):
-    rows, width = queries.shape
-    shard = residual.shape[0]
-    message = jax.ShapeDtypeStruct((rows + shard, width), BF16)
-    return pl.pallas_call(
-        functools.partial(pack_kernel, nctx),
-        out_shape=(jax.ShapeDtypeStruct((shard, width), BF16),) + (message,) * (nctx - 1),
-        in_specs=[SMEM, VMEM, VMEM],
+def pack_kernel(scal, residual, *outs):
+    cols = outs[0].shape[1]
+    for flip, out in enumerate(outs):
+        block = jnp.bitwise_xor(scal[0], flip)
+        out[...] = residual[:, pl.ds(pl.multiple_of(block * cols, cols), cols)]
+
+
+def pack(scal, residual, nctx):
+    shard, width = residual.shape
+    part = jax.ShapeDtypeStruct((shard, width // nctx), BF16)
+    return pl.pallas_call(
+        pack_kernel,
+        out_shape=(part,) * nctx,
+        in_specs=[SMEM, VMEM],
         out_specs=(VMEM,) * nctx,
         name="pack",
-    )(scal, queries, residual)
-
-
-def join_kernel(nctx, scal, *refs):
+        compiler_params=pltpu.CompilerParams(vmem_limit_bytes=GRANT),
+    )(scal, residual)
+
+
+def join_kernel(scal, *refs):
     out = refs[-1]
     cols = refs[0].shape[1]
-    for step, part in enumerate(refs[:-1]):
-        block = lax.rem(scal[0] + nctx - step, nctx)
+    for flip, part in enumerate(refs[:-1]):
+        block = jnp.bitwise_xor(scal[0], flip)
         out[:, pl.ds(pl.multiple_of(block * cols, cols), cols)] = part[...]
 
 
@@ -216,11 +211,12 @@
     nctx = len(parts)
     shard, cols = parts[0].shape
     return pl.pallas_call(
-        functools.partial(join_kernel, nctx),
+        join_kernel,
         out_shape=jax.ShapeDtypeStruct((shard, nctx * cols), BF16),
         in_specs=[SMEM] + [VMEM] * nctx,
         out_specs=VMEM,
         name="join",
+        compiler_params=pltpu.CompilerParams(vmem_limit_bytes=GRANT),
     )(scal, *parts)
 
 
@@ -230,7 +226,7 @@
     for flip, piece in enumerate(refs[:-1]):
         member = jnp.bitwise_xor(mp_index, flip)
         for step in range(nctx):
-            block = lax.rem(ctx_index + step, nctx)
+            block = jnp.bitwise_xor(ctx_index, step)
             first = pl.multiple_of(block * rows + member * shard, shard)
             out[pl.ds(first, shard), :] = piece[step * shard : (step + 1) * shard, :]
 
@@ -244,6 +240,7 @@
         in_specs=[SMEM] + [VMEM] * len(pieces),
         out_specs=VMEM,
         name="assemble",
+        compiler_params=pltpu.CompilerParams(vmem_limit_bytes=GRANT),
     )(scal, *pieces)
 
 
@@ -259,7 +256,7 @@
     window = min(back + 1, nctx) * rows
     scale = 1.0 / math.sqrt(HD)
     for j, step in enumerate(steps):
-        block = lax.rem(ctx_index + step, nctx)
+        block = jnp.bitwise_xor(ctx_index, step)
         first_key = pl.multiple_of(
             jnp.minimum(jnp.maximum(block - back, 0), nctx - window // rows) * rows, rows
         )
@@ -268,7 +265,7 @@
         kpos = first_key + lax.broadcasted_iota(jnp.int32, (1, window), 1)
         allowed = (kpos <= qpos) & (kpos >= start) & (qpos - kpos < WIN)
         for h in range(heads):
-            query = q_refs[j][0:rows, h * HD : (h + 1) * HD]
+            query = q_refs[j][:, h * HD : (h + 1) * HD]
             keys = kv[pl.ds(first_key, window), :HD]
             scores = lax.dot_general(
                 query, keys, (((1,), (1,)), ((), ())), preferred_element_type=F32
@@ -284,8 +281,7 @@
         for out, which in ((send, 1 - side), (keep, side)):
             cols = pl.ds(pl.multiple_of(which * half, half), half)
             acc[...] = jnp.dot(att[...], weight[:, cols], preferred_element_type=F32)
-            mine = resid_refs[j][resid_refs[j].shape[0] - shard :, cols]
-            acc[own, :] += mine.astype(F32)
+            acc[own, :] += resid_refs[j][:, cols].astype(F32)
             out[j * rows : (j + 1) * rows, :] = acc[...].astype(BF16)
 
 
@@ -301,89 +297,122 @@
         out_specs=(VMEM, VMEM),
         scratch_shapes=[pltpu.VMEM((rows, width), BF16), pltpu.VMEM((rows, half), F32)],
         name="attend",
+        compiler_params=pltpu.CompilerParams(vmem_limit_bytes=GRANT),
     )(scal, *queries, *residuals, kv, weight)
 
 
-def project_kernel(jobs, nhalves, shard, scal, *refs):
-    halves, (gain, weight), outs = refs[:nhalves], refs[nhalves : nhalves + 2], refs[nhalves + 2 :]
+def split_weights(gain, weight, ctx_index, side):
+    half = weight.shape[0] // 2
+    out = []
+    for which in (side, 1 - side):
+        span = pl.multiple_of(which * half, half)
+        cols = pl.ds(pl.multiple_of(ctx_index * 2 * half + span, half), half)
+        out.append((gain[:, cols], weight[pl.ds(span, half), :]))
+    return out
+
+
+def project_kernel(count, scal, own, other, gain, weight, *outs):
     ctx_index, mp_index = scal[0], scal[1]
     side = jnp.bitwise_and(mp_index, 1)
+    rows = own.shape[0] // count
+    half = weight.shape[0] // 2
+    shard = outs[1].shape[0]
+    (gain_own, weight_own), (gain_other, weight_other) = split_weights(gain, weight, ctx_index, side)
+    for j in range(count):
+        span = slice(j * rows, (j + 1) * rows)
+        scaled_own = (own[span, :].astype(F32) * gain_own).astype(BF16)
+        scaled_other = (other[span, :].astype(F32) * gain_other).astype(BF16)
+        outs[2 * j][...] = (
+            jnp.dot(scaled_own, weight_own, preferred_element_type=F32)
+            + jnp.dot(scaled_other, weight_other, preferred_element_type=F32)
+        ).astype(BF16)
+        mine = pl.ds(pl.multiple_of(j * rows + mp_index * shard, TILE), shard)
+        for which, ref in ((side, own), (1 - side, other)):
+            outs[2 * j + 1][:, pl.ds(pl.multiple_of(which * half, half), half)] = ref[mine, :]
+
+
+def project(scal, own, other, gain, weight, count, shard):
+    rows = own.shape[0] // count
+    features, channels = weight.shape
+    shapes = []
+    for _ in range(count):
+        shapes.append(jax.ShapeDtypeStruct((rows, channels), BF16))
+        shapes.append(jax.ShapeDtypeStruct((shard, features), BF16))
+    return pl.pallas_call(
+        functools.partial(project_kernel, count),
+        out_shape=tuple(shapes),
+        in_specs=[SMEM] + [VMEM] * 4,
+        out_specs=(VMEM,) * len(shapes),
+        name="project",
+        compiler_params=pltpu.CompilerParams(vmem_limit_bytes=GRANT),
+    )(scal, own, other, gain, weight)
+
+
+def tails_kernel(places, nhalves, rows, scal, *refs):
+    nctx = len(places)
+    halves, (gain, weight) = refs[:nhalves], refs[nhalves : nhalves + 2]
+    outs = refs[nhalves + 2 : nhalves + 2 + nctx]
+    edges, ends = refs[nhalves + 2 + nctx :]
+    ctx_index = scal[0]
+    side = jnp.bitwise_and(scal[1], 1)
     channels = weight.shape[1]
     half = weight.shape[0] // 2
-    gains, weights = [], []
-    for which in (side, 1 - side):
-        span = pl.multiple_of(which * half, half)
-        gains.append(gain[:, pl.ds(pl.multiple_of(ctx_index * 2 * half + span, half), half)])
-        weights.append(weight[pl.ds(span, half), :])
+    split = split_weights(gain, weight, ctx_index, side)
     ones = jnp.ones((SUB, half), BF16)
 
-    def parts_of(source, last):
-        (own_ref, other_ref), first, rows = source
-        begin = first + rows - last if last else first
-        stop = first + rows
-        return own_ref[begin:stop, :].astype(F32), other_ref[begin:stop, :].astype(F32)
-
-    def projected(parts):
-        total = None
-        for part, scale, matrix in zip(parts, gains, weights):
-            term = jnp.dot((part * scale).astype(BF16), matrix, preferred_element_type=F32)
-            total = term if total is None else total + term
-        return total
-
-    def squares(parts):
-        total = None
-        for part in parts:
-            term = lax.dot_general(
-                ones, (part * part).astype(BF16), (((1,), (1,)), ((), ())), preferred_element_type=F32
-            )
-            total = term if total is None else total + term
-        return total
-
-    at = 0
-    for main, prior in jobs:
-        sums = []
-        if main is not None:
-            source = ((halves[main[0]], halves[main[0] + 1]), main[1], main[2])
-            rows = main[2]
-            parts = parts_of(source, 0)
-            outs[at][0:rows, :] = projected(parts).astype(BF16)
-            sums = squares(parts)
-            mine = pl.ds(pl.multiple_of(main[1] + mp_index * shard, TILE), shard)
-            for which, ref in ((side, source[0][0]), (1 - side, source[0][1])):
-                outs[at + 1][:, pl.ds(pl.multiple_of(which * half, half), half)] = ref[mine, :]
-        if prior is not None:
-            source = ((halves[prior[0]], halves[prior[0] + 1]), prior[1], prior[2])
-            tail = projected(parts_of(source, TILE))[TILE - SUB :, :]
-            tail_sums = squares(parts_of(source, LANES))
-            line = outs[at]
-            base = rows if main is not None else 0
-            if main is None:
-                own = ((halves[prior[3]], halves[prior[3] + 1]), prior[4], prior[5])
-                sums = squares(parts_of(own, 0))
-            spare = channels - sums.shape[1] - LANES
-            pieces = [sums, tail_sums] + ([jnp.zeros((SUB, spare), F32)] if spare else [])
-            sums = jnp.concatenate(pieces, axis=1)
-            coarse = sums.astype(BF16).astype(F32)
-            index = lax.broadcasted_iota(jnp.int32, sums.shape, 0)
-            sums = jnp.where(index == 0, coarse, sums - coarse)
-            line[base : base + TILE, :] = jnp.concatenate([sums, tail], axis=0).astype(BF16)
-        at += 1 if main is None else 2
-
-
-def project(scal, halves, gain, weight, jobs, shard):
-    channels = weight.shape[1]
-    shapes = []
-    for main, prior in jobs:
-        extra = TILE if prior is not None else 0
-        shapes.append(jax.ShapeDtypeStruct(((main[2] if main else 0) + extra, channels), BF16))
-        if main is not None:
-            shapes.append(jax.ShapeDtypeStruct((shard, weight.shape[0]), BF16))
-    return pl.pallas_call(
-        functools.partial(project_kernel, jobs, len(halves), shard),
-        out_shape=tuple(shapes),
+    def squares(piece):
+        value = piece.astype(F32)
+        return lax.dot_general(
+            ones, (value * value).astype(BF16), (((1,), (1,)), ((), ())), preferred_element_type=F32
+        )
+
+    for flip, (at, first) in enumerate(places):
+        block = jnp.bitwise_xor(ctx_index, flip)
+        for k in range(2):
+            piece = halves[2 * at + k][first + rows - LANES : first + rows, :]
+            edges[k, pl.ds(pl.multiple_of(block * LANES, LANES), LANES), :] = piece
+    sums = []
+    for flip, (at, first) in enumerate(places):
+        before = lax.rem(jnp.bitwise_xor(ctx_index, flip) + nctx - 1, nctx)
+        main = edge = None
+        for k in range(2):
+            part = edges[k, pl.ds(pl.multiple_of(before * LANES, LANES), LANES), :]
+            ends[k, flip * TILE : (flip + 1) * TILE, :] = part[LANES - TILE :, :]
+            term, edge_term = squares(halves[2 * at + k][first : first + rows, :]), squares(part)
+            main = term if main is None else main + term
+            edge = edge_term if edge is None else edge + edge_term
+        sums.append((main, edge))
+    tails = None
+    for k, (scale, matrix) in enumerate(split):
+        term = jnp.dot(
+            (ends[k].astype(F32) * scale).astype(BF16), matrix, preferred_element_type=F32
+        )
+        tails = term if tails is None else tails + term
+    spare = channels - rows - LANES
+    for flip, (main, edge) in enumerate(sums):
+        pieces = [main, edge] + ([jnp.zeros((SUB, spare), F32)] if spare else [])
+        line = jnp.concatenate(pieces, axis=1)
+        coarse = line.astype(BF16).astype(F32)
+        index = lax.broadcasted_iota(jnp.int32, line.shape, 0)
+        line = jnp.where(index == 0, coarse, line - coarse)
+        tail = tails[(flip + 1) * TILE - SUB : (flip + 1) * TILE, :]
+        outs[flip][...] = jnp.concatenate([line, tail], axis=0).astype(BF16)
+
+
+def tails(scal, halves, places, gain, weight, rows):
+    nctx = len(places)
+    half, channels = weight.shape[0] // 2, weight.shape[1]
+    return pl.pallas_call(
+        functools.partial(tails_kernel, places, len(halves), rows),
+        out_shape=(jax.ShapeDtypeStruct((TILE, channels), BF16),) * nctx,
         in_specs=[SMEM] + [VMEM] * (len(halves) + 2),
-        out_specs=tuple([VMEM] * len(shapes)),
-        name="project",
+        out_specs=(VMEM,) * nctx,
+        scratch_shapes=[
+            pltpu.VMEM((2, nctx * LANES, half), BF16),
+            pltpu.VMEM((2, nctx * TILE, half), BF16),
+        ],
+        name="tails",
+        compiler_params=pltpu.CompilerParams(vmem_limit_bytes=GRANT),
     )(scal, *halves, gain, weight)
 
 
@@ -394,29 +423,49 @@
     return jnp.where(x > -0.3, -x * series, 1.0 - jnp.exp(x))
 
 
-def recur_kernel(features, scal, *refs):
-    count = (len(refs) - 12) // 2
-    mains, lines = refs[:count], refs[count : 2 * count]
-    conv_w, decay_w, input_w, decay_b, input_b, codes = refs[2 * count : 2 * count + 6]
-    local_ref, cum_ref, last_ref, ext, keep_s, state_s = refs[2 * count + 6 :]
+def stats_kernel(features, *refs):
+    lines, (factor_ref, ahead_ref) = refs[:-2], refs[-2:]
+    length = factor_ref.shape[0]
+    sums = tail = None
+    for line in lines:
+        term = line[0:1, :length].astype(F32) + line[1:2, :length].astype(F32)
+        tail_term = line[...].astype(F32)[SUB:, :]
+        sums = term if sums is None else sums + term
+        tail = tail_term if tail is None else tail + tail_term
+    factor = lax.rsqrt(sums * (1.0 / features) + 1e-06)
+    factor = jnp.transpose(jnp.broadcast_to(factor, (LANES, length)))
+    factor_ref[...] = factor
+    ahead_ref[...] = (tail * factor[length - SUB :, 0:1]).astype(BF16).astype(F32)
+
+
+def stats(lines, rows, features):
+    channels = lines[0].shape[1]
+    return pl.pallas_call(
+        functools.partial(stats_kernel, features),
+        out_shape=(
+            jax.ShapeDtypeStruct((rows + LANES, LANES), F32),
+            jax.ShapeDtypeStruct((SUB, channels), F32),
+        ),
+        in_specs=[VMEM] * len(lines),
+        out_specs=(VMEM, VMEM),
+        name="stats",
+        compiler_params=pltpu.CompilerParams(vmem_limit_bytes=GRANT),
+    )(*lines)
+
+
+def recur_kernel(count, scal, *refs):
+    mains, (factor, ahead) = refs[:count], refs[count : count + 2]
+    conv_w, decay_w, input_w, decay_b, input_b, codes = refs[count + 2 : count + 8]
+    local_ref, cum_ref, last_ref, ext, keep_s, state_s = refs[count + 8 :]
     rows = mains[0].shape[0]
     width = mains[0].shape[1]
     ctx_index, low, high = scal[0], scal[2], scal[3]
-    stats = None
-    for line in lines:
-        both = line[:, : rows + LANES].astype(F32)
-        term = both[0:1, :] + both[1:2, :]
-        stats = term if stats is None else stats + term
-    inverse = lax.rsqrt(stats * (1.0 / features) + 1e-06)
-    inverse = jnp.transpose(jnp.broadcast_to(inverse, (LANES, rows + LANES)))[:, 0:1]
-    lanes = pl.ds(pl.multiple_of(pl.program_id(0) * width, width), width)
-    main = tail = None
-    for piece, line in zip(mains, lines):
-        term, tail_term = piece[...].astype(F32), line[:, lanes].astype(F32)[SUB:, :]
+    main = None
+    for piece in mains:
+        term = piece[...].astype(F32)
         main = term if main is None else main + term
-        tail = tail_term if tail is None else tail + tail_term
-    ext[0:SUB, :] = (tail * inverse[rows + LANES - SUB :, :]).astype(BF16).astype(F32)
-    ext[SUB : SUB + rows, :] = (main * inverse[:rows, :]).astype(BF16).astype(F32)
+    ext[0:SUB, :] = ahead[...]
+    ext[SUB : SUB + rows, :] = (main * factor[:rows, 0:1]).astype(BF16).astype(F32)
     pos = ctx_index * rows + lax.broadcasted_iota(jnp.int32, (rows, 1), 0)
     start = segment_start(pos, low, high)
     conv = None
@@ -464,24 +513,22 @@
     last_ref[...] = jnp.where(line == 0, run_keep, run_state)
 
 
-def recur(scal, mains, lines, conv_w, decay_w, input_w, decay_b, input_b, codes, rows, features):
+def recur(scal, mains, factor, ahead, conv_w, decay_w, input_w, decay_b, input_b, codes, rows):
     channels = conv_w.shape[1]
     tiles = rows // SUB
     by_block = pl.BlockSpec((rows, BW), lambda j: (0, j))
     row_spec = pl.BlockSpec((1, BW), lambda j: (0, j))
     gate_spec = pl.BlockSpec((1, BW, BW), lambda j: (j, 0, 0))
-    line_specs = [
-        pl.BlockSpec((TILE, channels), functools.partial(lambda at, j: (at, 0), at))
-        for _, at in lines
-    ]
+    factor_spec = pl.BlockSpec(factor.shape, lambda j: (0, 0))
+    ahead_spec = pl.BlockSpec((SUB, BW), lambda j: (0, j))
     full = jax.ShapeDtypeStruct((rows, channels), F32)
     return pl.pallas_call(
-        functools.partial(recur_kernel, features),
+        functools.partial(recur_kernel, len(mains)),
         grid=(channels // BW,),
         out_shape=(full, full, jax.ShapeDtypeStruct((SUB, channels), F32)),
         in_specs=[SMEM]
         + [by_block] * len(mains)
-        + line_specs
+        + [factor_spec, ahead_spec]
         + [pl.BlockSpec((CONV, BW), lambda j: (0, j)), gate_spec, gate_spec]
         + [row_spec] * 3,
         out_specs=(by_block, by_block, pl.BlockSpec((SUB, BW), lambda j: (0, j))),
@@ -491,7 +538,8 @@
             pltpu.VMEM((tiles, SUB, BW), F32),
         ],
         name="recur",
-    )(scal, *mains, *[line for line, _ in lines], conv_w, decay_w, input_w, decay_b, input_b, codes)
+        compiler_params=pltpu.CompilerParams(vmem_limit_bytes=GRANT),
+    )(scal, *mains, factor, ahead, conv_w, decay_w, input_w, decay_b, input_b, codes)
 
 
 def local_near(
@@ -520,13 +568,17 @@
     reach = min(nctx - 1, -(-longest // rows))
     place = jnp.stack([ctx_index, mp_index]).astype(jnp.int32)
 
+    visiting = {0: queries}
+    for flip in range(nctx - 1, 0, -2):
+        visiting[flip] = swapped(queries, "ctx", flip)
+    for flip in range(nctx - 2, 0, -2):
+        visiting[flip] = swapped(visiting[flip + 1], "ctx", 1)
     kv_parts = [keyvals]
-    for step in range(1, nctx):
-        kv_parts.append(rotated(keyvals, "ctx", step))
-    own_resid, *messages_out = pack(place, queries, residual, nctx)
-    visiting = [queries]
-    for step in range(1, nctx):
-        visiting.append(rotated(messages_out[step - 1], "ctx", step))
+    for flip in range(1, nctx):
+        kv_parts.append(swapped(keyvals, "ctx", flip))
+    resid_parts = list(pack(place, residual, nctx))
+    for flip in range(1, nctx):
+        resid_parts[flip] = swapped(resid_parts[flip], "ctx", flip)
     pieces = {0: jnp.concatenate(kv_parts, axis=0)}
     flip = nmp // 2
     while flip >= 1:
@@ -538,20 +590,20 @@
     high = jnp.sum((segment_ids < 2).astype(jnp.int32))
     scal = jnp.stack([ctx_index, mp_index, low, high]).astype(jnp.int32)
 
-    chunks = [tuple(range(min(2, nctx)))] + [(step,) for step in range(2, nctx)]
+    chunks = [(0,)] + [(nctx - 1,)] + ([tuple(range(1, nctx - 1))] if nctx > 2 else [])
     gain = norm_gain.reshape(1, features)
-    where_is, chunk_halves = {}, []
-    messages, resid_rows = {}, {}
-    for at, steps in enumerate(chunks):
+    halves, places = [], {}
+    messages, give = {}, {}
+    for at, flips in enumerate(chunks):
         keep, send = attend(
             scal,
-            [visiting[s] for s in steps],
-            [visiting[s] if s else own_resid for s in steps],
+            [visiting[e] for e in flips],
+            [resid_parts[e] for e in flips],
             kv,
             out_weight,
             nctx,
             back,
-            steps,
+            flips,
             shard,
         )
         other = swapped(send, "mp", 1)
@@ -562,38 +614,25 @@
             mine = (mine.astype(F32) + other.astype(F32)).astype(BF16)
             flip *= 2
         other = swapped(mine, "mp", 1)
-        for j, s in enumerate(steps):
-            where_is[s] = (at, j * rows, rows)
-        chunk_halves.append((mine, other))
-        ends = steps[-1] == nctx - 1
-        used = sorted({where_is[s][0] for s in steps} | {where_is[s - 1][0] for s in steps if s} | ({0} if ends else set()))
-        slot = {c: 2 * i for i, c in enumerate(used)}
-        held = [piece for c in used for piece in chunk_halves[c]]
-
-        def found(s):
-            c, first, length = where_is[s]
-            return (slot[c], first, length)
-
-        jobs = [(found(s), found(s - 1) if s else None) for s in steps]
-        if ends:
-            jobs.append((None, found(nctx - 1) + found(0)))
-        outs = project(scal, held, gain, lru_weight, jobs, shard)
-        for j, s in enumerate(steps):
-            messages[s], resid_rows[s] = outs[2 * j], outs[2 * j + 1]
-        if ends:
-            own_line = outs[2 * len(steps)]
-    mains, lines = [messages[0]], [(own_line, 0)]
-    for step in range(1, nctx):
-        got = rotated(messages[step], "ctx", -step)
-        mains.append(got)
-        lines.append((got, rows // TILE))
-    resid_parts = [resid_rows[0]]
-    for step in range(1, nctx):
-        resid_parts.append(rotated(resid_rows[step], "ctx", -step))
+        halves += [mine, other]
+        outs = project(scal, mine, other, gain, lru_weight, len(flips), shard)
+        for j, e in enumerate(flips):
+            places[e] = (at, j * rows)
+            messages[e], give[e] = outs[2 * j], outs[2 * j + 1]
+    lines = list(tails(scal, halves, [places[e] for e in range(nctx)], gain, lru_weight, rows))
+    mains = [messages[0]]
+    for flip in range(1, nctx):
+        mains.append(swapped(messages[flip], "ctx", flip))
+        lines[flip] = swapped(lines[flip], "ctx", flip)
+    factor, ahead = stats(lines, rows, features)
+    given = [give[0]]
+    for flip in range(1, nctx):
+        given.append(swapped(give[flip], "ctx", flip))
     local_state, cum_keep, last = recur(
         scal,
         mains,
-        lines,
+        factor,
+        ahead,
         conv_weight,
         gate_decay_w,
         gate_input_w,
@@ -601,12 +640,11 @@
         gate_input_b.reshape(1, -1),
         decay_codes.reshape(1, -1),
         rows,
-        features,
     )
     before = []
     for step in range(1, reach + 1):
         before.append(rotated(last, "ctx", -step))
-    resid_out = join(place, resid_parts)
+    resid_out = join(place, given)
     incoming = jnp.zeros_like(last[0])
     for step in range(reach, 0, -1):
         piece = before[step - 1]
@@ -616,8 +654,10 @@
 
 
 def local(queries, keyvals, segment_ids, residual, out_weight, *rest):
+    nctx = lax.axis_size("ctx")
     near = (
         segment_ids.shape[0] <= WIN
+        and nctx & (nctx - 1) == 0
         and lax.axis_size("mp") % 2 == 0
         and queries.shape[1] == out_weight.shape[1]
     )

time: 181 us -> 158 us (0.87)
  Pallas kernels: 45.9 us -> 27 us
  local copies, waits for them, and re-layouts: 8.66 us -> 1.96 us
  starting transfers between devices: 53.9 us -> 58.7 us
  other arithmetic: 7.72 us -> 4.47 us
    ppermute x12 -> x30, starting transfers between devices: 4.99 us -> 57.7 us  [swapped(): return lax.ppermute(value, axis, [(s, s ^ flip) for s in range(count)])]
    ppermute x14 -> x2, starting transfers between devices: 48.9 us -> 1.03 us  [rotated(): lax.ppermute(value, axis, [(s, (s - steps) % count) for s in range(count)])]
    ppermute x12 -> x30, waiting for transfers between devices: 20.2 us -> 61.1 us  [swapped(): return lax.ppermute(value, axis, [(s, s ^ flip) for s in range(count)])]
    ppermute x14 -> x2, waiting for transfers between devices: 43.5 us -> 3.42 us  [rotated(): lax.ppermute(value, axis, [(s, (s - steps) % count) for s in range(count)])]
    pallas_call x6 -> x8, Pallas kernels: 24.4 us -> 13.3 us  [the longest x1 4.81 us: recur(): pl.pallas_call(functools.partial(recur_kernel, len(mains)), grid=(channel...]
    pallas_call x3, Pallas kernels: 19.3 us -> 12.5 us  [attend(): pl.pallas_call(functools.partial(attend_kernel, nctx, back, steps, shard)...]
    unnamed x51 -> x25, local copies, waits for them, and re-layouts: 8.65 us -> 1.96 us
  transfers between devices with their start and end apart: 26 -> 32, of which waited for: 9 -> 12; matrix products, arithmetic and copies ran while one was open for 3% -> 3% of each run, Pallas kernels for 25% -> 14%
where the time goes in v3:
time: 158 us
  waiting for transfers between devices  64.5 us (41%)
  starting transfers between devices  58.7 us (37%)
  Pallas kernels  27 us (17%)
  other arithmetic  4.47 us (3%)
  local copies, waits for them, and re-layouts  1.96 us (1%)
    ppermute x30, waiting for transfers between devices, swapped(): return lax.ppermute(value, axis, [(s, s ^ flip) for s in range(count)])  61.1 us
    ppermute x30, starting transfers between devices, swapped(): return lax.ppermute(value, axis, [(s, s ^ flip) for s in range(count)])  57.7 us
    pallas_call x3, Pallas kernels, attend(): pl.pallas_call(functools.partial(attend_kernel, nctx, back, steps, shard)...  12.5 us
    pallas_call x1, Pallas kernels, recur(): pl.pallas_call(functools.partial(recur_kernel, len(mains)), grid=(channel...  4.81 us
    pallas_call x3, Pallas kernels, project(): pl.pallas_call(functools.partial(project_kernel, count), out_shape=tuple(...  4.52 us
    ppermute x2, waiting for transfers between devices, rotated(): lax.ppermute(value, axis, [(s, (s - steps) % count) for s in range(count)])  3.42 us
  transfers between devices with their start and end apart: 32, of which 12 were waited for; matrix products, arithmetic and copies ran while one was open for 3% of the time, Pallas kernels for 14%

profile of v3, /device:TPU:0, one launch (start us, length us, event | category | flops | bytes accessed | tf_op | source)
XLA Modules:
  0.0 157.6 jit_solution(15771426738250038582)
XLA Ops:
  0.6 4.1 %collective-permute-start.1 = (bf16[64,512]{1,0:T(8,128)(2,1)}, bf16[64,512]{1,0:T(8,128)(2,1)S(1)}, u32[]{:S(2)}, u32[]{:S(2)}) collective-permute-start(bf16[64,512]{1,0:T(8,128)(2,1)} %param.14), channel_id=1, source_target_pairs={{0,8},{4,12},{8,0},{12,4},{1,9},{5,13},{9,1},{13,5},{2,10},{6,14},... | collective-permute-start | bytes 196616 | tf_op jit(solution)/shard_map/ppermute | solution.py:175
  4.8 1.6 %collective-permute-start = (bf16[64,512]{1,0:T(8,128)(2,1)}, bf16[64,512]{1,0:T(8,128)(2,1)S(1)}, u32[]{:S(2)}, u32[]{:S(2)}) collective-permute-start(bf16[64,512]{1,0:T(8,128)(2,1)} %param.14), channel_id=1, source_target_pairs={{0,4},{4,0},{8,12},{12,8},{1,5},{5,1},{9,13},{13,9},{2,6},{6,2},{1... | collective-permute-start | bytes 196616 | tf_op jit(solution)/shard_map/ppermute | solution.py:175
  6.3 3.8 %collective-permute-start.10 = (bf16[256,1024]{1,0:T(8,128)(2,1)}, bf16[256,1024]{1,0:T(8,128)(2,1)}, u32[]{:S(2)}, u32[]{:S(2)}) collective-permute-start(bf16[256,1024]{1,0:T(8,128)(2,1)} %refs_0_.1), channel_id=1, source_target_pairs={{0,12},{4,8},{8,4},{12,0},{1,13},{5,9},{9,5},{13,1},{2,14},{6,10},... | collective-permute-start | bytes 1572872 | tf_op jit(solution)/shard_map/ppermute | solution.py:175
  10.2 0.8 constant_dynamic-update-slice_fusion.3
  11.1 2.3 %collective-permute-done.2 = bf16[64,512]{1,0:T(8,128)(2,1)S(1)} collective-permute-done((bf16[64,512]{1,0:T(8,128)(2,1)}, bf16[64,512]{1,0:T(8,128)(2,1)S(1)}, u32[]{:S(2)}, u32[]{:S(2)}) %collective-permute-start.2) | collective-permute-done | bytes 65568 | tf_op jit(solution)/shard_map/ppermute | solution.py:175
  13.4 1.5 collective-permute-start.4
  14.9 11.2 %collective-permute-start.9 = (bf16[256,1024]{1,0:T(8,128)(2,1)}, bf16[256,1024]{1,0:T(8,128)(2,1)S(1)}, u32[]{:S(2)}, u32[]{:S(2)}) collective-permute-start(bf16[256,1024]{1,0:T(8,128)(2,1)} %refs_0_.1), channel_id=1, source_target_pairs={{0,4},{4,0},{8,12},{12,8},{1,5},{5,1},{9,13},{13,9},{2,6},{6,2},{1... | collective-permute-start | bytes 1572872 | tf_op jit(solution)/shard_map/ppermute | solution.py:175
  26.1 8.6 %collective-permute-start.11 = (bf16[256,1024]{1,0:T(8,128)(2,1)}, bf16[256,1024]{1,0:T(8,128)(2,1)S(1)}, u32[]{:S(2)}, u32[]{:S(2)}) collective-permute-start(bf16[256,1024]{1,0:T(8,128)(2,1)} %collective-permute-done.10.refs_0_), channel_id=1, source_target_pairs={{0,4},{4,0},{8,12},{12,8},{1,5},{5,1},{9,13},{13,9},{2,6},{6,2},{1... | collective-permute-start | bytes 1572872 | tf_op jit(solution)/shard_map/ppermute | solution.py:175
  34.7 0.5 collective-permute-start.5
  35.3 0.1 pad_add_fusion.scal
  35.3 1.0 copy-done.2
  36.4 0.6 pack.1
  37.0 0.1 collective-permute-start.12
  37.0 3.8 %collective-permute-start.13 = (bf16[64,1024]{1,0:T(8,128)(2,1)S(1)}, bf16[64,1024]{1,0:T(8,128)(2,1)S(1)}, u32[]{:S(2)}, u32[]{:S(2)}) collective-permute-start(bf16[64,1024]{1,0:T(8,128)(2,1)S(1)} %get-tuple-element.34), channel_id=1, source_target_pairs={{0,8},{4,12},{8,0},{12,4},{1,9},{5,13},{9,1},{13,5},{2,10},{6,14},... | collective-permute-start | bytes 393224 | tf_op jit(solution)/shard_map/ppermute | solution.py:175
  40.8 1.4 convert_reduce_fusion.1
  42.2 1.4 pad_add_fusion.1.scal
  43.7 1.1 assemble.1.refs_2_.refs_4_
  44.8 8.5 %collective-permute-done.12.refs_2_ = bf16[64,1024]{1,0:T(8,128)(2,1)S(1)} collective-permute-done((bf16[64,1024]{1,0:T(8,128)(2,1)S(1)}, bf16[64,1024]{1,0:T(8,128)(2,1)S(1)}, u32[]{:S(2)}, u32[]{:S(2)}) %collective-permute-start.12) | collective-permute-done | bytes 131104 | tf_op jit(solution)/shard_map/ppermute | solution.py:175
  53.3 5.6 %attend.4 = (bf16[512,512]{1,0:T(8,128)(2,1)S(1)}, bf16[512,512]{1,0:T(8,128)(2,1)S(1)}) custom-call(s32[4]{0:T(128)S(1)} %pad_add_fusion.1.scal, bf16[256,1024]{1,0:T(8,128)(2,1)S(1)} %collective-permute-done.9.refs_0_, bf16[256,1024]{1,0:T(8,128)(2,1)S(1)} %collective-permute-done.11.refs_1_, bf16[64,1024]{1,0:T(8,128)(2,1)S(1)} %collective-permute-done.12.refs_2_, ...), custom_call_target="tpu_custom_call" | custom-call | tf_op jit(solution)/shard_map/attend/pallas_call | solution.py:293
  58.9 0.1 collective-permute-start.14
  58.9 3.5 %collective-permute-start.19 = (bf16[64,1024]{1,0:T(8,128)(2,1)S(1)}, bf16[64,1024]{1,0:T(8,128)(2,1)S(1)}, u32[]{:S(2)}, u32[]{:S(2)}) collective-permute-start(bf16[64,1024]{1,0:T(8,128)(2,1)S(1)} %get-tuple-element.39), channel_id=1, source_target_pairs={{0,12},{4,8},{8,4},{12,0},{1,13},{5,9},{9,5},{13,1},{2,14},{6,10},... | collective-permute-start | bytes 393224 | tf_op jit(solution)/shard_map/ppermute | solution.py:175
  62.4 0.1 add_convert_fusion.2
  62.6 0.6 collective-permute-start.15
  63.2 3.6 %collective-permute-done.19.refs_1_ = bf16[64,1024]{1,0:T(8,128)(2,1)S(1)} collective-permute-done((bf16[64,1024]{1,0:T(8,128)(2,1)S(1)}, bf16[64,1024]{1,0:T(8,128)(2,1)S(1)}, u32[]{:S(2)}, u32[]{:S(2)}) %collective-permute-start.19) | collective-permute-done | bytes 131104 | tf_op jit(solution)/shard_map/ppermute | solution.py:175
  66.7 3.7 %attend.5 = (bf16[256,512]{1,0:T(8,128)(2,1)S(1)}, bf16[256,512]{1,0:T(8,128)(2,1)S(1)}) custom-call(s32[4]{0:T(128)S(1)} %pad_add_fusion.1.scal, bf16[256,1024]{1,0:T(8,128)(2,1)} %collective-permute-done.10.refs_0_, bf16[64,1024]{1,0:T(8,128)(2,1)S(1)} %collective-permute-done.19.refs_1_, bf16[1024,512]{1,0:T(8,128)(2,1)S(1)} %assemble.1.refs_2_.refs_4_, ...), custom_call_target="tpu_custom_call" | custom-call | tf_op jit(solution)/shard_map/attend/pallas_call | solution.py:293
  70.5 0.1 collective-permute-start.20
  70.6 3.2 %attend.3 = (bf16[256,512]{1,0:T(8,128)(2,1)S(1)}, bf16[256,512]{1,0:T(8,128)(2,1)S(1)}) custom-call(s32[4]{0:T(128)S(1)} %pad_add_fusion.1.scal, bf16[256,1024]{1,0:T(8,128)(2,1)S(1)} %copy-done.3, bf16[64,1024]{1,0:T(8,128)(2,1)S(1)} %get-tuple-element.29.refs_1_, bf16[1024,512]{1,0:T(8,128)(2,1)S(1)} %assemble.1.refs_2_.refs_4_, ...), custom_call_target="tpu_custom_call" | custom-call | tf_op jit(solution)/shard_map/attend/pallas_call | solution.py:293
  73.8 0.5 collective-permute-start.6
  74.4 0.1 add_convert_fusion.4
  74.4 0.6 collective-permute-start.21
  75.0 1.6 collective-permute-done.15
  76.6 0.1 add_convert_fusion.1.own.refs_4_
  76.8 0.1 collective-permute-start.16
  76.8 5.9 %collective-permute-done.21 = bf16[256,512]{1,0:T(8,128)(2,1)S(1)} collective-permute-done((bf16[256,512]{1,0:T(8,128)(2,1)S(1)}, bf16[256,512]{1,0:T(8,128)(2,1)S(1)}, u32[]{:S(2)}, u32[]{:S(2)}) %collective-permute-start.21) | collective-permute-done | bytes 262176 | tf_op jit(solution)/shard_map/ppermute | solution.py:175
  82.8 0.1 add_convert_fusion.3.own.refs_2_
  82.8 0.1 collective-permute-start.22
  82.9 0.1 add_convert_fusion.6
  83.0 0.6 collective-permute-start.7
  83.6 0.8 collective-permute-done.22.other.refs_3_
  84.4 1.4 project.5
  85.9 3.5 %collective-permute-start.26 = (bf16[256,1024]{1,0:T(8,128)(2,1)S(1)}, bf16[256,1024]{1,0:T(8,128)(2,1)S(1)}, u32[]{:S(2)}, u32[]{:S(2)}) collective-permute-start(bf16[256,1024]{1,0:T(8,128)(2,1)S(1)} %get-tuple-element.46), channel_id=1, source_target_pairs={{0,12},{4,8},{8,4},{12,0},{1,13},{5,9},{9,5},{13,1},{2,14},{6,10},... | collective-permute-start | bytes 1572872 | tf_op jit(solution)/shard_map/ppermute | solution.py:175
  89.4 1.8 %project.4 = (bf16[256,1024]{1,0:T(8,128)(2,1)S(1)}, bf16[64,1024]{1,0:T(8,128)(2,1)S(1)}, bf16[256,1024]{1,0:T(8,128)(2,1)S(1)}, bf16[64,1024]{1,0:T(8,128)(2,1)S(1)}) custom-call(s32[4]{0:T(128)S(1)} %pad_add_fusion.1.scal, bf16[512,512]{1,0:T(8,128)(2,1)S(1)} %add_convert_fusion.1.own.refs_4_, bf16[512,512]{1,0:T(8,128)(2,1)S(1)} %collective-permute-done.16.other.refs_5_, ...), custom_call_target="tpu_custom_call" | custom-call | tf_op jit(solution)/shard_map/project/pallas_call | solution.py:341
  91.2 1.5 collective-permute-start.24
  92.8 0.1 collective-permute-start.8
  92.9 1.5 collective-permute-done.8.other.refs_1_
  94.4 1.8 %tails.1 = (bf16[16,1024]{1,0:T(8,128)(2,1)S(1)}, bf16[16,1024]{1,0:T(8,128)(2,1)S(1)}, bf16[16,1024]{1,0:T(8,128)(2,1)S(1)}, bf16[16,1024]{1,0:T(8,128)(2,1)S(1)}) custom-call(s32[4]{0:T(128)S(1)} %pad_add_fusion.1.scal, bf16[256,512]{1,0:T(8,128)(2,1)S(1)} %add_convert_fusion.5.own.refs_0_, bf16[256,512]{1,0:T(8,128)(2,1)S(1)} %collective-permute-done.8.other.refs_1_, ...), custom_call_target="tpu_custom_call" | custom-call | tf_op jit(solution)/shard_map/tails/pallas_call | solution.py:405
  96.3 2.4 %collective-permute-start.27 = (bf16[16,1024]{1,0:T(8,128)(2,1)S(1)}, bf16[16,1024]{1,0:T(8,128)(2,1)S(1)}, u32[]{:S(2)}, u32[]{:S(2)}) collective-permute-start(bf16[16,1024]{1,0:T(8,128)(2,1)S(1)} %get-tuple-element.48), channel_id=1, source_target_pairs={{0,4},{4,0},{8,12},{12,8},{1,5},{5,1},{9,13},{13,9},{2,6},{6,2},{1... | collective-permute-start | bytes 98312 | tf_op jit(solution)/shard_map/ppermute | solution.py:175
  98.7 1.2 collective-permute-start.28
  99.9 2.7 %collective-permute-done.26.refs_3_ = bf16[256,1024]{1,0:T(8,128)(2,1)S(1)} collective-permute-done((bf16[256,1024]{1,0:T(8,128)(2,1)S(1)}, bf16[256,1024]{1,0:T(8,128)(2,1)S(1)}, u32[]{:S(2)}, u32[]{:S(2)}) %collective-permute-start.26) | collective-permute-done | bytes 524320 | tf_op jit(solution)/shard_map/ppermute | solution.py:175
  102.6 3.4 %collective-permute-start.29 = (bf16[16,1024]{1,0:T(8,128)(2,1)S(1)}, bf16[16,1024]{1,0:T(8,128)(2,1)S(1)}, u32[]{:S(2)}, u32[]{:S(2)}) collective-permute-start(bf16[16,1024]{1,0:T(8,128)(2,1)S(1)} %get-tuple-element.50), channel_id=1, source_target_pairs={{0,12},{4,8},{8,4},{12,0},{1,13},{5,9},{9,5},{13,1},{2,14},{6,10},... | collective-permute-start | bytes 98312 | tf_op jit(solution)/shard_map/ppermute | solution.py:175
  106.0 18.9 %collective-permute-done.27.refs_1_ = bf16[16,1024]{1,0:T(8,128)(2,1)S(1)} collective-permute-done((bf16[16,1024]{1,0:T(8,128)(2,1)S(1)}, bf16[16,1024]{1,0:T(8,128)(2,1)S(1)}, u32[]{:S(2)}, u32[]{:S(2)}) %collective-permute-start.27) | collective-permute-done | bytes 32800 | tf_op jit(solution)/shard_map/ppermute | solution.py:175
  125.0 0.3 collective-permute-start.23
  125.3 15.1 %collective-permute-done.28.refs_2_ = bf16[16,1024]{1,0:T(8,128)(2,1)S(1)} collective-permute-done((bf16[16,1024]{1,0:T(8,128)(2,1)S(1)}, bf16[16,1024]{1,0:T(8,128)(2,1)S(1)}, u32[]{:S(2)}, u32[]{:S(2)}) %collective-permute-start.28) | collective-permute-done | bytes 32800 | tf_op jit(solution)/shard_map/ppermute | solution.py:175
  140.4 0.6 collective-permute-start.17
  141.0 3.4 %collective-permute-start.18 = (bf16[64,1024]{1,0:T(8,128)(2,1)S(1)}, bf16[64,1024]{1,0:T(8,128)(2,1)S(1)}, u32[]{:S(2)}, u32[]{:S(2)}) collective-permute-start(bf16[64,1024]{1,0:T(8,128)(2,1)S(1)} %get-tuple-element.38), channel_id=1, source_target_pairs={{0,8},{4,12},{8,0},{12,4},{1,9},{5,13},{9,1},{13,5},{2,10},{6,14},... | collective-permute-start | bytes 393224 | tf_op jit(solution)/shard_map/ppermute | solution.py:175
  144.4 1.3 project.3
  145.7 0.2 stats.1
  145.9 4.8 %recur.1 = (f32[256,1024]{1,0:T(8,128)S(1)}, f32[256,1024]{1,0:T(8,128)S(1)}, f32[8,1024]{1,0:T(8,128)S(1)}) custom-call(s32[4]{0:T(128)S(1)} %pad_add_fusion.1.scal, bf16[256,1024]{1,0:T(8,128)(2,1)S(1)} %get-tuple-element.43.refs_0_, bf16[256,1024]{1,0:T(8,128)(2,1)S(1)} %collective-permute-done.24.refs_1_, ...), custom_call_target="tpu_custom_call" | custom-call | tf_op jit(solution)/shard_map/recur/pallas_call | solution.py:525
  150.7 0.1 collective-permute-start.31
  150.8 1.0 collective-permute-start.30
  151.8 1.4 join.1
  153.2 2.6 %collective-permute-done.31 = f32[8,1024]{1,0:T(8,128)S(1)} collective-permute-done((f32[8,1024]{1,0:T(8,128)S(1)}, f32[8,1024]{1,0:T(8,128)S(1)}, u32[]{:S(2)}, u32[]{:S(2)}) %collective-permute-start.31) | collective-permute-done | bytes 32800 | tf_op jit(solution)/shard_map/ppermute | solution.py:170
  155.7 0.9 collective-permute-done.30
  156.6 1.0 add_convert_fusion
  (49 shorter events, 0.2 us)
Async XLA Ops:
  0.6 52.6 %copy-start.1 = (bf16[1024,1024]{1,0:T(8,128)(2,1)S(1)}, bf16[1024,1024]{1,0:T(8,128)(2,1)}, u32[]{:S(2)}) copy-start(bf16[1024,1024]{1,0:T(8,128)(2,1)} %refs_3_.3) | copy-start | bytes 6291460
  0.6 10.4 %collective-permute-start.1 = (bf16[64,512]{1,0:T(8,128)(2,1)}, bf16[64,512]{1,0:T(8,128)(2,1)S(1)}, u32[]{:S(2)}, u32[]{:S(2)}) collective-permute-start(bf16[64,512]{1,0:T(8,128)(2,1)} %param.14), channel_id=1, source_target_pairs={{0,8},{4,12},{8,0},{12,4},{1,9},{5,13},{9,1},{13,5},{2,10},{6,14},... | collective-permute-start | bytes 196616 | tf_op jit(solution)/shard_map/ppermute | solution.py:175
  4.8 6.2 %collective-permute-start = (bf16[64,512]{1,0:T(8,128)(2,1)}, bf16[64,512]{1,0:T(8,128)(2,1)S(1)}, u32[]{:S(2)}, u32[]{:S(2)}) collective-permute-start(bf16[64,512]{1,0:T(8,128)(2,1)} %param.14), channel_id=1, source_target_pairs={{0,4},{4,0},{8,12},{12,8},{1,5},{5,1},{9,13},{13,9},{2,6},{6,2},{1... | collective-permute-start | bytes 196616 | tf_op jit(solution)/shard_map/ppermute | solution.py:175
  6.3 7.0 %collective-permute-start.2 = (bf16[64,512]{1,0:T(8,128)(2,1)}, bf16[64,512]{1,0:T(8,128)(2,1)S(1)}, u32[]{:S(2)}, u32[]{:S(2)}) collective-permute-start(bf16[64,512]{1,0:T(8,128)(2,1)} %param.14), channel_id=1, source_target_pairs={{0,12},{4,8},{8,4},{12,0},{1,13},{5,9},{9,5},{13,1},{2,14},{6,10},... | collective-permute-start | bytes 196616 | tf_op jit(solution)/shard_map/ppermute | solution.py:175
  6.3 19.8 %collective-permute-start.10 = (bf16[256,1024]{1,0:T(8,128)(2,1)}, bf16[256,1024]{1,0:T(8,128)(2,1)}, u32[]{:S(2)}, u32[]{:S(2)}) collective-permute-start(bf16[256,1024]{1,0:T(8,128)(2,1)} %refs_0_.1), channel_id=1, source_target_pairs={{0,12},{4,8},{8,4},{12,0},{1,13},{5,9},{9,5},{13,1},{2,14},{6,10},... | collective-permute-start | bytes 1572872 | tf_op jit(solution)/shard_map/ppermute | solution.py:175
  13.4 21.4 %collective-permute-start.4 = (bf16[256,512]{1,0:T(8,128)(2,1)S(1)}, bf16[256,512]{1,0:T(8,128)(2,1)}, u32[]{:S(2)}, u32[]{:S(2)}) collective-permute-start(bf16[256,512]{1,0:T(8,128)(2,1)S(1)} %constant_dynamic-update-slice_fusion.refs_0_), channel_id=1, source_target_pairs={{0,2},{1,3},{2,0},{3,1},{4,6},{5,7},{6,4},{7,5},{8,10},{9,11},{10,... | collective-permute-start | bytes 786440 | tf_op jit(solution)/shard_map/ppermute | solution.py:175
  14.9 38.4 %collective-permute-start.9 = (bf16[256,1024]{1,0:T(8,128)(2,1)}, bf16[256,1024]{1,0:T(8,128)(2,1)S(1)}, u32[]{:S(2)}, u32[]{:S(2)}) collective-permute-start(bf16[256,1024]{1,0:T(8,128)(2,1)} %refs_0_.1), channel_id=1, source_target_pairs={{0,4},{4,0},{8,12},{12,8},{1,5},{5,1},{9,13},{13,9},{2,6},{6,2},{1... | collective-permute-start | bytes 1572872 | tf_op jit(solution)/shard_map/ppermute | solution.py:175
  26.1 27.1 %collective-permute-start.11 = (bf16[256,1024]{1,0:T(8,128)(2,1)}, bf16[256,1024]{1,0:T(8,128)(2,1)S(1)}, u32[]{:S(2)}, u32[]{:S(2)}) collective-permute-start(bf16[256,1024]{1,0:T(8,128)(2,1)} %collective-permute-done.10.refs_0_), channel_id=1, source_target_pairs={{0,4},{4,0},{8,12},{12,8},{1,5},{5,1},{9,13},{13,9},{2,6},{6,2},{1... | collective-permute-start | bytes 1572872 | tf_op jit(solution)/shard_map/ppermute | solution.py:175
  34.7 2.3 %collective-permute-start.3 = (bf16[256,512]{1,0:T(8,128)(2,1)S(1)}, bf16[256,512]{1,0:T(8,128)(2,1)}, u32[]{:S(2)}, u32[]{:S(2)}) collective-permute-start(bf16[256,512]{1,0:T(8,128)(2,1)S(1)} %constant_dynamic-update-slice_fusion.refs_0_), channel_id=1, source_target_pairs={{0,1},{1,0},{2,3},{3,2},{4,5},{5,4},{6,7},{7,6},{8,9},{9,8},{10,11... | collective-permute-start | bytes 786440 | tf_op jit(solution)/shard_map/ppermute | solution.py:175
  34.7 8.9 %collective-permute-start.5 = (bf16[256,512]{1,0:T(8,128)(2,1)}, bf16[256,512]{1,0:T(8,128)(2,1)S(1)}, u32[]{:S(2)}, u32[]{:S(2)}) collective-permute-start(bf16[256,512]{1,0:T(8,128)(2,1)} %collective-permute-done.4.refs_2_), channel_id=1, source_target_pairs={{0,1},{1,0},{2,3},{3,2},{4,5},{5,4},{6,7},{7,6},{8,9},{9,8},{10,11... | collective-permute-start | bytes 786440 | tf_op jit(solution)/shard_map/ppermute | solution.py:175
  35.3 1.0 copy-start.2
  37.0 16.3 %collective-permute-start.12 = (bf16[64,1024]{1,0:T(8,128)(2,1)S(1)}, bf16[64,1024]{1,0:T(8,128)(2,1)S(1)}, u32[]{:S(2)}, u32[]{:S(2)}) collective-permute-start(bf16[64,1024]{1,0:T(8,128)(2,1)S(1)} %get-tuple-element.33), channel_id=1, source_target_pairs={{0,4},{4,0},{8,12},{12,8},{1,5},{5,1},{9,13},{13,9},{2,6},{6,2},{1... | collective-permute-start | bytes 393224 | tf_op jit(solution)/shard_map/ppermute | solution.py:175
  37.0 16.2 %collective-permute-start.13 = (bf16[64,1024]{1,0:T(8,128)(2,1)S(1)}, bf16[64,1024]{1,0:T(8,128)(2,1)S(1)}, u32[]{:S(2)}, u32[]{:S(2)}) collective-permute-start(bf16[64,1024]{1,0:T(8,128)(2,1)S(1)} %get-tuple-element.34), channel_id=1, source_target_pairs={{0,8},{4,12},{8,0},{12,4},{1,9},{5,13},{9,1},{13,5},{2,10},{6,14},... | collective-permute-start | bytes 393224 | tf_op jit(solution)/shard_map/ppermute | solution.py:175
  58.9 3.6 %collective-permute-start.14 = (bf16[512,512]{1,0:T(8,128)(2,1)S(1)}, bf16[512,512]{1,0:T(8,128)(2,1)S(1)}, u32[]{:S(2)}, u32[]{:S(2)}) collective-permute-start(bf16[512,512]{1,0:T(8,128)(2,1)S(1)} %get-tuple-element.36), channel_id=1, source_target_pairs={{0,1},{1,0},{2,3},{3,2},{4,5},{5,4},{6,7},{7,6},{8,9},{9,8},{10,11... | collective-permute-start | bytes 1572872 | tf_op jit(solution)/shard_map/ppermute | solution.py:175
  58.9 7.8 %collective-permute-start.19 = (bf16[64,1024]{1,0:T(8,128)(2,1)S(1)}, bf16[64,1024]{1,0:T(8,128)(2,1)S(1)}, u32[]{:S(2)}, u32[]{:S(2)}) collective-permute-start(bf16[64,1024]{1,0:T(8,128)(2,1)S(1)} %get-tuple-element.39), channel_id=1, source_target_pairs={{0,12},{4,8},{8,4},{12,0},{1,13},{5,9},{9,5},{13,1},{2,14},{6,10},... | collective-permute-start | bytes 393224 | tf_op jit(solution)/shard_map/ppermute | solution.py:175
  62.6 8.0 %copy-start.3 = (bf16[256,1024]{1,0:T(8,128)(2,1)S(1)}, bf16[256,1024]{1,0:T(8,128)(2,1)}, u32[]{:S(2)}) copy-start(bf16[256,1024]{1,0:T(8,128)(2,1)} %refs_0_.1) | copy-start | bytes 1572868
  62.6 14.0 %collective-permute-start.15 = (bf16[512,512]{1,0:T(8,128)(2,1)S(1)}, bf16[512,512]{1,0:T(8,128)(2,1)S(1)}, u32[]{:S(2)}, u32[]{:S(2)}) collective-permute-start(bf16[512,512]{1,0:T(8,128)(2,1)S(1)} %add_convert_fusion.2), channel_id=1, source_target_pairs={{0,2},{1,3},{2,0},{3,1},{4,6},{5,7},{6,4},{7,5},{8,10},{9,11},{10,... | collective-permute-start | bytes 1572872 | tf_op jit(solution)/shard_map/ppermute | solution.py:175
  70.5 3.9 %collective-permute-start.20 = (bf16[256,512]{1,0:T(8,128)(2,1)S(1)}, bf16[256,512]{1,0:T(8,128)(2,1)S(1)}, u32[]{:S(2)}, u32[]{:S(2)}) collective-permute-start(bf16[256,512]{1,0:T(8,128)(2,1)S(1)} %get-tuple-element.41), channel_id=1, source_target_pairs={{0,1},{1,0},{2,3},{3,2},{4,5},{5,4},{6,7},{7,6},{8,9},{9,8},{10,11... | collective-permute-start | bytes 786440 | tf_op jit(solution)/shard_map/ppermute | solution.py:175
  73.8 10.6 %copy-start = (bf16[1024,1024]{1,0:T(8,128)(2,1)S(1)}, bf16[1024,1024]{1,0:T(8,128)(2,1)}, u32[]{:S(2)}) copy-start(bf16[1024,1024]{1,0:T(8,128)(2,1)} %refs_7_.2) | copy-start | bytes 6291460
  73.8 10.6 %copy-start.6 = (f32[4096]{0:T(1024)S(1)}, f32[4096]{0:T(1024)}, u32[]{:S(2)}) copy-start(f32[4096]{0:T(1024)} %param.25) | copy-start | bytes 49156
  73.8 9.1 %collective-permute-start.6 = (bf16[256,512]{1,0:T(8,128)(2,1)S(1)}, bf16[256,512]{1,0:T(8,128)(2,1)S(1)}, u32[]{:S(2)}, u32[]{:S(2)}) collective-permute-start(bf16[256,512]{1,0:T(8,128)(2,1)S(1)} %get-tuple-element.31), channel_id=1, source_target_pairs={{0,1},{1,0},{2,3},{3,2},{4,5},{5,4},{6,7},{7,6},{8,9},{9,8},{10,11... | collective-permute-start | bytes 786440 | tf_op jit(solution)/shard_map/ppermute | solution.py:175
  74.4 8.3 %collective-permute-start.21 = (bf16[256,512]{1,0:T(8,128)(2,1)S(1)}, bf16[256,512]{1,0:T(8,128)(2,1)S(1)}, u32[]{:S(2)}, u32[]{:S(2)}) collective-permute-start(bf16[256,512]{1,0:T(8,128)(2,1)S(1)} %add_convert_fusion.4), channel_id=1, source_target_pairs={{0,2},{1,3},{2,0},{3,1},{4,6},{5,7},{6,4},{7,5},{8,10},{9,11},{10,... | collective-permute-start | bytes 786440 | tf_op jit(solution)/shard_map/ppermute | solution.py:175
  76.8 12.6 %collective-permute-start.16 = (bf16[512,512]{1,0:T(8,128)(2,1)S(1)}, bf16[512,512]{1,0:T(8,128)(2,1)S(1)}, u32[]{:S(2)}, u32[]{:S(2)}) collective-permute-start(bf16[512,512]{1,0:T(8,128)(2,1)S(1)} %add_convert_fusion.1.own.refs_4_), channel_id=1, source_target_pairs={{0,1},{1,0},{2,3},{3,2},{4,5},{5,4},{6,7},{7,6},{8,9},{9,8},{10,11... | collective-permute-start | bytes 1572872 | tf_op jit(solution)/shard_map/ppermute | solution.py:175
  82.8 1.6 %collective-permute-start.22 = (bf16[256,512]{1,0:T(8,128)(2,1)S(1)}, bf16[256,512]{1,0:T(8,128)(2,1)S(1)}, u32[]{:S(2)}, u32[]{:S(2)}) collective-permute-start(bf16[256,512]{1,0:T(8,128)(2,1)S(1)} %add_convert_fusion.3.own.refs_2_), channel_id=1, source_target_pairs={{0,1},{1,0},{2,3},{3,2},{4,5},{5,4},{6,7},{7,6},{8,9},{9,8},{10,11... | collective-permute-start | bytes 786440 | tf_op jit(solution)/shard_map/ppermute | solution.py:175
  83.0 9.7 %collective-permute-start.7 = (bf16[256,512]{1,0:T(8,128)(2,1)S(1)}, bf16[256,512]{1,0:T(8,128)(2,1)S(1)}, u32[]{:S(2)}, u32[]{:S(2)}) collective-permute-start(bf16[256,512]{1,0:T(8,128)(2,1)S(1)} %add_convert_fusion.6), channel_id=1, source_target_pairs={{0,2},{1,3},{2,0},{3,1},{4,6},{5,7},{6,4},{7,5},{8,10},{9,11},{10,... | collective-permute-start | bytes 786440 | tf_op jit(solution)/shard_map/ppermute | solution.py:175
  85.9 16.7 %collective-permute-start.26 = (bf16[256,1024]{1,0:T(8,128)(2,1)S(1)}, bf16[256,1024]{1,0:T(8,128)(2,1)S(1)}, u32[]{:S(2)}, u32[]{:S(2)}) collective-permute-start(bf16[256,1024]{1,0:T(8,128)(2,1)S(1)} %get-tuple-element.46), channel_id=1, source_target_pairs={{0,12},{4,8},{8,4},{12,0},{1,13},{5,9},{9,5},{13,1},{2,14},{6,10},... | collective-permute-start | bytes 1572872 | tf_op jit(solution)/shard_map/ppermute | solution.py:175
  91.2 54.6 %collective-permute-start.24 = (bf16[256,1024]{1,0:T(8,128)(2,1)S(1)}, bf16[256,1024]{1,0:T(8,128)(2,1)S(1)}, u32[]{:S(2)}, u32[]{:S(2)}) collective-permute-start(bf16[256,1024]{1,0:T(8,128)(2,1)S(1)} %get-tuple-element.44), channel_id=1, source_target_pairs={{0,4},{4,0},{8,12},{12,8},{1,5},{5,1},{9,13},{13,9},{2,6},{6,2},{1... | collective-permute-start | bytes 1572872 | tf_op jit(solution)/shard_map/ppermute | solution.py:175
  92.7 53.1 %collective-permute-start.25 = (bf16[256,1024]{1,0:T(8,128)(2,1)S(1)}, bf16[256,1024]{1,0:T(8,128)(2,1)S(1)}, u32[]{:S(2)}, u32[]{:S(2)}) collective-permute-start(bf16[256,1024]{1,0:T(8,128)(2,1)S(1)} %get-tuple-element.45), channel_id=1, source_target_pairs={{0,8},{4,12},{8,0},{12,4},{1,9},{5,13},{9,1},{13,5},{2,10},{6,14},... | collective-permute-start | bytes 1572872 | tf_op jit(solution)/shard_map/ppermute | solution.py:175
  92.8 1.6 %collective-permute-start.8 = (bf16[256,512]{1,0:T(8,128)(2,1)S(1)}, bf16[256,512]{1,0:T(8,128)(2,1)S(1)}, u32[]{:S(2)}, u32[]{:S(2)}) collective-permute-start(bf16[256,512]{1,0:T(8,128)(2,1)S(1)} %add_convert_fusion.5.own.refs_0_), channel_id=1, source_target_pairs={{0,1},{1,0},{2,3},{3,2},{4,5},{5,4},{6,7},{7,6},{8,9},{9,8},{10,11... | collective-permute-start | bytes 786440 | tf_op jit(solution)/shard_map/ppermute | solution.py:175
  96.3 49.6 %copy-start.4 = (bf16[4,256,256]{2,1,0:T(8,128)(2,1)S(1)}, bf16[4,256,256]{2,1,0:T(8,128)(2,1)}, u32[]{:S(2)}) copy-start(bf16[4,256,256]{2,1,0:T(8,128)(2,1)} %refs_7_.3) | copy-start | bytes 1572868
  96.3 49.6 %copy-start.5 = (bf16[4,256,256]{2,1,0:T(8,128)(2,1)S(1)}, bf16[4,256,256]{2,1,0:T(8,128)(2,1)}, u32[]{:S(2)}) copy-start(bf16[4,256,256]{2,1,0:T(8,128)(2,1)} %refs_8_.1) | copy-start | bytes 1572868
  96.3 49.6 %copy-start.7 = (f32[4,1024]{1,0:T(4,128)S(1)}, f32[4,1024]{1,0:T(4,128)}, u32[]{:S(2)}) copy-start(f32[4,1024]{1,0:T(4,128)} %refs_6_.1) | copy-start | bytes 49156
  96.3 49.6 %copy-start.8 = (f32[1024]{0:T(1024)S(1)}, f32[1024]{0:T(1024)}, u32[]{:S(2)}) copy-start(f32[1024]{0:T(1024)} %param.22) | copy-start | bytes 12292
  96.3 49.6 %copy-start.9 = (f32[1024]{0:T(1024)S(1)}, f32[1024]{0:T(1024)}, u32[]{:S(2)}) copy-start(f32[1024]{0:T(1024)} %param.23) | copy-start | bytes 12292
  96.3 49.6 %copy-start.10 = (s32[1024]{0:T(1024)S(1)}, s32[1024]{0:T(1024)}, u32[]{:S(2)}) copy-start(s32[1024]{0:T(1024)} %param.24) | copy-start | bytes 12292
  96.3 28.7 %collective-permute-start.27 = (bf16[16,1024]{1,0:T(8,128)(2,1)S(1)}, bf16[16,1024]{1,0:T(8,128)(2,1)S(1)}, u32[]{:S(2)}, u32[]{:S(2)}) collective-permute-start(bf16[16,1024]{1,0:T(8,128)(2,1)S(1)} %get-tuple-element.48), channel_id=1, source_target_pairs={{0,4},{4,0},{8,12},{12,8},{1,5},{5,1},{9,13},{13,9},{2,6},{6,2},{1... | collective-permute-start | bytes 98312 | tf_op jit(solution)/shard_map/ppermute | solution.py:175
  98.7 41.7 %collective-permute-start.28 = (bf16[16,1024]{1,0:T(8,128)(2,1)S(1)}, bf16[16,1024]{1,0:T(8,128)(2,1)S(1)}, u32[]{:S(2)}, u32[]{:S(2)}) collective-permute-start(bf16[16,1024]{1,0:T(8,128)(2,1)S(1)} %get-tuple-element.49), channel_id=1, source_target_pairs={{0,8},{4,12},{8,0},{12,4},{1,9},{5,13},{9,1},{13,5},{2,10},{6,14},... | collective-permute-start | bytes 98312 | tf_op jit(solution)/shard_map/ppermute | solution.py:175
  102.6 38.4 %collective-permute-start.29 = (bf16[16,1024]{1,0:T(8,128)(2,1)S(1)}, bf16[16,1024]{1,0:T(8,128)(2,1)S(1)}, u32[]{:S(2)}, u32[]{:S(2)}) collective-permute-start(bf16[16,1024]{1,0:T(8,128)(2,1)S(1)} %get-tuple-element.50), channel_id=1, source_target_pairs={{0,12},{4,8},{8,4},{12,0},{1,13},{5,9},{9,5},{13,1},{2,14},{6,10},... | collective-permute-start | bytes 98312 | tf_op jit(solution)/shard_map/ppermute | solution.py:175
  125.0 26.8 %collective-permute-start.23 = (bf16[64,1024]{1,0:T(8,128)(2,1)S(1)}, bf16[64,1024]{1,0:T(8,128)(2,1)S(1)}, u32[]{:S(2)}, u32[]{:S(2)}) collective-permute-start(bf16[64,1024]{1,0:T(8,128)(2,1)S(1)} %get-tuple-element.42), channel_id=1, source_target_pairs={{0,12},{4,8},{8,4},{12,0},{1,13},{5,9},{9,5},{13,1},{2,14},{6,10},... | collective-permute-start | bytes 393224 | tf_op jit(solution)/shard_map/ppermute | solution.py:175
  140.4 11.4 %collective-permute-start.17 = (bf16[64,1024]{1,0:T(8,128)(2,1)S(1)}, bf16[64,1024]{1,0:T(8,128)(2,1)S(1)}, u32[]{:S(2)}, u32[]{:S(2)}) collective-permute-start(bf16[64,1024]{1,0:T(8,128)(2,1)S(1)} %get-tuple-element.37), channel_id=1, source_target_pairs={{0,4},{4,0},{8,12},{12,8},{1,5},{5,1},{9,13},{13,9},{2,6},{6,2},{1... | collective-permute-start | bytes 393224 | tf_op jit(solution)/shard_map/ppermute | solution.py:175
  141.0 10.8 %collective-permute-start.18 = (bf16[64,1024]{1,0:T(8,128)(2,1)S(1)}, bf16[64,1024]{1,0:T(8,128)(2,1)S(1)}, u32[]{:S(2)}, u32[]{:S(2)}) collective-permute-start(bf16[64,1024]{1,0:T(8,128)(2,1)S(1)} %get-tuple-element.38), channel_id=1, source_target_pairs={{0,8},{4,12},{8,0},{12,4},{1,9},{5,13},{9,1},{13,5},{2,10},{6,14},... | collective-permute-start | bytes 393224 | tf_op jit(solution)/shard_map/ppermute | solution.py:175
  150.7 5.0 %collective-permute-start.31 = (f32[8,1024]{1,0:T(8,128)S(1)}, f32[8,1024]{1,0:T(8,128)S(1)}, u32[]{:S(2)}, u32[]{:S(2)}) collective-permute-start(f32[8,1024]{1,0:T(8,128)S(1)} %get-tuple-element.55), channel_id=1, source_target_pairs={{0,8},{4,12},{8,0},{12,4},{1,9},{5,13},{9,1},{13,5},{2,10},{6,14},... | collective-permute-start | bytes 98312 | tf_op jit(solution)/shard_map/ppermute | solution.py:170
  150.8 5.8 %collective-permute-start.30 = (f32[8,1024]{1,0:T(8,128)S(1)}, f32[8,1024]{1,0:T(8,128)S(1)}, u32[]{:S(2)}, u32[]{:S(2)}) collective-permute-start(f32[8,1024]{1,0:T(8,128)S(1)} %get-tuple-element.55), channel_id=1, source_target_pairs={{0,4},{4,8},{8,12},{12,0},{1,5},{5,9},{9,13},{13,1},{2,6},{6,10},{... | collective-permute-start | bytes 98312 | tf_op jit(solution)/shard_map/ppermute | solution.py:170

commit v4 on v3

--- a/solution.py
+++ b/solution.py
@@ -179,24 +179,31 @@
     return jnp.where(pos >= high, high, jnp.where(pos >= low, low, 0))
 
 
-def pack_kernel(scal, residual, *outs):
+def pack_kernel(residual, segments, scal, *outs):
     cols = outs[0].shape[1]
+    ctx_index = lax.axis_index("ctx")
+    ids = segments[...]
+    scal[0] = ctx_index
+    scal[1] = lax.axis_index("mp")
+    for at in (1, 2):
+        scal[at + 1] = jnp.sum((ids < at).astype(F32)).astype(jnp.int32)
     for flip, out in enumerate(outs):
-        block = jnp.bitwise_xor(scal[0], flip)
+        block = jnp.bitwise_xor(ctx_index, flip)
         out[...] = residual[:, pl.ds(pl.multiple_of(block * cols, cols), cols)]
 
 
-def pack(scal, residual, nctx):
+def pack(residual, segments, nctx):
     shard, width = residual.shape
     part = jax.ShapeDtypeStruct((shard, width // nctx), BF16)
-    return pl.pallas_call(
+    scal, *parts = pl.pallas_call(
         pack_kernel,
-        out_shape=(part,) * nctx,
-        in_specs=[SMEM, VMEM],
-        out_specs=(VMEM,) * nctx,
+        out_shape=(jax.ShapeDtypeStruct((4,), jnp.int32),) + (part,) * nctx,
+        in_specs=[VMEM, VMEM],
+        out_specs=(SMEM,) + (VMEM,) * nctx,
         name="pack",
         compiler_params=pltpu.CompilerParams(vmem_limit_bytes=GRANT),
-    )(scal, residual)
+    )(residual, segments)
+    return scal, parts
 
 
 def join_kernel(scal, *refs):
@@ -561,12 +568,11 @@
     shard = keyvals.shape[0]
     tokens = segment_ids.shape[0]
     nctx, nmp = lax.axis_size("ctx"), lax.axis_size("mp")
-    ctx_index, mp_index = lax.axis_index("ctx"), lax.axis_index("mp")
+    ctx_index = lax.axis_index("ctx")
     features = residual.shape[1]
     longest = tokens // 2
     back = -(-(min(WIN, longest) - 1) // rows)
     reach = min(nctx - 1, -(-longest // rows))
-    place = jnp.stack([ctx_index, mp_index]).astype(jnp.int32)
 
     visiting = {0: queries}
     for flip in range(nctx - 1, 0, -2):
@@ -576,7 +582,7 @@
     kv_parts = [keyvals]
     for flip in range(1, nctx):
         kv_parts.append(swapped(keyvals, "ctx", flip))
-    resid_parts = list(pack(place, residual, nctx))
+    scal, resid_parts = pack(residual, segment_ids.reshape(-1, LANES), nctx)
     for flip in range(1, nctx):
         resid_parts[flip] = swapped(resid_parts[flip], "ctx", flip)
     pieces = {0: jnp.concatenate(kv_parts, axis=0)}
@@ -585,12 +591,8 @@
         for done in sorted(pieces):
             pieces[done | flip] = swapped(pieces[done], "mp", flip)
         flip //= 2
-    kv = assemble(place, [pieces[e] for e in range(nmp)], rows, shard, nctx)
-    low = jnp.sum((segment_ids < 1).astype(jnp.int32))
-    high = jnp.sum((segment_ids < 2).astype(jnp.int32))
-    scal = jnp.stack([ctx_index, mp_index, low, high]).astype(jnp.int32)
-
-    chunks = [(0,)] + [(nctx - 1,)] + ([tuple(range(1, nctx - 1))] if nctx > 2 else [])
+    kv = assemble(scal, [pieces[e] for e in range(nmp)], rows, shard, nctx)
+    chunks = [(0,)] + [(flip,) for flip in range(nctx - 1, 0, -1)]
     gain = norm_gain.reshape(1, features)
     halves, places = [], {}
     messages, give = {}, {}
@@ -621,8 +623,14 @@
             messages[e], give[e] = outs[2 * j], outs[2 * j + 1]
     lines = list(tails(scal, halves, [places[e] for e in range(nctx)], gain, lru_weight, rows))
     mains = [messages[0]]
+    for flip in range(nctx - 1, 0, -1):
+        if flip % 2 and flip > 1:
+            passed = swapped(messages[flip], "ctx", 1)
+            both = messages[flip - 1].astype(F32) + passed.astype(F32)
+            messages[flip - 1] = both.astype(BF16)
+        else:
+            mains.append(swapped(messages[flip], "ctx", flip))
     for flip in range(1, nctx):
-        mains.append(swapped(messages[flip], "ctx", flip))
         lines[flip] = swapped(lines[flip], "ctx", flip)
     factor, ahead = stats(lines, rows, features)
     given = [give[0]]
@@ -644,7 +652,7 @@
     before = []
     for step in range(1, reach + 1):
         before.append(rotated(last, "ctx", -step))
-    resid_out = join(place, given)
+    resid_out = join(scal, given)
     incoming = jnp.zeros_like(last[0])
     for step in range(reach, 0, -1):
         piece = before[step - 1]

time: 158 us -> 154 us (0.975)
  starting transfers between devices: 58.7 us -> 44.4 us
  waiting for transfers between devices: 64.5 us -> 76.4 us
  other arithmetic: 4.47 us -> 1.91 us
    ppermute x30 -> x33, starting transfers between devices: 57.7 us -> 42.5 us  [swapped(): return lax.ppermute(value, axis, [(s, s ^ flip) for s in range(count)])]
    ppermute x30 -> x33, waiting for transfers between devices: 61.1 us -> 74 us  [swapped(): return lax.ppermute(value, axis, [(s, s ^ flip) for s in range(count)])]
    pallas_call x3 -> x4, Pallas kernels: 4.52 us -> 5.06 us  [project(): pl.pallas_call(functools.partial(project_kernel, count), out_shape=tuple(...]
    pallas_call x3 -> x4, Pallas kernels: 12.5 us -> 13 us  [attend(): pl.pallas_call(functools.partial(attend_kernel, nctx, back, steps, shard)...]
  transfers between devices with their start and end apart: 32 -> 35, of which waited for: 12 -> 14; matrix products, arithmetic and copies ran while one was open for 3% -> 1% of each run, Pallas kernels for 14% -> 16%
where the time goes in v4:
time: 154 us
  waiting for transfers between devices  76.4 us (50%)
  starting transfers between devices  44.4 us (29%)
  Pallas kernels  27.4 us (18%)
  local copies, waits for them, and re-layouts  2.71 us (2%)
  other arithmetic  1.91 us (1%)
    ppermute x33, waiting for transfers between devices, swapped(): return lax.ppermute(value, axis, [(s, s ^ flip) for s in range(count)])  74 us
    ppermute x33, starting transfers between devices, swapped(): return lax.ppermute(value, axis, [(s, s ^ flip) for s in range(count)])  42.5 us
    pallas_call x4, Pallas kernels, attend(): pl.pallas_call(functools.partial(attend_kernel, nctx, back, steps, shard)...  13 us
    pallas_call x4, Pallas kernels, project(): pl.pallas_call(functools.partial(project_kernel, count), out_shape=tuple(...  5.06 us
    pallas_call x1, Pallas kernels, recur(): pl.pallas_call(functools.partial(recur_kernel, len(mains)), grid=(channel...  4.65 us
  transfers between devices with their start and end apart: 35, of which 14 were waited for; matrix products, arithmetic and copies ran while one was open for 1% of the time, Pallas kernels for 16%

profile of v4, /device:TPU:0, one launch (start us, length us, event | category | flops | bytes accessed | tf_op | source)
XLA Modules:
  0.0 154.0 jit_solution(11696431869072572152)
XLA Ops:
  0.6 3.1 %collective-permute-start = (bf16[64,512]{1,0:T(8,128)(2,1)}, bf16[64,512]{1,0:T(8,128)(2,1)S(1)}, u32[]{:S(2)}, u32[]{:S(2)}) collective-permute-start(bf16[64,512]{1,0:T(8,128)(2,1)} %param.14), channel_id=1, source_target_pairs={{0,4},{4,0},{8,12},{12,8},{1,5},{5,1},{9,13},{13,9},{2,6},{6,2},{1... | collective-permute-start | bytes 196616 | tf_op jit(solution)/shard_map/ppermute | solution.py:175
  3.8 2.6 %collective-permute-start.1 = (bf16[64,512]{1,0:T(8,128)(2,1)}, bf16[64,512]{1,0:T(8,128)(2,1)S(1)}, u32[]{:S(2)}, u32[]{:S(2)}) collective-permute-start(bf16[64,512]{1,0:T(8,128)(2,1)} %param.14), channel_id=1, source_target_pairs={{0,8},{4,12},{8,0},{12,4},{1,9},{5,13},{9,1},{13,5},{2,10},{6,14},... | collective-permute-start | bytes 196616 | tf_op jit(solution)/shard_map/ppermute | solution.py:175
  6.3 0.9 constant_dynamic-update-slice_fusion.3
  7.3 4.0 %collective-permute-done.1 = bf16[64,512]{1,0:T(8,128)(2,1)S(1)} collective-permute-done((bf16[64,512]{1,0:T(8,128)(2,1)}, bf16[64,512]{1,0:T(8,128)(2,1)S(1)}, u32[]{:S(2)}, u32[]{:S(2)}) %collective-permute-start.1) | collective-permute-done | bytes 65568 | tf_op jit(solution)/shard_map/ppermute | solution.py:175
  11.3 1.4 collective-permute-done.2
  12.7 1.5 collective-permute-start.4
  14.1 1.8 %collective-permute-start.15 = (bf16[256,1024]{1,0:T(8,128)(2,1)}, bf16[256,1024]{1,0:T(8,128)(2,1)S(1)}, u32[]{:S(2)}, u32[]{:S(2)}) collective-permute-start(bf16[256,1024]{1,0:T(8,128)(2,1)} %refs_0_.1), channel_id=1, source_target_pairs={{0,12},{4,8},{8,4},{12,0},{1,13},{5,9},{9,5},{13,1},{2,14},{6,10},... | collective-permute-start | bytes 1572872 | tf_op jit(solution)/shard_map/ppermute | solution.py:175
  16.0 3.1 %collective-permute-done.4.refs_2_ = bf16[256,512]{1,0:T(8,128)(2,1)S(1)} collective-permute-done((bf16[256,512]{1,0:T(8,128)(2,1)S(1)}, bf16[256,512]{1,0:T(8,128)(2,1)S(1)}, u32[]{:S(2)}, u32[]{:S(2)}) %collective-permute-start.4) | collective-permute-done | bytes 262176 | tf_op jit(solution)/shard_map/ppermute | solution.py:175
  19.1 1.0 copy-done.2
  20.1 0.7 copy-done.8
  20.8 0.7 pack.1
  21.5 1.9 %collective-permute-start.22 = (bf16[64,1024]{1,0:T(8,128)(2,1)S(1)}, bf16[64,1024]{1,0:T(8,128)(2,1)S(1)}, u32[]{:S(2)}, u32[]{:S(2)}) collective-permute-start(bf16[64,1024]{1,0:T(8,128)(2,1)S(1)} %get-tuple-element.45), channel_id=1, source_target_pairs={{0,12},{4,8},{8,4},{12,0},{1,13},{5,9},{9,5},{13,1},{2,14},{6,10},... | collective-permute-start | bytes 393224 | tf_op jit(solution)/shard_map/ppermute | solution.py:175
  23.4 0.6 assemble.1.refs_2_
  24.0 6.8 %collective-permute-done.22.refs_1_ = bf16[64,1024]{1,0:T(8,128)(2,1)S(1)} collective-permute-done((bf16[64,1024]{1,0:T(8,128)(2,1)S(1)}, bf16[64,1024]{1,0:T(8,128)(2,1)S(1)}, u32[]{:S(2)}, u32[]{:S(2)}) %collective-permute-start.22) | collective-permute-done | bytes 131104 | tf_op jit(solution)/shard_map/ppermute | solution.py:175
  30.8 3.3 %attend.7 = (bf16[256,512]{1,0:T(8,128)(2,1)S(1)}, bf16[256,512]{1,0:T(8,128)(2,1)S(1)}) custom-call(s32[4]{0:T(128)S(1)} %get-tuple-element.32.scal, bf16[256,1024]{1,0:T(8,128)(2,1)S(1)} %collective-permute-done.15.refs_0_, bf16[64,1024]{1,0:T(8,128)(2,1)S(1)} %collective-permute-done.22.refs_1_, bf16[1024,512]{1,0:T(8,128)(2,1)S(1)} %assemble.1.refs_2_, ...), custom_call_target="tpu_custom_call" | custom-call | tf_op jit(solution)/shard_map/attend/pallas_call | solution.py:300
  34.1 0.1 collective-permute-start.23
  34.2 13.1 %collective-permute-start.9 = (bf16[256,1024]{1,0:T(8,128)(2,1)S(1)}, bf16[256,1024]{1,0:T(8,128)(2,1)S(1)}, u32[]{:S(2)}, u32[]{:S(2)}) collective-permute-start(bf16[256,1024]{1,0:T(8,128)(2,1)S(1)} %copy-done.3), channel_id=1, source_target_pairs={{0,4},{4,0},{8,12},{12,8},{1,5},{5,1},{9,13},{13,9},{2,6},{6,2},{1... | collective-permute-start | bytes 1572872 | tf_op jit(solution)/shard_map/ppermute | solution.py:175
  47.3 0.1 collective-permute-start.16
  47.4 0.6 collective-permute-start.24
  48.0 1.9 %collective-permute-start.10 = (bf16[64,1024]{1,0:T(8,128)(2,1)S(1)}, bf16[64,1024]{1,0:T(8,128)(2,1)S(1)}, u32[]{:S(2)}, u32[]{:S(2)}) collective-permute-start(bf16[64,1024]{1,0:T(8,128)(2,1)S(1)} %get-tuple-element.37), channel_id=1, source_target_pairs={{0,4},{4,0},{8,12},{12,8},{1,5},{5,1},{9,13},{13,9},{2,6},{6,2},{1... | collective-permute-start | bytes 393224 | tf_op jit(solution)/shard_map/ppermute | solution.py:175
  50.0 1.1 collective-permute-start.17
  51.1 25.6 %collective-permute-done.10.refs_1_ = bf16[64,1024]{1,0:T(8,128)(2,1)S(1)} collective-permute-done((bf16[64,1024]{1,0:T(8,128)(2,1)S(1)}, bf16[64,1024]{1,0:T(8,128)(2,1)S(1)}, u32[]{:S(2)}, u32[]{:S(2)}) %collective-permute-start.10) | collective-permute-done | bytes 131104 | tf_op jit(solution)/shard_map/ppermute | solution.py:175
  76.6 3.2 %attend.5 = (bf16[256,512]{1,0:T(8,128)(2,1)S(1)}, bf16[256,512]{1,0:T(8,128)(2,1)S(1)}) custom-call(s32[4]{0:T(128)S(1)} %get-tuple-element.32.scal, bf16[256,1024]{1,0:T(8,128)(2,1)S(1)} %collective-permute-done.9.refs_0_, bf16[64,1024]{1,0:T(8,128)(2,1)S(1)} %collective-permute-done.10.refs_1_, bf16[1024,512]{1,0:T(8,128)(2,1)S(1)} %assemble.1.refs_2_, ...), custom_call_target="tpu_custom_call" | custom-call | tf_op jit(solution)/shard_map/attend/pallas_call | solution.py:300
  79.9 0.1 collective-permute-start.11
  80.0 3.2 %attend.6 = (bf16[256,512]{1,0:T(8,128)(2,1)S(1)}, bf16[256,512]{1,0:T(8,128)(2,1)S(1)}) custom-call(s32[4]{0:T(128)S(1)} %get-tuple-element.32.scal, bf16[256,1024]{1,0:T(8,128)(2,1)S(1)} %collective-permute-done.16.refs_0_, bf16[64,1024]{1,0:T(8,128)(2,1)S(1)} %collective-permute-done.17.refs_1_, bf16[1024,512]{1,0:T(8,128)(2,1)S(1)} %assemble.1.refs_2_, ...), custom_call_target="tpu_custom_call" | custom-call | tf_op jit(solution)/shard_map/attend/pallas_call | solution.py:300
  83.2 0.6 collective-permute-start.18
  83.9 0.1 collective-permute-start.25
  84.0 0.6 collective-permute-start.12
  84.6 0.3 collective-permute-done.18
  85.1 1.2 collective-permute-start.19
  86.3 3.2 %attend.4 = (bf16[256,512]{1,0:T(8,128)(2,1)S(1)}, bf16[256,512]{1,0:T(8,128)(2,1)S(1)}) custom-call(s32[4]{0:T(128)S(1)} %get-tuple-element.32.scal, bf16[256,1024]{1,0:T(8,128)(2,1)S(1)} %copy-done.3, bf16[64,1024]{1,0:T(8,128)(2,1)S(1)} %get-tuple-element.33.refs_1_, bf16[1024,512]{1,0:T(8,128)(2,1)S(1)} %assemble.1.refs_2_, bf16[1024,1024]{1,0:T(8,128)(2,1)S(1)} %copy-done.1), custom_call_target="tpu_custom_call" | custom-call | tf_op jit(solution)/shard_map/attend/pallas_call | solution.py:300
  89.5 0.1 collective-permute-start.6
  89.6 1.3 project.7
  90.9 0.1 collective-permute-start.27
  91.0 2.3 %collective-permute-done.12 = bf16[256,512]{1,0:T(8,128)(2,1)S(1)} collective-permute-done((bf16[256,512]{1,0:T(8,128)(2,1)S(1)}, bf16[256,512]{1,0:T(8,128)(2,1)S(1)}, u32[]{:S(2)}, u32[]{:S(2)}) %collective-permute-start.12) | collective-permute-done | bytes 262176 | tf_op jit(solution)/shard_map/ppermute | solution.py:175
  93.3 0.2 add_convert_fusion.6.own.refs_6_
  93.5 0.1 collective-permute-start.13
  93.6 4.8 %collective-permute-done.19 = bf16[256,512]{1,0:T(8,128)(2,1)S(1)} collective-permute-done((bf16[256,512]{1,0:T(8,128)(2,1)S(1)}, bf16[256,512]{1,0:T(8,128)(2,1)S(1)}, u32[]{:S(2)}, u32[]{:S(2)}) %collective-permute-start.19) | collective-permute-done | bytes 262176 | tf_op jit(solution)/shard_map/ppermute | solution.py:175
  98.5 0.1 collective-permute-start.20
  98.6 0.6 collective-permute-start.7
  99.2 1.3 project.5
  100.5 0.1 collective-permute-start.29
  100.6 1.3 project.6
  101.9 3.9 %collective-permute-done.27 = bf16[256,1024]{1,0:T(8,128)(2,1)S(1)} collective-permute-done((bf16[256,1024]{1,0:T(8,128)(2,1)S(1)}, bf16[256,1024]{1,0:T(8,128)(2,1)S(1)}, u32[]{:S(2)}, u32[]{:S(2)}) %collective-permute-start.27) | collective-permute-done | bytes 524320 | tf_op jit(solution)/shard_map/ppermute | solution.py:175
  105.8 0.2 add_convert_fusion.1
  106.0 1.1 collective-permute-start.28
  107.1 0.3 collective-permute-done.7
  107.5 0.1 collective-permute-start.8
  107.6 1.5 collective-permute-done.8.other.refs_1_
  109.1 1.8 %tails.1 = (bf16[16,1024]{1,0:T(8,128)(2,1)S(1)}, bf16[16,1024]{1,0:T(8,128)(2,1)S(1)}, bf16[16,1024]{1,0:T(8,128)(2,1)S(1)}, bf16[16,1024]{1,0:T(8,128)(2,1)S(1)}) custom-call(s32[4]{0:T(128)S(1)} %get-tuple-element.32.scal, bf16[256,512]{1,0:T(8,128)(2,1)S(1)} %add_convert_fusion.8.own.refs_0_, bf16[256,512]{1,0:T(8,128)(2,1)S(1)} %collective-permute-done.8.other.refs_1_, ...), custom_call_target="tpu_custom_call" | custom-call | tf_op jit(solution)/shard_map/tails/pallas_call | solution.py:412
  111.0 1.8 %collective-permute-start.30 = (bf16[16,1024]{1,0:T(8,128)(2,1)S(1)}, bf16[16,1024]{1,0:T(8,128)(2,1)S(1)}, u32[]{:S(2)}, u32[]{:S(2)}) collective-permute-start(bf16[16,1024]{1,0:T(8,128)(2,1)S(1)} %get-tuple-element.54), channel_id=1, source_target_pairs={{0,4},{4,0},{8,12},{12,8},{1,5},{5,1},{9,13},{13,9},{2,6},{6,2},{1... | collective-permute-start | bytes 98312 | tf_op jit(solution)/shard_map/ppermute | solution.py:175
  112.8 1.4 collective-permute-start.31
  114.1 1.3 collective-permute-start.32
  115.5 11.1 %collective-permute-done.30.refs_1_ = bf16[16,1024]{1,0:T(8,128)(2,1)S(1)} collective-permute-done((bf16[16,1024]{1,0:T(8,128)(2,1)S(1)}, bf16[16,1024]{1,0:T(8,128)(2,1)S(1)}, u32[]{:S(2)}, u32[]{:S(2)}) %collective-permute-start.30) | collective-permute-done | bytes 32800 | tf_op jit(solution)/shard_map/ppermute | solution.py:175
  126.5 2.5 %collective-permute-start.26 = (bf16[64,1024]{1,0:T(8,128)(2,1)S(1)}, bf16[64,1024]{1,0:T(8,128)(2,1)S(1)}, u32[]{:S(2)}, u32[]{:S(2)}) collective-permute-start(bf16[64,1024]{1,0:T(8,128)(2,1)S(1)} %get-tuple-element.48), channel_id=1, source_target_pairs={{0,12},{4,8},{8,4},{12,0},{1,13},{5,9},{9,5},{13,1},{2,14},{6,10},... | collective-permute-start | bytes 393224 | tf_op jit(solution)/shard_map/ppermute | solution.py:175
  129.0 8.9 %collective-permute-done.31.refs_2_ = bf16[16,1024]{1,0:T(8,128)(2,1)S(1)} collective-permute-done((bf16[16,1024]{1,0:T(8,128)(2,1)S(1)}, bf16[16,1024]{1,0:T(8,128)(2,1)S(1)}, u32[]{:S(2)}, u32[]{:S(2)}) %collective-permute-start.31) | collective-permute-done | bytes 32800 | tf_op jit(solution)/shard_map/ppermute | solution.py:175
  138.0 3.1 %collective-permute-start.21 = (bf16[64,1024]{1,0:T(8,128)(2,1)S(1)}, bf16[64,1024]{1,0:T(8,128)(2,1)S(1)}, u32[]{:S(2)}, u32[]{:S(2)}) collective-permute-start(bf16[64,1024]{1,0:T(8,128)(2,1)S(1)} %get-tuple-element.44), channel_id=1, source_target_pairs={{0,8},{4,12},{8,0},{12,4},{1,9},{5,13},{9,1},{13,5},{2,10},{6,14},... | collective-permute-start | bytes 393224 | tf_op jit(solution)/shard_map/ppermute | solution.py:175
  141.0 1.3 project.4
  142.3 0.2 stats.1
  142.6 4.6 %recur.1 = (f32[256,1024]{1,0:T(8,128)S(1)}, f32[256,1024]{1,0:T(8,128)S(1)}, f32[8,1024]{1,0:T(8,128)S(1)}) custom-call(s32[4]{0:T(128)S(1)} %get-tuple-element.32.scal, bf16[256,1024]{1,0:T(8,128)(2,1)S(1)} %get-tuple-element.49.refs_0_, bf16[256,1024]{1,0:T(8,128)(2,1)S(1)} %collective-permute-done.28.refs_1_, ...), custom_call_target="tpu_custom_call" | custom-call | tf_op jit(solution)/shard_map/recur/pallas_call | solution.py:532
  147.3 1.9 %collective-permute-start.34 = (f32[8,1024]{1,0:T(8,128)S(1)}, f32[8,1024]{1,0:T(8,128)S(1)}, u32[]{:S(2)}, u32[]{:S(2)}) collective-permute-start(f32[8,1024]{1,0:T(8,128)S(1)} %get-tuple-element.61), channel_id=1, source_target_pairs={{0,8},{4,12},{8,0},{12,4},{1,9},{5,13},{9,1},{13,5},{2,10},{6,14},... | collective-permute-start | bytes 98312 | tf_op jit(solution)/shard_map/ppermute | solution.py:170
  149.2 1.4 join.1
  150.5 2.4 %collective-permute-done.33 = f32[8,1024]{1,0:T(8,128)S(1)} collective-permute-done((f32[8,1024]{1,0:T(8,128)S(1)}, f32[8,1024]{1,0:T(8,128)S(1)}, u32[]{:S(2)}, u32[]{:S(2)}) %collective-permute-start.33) | collective-permute-done | bytes 32800 | tf_op jit(solution)/shard_map/ppermute | solution.py:170
  153.0 1.0 add_convert_fusion
  (59 shorter events, 0.7 us)
Async XLA Ops:
  0.6 30.2 %copy-start.1 = (bf16[1024,1024]{1,0:T(8,128)(2,1)S(1)}, bf16[1024,1024]{1,0:T(8,128)(2,1)}, u32[]{:S(2)}) copy-start(bf16[1024,1024]{1,0:T(8,128)(2,1)} %refs_3_.7) | copy-start | bytes 6291460
  0.6 6.6 %collective-permute-start = (bf16[64,512]{1,0:T(8,128)(2,1)}, bf16[64,512]{1,0:T(8,128)(2,1)S(1)}, u32[]{:S(2)}, u32[]{:S(2)}) collective-permute-start(bf16[64,512]{1,0:T(8,128)(2,1)} %param.14), channel_id=1, source_target_pairs={{0,4},{4,0},{8,12},{12,8},{1,5},{5,1},{9,13},{13,9},{2,6},{6,2},{1... | collective-permute-start | bytes 196616 | tf_op jit(solution)/shard_map/ppermute | solution.py:175
  3.8 7.5 %collective-permute-start.1 = (bf16[64,512]{1,0:T(8,128)(2,1)}, bf16[64,512]{1,0:T(8,128)(2,1)S(1)}, u32[]{:S(2)}, u32[]{:S(2)}) collective-permute-start(bf16[64,512]{1,0:T(8,128)(2,1)} %param.14), channel_id=1, source_target_pairs={{0,8},{4,12},{8,0},{12,4},{1,9},{5,13},{9,1},{13,5},{2,10},{6,14},... | collective-permute-start | bytes 196616 | tf_op jit(solution)/shard_map/ppermute | solution.py:175
  6.3 6.3 %collective-permute-start.2 = (bf16[64,512]{1,0:T(8,128)(2,1)}, bf16[64,512]{1,0:T(8,128)(2,1)S(1)}, u32[]{:S(2)}, u32[]{:S(2)}) collective-permute-start(bf16[64,512]{1,0:T(8,128)(2,1)} %param.14), channel_id=1, source_target_pairs={{0,12},{4,8},{8,4},{12,0},{1,13},{5,9},{9,5},{13,1},{2,14},{6,10},... | collective-permute-start | bytes 196616 | tf_op jit(solution)/shard_map/ppermute | solution.py:175
  12.7 6.4 %collective-permute-start.4 = (bf16[256,512]{1,0:T(8,128)(2,1)S(1)}, bf16[256,512]{1,0:T(8,128)(2,1)S(1)}, u32[]{:S(2)}, u32[]{:S(2)}) collective-permute-start(bf16[256,512]{1,0:T(8,128)(2,1)S(1)} %constant_dynamic-update-slice_fusion.refs_0_), channel_id=1, source_target_pairs={{0,2},{1,3},{2,0},{3,1},{4,6},{5,7},{6,4},{7,5},{8,10},{9,11},{10,... | collective-permute-start | bytes 786440 | tf_op jit(solution)/shard_map/ppermute | solution.py:175
  14.1 16.7 %collective-permute-start.15 = (bf16[256,1024]{1,0:T(8,128)(2,1)}, bf16[256,1024]{1,0:T(8,128)(2,1)S(1)}, u32[]{:S(2)}, u32[]{:S(2)}) collective-permute-start(bf16[256,1024]{1,0:T(8,128)(2,1)} %refs_0_.1), channel_id=1, source_target_pairs={{0,12},{4,8},{8,4},{12,0},{1,13},{5,9},{9,5},{13,1},{2,14},{6,10},... | collective-permute-start | bytes 1572872 | tf_op jit(solution)/shard_map/ppermute | solution.py:175
  16.0 7.4 %collective-permute-start.3 = (bf16[256,512]{1,0:T(8,128)(2,1)S(1)}, bf16[256,512]{1,0:T(8,128)(2,1)S(1)}, u32[]{:S(2)}, u32[]{:S(2)}) collective-permute-start(bf16[256,512]{1,0:T(8,128)(2,1)S(1)} %constant_dynamic-update-slice_fusion.refs_0_), channel_id=1, source_target_pairs={{0,1},{1,0},{2,3},{3,2},{4,5},{5,4},{6,7},{7,6},{8,9},{9,8},{10,11... | collective-permute-start | bytes 786440 | tf_op jit(solution)/shard_map/ppermute | solution.py:175
  19.1 4.3 %collective-permute-start.5 = (bf16[256,512]{1,0:T(8,128)(2,1)S(1)}, bf16[256,512]{1,0:T(8,128)(2,1)S(1)}, u32[]{:S(2)}, u32[]{:S(2)}) collective-permute-start(bf16[256,512]{1,0:T(8,128)(2,1)S(1)} %collective-permute-done.4.refs_2_), channel_id=1, source_target_pairs={{0,1},{1,0},{2,3},{3,2},{4,5},{5,4},{6,7},{7,6},{8,9},{9,8},{10,11... | collective-permute-start | bytes 786440 | tf_op jit(solution)/shard_map/ppermute | solution.py:175
  19.1 1.0 copy-start.2
  20.1 0.7 copy-start.8
  21.5 9.3 %collective-permute-start.22 = (bf16[64,1024]{1,0:T(8,128)(2,1)S(1)}, bf16[64,1024]{1,0:T(8,128)(2,1)S(1)}, u32[]{:S(2)}, u32[]{:S(2)}) collective-permute-start(bf16[64,1024]{1,0:T(8,128)(2,1)S(1)} %get-tuple-element.45), channel_id=1, source_target_pairs={{0,12},{4,8},{8,4},{12,0},{1,13},{5,9},{9,5},{13,1},{2,14},{6,10},... | collective-permute-start | bytes 393224 | tf_op jit(solution)/shard_map/ppermute | solution.py:175
  24.0 10.1 %copy-start.3 = (bf16[256,1024]{1,0:T(8,128)(2,1)S(1)}, bf16[256,1024]{1,0:T(8,128)(2,1)}, u32[]{:S(2)}) copy-start(bf16[256,1024]{1,0:T(8,128)(2,1)} %refs_0_.1) | copy-start | bytes 1572868
  34.1 13.3 %collective-permute-start.23 = (bf16[256,512]{1,0:T(8,128)(2,1)S(1)}, bf16[256,512]{1,0:T(8,128)(2,1)S(1)}, u32[]{:S(2)}, u32[]{:S(2)}) collective-permute-start(bf16[256,512]{1,0:T(8,128)(2,1)S(1)} %get-tuple-element.47), channel_id=1, source_target_pairs={{0,1},{1,0},{2,3},{3,2},{4,5},{5,4},{6,7},{7,6},{8,9},{9,8},{10,11... | collective-permute-start | bytes 786440 | tf_op jit(solution)/shard_map/ppermute | solution.py:175
  34.2 42.5 %collective-permute-start.9 = (bf16[256,1024]{1,0:T(8,128)(2,1)S(1)}, bf16[256,1024]{1,0:T(8,128)(2,1)S(1)}, u32[]{:S(2)}, u32[]{:S(2)}) collective-permute-start(bf16[256,1024]{1,0:T(8,128)(2,1)S(1)} %copy-done.3), channel_id=1, source_target_pairs={{0,4},{4,0},{8,12},{12,8},{1,5},{5,1},{9,13},{13,9},{2,6},{6,2},{1... | collective-permute-start | bytes 1572872 | tf_op jit(solution)/shard_map/ppermute | solution.py:175
  47.3 32.7 %collective-permute-start.16 = (bf16[256,1024]{1,0:T(8,128)(2,1)S(1)}, bf16[256,1024]{1,0:T(8,128)(2,1)S(1)}, u32[]{:S(2)}, u32[]{:S(2)}) collective-permute-start(bf16[256,1024]{1,0:T(8,128)(2,1)S(1)} %collective-permute-done.15.refs_0_), channel_id=1, source_target_pairs={{0,4},{4,0},{8,12},{12,8},{1,5},{5,1},{9,13},{13,9},{2,6},{6,2},{1... | collective-permute-start | bytes 1572872 | tf_op jit(solution)/shard_map/ppermute | solution.py:175
  47.4 36.4 %collective-permute-start.24 = (bf16[256,512]{1,0:T(8,128)(2,1)S(1)}, bf16[256,512]{1,0:T(8,128)(2,1)S(1)}, u32[]{:S(2)}, u32[]{:S(2)}) collective-permute-start(bf16[256,512]{1,0:T(8,128)(2,1)S(1)} %add_convert_fusion.3), channel_id=1, source_target_pairs={{0,2},{1,3},{2,0},{3,1},{4,6},{5,7},{6,4},{7,5},{8,10},{9,11},{10,... | collective-permute-start | bytes 786440 | tf_op jit(solution)/shard_map/ppermute | solution.py:175
  48.0 28.6 %collective-permute-start.10 = (bf16[64,1024]{1,0:T(8,128)(2,1)S(1)}, bf16[64,1024]{1,0:T(8,128)(2,1)S(1)}, u32[]{:S(2)}, u32[]{:S(2)}) collective-permute-start(bf16[64,1024]{1,0:T(8,128)(2,1)S(1)} %get-tuple-element.37), channel_id=1, source_target_pairs={{0,4},{4,0},{8,12},{12,8},{1,5},{5,1},{9,13},{13,9},{2,6},{6,2},{1... | collective-permute-start | bytes 393224 | tf_op jit(solution)/shard_map/ppermute | solution.py:175
  50.0 30.0 %collective-permute-start.17 = (bf16[64,1024]{1,0:T(8,128)(2,1)S(1)}, bf16[64,1024]{1,0:T(8,128)(2,1)S(1)}, u32[]{:S(2)}, u32[]{:S(2)}) collective-permute-start(bf16[64,1024]{1,0:T(8,128)(2,1)S(1)} %get-tuple-element.41), channel_id=1, source_target_pairs={{0,8},{4,12},{8,0},{12,4},{1,9},{5,13},{9,1},{13,5},{2,10},{6,14},... | collective-permute-start | bytes 393224 | tf_op jit(solution)/shard_map/ppermute | solution.py:175
  79.9 4.1 %collective-permute-start.11 = (bf16[256,512]{1,0:T(8,128)(2,1)S(1)}, bf16[256,512]{1,0:T(8,128)(2,1)S(1)}, u32[]{:S(2)}, u32[]{:S(2)}) collective-permute-start(bf16[256,512]{1,0:T(8,128)(2,1)S(1)} %get-tuple-element.39), channel_id=1, source_target_pairs={{0,1},{1,0},{2,3},{3,2},{4,5},{5,4},{6,7},{7,6},{8,9},{9,8},{10,11... | collective-permute-start | bytes 786440 | tf_op jit(solution)/shard_map/ppermute | solution.py:175
  83.2 1.7 %collective-permute-start.18 = (bf16[256,512]{1,0:T(8,128)(2,1)S(1)}, bf16[256,512]{1,0:T(8,128)(2,1)S(1)}, u32[]{:S(2)}, u32[]{:S(2)}) collective-permute-start(bf16[256,512]{1,0:T(8,128)(2,1)S(1)} %get-tuple-element.43), channel_id=1, source_target_pairs={{0,1},{1,0},{2,3},{3,2},{4,5},{5,4},{6,7},{7,6},{8,9},{9,8},{10,11... | collective-permute-start | bytes 786440 | tf_op jit(solution)/shard_map/ppermute | solution.py:175
  83.9 5.7 %collective-permute-start.25 = (bf16[256,512]{1,0:T(8,128)(2,1)S(1)}, bf16[256,512]{1,0:T(8,128)(2,1)S(1)}, u32[]{:S(2)}, u32[]{:S(2)}) collective-permute-start(bf16[256,512]{1,0:T(8,128)(2,1)S(1)} %add_convert_fusion.2.own.refs_2_), channel_id=1, source_target_pairs={{0,1},{1,0},{2,3},{3,2},{4,5},{5,4},{6,7},{7,6},{8,9},{9,8},{10,11... | collective-permute-start | bytes 786440 | tf_op jit(solution)/shard_map/ppermute | solution.py:175
  84.0 9.2 %collective-permute-start.12 = (bf16[256,512]{1,0:T(8,128)(2,1)S(1)}, bf16[256,512]{1,0:T(8,128)(2,1)S(1)}, u32[]{:S(2)}, u32[]{:S(2)}) collective-permute-start(bf16[256,512]{1,0:T(8,128)(2,1)S(1)} %add_convert_fusion.7), channel_id=1, source_target_pairs={{0,2},{1,3},{2,0},{3,1},{4,6},{5,7},{6,4},{7,5},{8,10},{9,11},{10,... | collective-permute-start | bytes 786440 | tf_op jit(solution)/shard_map/ppermute | solution.py:175
  85.0 4.6 %copy-start = (bf16[1024,1024]{1,0:T(8,128)(2,1)S(1)}, bf16[1024,1024]{1,0:T(8,128)(2,1)}, u32[]{:S(2)}) copy-start(bf16[1024,1024]{1,0:T(8,128)(2,1)} %refs_9_.1) | copy-start | bytes 6291460
  85.0 4.6 %copy-start.6 = (f32[4096]{0:T(1024)S(1)}, f32[4096]{0:T(1024)}, u32[]{:S(2)}) copy-start(f32[4096]{0:T(1024)} %param.25) | copy-start | bytes 49156
  85.1 13.4 %collective-permute-start.19 = (bf16[256,512]{1,0:T(8,128)(2,1)S(1)}, bf16[256,512]{1,0:T(8,128)(2,1)S(1)}, u32[]{:S(2)}, u32[]{:S(2)}) collective-permute-start(bf16[256,512]{1,0:T(8,128)(2,1)S(1)} %add_convert_fusion.5), channel_id=1, source_target_pairs={{0,2},{1,3},{2,0},{3,1},{4,6},{5,7},{6,4},{7,5},{8,10},{9,11},{10,... | collective-permute-start | bytes 786440 | tf_op jit(solution)/shard_map/ppermute | solution.py:175
  89.5 9.0 %collective-permute-start.6 = (bf16[256,512]{1,0:T(8,128)(2,1)S(1)}, bf16[256,512]{1,0:T(8,128)(2,1)S(1)}, u32[]{:S(2)}, u32[]{:S(2)}) collective-permute-start(bf16[256,512]{1,0:T(8,128)(2,1)S(1)} %get-tuple-element.35), channel_id=1, source_target_pairs={{0,1},{1,0},{2,3},{3,2},{4,5},{5,4},{6,7},{7,6},{8,9},{9,8},{10,11... | collective-permute-start | bytes 786440 | tf_op jit(solution)/shard_map/ppermute | solution.py:175
  90.9 14.9 %collective-permute-start.27 = (bf16[256,1024]{1,0:T(8,128)(2,1)S(1)}, bf16[256,1024]{1,0:T(8,128)(2,1)S(1)}, u32[]{:S(2)}, u32[]{:S(2)}) collective-permute-start(bf16[256,1024]{1,0:T(8,128)(2,1)S(1)} %get-tuple-element.51), channel_id=1, source_target_pairs={{0,4},{4,0},{8,12},{12,8},{1,5},{5,1},{9,13},{13,9},{2,6},{6,2},{1... | collective-permute-start | bytes 1572872 | tf_op jit(solution)/shard_map/ppermute | solution.py:175
  93.5 5.7 %collective-permute-start.13 = (bf16[256,512]{1,0:T(8,128)(2,1)S(1)}, bf16[256,512]{1,0:T(8,128)(2,1)S(1)}, u32[]{:S(2)}, u32[]{:S(2)}) collective-permute-start(bf16[256,512]{1,0:T(8,128)(2,1)S(1)} %add_convert_fusion.6.own.refs_6_), channel_id=1, source_target_pairs={{0,1},{1,0},{2,3},{3,2},{4,5},{5,4},{6,7},{7,6},{8,9},{9,8},{10,11... | collective-permute-start | bytes 786440 | tf_op jit(solution)/shard_map/ppermute | solution.py:175
  98.5 2.1 %collective-permute-start.20 = (bf16[256,512]{1,0:T(8,128)(2,1)S(1)}, bf16[256,512]{1,0:T(8,128)(2,1)S(1)}, u32[]{:S(2)}, u32[]{:S(2)}) collective-permute-start(bf16[256,512]{1,0:T(8,128)(2,1)S(1)} %add_convert_fusion.4.own.refs_4_), channel_id=1, source_target_pairs={{0,1},{1,0},{2,3},{3,2},{4,5},{5,4},{6,7},{7,6},{8,9},{9,8},{10,11... | collective-permute-start | bytes 786440 | tf_op jit(solution)/shard_map/ppermute | solution.py:175
  98.6 8.8 %collective-permute-start.7 = (bf16[256,512]{1,0:T(8,128)(2,1)S(1)}, bf16[256,512]{1,0:T(8,128)(2,1)S(1)}, u32[]{:S(2)}, u32[]{:S(2)}) collective-permute-start(bf16[256,512]{1,0:T(8,128)(2,1)S(1)} %add_convert_fusion.9), channel_id=1, source_target_pairs={{0,2},{1,3},{2,0},{3,1},{4,6},{5,7},{6,4},{7,5},{8,10},{9,11},{10,... | collective-permute-start | bytes 786440 | tf_op jit(solution)/shard_map/ppermute | solution.py:175
  100.5 42.0 %collective-permute-start.29 = (bf16[256,1024]{1,0:T(8,128)(2,1)S(1)}, bf16[256,1024]{1,0:T(8,128)(2,1)S(1)}, u32[]{:S(2)}, u32[]{:S(2)}) collective-permute-start(bf16[256,1024]{1,0:T(8,128)(2,1)S(1)} %get-tuple-element.52), channel_id=1, source_target_pairs={{0,4},{4,0},{8,12},{12,8},{1,5},{5,1},{9,13},{13,9},{2,6},{6,2},{1... | collective-permute-start | bytes 1572872 | tf_op jit(solution)/shard_map/ppermute | solution.py:175
  106.0 36.5 %collective-permute-start.28 = (bf16[256,1024]{1,0:T(8,128)(2,1)S(1)}, bf16[256,1024]{1,0:T(8,128)(2,1)S(1)}, u32[]{:S(2)}, u32[]{:S(2)}) collective-permute-start(bf16[256,1024]{1,0:T(8,128)(2,1)S(1)} %add_convert_fusion.1), channel_id=1, source_target_pairs={{0,8},{4,12},{8,0},{12,4},{1,9},{5,13},{9,1},{13,5},{2,10},{6,14},... | collective-permute-start | bytes 1572872 | tf_op jit(solution)/shard_map/ppermute | solution.py:175
  107.5 1.6 %collective-permute-start.8 = (bf16[256,512]{1,0:T(8,128)(2,1)S(1)}, bf16[256,512]{1,0:T(8,128)(2,1)S(1)}, u32[]{:S(2)}, u32[]{:S(2)}) collective-permute-start(bf16[256,512]{1,0:T(8,128)(2,1)S(1)} %add_convert_fusion.8.own.refs_0_), channel_id=1, source_target_pairs={{0,1},{1,0},{2,3},{3,2},{4,5},{5,4},{6,7},{7,6},{8,9},{9,8},{10,11... | collective-permute-start | bytes 786440 | tf_op jit(solution)/shard_map/ppermute | solution.py:175
  110.9 31.6 %copy-start.4 = (bf16[4,256,256]{2,1,0:T(8,128)(2,1)S(1)}, bf16[4,256,256]{2,1,0:T(8,128)(2,1)}, u32[]{:S(2)}) copy-start(bf16[4,256,256]{2,1,0:T(8,128)(2,1)} %refs_6_.1) | copy-start | bytes 1572868
  110.9 31.6 %copy-start.5 = (bf16[4,256,256]{2,1,0:T(8,128)(2,1)S(1)}, bf16[4,256,256]{2,1,0:T(8,128)(2,1)}, u32[]{:S(2)}) copy-start(bf16[4,256,256]{2,1,0:T(8,128)(2,1)} %refs_7_.1) | copy-start | bytes 1572868
  111.0 31.6 %copy-start.7 = (f32[4,1024]{1,0:T(4,128)S(1)}, f32[4,1024]{1,0:T(4,128)}, u32[]{:S(2)}) copy-start(f32[4,1024]{1,0:T(4,128)} %refs_5_.1) | copy-start | bytes 49156
  111.0 31.6 %copy-start.9 = (f32[1024]{0:T(1024)S(1)}, f32[1024]{0:T(1024)}, u32[]{:S(2)}) copy-start(f32[1024]{0:T(1024)} %param.22) | copy-start | bytes 12292
  111.0 31.6 %copy-start.10 = (f32[1024]{0:T(1024)S(1)}, f32[1024]{0:T(1024)}, u32[]{:S(2)}) copy-start(f32[1024]{0:T(1024)} %param.23) | copy-start | bytes 12292
  111.0 31.6 %copy-start.11 = (s32[1024]{0:T(1024)S(1)}, s32[1024]{0:T(1024)}, u32[]{:S(2)}) copy-start(s32[1024]{0:T(1024)} %param.24) | copy-start | bytes 12292
  111.0 15.5 %collective-permute-start.30 = (bf16[16,1024]{1,0:T(8,128)(2,1)S(1)}, bf16[16,1024]{1,0:T(8,128)(2,1)S(1)}, u32[]{:S(2)}, u32[]{:S(2)}) collective-permute-start(bf16[16,1024]{1,0:T(8,128)(2,1)S(1)} %get-tuple-element.54), channel_id=1, source_target_pairs={{0,4},{4,0},{8,12},{12,8},{1,5},{5,1},{9,13},{13,9},{2,6},{6,2},{1... | collective-permute-start | bytes 98312 | tf_op jit(solution)/shard_map/ppermute | solution.py:175
  112.8 25.2 %collective-permute-start.31 = (bf16[16,1024]{1,0:T(8,128)(2,1)S(1)}, bf16[16,1024]{1,0:T(8,128)(2,1)S(1)}, u32[]{:S(2)}, u32[]{:S(2)}) collective-permute-start(bf16[16,1024]{1,0:T(8,128)(2,1)S(1)} %get-tuple-element.55), channel_id=1, source_target_pairs={{0,8},{4,12},{8,0},{12,4},{1,9},{5,13},{9,1},{13,5},{2,10},{6,14},... | collective-permute-start | bytes 98312 | tf_op jit(solution)/shard_map/ppermute | solution.py:175
  114.1 23.8 %collective-permute-start.32 = (bf16[16,1024]{1,0:T(8,128)(2,1)S(1)}, bf16[16,1024]{1,0:T(8,128)(2,1)S(1)}, u32[]{:S(2)}, u32[]{:S(2)}) collective-permute-start(bf16[16,1024]{1,0:T(8,128)(2,1)S(1)} %get-tuple-element.56), channel_id=1, source_target_pairs={{0,12},{4,8},{8,4},{12,0},{1,13},{5,9},{9,5},{13,1},{2,14},{6,10},... | collective-permute-start | bytes 98312 | tf_op jit(solution)/shard_map/ppermute | solution.py:175
  126.5 22.6 %collective-permute-start.26 = (bf16[64,1024]{1,0:T(8,128)(2,1)S(1)}, bf16[64,1024]{1,0:T(8,128)(2,1)S(1)}, u32[]{:S(2)}, u32[]{:S(2)}) collective-permute-start(bf16[64,1024]{1,0:T(8,128)(2,1)S(1)} %get-tuple-element.48), channel_id=1, source_target_pairs={{0,12},{4,8},{8,4},{12,0},{1,13},{5,9},{9,5},{13,1},{2,14},{6,10},... | collective-permute-start | bytes 393224 | tf_op jit(solution)/shard_map/ppermute | solution.py:175
  138.0 11.2 %collective-permute-start.14 = (bf16[64,1024]{1,0:T(8,128)(2,1)S(1)}, bf16[64,1024]{1,0:T(8,128)(2,1)S(1)}, u32[]{:S(2)}, u32[]{:S(2)}) collective-permute-start(bf16[64,1024]{1,0:T(8,128)(2,1)S(1)} %get-tuple-element.40), channel_id=1, source_target_pairs={{0,4},{4,0},{8,12},{12,8},{1,5},{5,1},{9,13},{13,9},{2,6},{6,2},{1... | collective-permute-start | bytes 393224 | tf_op jit(solution)/shard_map/ppermute | solution.py:175
  138.0 11.2 %collective-permute-start.21 = (bf16[64,1024]{1,0:T(8,128)(2,1)S(1)}, bf16[64,1024]{1,0:T(8,128)(2,1)S(1)}, u32[]{:S(2)}, u32[]{:S(2)}) collective-permute-start(bf16[64,1024]{1,0:T(8,128)(2,1)S(1)} %get-tuple-element.44), channel_id=1, source_target_pairs={{0,8},{4,12},{8,0},{12,4},{1,9},{5,13},{9,1},{13,5},{2,10},{6,14},... | collective-permute-start | bytes 393224 | tf_op jit(solution)/shard_map/ppermute | solution.py:175
  147.2 5.8 %collective-permute-start.33 = (f32[8,1024]{1,0:T(8,128)S(1)}, f32[8,1024]{1,0:T(8,128)S(1)}, u32[]{:S(2)}, u32[]{:S(2)}) collective-permute-start(f32[8,1024]{1,0:T(8,128)S(1)} %get-tuple-element.61), channel_id=1, source_target_pairs={{0,4},{4,8},{8,12},{12,0},{1,5},{5,9},{9,13},{13,1},{2,6},{6,10},{... | collective-permute-start | bytes 98312 | tf_op jit(solution)/shard_map/ppermute | solution.py:170
  147.3 5.7 %collective-permute-start.34 = (f32[8,1024]{1,0:T(8,128)S(1)}, f32[8,1024]{1,0:T(8,128)S(1)}, u32[]{:S(2)}, u32[]{:S(2)}) collective-permute-start(f32[8,1024]{1,0:T(8,128)S(1)} %get-tuple-element.61), channel_id=1, source_target_pairs={{0,8},{4,12},{8,0},{12,4},{1,9},{5,13},{9,1},{13,5},{2,10},{6,14},... | collective-permute-start | bytes 98312 | tf_op jit(solution)/shard_map/ppermute | solution.py:170

commit v5 on v4

--- a/solution.py
+++ b/solution.py
@@ -355,11 +355,12 @@
     )(scal, own, other, gain, weight)
 
 
-def tails_kernel(places, nhalves, rows, scal, *refs):
+def tails_kernel(places, nhalves, rows, near, scal, *refs):
     nctx = len(places)
-    halves, (gain, weight) = refs[:nhalves], refs[nhalves : nhalves + 2]
-    outs = refs[nhalves + 2 : nhalves + 2 + nctx]
-    edges, ends = refs[nhalves + 2 + nctx :]
+    halves, (gain, weight, message) = refs[:nhalves], refs[nhalves : nhalves + 3]
+    outs = refs[nhalves + 3 : nhalves + 3 + nctx]
+    edges, ends = refs[nhalves + 3 + nctx :]
+    outs[near][0:rows, :] = message[...]
     ctx_index = scal[0]
     side = jnp.bitwise_and(scal[1], 1)
     channels = weight.shape[1]
@@ -403,16 +404,21 @@
         index = lax.broadcasted_iota(jnp.int32, line.shape, 0)
         line = jnp.where(index == 0, coarse, line - coarse)
         tail = tails[(flip + 1) * TILE - SUB : (flip + 1) * TILE, :]
-        outs[flip][...] = jnp.concatenate([line, tail], axis=0).astype(BF16)
-
-
-def tails(scal, halves, places, gain, weight, rows):
+        base = rows if flip == near else 0
+        outs[flip][base : base + TILE, :] = jnp.concatenate([line, tail], axis=0).astype(BF16)
+
+
+def tails(scal, halves, places, gain, weight, message, near):
     nctx = len(places)
     half, channels = weight.shape[0] // 2, weight.shape[1]
+    rows = message.shape[0]
     return pl.pallas_call(
-        functools.partial(tails_kernel, places, len(halves), rows),
-        out_shape=(jax.ShapeDtypeStruct((TILE, channels), BF16),) * nctx,
-        in_specs=[SMEM] + [VMEM] * (len(halves) + 2),
+        functools.partial(tails_kernel, places, len(halves), rows, near),
+        out_shape=tuple(
+            jax.ShapeDtypeStruct((TILE + (rows if flip == near else 0), channels), BF16)
+            for flip in range(nctx)
+        ),
+        in_specs=[SMEM] + [VMEM] * (len(halves) + 3),
         out_specs=(VMEM,) * nctx,
         scratch_shapes=[
             pltpu.VMEM((2, nctx * LANES, half), BF16),
@@ -420,7 +426,25 @@
         ],
         name="tails",
         compiler_params=pltpu.CompilerParams(vmem_limit_bytes=GRANT),
-    )(scal, *halves, gain, weight)
+    )(scal, *halves, gain, weight, message)
+
+
+def merge_kernel(message, passed, line, out):
+    rows = message.shape[0]
+    out[0:rows, :] = (message[...].astype(F32) + passed[...].astype(F32)).astype(BF16)
+    out[rows:, :] = line[...]
+
+
+def merge(message, passed, line):
+    rows, channels = message.shape
+    return pl.pallas_call(
+        merge_kernel,
+        out_shape=jax.ShapeDtypeStruct((rows + TILE, channels), BF16),
+        in_specs=[VMEM] * 3,
+        out_specs=VMEM,
+        name="merge",
+        compiler_params=pltpu.CompilerParams(vmem_limit_bytes=GRANT),
+    )(message, passed, line)
 
 
 def minus_expm1(x):
@@ -430,55 +454,41 @@
     return jnp.where(x > -0.3, -x * series, 1.0 - jnp.exp(x))
 
 
-def stats_kernel(features, *refs):
-    lines, (factor_ref, ahead_ref) = refs[:-2], refs[-2:]
-    length = factor_ref.shape[0]
-    sums = tail = None
-    for line in lines:
-        term = line[0:1, :length].astype(F32) + line[1:2, :length].astype(F32)
-        tail_term = line[...].astype(F32)[SUB:, :]
-        sums = term if sums is None else sums + term
-        tail = tail_term if tail is None else tail + tail_term
-    factor = lax.rsqrt(sums * (1.0 / features) + 1e-06)
-    factor = jnp.transpose(jnp.broadcast_to(factor, (LANES, length)))
-    factor_ref[...] = factor
-    ahead_ref[...] = (tail * factor[length - SUB :, 0:1]).astype(BF16).astype(F32)
-
-
-def stats(lines, rows, features):
-    channels = lines[0].shape[1]
-    return pl.pallas_call(
-        functools.partial(stats_kernel, features),
-        out_shape=(
-            jax.ShapeDtypeStruct((rows + LANES, LANES), F32),
-            jax.ShapeDtypeStruct((SUB, channels), F32),
-        ),
-        in_specs=[VMEM] * len(lines),
-        out_specs=(VMEM, VMEM),
-        name="stats",
-        compiler_params=pltpu.CompilerParams(vmem_limit_bytes=GRANT),
-    )(*lines)
-
-
-def recur_kernel(count, scal, *refs):
-    mains, (factor, ahead) = refs[:count], refs[count : count + 2]
-    conv_w, decay_w, input_w, decay_b, input_b, codes = refs[count + 2 : count + 8]
-    local_ref, cum_ref, last_ref, ext, keep_s, state_s = refs[count + 8 :]
-    rows = mains[0].shape[0]
-    width = mains[0].shape[1]
+def recur_kernel(count, nlines, features, scal, *refs):
+    mains, lines = refs[:count], refs[count : count + nlines]
+    conv_w, decay_w, input_w, decay_b, input_b, codes = refs[count + nlines : count + nlines + 6]
+    local_ref, cum_ref, last_ref, ext, keep_s, state_s, factor_s = refs[count + nlines + 6 :]
+    rows, width = mains[0].shape
     ctx_index, low, high = scal[0], scal[2], scal[3]
-    main = None
+
+    @pl.when(pl.program_id(0) == 0)
+    def _():
+        sums = None
+        for line in lines:
+            both = line[...].astype(F32)[0:2, : rows + LANES]
+            term = both[0:1, :] + both[1:2, :]
+            sums = term if sums is None else sums + term
+        factor = lax.rsqrt(sums * (1.0 / features) + 1e-06)
+        factor_s[...] = jnp.transpose(jnp.broadcast_to(factor, (LANES, rows + LANES)))
+
+    lanes = pl.ds(pl.multiple_of(pl.program_id(0) * width, width), width)
+    main = tail = None
     for piece in mains:
         term = piece[...].astype(F32)
         main = term if main is None else main + term
-    ext[0:SUB, :] = ahead[...]
-    ext[SUB : SUB + rows, :] = (main * factor[:rows, 0:1]).astype(BF16).astype(F32)
+    for line in lines:
+        term = line[:, lanes].astype(F32)[SUB:, :]
+        tail = term if tail is None else tail + term
+    ext[0:SUB, :] = (tail * factor_s[rows + LANES - SUB :, 0:1]).astype(BF16).astype(F32)
+    ext[SUB : SUB + rows, :] = (main * factor_s[:rows, 0:1]).astype(BF16).astype(F32)
     pos = ctx_index * rows + lax.broadcasted_iota(jnp.int32, (rows, 1), 0)
     start = segment_start(pos, low, high)
     conv = None
     for lag in range(CONV):
         shifted = ext[SUB - lag : SUB - lag + rows, :]
-        term = jnp.where(pos - lag >= start, conv_w[lag : lag + 1, :] * shifted, 0.0)
+        term = conv_w[lag : lag + 1, :] * shifted
+        if lag:
+            term = jnp.where(pos - lag >= start, term, 0.0)
         conv = term if conv is None else conv + term
     conv = conv.astype(BF16)
     gate_d = jax.nn.sigmoid(
@@ -520,22 +530,23 @@
     last_ref[...] = jnp.where(line == 0, run_keep, run_state)
 
 
-def recur(scal, mains, factor, ahead, conv_w, decay_w, input_w, decay_b, input_b, codes, rows):
+def recur(scal, mains, lines, conv_w, decay_w, input_w, decay_b, input_b, codes, rows, features):
     channels = conv_w.shape[1]
     tiles = rows // SUB
     by_block = pl.BlockSpec((rows, BW), lambda j: (0, j))
     row_spec = pl.BlockSpec((1, BW), lambda j: (0, j))
     gate_spec = pl.BlockSpec((1, BW, BW), lambda j: (j, 0, 0))
-    factor_spec = pl.BlockSpec(factor.shape, lambda j: (0, 0))
-    ahead_spec = pl.BlockSpec((SUB, BW), lambda j: (0, j))
+    line_specs = [
+        pl.BlockSpec((TILE, channels), functools.partial(lambda at, j: (at, 0), at)) for _, at in lines
+    ]
     full = jax.ShapeDtypeStruct((rows, channels), F32)
     return pl.pallas_call(
-        functools.partial(recur_kernel, len(mains)),
+        functools.partial(recur_kernel, len(mains), len(lines), features),
         grid=(channels // BW,),
         out_shape=(full, full, jax.ShapeDtypeStruct((SUB, channels), F32)),
         in_specs=[SMEM]
         + [by_block] * len(mains)
-        + [factor_spec, ahead_spec]
+        + line_specs
         + [pl.BlockSpec((CONV, BW), lambda j: (0, j)), gate_spec, gate_spec]
         + [row_spec] * 3,
         out_specs=(by_block, by_block, pl.BlockSpec((SUB, BW), lambda j: (0, j))),
@@ -543,10 +554,11 @@
             pltpu.VMEM((rows + SUB, BW), F32),
             pltpu.VMEM((tiles, SUB, BW), F32),
             pltpu.VMEM((tiles, SUB, BW), F32),
+            pltpu.VMEM((rows + LANES, LANES), F32),
         ],
         name="recur",
         compiler_params=pltpu.CompilerParams(vmem_limit_bytes=GRANT),
-    )(scal, *mains, factor, ahead, conv_w, decay_w, input_w, decay_b, input_b, codes)
+    )(scal, *mains, *[line for line, _ in lines], conv_w, decay_w, input_w, decay_b, input_b, codes)
 
 
 def local_near(
@@ -592,21 +604,13 @@
             pieces[done | flip] = swapped(pieces[done], "mp", flip)
         flip //= 2
     kv = assemble(scal, [pieces[e] for e in range(nmp)], rows, shard, nctx)
-    chunks = [(0,)] + [(flip,) for flip in range(nctx - 1, 0, -1)]
+    chunks = [0, 1] + list(range(nctx - 1, 1, -1))
     gain = norm_gain.reshape(1, features)
     halves, places = [], {}
     messages, give = {}, {}
-    for at, flips in enumerate(chunks):
+    for at, e in enumerate(chunks):
         keep, send = attend(
-            scal,
-            [visiting[e] for e in flips],
-            [resid_parts[e] for e in flips],
-            kv,
-            out_weight,
-            nctx,
-            back,
-            flips,
-            shard,
+            scal, [visiting[e]], [resid_parts[e]], kv, out_weight, nctx, back, (e,), shard
         )
         other = swapped(send, "mp", 1)
         mine = (keep.astype(F32) + other.astype(F32)).astype(BF16)
@@ -617,30 +621,30 @@
             flip *= 2
         other = swapped(mine, "mp", 1)
         halves += [mine, other]
-        outs = project(scal, mine, other, gain, lru_weight, len(flips), shard)
-        for j, e in enumerate(flips):
-            places[e] = (at, j * rows)
-            messages[e], give[e] = outs[2 * j], outs[2 * j + 1]
-    lines = list(tails(scal, halves, [places[e] for e in range(nctx)], gain, lru_weight, rows))
-    mains = [messages[0]]
-    for flip in range(nctx - 1, 0, -1):
-        if flip % 2 and flip > 1:
-            passed = swapped(messages[flip], "ctx", 1)
-            both = messages[flip - 1].astype(F32) + passed.astype(F32)
-            messages[flip - 1] = both.astype(BF16)
-        else:
-            mains.append(swapped(messages[flip], "ctx", flip))
-    for flip in range(1, nctx):
-        lines[flip] = swapped(lines[flip], "ctx", flip)
-    factor, ahead = stats(lines, rows, features)
+        places[e] = (at, 0)
+        messages[e], give[e] = project(scal, mine, other, gain, lru_weight, 1, shard)
+    tail_lines = tails(
+        scal, halves, [places[e] for e in range(nctx)], gain, lru_weight, messages[1], 1
+    )
+    mains, lines = [messages[0]], []
+    lines.append((tail_lines[0], 0))
+    got = swapped(tail_lines[1], "ctx", 1)
+    mains.append(got)
+    lines.append((got, rows // TILE))
+    for flip in range(nctx - 1, 1, -2):
+        passed = swapped(messages[flip], "ctx", 1)
+        lines.append((swapped(tail_lines[flip], "ctx", flip), 0))
+        both = merge(messages[flip - 1], passed, tail_lines[flip - 1])
+        got = swapped(both, "ctx", flip - 1)
+        mains.append(got)
+        lines.append((got, rows // TILE))
     given = [give[0]]
     for flip in range(1, nctx):
         given.append(swapped(give[flip], "ctx", flip))
     local_state, cum_keep, last = recur(
         scal,
         mains,
-        factor,
-        ahead,
+        lines,
         conv_weight,
         gate_decay_w,
         gate_input_w,
@@ -648,6 +652,7 @@
         gate_input_b.reshape(1, -1),
         decay_codes.reshape(1, -1),
         rows,
+        features,
     )
     before = []
     for step in range(1, reach + 1):
@@ -665,6 +670,7 @@
     nctx = lax.axis_size("ctx")
     near = (
         segment_ids.shape[0] <= WIN
+        and nctx > 1
         and nctx & (nctx - 1) == 0
         and lax.axis_size("mp") % 2 == 0
         and queries.shape[1] == out_weight.shape[1]

time: 154 us -> 139 us (0.903)
  starting transfers between devices: 44.4 us -> 35.9 us
  waiting for transfers between devices: 76.4 us -> 69.8 us
    ppermute x33 -> x31, starting transfers between devices: 42.5 us -> 32.8 us  [swapped(): return lax.ppermute(value, axis, [(s, s ^ flip) for s in range(count)])]
    ppermute x33 -> x31, waiting for transfers between devices: 74 us -> 68.5 us  [swapped(): return lax.ppermute(value, axis, [(s, s ^ flip) for s in range(count)])]
  transfers between devices with their start and end apart: 35 -> 33, of which waited for: 14 -> 15; matrix products, arithmetic and copies ran while one was open for 1% -> 1% of each run, Pallas kernels for 16% -> 20%
where the time goes in v5:
time: 139 us
  waiting for transfers between devices  69.8 us (50%)
  starting transfers between devices  35.9 us (26%)
  Pallas kernels  27.9 us (20%)
  local copies, waits for them, and re-layouts  2.7 us (2%)
  other arithmetic  1.55 us (1%)
    ppermute x31, waiting for transfers between devices, swapped(): return lax.ppermute(value, axis, [(s, s ^ flip) for s in range(count)])  68.5 us
    ppermute x31, starting transfers between devices, swapped(): return lax.ppermute(value, axis, [(s, s ^ flip) for s in range(count)])  32.8 us
    pallas_call x4, Pallas kernels, attend(): pl.pallas_call(functools.partial(attend_kernel, nctx, back, steps, shard)...  13 us
    pallas_call x4, Pallas kernels, project(): pl.pallas_call(functools.partial(project_kernel, count), out_shape=tuple(...  5.27 us
    pallas_call x1, Pallas kernels, recur(): pl.pallas_call(functools.partial(recur_kernel, len(mains), len(lines), fe...  4.93 us
    ppermute x2, starting transfers between devices, rotated(): lax.ppermute(value, axis, [(s, (s - steps) % count) for s in range(count)])  3.11 us
  transfers between devices with their start and end apart: 33, of which 15 were waited for; matrix products, arithmetic and copies ran while one was open for 1% of the time, Pallas kernels for 20%

profile of v5, /device:TPU:0, one launch (start us, length us, event | category | flops | bytes accessed | tf_op | source)
XLA Modules:
  0.0 138.8 jit_solution(15740079824795225383)
XLA Ops:
  0.6 3.1 %collective-permute-start = (bf16[64,512]{1,0:T(8,128)(2,1)}, bf16[64,512]{1,0:T(8,128)(2,1)S(1)}, u32[]{:S(2)}, u32[]{:S(2)}) collective-permute-start(bf16[64,512]{1,0:T(8,128)(2,1)} %param.14), channel_id=1, source_target_pairs={{0,4},{4,0},{8,12},{12,8},{1,5},{5,1},{9,13},{13,9},{2,6},{6,2},{1... | collective-permute-start | bytes 196616 | tf_op jit(solution)/shard_map/ppermute | solution.py:175
  3.8 2.6 %collective-permute-start.1 = (bf16[64,512]{1,0:T(8,128)(2,1)}, bf16[64,512]{1,0:T(8,128)(2,1)S(1)}, u32[]{:S(2)}, u32[]{:S(2)}) collective-permute-start(bf16[64,512]{1,0:T(8,128)(2,1)} %param.14), channel_id=1, source_target_pairs={{0,8},{4,12},{8,0},{12,4},{1,9},{5,13},{9,1},{13,5},{2,10},{6,14},... | collective-permute-start | bytes 196616 | tf_op jit(solution)/shard_map/ppermute | solution.py:175
  6.3 0.9 constant_dynamic-update-slice_fusion.3
  7.3 4.0 %collective-permute-done.1 = bf16[64,512]{1,0:T(8,128)(2,1)S(1)} collective-permute-done((bf16[64,512]{1,0:T(8,128)(2,1)}, bf16[64,512]{1,0:T(8,128)(2,1)S(1)}, u32[]{:S(2)}, u32[]{:S(2)}) %collective-permute-start.1) | collective-permute-done | bytes 65568 | tf_op jit(solution)/shard_map/ppermute | solution.py:175
  11.3 1.4 %collective-permute-done.2 = bf16[64,512]{1,0:T(8,128)(2,1)S(1)} collective-permute-done((bf16[64,512]{1,0:T(8,128)(2,1)}, bf16[64,512]{1,0:T(8,128)(2,1)S(1)}, u32[]{:S(2)}, u32[]{:S(2)}) %collective-permute-start.2) | collective-permute-done | bytes 65568 | tf_op jit(solution)/shard_map/ppermute | solution.py:175
  12.7 1.5 %collective-permute-start.4 = (bf16[256,512]{1,0:T(8,128)(2,1)S(1)}, bf16[256,512]{1,0:T(8,128)(2,1)S(1)}, u32[]{:S(2)}, u32[]{:S(2)}) collective-permute-start(bf16[256,512]{1,0:T(8,128)(2,1)S(1)} %constant_dynamic-update-slice_fusion.refs_0_), channel_id=1, source_target_pairs={{0,2},{1,3},{2,0},{3,1},{4,6},{5,7},{6,4},{7,5},{8,10},{9,11},{10,... | collective-permute-start | bytes 786440 | tf_op jit(solution)/shard_map/ppermute | solution.py:175
  14.1 1.8 %collective-permute-start.15 = (bf16[256,1024]{1,0:T(8,128)(2,1)}, bf16[256,1024]{1,0:T(8,128)(2,1)S(1)}, u32[]{:S(2)}, u32[]{:S(2)}) collective-permute-start(bf16[256,1024]{1,0:T(8,128)(2,1)} %refs_0_.1), channel_id=1, source_target_pairs={{0,12},{4,8},{8,4},{12,0},{1,13},{5,9},{9,5},{13,1},{2,14},{6,10},... | collective-permute-start | bytes 1572872 | tf_op jit(solution)/shard_map/ppermute | solution.py:175
  16.0 0.3 collective-permute-start.9
  16.3 2.8 %collective-permute-done.4.refs_2_ = bf16[256,512]{1,0:T(8,128)(2,1)S(1)} collective-permute-done((bf16[256,512]{1,0:T(8,128)(2,1)S(1)}, bf16[256,512]{1,0:T(8,128)(2,1)S(1)}, u32[]{:S(2)}, u32[]{:S(2)}) %collective-permute-start.4) | collective-permute-done | bytes 262176 | tf_op jit(solution)/shard_map/ppermute | solution.py:175
  19.1 1.0 copy-done.4
  20.1 0.7 copy-done.8
  20.8 0.7 pack.1
  21.5 1.9 %collective-permute-start.22 = (bf16[64,1024]{1,0:T(8,128)(2,1)S(1)}, bf16[64,1024]{1,0:T(8,128)(2,1)S(1)}, u32[]{:S(2)}, u32[]{:S(2)}) collective-permute-start(bf16[64,1024]{1,0:T(8,128)(2,1)S(1)} %get-tuple-element.43), channel_id=1, source_target_pairs={{0,12},{4,8},{8,4},{12,0},{1,13},{5,9},{9,5},{13,1},{2,14},{6,10},... | collective-permute-start | bytes 393224 | tf_op jit(solution)/shard_map/ppermute | solution.py:175
  23.4 0.6 assemble.1.refs_2_
  24.0 18.1 %collective-permute-done.22.refs_1_ = bf16[64,1024]{1,0:T(8,128)(2,1)S(1)} collective-permute-done((bf16[64,1024]{1,0:T(8,128)(2,1)S(1)}, bf16[64,1024]{1,0:T(8,128)(2,1)S(1)}, u32[]{:S(2)}, u32[]{:S(2)}) %collective-permute-start.22) | collective-permute-done | bytes 131104 | tf_op jit(solution)/shard_map/ppermute | solution.py:175
  42.1 3.3 %attend.7 = (bf16[256,512]{1,0:T(8,128)(2,1)S(1)}, bf16[256,512]{1,0:T(8,128)(2,1)S(1)}) custom-call(s32[4]{0:T(128)S(1)} %get-tuple-element.30.scal, bf16[256,1024]{1,0:T(8,128)(2,1)S(1)} %collective-permute-done.15.refs_0_, bf16[64,1024]{1,0:T(8,128)(2,1)S(1)} %collective-permute-done.22.refs_1_, bf16[1024,512]{1,0:T(8,128)(2,1)S(1)} %assemble.1.refs_2_, ...), custom_call_target="tpu_custom_call" | custom-call | tf_op jit(solution)/shard_map/attend/pallas_call | solution.py:300
  45.4 0.1 collective-permute-start.23
  45.5 1.8 %collective-permute-start.10 = (bf16[64,1024]{1,0:T(8,128)(2,1)S(1)}, bf16[64,1024]{1,0:T(8,128)(2,1)S(1)}, u32[]{:S(2)}, u32[]{:S(2)}) collective-permute-start(bf16[64,1024]{1,0:T(8,128)(2,1)S(1)} %get-tuple-element.35), channel_id=1, source_target_pairs={{0,4},{4,0},{8,12},{12,8},{1,5},{5,1},{9,13},{13,9},{2,6},{6,2},{1... | collective-permute-start | bytes 393224 | tf_op jit(solution)/shard_map/ppermute | solution.py:175
  47.3 0.3 collective-permute-start.16
  47.5 4.3 %collective-permute-done.10.refs_1_ = bf16[64,1024]{1,0:T(8,128)(2,1)S(1)} collective-permute-done((bf16[64,1024]{1,0:T(8,128)(2,1)S(1)}, bf16[64,1024]{1,0:T(8,128)(2,1)S(1)}, u32[]{:S(2)}, u32[]{:S(2)}) %collective-permute-start.10) | collective-permute-done | bytes 131104 | tf_op jit(solution)/shard_map/ppermute | solution.py:175
  51.9 3.2 %attend.5 = (bf16[256,512]{1,0:T(8,128)(2,1)S(1)}, bf16[256,512]{1,0:T(8,128)(2,1)S(1)}) custom-call(s32[4]{0:T(128)S(1)} %get-tuple-element.30.scal, bf16[256,1024]{1,0:T(8,128)(2,1)S(1)} %collective-permute-done.9.refs_0_, bf16[64,1024]{1,0:T(8,128)(2,1)S(1)} %collective-permute-done.10.refs_1_, bf16[1024,512]{1,0:T(8,128)(2,1)S(1)} %assemble.1.refs_2_, ...), custom_call_target="tpu_custom_call" | custom-call | tf_op jit(solution)/shard_map/attend/pallas_call | solution.py:300
  55.1 0.1 collective-permute-start.11
  55.2 2.8 %collective-permute-start.17 = (bf16[64,1024]{1,0:T(8,128)(2,1)S(1)}, bf16[64,1024]{1,0:T(8,128)(2,1)S(1)}, u32[]{:S(2)}, u32[]{:S(2)}) collective-permute-start(bf16[64,1024]{1,0:T(8,128)(2,1)S(1)} %get-tuple-element.39), channel_id=1, source_target_pairs={{0,8},{4,12},{8,0},{12,4},{1,9},{5,13},{9,1},{13,5},{2,10},{6,14},... | collective-permute-start | bytes 393224 | tf_op jit(solution)/shard_map/ppermute | solution.py:175
  58.1 3.2 %attend.4 = (bf16[256,512]{1,0:T(8,128)(2,1)S(1)}, bf16[256,512]{1,0:T(8,128)(2,1)S(1)}) custom-call(s32[4]{0:T(128)S(1)} %get-tuple-element.30.scal, bf16[256,1024]{1,0:T(8,128)(2,1)S(1)} %copy-done.5, bf16[64,1024]{1,0:T(8,128)(2,1)S(1)} %get-tuple-element.31.refs_1_, bf16[1024,512]{1,0:T(8,128)(2,1)S(1)} %assemble.1.refs_2_, bf16[1024,1024]{1,0:T(8,128)(2,1)S(1)} %copy-done.1), custom_call_target="tpu_custom_call" | custom-call | tf_op jit(solution)/shard_map/attend/pallas_call | solution.py:300
  61.3 0.2 collective-permute-start.6
  61.6 0.6 collective-permute-start.24
  62.3 1.6 %collective-permute-start.12 = (bf16[256,512]{1,0:T(8,128)(2,1)S(1)}, bf16[256,512]{1,0:T(8,128)(2,1)S(1)}, u32[]{:S(2)}, u32[]{:S(2)}) collective-permute-start(bf16[256,512]{1,0:T(8,128)(2,1)S(1)} %add_convert_fusion.6), channel_id=1, source_target_pairs={{0,2},{1,3},{2,0},{3,1},{4,6},{5,7},{6,4},{7,5},{8,10},{9,11},{10,... | collective-permute-start | bytes 786440 | tf_op jit(solution)/shard_map/ppermute | solution.py:175
  63.9 0.8 collective-permute-done.17.refs_1_
  64.7 0.7 collective-permute-done.16.refs_0_
  65.4 3.2 %attend.6 = (bf16[256,512]{1,0:T(8,128)(2,1)S(1)}, bf16[256,512]{1,0:T(8,128)(2,1)S(1)}) custom-call(s32[4]{0:T(128)S(1)} %get-tuple-element.30.scal, bf16[256,1024]{1,0:T(8,128)(2,1)S(1)} %collective-permute-done.16.refs_0_, bf16[64,1024]{1,0:T(8,128)(2,1)S(1)} %collective-permute-done.17.refs_1_, bf16[1024,512]{1,0:T(8,128)(2,1)S(1)} %assemble.1.refs_2_, ...), custom_call_target="tpu_custom_call" | custom-call | tf_op jit(solution)/shard_map/attend/pallas_call | solution.py:300
  68.7 0.1 collective-permute-start.18
  68.8 0.1 add_convert_fusion.8
  68.8 0.6 collective-permute-start.7
  69.4 1.4 %collective-permute-done.24 = bf16[256,512]{1,0:T(8,128)(2,1)S(1)} collective-permute-done((bf16[256,512]{1,0:T(8,128)(2,1)S(1)}, bf16[256,512]{1,0:T(8,128)(2,1)S(1)}, u32[]{:S(2)}, u32[]{:S(2)}) %collective-permute-start.24) | collective-permute-done | bytes 262176 | tf_op jit(solution)/shard_map/ppermute | solution.py:175
  70.9 0.1 collective-permute-start.25
  71.0 0.1 add_convert_fusion.4
  71.1 0.6 collective-permute-start.19
  71.7 4.8 %collective-permute-done.12 = bf16[256,512]{1,0:T(8,128)(2,1)S(1)} collective-permute-done((bf16[256,512]{1,0:T(8,128)(2,1)S(1)}, bf16[256,512]{1,0:T(8,128)(2,1)S(1)}, u32[]{:S(2)}, u32[]{:S(2)}) %collective-permute-start.12) | collective-permute-done | bytes 262176 | tf_op jit(solution)/shard_map/ppermute | solution.py:175
  76.6 0.1 collective-permute-start.13
  76.7 1.5 %project.7 = (bf16[256,1024]{1,0:T(8,128)(2,1)S(1)}, bf16[64,1024]{1,0:T(8,128)(2,1)S(1)}) custom-call(s32[4]{0:T(128)S(1)} %get-tuple-element.30.scal, bf16[256,512]{1,0:T(8,128)(2,1)S(1)} %add_convert_fusion.1.own.refs_4_, bf16[256,512]{1,0:T(8,128)(2,1)S(1)} %collective-permute-done.25.other.refs_5_, f32[1,4096]{1,0:T(1,128)S(1)} %bitcast.6, ...), custom_call_target="tpu_custom_call" | custom-call | tf_op jit(solution)/shard_map/project/pallas_call | solution.py:348
  78.1 0.1 collective-permute-start.28
  78.2 3.9 %collective-permute-done.7 = bf16[256,512]{1,0:T(8,128)(2,1)S(1)} collective-permute-done((bf16[256,512]{1,0:T(8,128)(2,1)S(1)}, bf16[256,512]{1,0:T(8,128)(2,1)S(1)}, u32[]{:S(2)}, u32[]{:S(2)}) %collective-permute-start.7) | collective-permute-done | bytes 262176 | tf_op jit(solution)/shard_map/ppermute | solution.py:175
  82.2 0.1 collective-permute-start.8
  82.3 4.8 %collective-permute-done.19 = bf16[256,512]{1,0:T(8,128)(2,1)S(1)} collective-permute-done((bf16[256,512]{1,0:T(8,128)(2,1)S(1)}, bf16[256,512]{1,0:T(8,128)(2,1)S(1)}, u32[]{:S(2)}, u32[]{:S(2)}) %collective-permute-start.19) | collective-permute-done | bytes 262176 | tf_op jit(solution)/shard_map/ppermute | solution.py:175
  87.2 0.1 collective-permute-start.20
  87.3 1.3 project.5
  88.5 0.2 collective-permute-done.20.other.refs_7_
  88.8 1.9 %tails.1 = (bf16[16,1024]{1,0:T(8,128)(2,1)S(1)}, bf16[272,1024]{1,0:T(8,128)(2,1)S(1)}, bf16[16,1024]{1,0:T(8,128)(2,1)S(1)}, bf16[16,1024]{1,0:T(8,128)(2,1)S(1)}) custom-call(s32[4]{0:T(128)S(1)} %get-tuple-element.30.scal, bf16[256,512]{1,0:T(8,128)(2,1)S(1)} %add_convert_fusion.7.own.refs_0_, bf16[256,512]{1,0:T(8,128)(2,1)S(1)} %collective-permute-done.8.other.refs_1_, ...), custom_call_target="tpu_custom_call" | custom-call | tf_op jit(solution)/shard_map/tails/pallas_call | solution.py:415
  90.6 0.1 collective-permute-start.27
  90.7 1.3 project.6
  92.0 0.5 collective-permute-done.28.passed
  92.6 0.1 merge.1
  92.7 1.5 %collective-permute-start.29 = (bf16[272,1024]{1,0:T(8,128)(2,1)S(1)}, bf16[272,1024]{1,0:T(8,128)(2,1)S(1)}, u32[]{:S(2)}, u32[]{:S(2)}) collective-permute-start(bf16[272,1024]{1,0:T(8,128)(2,1)S(1)} %merge.1), channel_id=1, source_target_pairs={{0,8},{4,12},{8,0},{12,4},{1,9},{5,13},{9,1},{13,5},{2,10},{6,14},... | collective-permute-start | bytes 1671176 | tf_op jit(solution)/shard_map/ppermute | solution.py:175
  94.2 2.5 %collective-permute-start.30 = (bf16[16,1024]{1,0:T(8,128)(2,1)S(1)}, bf16[16,1024]{1,0:T(8,128)(2,1)S(1)}, u32[]{:S(2)}, u32[]{:S(2)}) collective-permute-start(bf16[16,1024]{1,0:T(8,128)(2,1)S(1)} %get-tuple-element.54), channel_id=1, source_target_pairs={{0,12},{4,8},{8,4},{12,0},{1,13},{5,9},{9,5},{13,1},{2,14},{6,10},... | collective-permute-start | bytes 98312 | tf_op jit(solution)/shard_map/ppermute | solution.py:175
  96.6 1.3 collective-permute-start.26
  98.0 20.6 %collective-permute-done.30.refs_5_ = bf16[16,1024]{1,0:T(8,128)(2,1)S(1)} collective-permute-done((bf16[16,1024]{1,0:T(8,128)(2,1)S(1)}, bf16[16,1024]{1,0:T(8,128)(2,1)S(1)}, u32[]{:S(2)}, u32[]{:S(2)}) %collective-permute-start.30) | collective-permute-done | bytes 32800 | tf_op jit(solution)/shard_map/ppermute | solution.py:175
  118.6 7.1 %collective-permute-start.21 = (bf16[64,1024]{1,0:T(8,128)(2,1)S(1)}, bf16[64,1024]{1,0:T(8,128)(2,1)S(1)}, u32[]{:S(2)}, u32[]{:S(2)}) collective-permute-start(bf16[64,1024]{1,0:T(8,128)(2,1)S(1)} %get-tuple-element.42), channel_id=1, source_target_pairs={{0,8},{4,12},{8,0},{12,4},{1,9},{5,13},{9,1},{13,5},{2,10},{6,14},... | collective-permute-start | bytes 393224 | tf_op jit(solution)/shard_map/ppermute | solution.py:175
  125.8 1.3 project.4
  127.1 4.9 %recur.1 = (f32[256,1024]{1,0:T(8,128)S(1)}, f32[256,1024]{1,0:T(8,128)S(1)}, f32[8,1024]{1,0:T(8,128)S(1)}) custom-call(s32[4]{0:T(128)S(1)} %get-tuple-element.30.scal, bf16[256,1024]{1,0:T(8,128)(2,1)S(1)} %get-tuple-element.47.refs_0_, bf16[272,1024]{1,0:T(8,128)(2,1)S(1)} %collective-permute-done.27.refs_1_.refs_4_, ...), custom_call_target="tpu_custom_call" | custom-call | tf_op jit(solution)/shard_map/recur/pallas_call | solution.py:543
  132.1 0.2 collective-permute-start.31
  132.2 2.9 %collective-permute-start.32 = (f32[8,1024]{1,0:T(8,128)S(1)}, f32[8,1024]{1,0:T(8,128)S(1)}, u32[]{:S(2)}, u32[]{:S(2)}) collective-permute-start(f32[8,1024]{1,0:T(8,128)S(1)} %get-tuple-element.57), channel_id=1, source_target_pairs={{0,8},{4,12},{8,0},{12,4},{1,9},{5,13},{9,1},{13,5},{2,10},{6,14},... | collective-permute-start | bytes 98312 | tf_op jit(solution)/shard_map/ppermute | solution.py:170
  135.2 1.4 join.1
  136.6 1.3 collective-permute-done.31
  137.8 1.0 add_convert_fusion
  (54 shorter events, 0.5 us)
Async XLA Ops:
  0.6 41.5 %copy-start.1 = (bf16[1024,1024]{1,0:T(8,128)(2,1)S(1)}, bf16[1024,1024]{1,0:T(8,128)(2,1)}, u32[]{:S(2)}) copy-start(bf16[1024,1024]{1,0:T(8,128)(2,1)} %refs_3_.7) | copy-start | bytes 6291460
  0.6 6.6 %collective-permute-start = (bf16[64,512]{1,0:T(8,128)(2,1)}, bf16[64,512]{1,0:T(8,128)(2,1)S(1)}, u32[]{:S(2)}, u32[]{:S(2)}) collective-permute-start(bf16[64,512]{1,0:T(8,128)(2,1)} %param.14), channel_id=1, source_target_pairs={{0,4},{4,0},{8,12},{12,8},{1,5},{5,1},{9,13},{13,9},{2,6},{6,2},{1... | collective-permute-start | bytes 196616 | tf_op jit(solution)/shard_map/ppermute | solution.py:175
  3.8 7.5 %collective-permute-start.1 = (bf16[64,512]{1,0:T(8,128)(2,1)}, bf16[64,512]{1,0:T(8,128)(2,1)S(1)}, u32[]{:S(2)}, u32[]{:S(2)}) collective-permute-start(bf16[64,512]{1,0:T(8,128)(2,1)} %param.14), channel_id=1, source_target_pairs={{0,8},{4,12},{8,0},{12,4},{1,9},{5,13},{9,1},{13,5},{2,10},{6,14},... | collective-permute-start | bytes 196616 | tf_op jit(solution)/shard_map/ppermute | solution.py:175
  6.3 6.3 %collective-permute-start.2 = (bf16[64,512]{1,0:T(8,128)(2,1)}, bf16[64,512]{1,0:T(8,128)(2,1)S(1)}, u32[]{:S(2)}, u32[]{:S(2)}) collective-permute-start(bf16[64,512]{1,0:T(8,128)(2,1)} %param.14), channel_id=1, source_target_pairs={{0,12},{4,8},{8,4},{12,0},{1,13},{5,9},{9,5},{13,1},{2,14},{6,10},... | collective-permute-start | bytes 196616 | tf_op jit(solution)/shard_map/ppermute | solution.py:175
  12.7 6.4 %collective-permute-start.4 = (bf16[256,512]{1,0:T(8,128)(2,1)S(1)}, bf16[256,512]{1,0:T(8,128)(2,1)S(1)}, u32[]{:S(2)}, u32[]{:S(2)}) collective-permute-start(bf16[256,512]{1,0:T(8,128)(2,1)S(1)} %constant_dynamic-update-slice_fusion.refs_0_), channel_id=1, source_target_pairs={{0,2},{1,3},{2,0},{3,1},{4,6},{5,7},{6,4},{7,5},{8,10},{9,11},{10,... | collective-permute-start | bytes 786440 | tf_op jit(solution)/shard_map/ppermute | solution.py:175
  14.1 27.9 %collective-permute-start.15 = (bf16[256,1024]{1,0:T(8,128)(2,1)}, bf16[256,1024]{1,0:T(8,128)(2,1)S(1)}, u32[]{:S(2)}, u32[]{:S(2)}) collective-permute-start(bf16[256,1024]{1,0:T(8,128)(2,1)} %refs_0_.1), channel_id=1, source_target_pairs={{0,12},{4,8},{8,4},{12,0},{1,13},{5,9},{9,5},{13,1},{2,14},{6,10},... | collective-permute-start | bytes 1572872 | tf_op jit(solution)/shard_map/ppermute | solution.py:175
  16.0 35.9 %collective-permute-start.9 = (bf16[256,1024]{1,0:T(8,128)(2,1)}, bf16[256,1024]{1,0:T(8,128)(2,1)S(1)}, u32[]{:S(2)}, u32[]{:S(2)}) collective-permute-start(bf16[256,1024]{1,0:T(8,128)(2,1)} %refs_0_.1), channel_id=1, source_target_pairs={{0,4},{4,0},{8,12},{12,8},{1,5},{5,1},{9,13},{13,9},{2,6},{6,2},{1... | collective-permute-start | bytes 1572872 | tf_op jit(solution)/shard_map/ppermute | solution.py:175
  16.3 7.1 %collective-permute-start.3 = (bf16[256,512]{1,0:T(8,128)(2,1)S(1)}, bf16[256,512]{1,0:T(8,128)(2,1)S(1)}, u32[]{:S(2)}, u32[]{:S(2)}) collective-permute-start(bf16[256,512]{1,0:T(8,128)(2,1)S(1)} %constant_dynamic-update-slice_fusion.refs_0_), channel_id=1, source_target_pairs={{0,1},{1,0},{2,3},{3,2},{4,5},{5,4},{6,7},{7,6},{8,9},{9,8},{10,11... | collective-permute-start | bytes 786440 | tf_op jit(solution)/shard_map/ppermute | solution.py:175
  19.1 4.3 %collective-permute-start.5 = (bf16[256,512]{1,0:T(8,128)(2,1)S(1)}, bf16[256,512]{1,0:T(8,128)(2,1)S(1)}, u32[]{:S(2)}, u32[]{:S(2)}) collective-permute-start(bf16[256,512]{1,0:T(8,128)(2,1)S(1)} %collective-permute-done.4.refs_2_), channel_id=1, source_target_pairs={{0,1},{1,0},{2,3},{3,2},{4,5},{5,4},{6,7},{7,6},{8,9},{9,8},{10,11... | collective-permute-start | bytes 786440 | tf_op jit(solution)/shard_map/ppermute | solution.py:175
  19.1 1.0 copy-start.4
  20.1 0.7 copy-start.8
  21.5 20.6 %collective-permute-start.22 = (bf16[64,1024]{1,0:T(8,128)(2,1)S(1)}, bf16[64,1024]{1,0:T(8,128)(2,1)S(1)}, u32[]{:S(2)}, u32[]{:S(2)}) collective-permute-start(bf16[64,1024]{1,0:T(8,128)(2,1)S(1)} %get-tuple-element.43), channel_id=1, source_target_pairs={{0,12},{4,8},{8,4},{12,0},{1,13},{5,9},{9,5},{13,1},{2,14},{6,10},... | collective-permute-start | bytes 393224 | tf_op jit(solution)/shard_map/ppermute | solution.py:175
  45.4 12.7 %copy-start.5 = (bf16[256,1024]{1,0:T(8,128)(2,1)S(1)}, bf16[256,1024]{1,0:T(8,128)(2,1)}, u32[]{:S(2)}) copy-start(bf16[256,1024]{1,0:T(8,128)(2,1)} %refs_0_.1) | copy-start | bytes 1572868
  45.4 16.2 %collective-permute-start.23 = (bf16[256,512]{1,0:T(8,128)(2,1)S(1)}, bf16[256,512]{1,0:T(8,128)(2,1)S(1)}, u32[]{:S(2)}, u32[]{:S(2)}) collective-permute-start(bf16[256,512]{1,0:T(8,128)(2,1)S(1)} %get-tuple-element.45), channel_id=1, source_target_pairs={{0,1},{1,0},{2,3},{3,2},{4,5},{5,4},{6,7},{7,6},{8,9},{9,8},{10,11... | collective-permute-start | bytes 786440 | tf_op jit(solution)/shard_map/ppermute | solution.py:175
  45.5 6.4 %collective-permute-start.10 = (bf16[64,1024]{1,0:T(8,128)(2,1)S(1)}, bf16[64,1024]{1,0:T(8,128)(2,1)S(1)}, u32[]{:S(2)}, u32[]{:S(2)}) collective-permute-start(bf16[64,1024]{1,0:T(8,128)(2,1)S(1)} %get-tuple-element.35), channel_id=1, source_target_pairs={{0,4},{4,0},{8,12},{12,8},{1,5},{5,1},{9,13},{13,9},{2,6},{6,2},{1... | collective-permute-start | bytes 393224 | tf_op jit(solution)/shard_map/ppermute | solution.py:175
  47.3 18.1 %collective-permute-start.16 = (bf16[256,1024]{1,0:T(8,128)(2,1)S(1)}, bf16[256,1024]{1,0:T(8,128)(2,1)S(1)}, u32[]{:S(2)}, u32[]{:S(2)}) collective-permute-start(bf16[256,1024]{1,0:T(8,128)(2,1)S(1)} %collective-permute-done.15.refs_0_), channel_id=1, source_target_pairs={{0,4},{4,0},{8,12},{12,8},{1,5},{5,1},{9,13},{13,9},{2,6},{6,2},{1... | collective-permute-start | bytes 1572872 | tf_op jit(solution)/shard_map/ppermute | solution.py:175
  55.1 7.1 %collective-permute-start.11 = (bf16[256,512]{1,0:T(8,128)(2,1)S(1)}, bf16[256,512]{1,0:T(8,128)(2,1)S(1)}, u32[]{:S(2)}, u32[]{:S(2)}) collective-permute-start(bf16[256,512]{1,0:T(8,128)(2,1)S(1)} %get-tuple-element.37), channel_id=1, source_target_pairs={{0,1},{1,0},{2,3},{3,2},{4,5},{5,4},{6,7},{7,6},{8,9},{9,8},{10,11... | collective-permute-start | bytes 786440 | tf_op jit(solution)/shard_map/ppermute | solution.py:175
  55.2 9.4 %collective-permute-start.17 = (bf16[64,1024]{1,0:T(8,128)(2,1)S(1)}, bf16[64,1024]{1,0:T(8,128)(2,1)S(1)}, u32[]{:S(2)}, u32[]{:S(2)}) collective-permute-start(bf16[64,1024]{1,0:T(8,128)(2,1)S(1)} %get-tuple-element.39), channel_id=1, source_target_pairs={{0,8},{4,12},{8,0},{12,4},{1,9},{5,13},{9,1},{13,5},{2,10},{6,14},... | collective-permute-start | bytes 393224 | tf_op jit(solution)/shard_map/ppermute | solution.py:175
  61.3 7.4 %collective-permute-start.6 = (bf16[256,512]{1,0:T(8,128)(2,1)S(1)}, bf16[256,512]{1,0:T(8,128)(2,1)S(1)}, u32[]{:S(2)}, u32[]{:S(2)}) collective-permute-start(bf16[256,512]{1,0:T(8,128)(2,1)S(1)} %get-tuple-element.33), channel_id=1, source_target_pairs={{0,1},{1,0},{2,3},{3,2},{4,5},{5,4},{6,7},{7,6},{8,9},{9,8},{10,11... | collective-permute-start | bytes 786440 | tf_op jit(solution)/shard_map/ppermute | solution.py:175
  61.6 9.2 %collective-permute-start.24 = (bf16[256,512]{1,0:T(8,128)(2,1)S(1)}, bf16[256,512]{1,0:T(8,128)(2,1)S(1)}, u32[]{:S(2)}, u32[]{:S(2)}) collective-permute-start(bf16[256,512]{1,0:T(8,128)(2,1)S(1)} %add_convert_fusion.2), channel_id=1, source_target_pairs={{0,2},{1,3},{2,0},{3,1},{4,6},{5,7},{6,4},{7,5},{8,10},{9,11},{10,... | collective-permute-start | bytes 786440 | tf_op jit(solution)/shard_map/ppermute | solution.py:175
  62.3 14.2 %collective-permute-start.12 = (bf16[256,512]{1,0:T(8,128)(2,1)S(1)}, bf16[256,512]{1,0:T(8,128)(2,1)S(1)}, u32[]{:S(2)}, u32[]{:S(2)}) collective-permute-start(bf16[256,512]{1,0:T(8,128)(2,1)S(1)} %add_convert_fusion.6), channel_id=1, source_target_pairs={{0,2},{1,3},{2,0},{3,1},{4,6},{5,7},{6,4},{7,5},{8,10},{9,11},{10,... | collective-permute-start | bytes 786440 | tf_op jit(solution)/shard_map/ppermute | solution.py:175
  68.7 8.0 %copy-start = (bf16[1024,1024]{1,0:T(8,128)(2,1)S(1)}, bf16[1024,1024]{1,0:T(8,128)(2,1)}, u32[]{:S(2)}) copy-start(bf16[1024,1024]{1,0:T(8,128)(2,1)} %refs_9_.2) | copy-start | bytes 6291460
  68.7 8.0 %copy-start.6 = (f32[4096]{0:T(1024)S(1)}, f32[4096]{0:T(1024)}, u32[]{:S(2)}) copy-start(f32[4096]{0:T(1024)} %param.25) | copy-start | bytes 49156
  68.7 2.3 %collective-permute-start.18 = (bf16[256,512]{1,0:T(8,128)(2,1)S(1)}, bf16[256,512]{1,0:T(8,128)(2,1)S(1)}, u32[]{:S(2)}, u32[]{:S(2)}) collective-permute-start(bf16[256,512]{1,0:T(8,128)(2,1)S(1)} %get-tuple-element.41), channel_id=1, source_target_pairs={{0,1},{1,0},{2,3},{3,2},{4,5},{5,4},{6,7},{7,6},{8,9},{9,8},{10,11... | collective-permute-start | bytes 786440 | tf_op jit(solution)/shard_map/ppermute | solution.py:175
  68.8 13.3 %collective-permute-start.7 = (bf16[256,512]{1,0:T(8,128)(2,1)S(1)}, bf16[256,512]{1,0:T(8,128)(2,1)S(1)}, u32[]{:S(2)}, u32[]{:S(2)}) collective-permute-start(bf16[256,512]{1,0:T(8,128)(2,1)S(1)} %add_convert_fusion.8), channel_id=1, source_target_pairs={{0,2},{1,3},{2,0},{3,1},{4,6},{5,7},{6,4},{7,5},{8,10},{9,11},{10,... | collective-permute-start | bytes 786440 | tf_op jit(solution)/shard_map/ppermute | solution.py:175
  70.9 5.7 %collective-permute-start.25 = (bf16[256,512]{1,0:T(8,128)(2,1)S(1)}, bf16[256,512]{1,0:T(8,128)(2,1)S(1)}, u32[]{:S(2)}, u32[]{:S(2)}) collective-permute-start(bf16[256,512]{1,0:T(8,128)(2,1)S(1)} %add_convert_fusion.1.own.refs_4_), channel_id=1, source_target_pairs={{0,1},{1,0},{2,3},{3,2},{4,5},{5,4},{6,7},{7,6},{8,9},{9,8},{10,11... | collective-permute-start | bytes 786440 | tf_op jit(solution)/shard_map/ppermute | solution.py:175
  71.1 16.0 %collective-permute-start.19 = (bf16[256,512]{1,0:T(8,128)(2,1)S(1)}, bf16[256,512]{1,0:T(8,128)(2,1)S(1)}, u32[]{:S(2)}, u32[]{:S(2)}) collective-permute-start(bf16[256,512]{1,0:T(8,128)(2,1)S(1)} %add_convert_fusion.4), channel_id=1, source_target_pairs={{0,2},{1,3},{2,0},{3,1},{4,6},{5,7},{6,4},{7,5},{8,10},{9,11},{10,... | collective-permute-start | bytes 786440 | tf_op jit(solution)/shard_map/ppermute | solution.py:175
  76.6 10.7 %collective-permute-start.13 = (bf16[256,512]{1,0:T(8,128)(2,1)S(1)}, bf16[256,512]{1,0:T(8,128)(2,1)S(1)}, u32[]{:S(2)}, u32[]{:S(2)}) collective-permute-start(bf16[256,512]{1,0:T(8,128)(2,1)S(1)} %add_convert_fusion.5.own.refs_2_), channel_id=1, source_target_pairs={{0,1},{1,0},{2,3},{3,2},{4,5},{5,4},{6,7},{7,6},{8,9},{9,8},{10,11... | collective-permute-start | bytes 786440 | tf_op jit(solution)/shard_map/ppermute | solution.py:175
  78.1 14.4 %collective-permute-start.28 = (bf16[256,1024]{1,0:T(8,128)(2,1)S(1)}, bf16[256,1024]{1,0:T(8,128)(2,1)S(1)}, u32[]{:S(2)}, u32[]{:S(2)}) collective-permute-start(bf16[256,1024]{1,0:T(8,128)(2,1)S(1)} %get-tuple-element.51), channel_id=1, source_target_pairs={{0,4},{4,0},{8,12},{12,8},{1,5},{5,1},{9,13},{13,9},{2,6},{6,2},{1... | collective-permute-start | bytes 1572872 | tf_op jit(solution)/shard_map/ppermute | solution.py:175
  82.2 6.4 %collective-permute-start.8 = (bf16[256,512]{1,0:T(8,128)(2,1)S(1)}, bf16[256,512]{1,0:T(8,128)(2,1)S(1)}, u32[]{:S(2)}, u32[]{:S(2)}) collective-permute-start(bf16[256,512]{1,0:T(8,128)(2,1)S(1)} %add_convert_fusion.7.own.refs_0_), channel_id=1, source_target_pairs={{0,1},{1,0},{2,3},{3,2},{4,5},{5,4},{6,7},{7,6},{8,9},{9,8},{10,11... | collective-permute-start | bytes 786440 | tf_op jit(solution)/shard_map/ppermute | solution.py:175
  87.2 1.6 %collective-permute-start.20 = (bf16[256,512]{1,0:T(8,128)(2,1)S(1)}, bf16[256,512]{1,0:T(8,128)(2,1)S(1)}, u32[]{:S(2)}, u32[]{:S(2)}) collective-permute-start(bf16[256,512]{1,0:T(8,128)(2,1)S(1)} %add_convert_fusion.3.own.refs_6_), channel_id=1, source_target_pairs={{0,1},{1,0},{2,3},{3,2},{4,5},{5,4},{6,7},{7,6},{8,9},{9,8},{10,11... | collective-permute-start | bytes 786440 | tf_op jit(solution)/shard_map/ppermute | solution.py:175
  90.6 36.4 %collective-permute-start.27 = (bf16[272,1024]{1,0:T(8,128)(2,1)S(1)}, bf16[272,1024]{1,0:T(8,128)(2,1)S(1)}, u32[]{:S(2)}, u32[]{:S(2)}) collective-permute-start(bf16[272,1024]{1,0:T(8,128)(2,1)S(1)} %get-tuple-element.49), channel_id=1, source_target_pairs={{0,4},{4,0},{8,12},{12,8},{1,5},{5,1},{9,13},{13,9},{2,6},{6,2},{1... | collective-permute-start | bytes 1671176 | tf_op jit(solution)/shard_map/ppermute | solution.py:175
  92.5 34.5 %copy-start.2 = (bf16[4,256,256]{2,1,0:T(8,128)(2,1)S(1)}, bf16[4,256,256]{2,1,0:T(8,128)(2,1)}, u32[]{:S(2)}) copy-start(bf16[4,256,256]{2,1,0:T(8,128)(2,1)} %refs_8_.1) | copy-start | bytes 1572868
  92.5 34.6 %copy-start.3 = (bf16[4,256,256]{2,1,0:T(8,128)(2,1)S(1)}, bf16[4,256,256]{2,1,0:T(8,128)(2,1)}, u32[]{:S(2)}) copy-start(bf16[4,256,256]{2,1,0:T(8,128)(2,1)} %refs_9_.3) | copy-start | bytes 1572868
  92.5 34.6 %copy-start.7 = (f32[4,1024]{1,0:T(4,128)S(1)}, f32[4,1024]{1,0:T(4,128)}, u32[]{:S(2)}) copy-start(f32[4,1024]{1,0:T(4,128)} %refs_7_.1) | copy-start | bytes 49156
  92.5 34.6 %copy-start.9 = (f32[1024]{0:T(1024)S(1)}, f32[1024]{0:T(1024)}, u32[]{:S(2)}) copy-start(f32[1024]{0:T(1024)} %param.22) | copy-start | bytes 12292
  92.5 34.6 %copy-start.10 = (f32[1024]{0:T(1024)S(1)}, f32[1024]{0:T(1024)}, u32[]{:S(2)}) copy-start(f32[1024]{0:T(1024)} %param.23) | copy-start | bytes 12292
  92.5 34.6 %copy-start.11 = (s32[1024]{0:T(1024)S(1)}, s32[1024]{0:T(1024)}, u32[]{:S(2)}) copy-start(s32[1024]{0:T(1024)} %param.24) | copy-start | bytes 12292
  92.7 34.4 %collective-permute-start.29 = (bf16[272,1024]{1,0:T(8,128)(2,1)S(1)}, bf16[272,1024]{1,0:T(8,128)(2,1)S(1)}, u32[]{:S(2)}, u32[]{:S(2)}) collective-permute-start(bf16[272,1024]{1,0:T(8,128)(2,1)S(1)} %merge.1), channel_id=1, source_target_pairs={{0,8},{4,12},{8,0},{12,4},{1,9},{5,13},{9,1},{13,5},{2,10},{6,14},... | collective-permute-start | bytes 1671176 | tf_op jit(solution)/shard_map/ppermute | solution.py:175
  94.2 24.5 %collective-permute-start.30 = (bf16[16,1024]{1,0:T(8,128)(2,1)S(1)}, bf16[16,1024]{1,0:T(8,128)(2,1)S(1)}, u32[]{:S(2)}, u32[]{:S(2)}) collective-permute-start(bf16[16,1024]{1,0:T(8,128)(2,1)S(1)} %get-tuple-element.54), channel_id=1, source_target_pairs={{0,12},{4,8},{8,4},{12,0},{1,13},{5,9},{9,5},{13,1},{2,14},{6,10},... | collective-permute-start | bytes 98312 | tf_op jit(solution)/shard_map/ppermute | solution.py:175
  96.6 38.5 %collective-permute-start.26 = (bf16[64,1024]{1,0:T(8,128)(2,1)S(1)}, bf16[64,1024]{1,0:T(8,128)(2,1)S(1)}, u32[]{:S(2)}, u32[]{:S(2)}) collective-permute-start(bf16[64,1024]{1,0:T(8,128)(2,1)S(1)} %get-tuple-element.46), channel_id=1, source_target_pairs={{0,12},{4,8},{8,4},{12,0},{1,13},{5,9},{9,5},{13,1},{2,14},{6,10},... | collective-permute-start | bytes 393224 | tf_op jit(solution)/shard_map/ppermute | solution.py:175
  98.0 37.2 %collective-permute-start.14 = (bf16[64,1024]{1,0:T(8,128)(2,1)S(1)}, bf16[64,1024]{1,0:T(8,128)(2,1)S(1)}, u32[]{:S(2)}, u32[]{:S(2)}) collective-permute-start(bf16[64,1024]{1,0:T(8,128)(2,1)S(1)} %get-tuple-element.38), channel_id=1, source_target_pairs={{0,4},{4,0},{8,12},{12,8},{1,5},{5,1},{9,13},{13,9},{2,6},{6,2},{1... | collective-permute-start | bytes 393224 | tf_op jit(solution)/shard_map/ppermute | solution.py:175
  118.6 16.5 %collective-permute-start.21 = (bf16[64,1024]{1,0:T(8,128)(2,1)S(1)}, bf16[64,1024]{1,0:T(8,128)(2,1)S(1)}, u32[]{:S(2)}, u32[]{:S(2)}) collective-permute-start(bf16[64,1024]{1,0:T(8,128)(2,1)S(1)} %get-tuple-element.42), channel_id=1, source_target_pairs={{0,8},{4,12},{8,0},{12,4},{1,9},{5,13},{9,1},{13,5},{2,10},{6,14},... | collective-permute-start | bytes 393224 | tf_op jit(solution)/shard_map/ppermute | solution.py:175
  132.1 5.8 %collective-permute-start.31 = (f32[8,1024]{1,0:T(8,128)S(1)}, f32[8,1024]{1,0:T(8,128)S(1)}, u32[]{:S(2)}, u32[]{:S(2)}) collective-permute-start(f32[8,1024]{1,0:T(8,128)S(1)} %get-tuple-element.57), channel_id=1, source_target_pairs={{0,4},{4,8},{8,12},{12,0},{1,5},{5,9},{9,13},{13,1},{2,6},{6,10},{... | collective-permute-start | bytes 98312 | tf_op jit(solution)/shard_map/ppermute | solution.py:170
  132.2 5.6 %collective-permute-start.32 = (f32[8,1024]{1,0:T(8,128)S(1)}, f32[8,1024]{1,0:T(8,128)S(1)}, u32[]{:S(2)}, u32[]{:S(2)}) collective-permute-start(f32[8,1024]{1,0:T(8,128)S(1)} %get-tuple-element.57), channel_id=1, source_target_pairs={{0,8},{4,12},{8,0},{12,4},{1,9},{5,13},{9,1},{13,5},{2,10},{6,14},... | collective-permute-start | bytes 98312 | tf_op jit(solution)/shard_map/ppermute | solution.py:170

commit v6 on v5

--- a/solution.py
+++ b/solution.py
@@ -355,12 +355,11 @@
     )(scal, own, other, gain, weight)
 
 
-def tails_kernel(places, nhalves, rows, near, scal, *refs):
+def tails_kernel(places, nhalves, rows, scal, *refs):
     nctx = len(places)
-    halves, (gain, weight, message) = refs[:nhalves], refs[nhalves : nhalves + 3]
-    outs = refs[nhalves + 3 : nhalves + 3 + nctx]
-    edges, ends = refs[nhalves + 3 + nctx :]
-    outs[near][0:rows, :] = message[...]
+    halves, (gain, weight) = refs[:nhalves], refs[nhalves : nhalves + 2]
+    outs = refs[nhalves + 2 : nhalves + 2 + nctx]
+    edges, ends = refs[nhalves + 2 + nctx :]
     ctx_index = scal[0]
     side = jnp.bitwise_and(scal[1], 1)
     channels = weight.shape[1]
@@ -404,21 +403,16 @@
         index = lax.broadcasted_iota(jnp.int32, line.shape, 0)
         line = jnp.where(index == 0, coarse, line - coarse)
         tail = tails[(flip + 1) * TILE - SUB : (flip + 1) * TILE, :]
-        base = rows if flip == near else 0
-        outs[flip][base : base + TILE, :] = jnp.concatenate([line, tail], axis=0).astype(BF16)
-
-
-def tails(scal, halves, places, gain, weight, message, near):
+        outs[flip][...] = jnp.concatenate([line, tail], axis=0).astype(BF16)
+
+
+def tails(scal, halves, places, gain, weight, rows):
     nctx = len(places)
     half, channels = weight.shape[0] // 2, weight.shape[1]
-    rows = message.shape[0]
     return pl.pallas_call(
-        functools.partial(tails_kernel, places, len(halves), rows, near),
-        out_shape=tuple(
-            jax.ShapeDtypeStruct((TILE + (rows if flip == near else 0), channels), BF16)
-            for flip in range(nctx)
-        ),
-        in_specs=[SMEM] + [VMEM] * (len(halves) + 3),
+        functools.partial(tails_kernel, places, len(halves), rows),
+        out_shape=(jax.ShapeDtypeStruct((TILE, channels), BF16),) * nctx,
+        in_specs=[SMEM] + [VMEM] * (len(halves) + 2),
         out_specs=(VMEM,) * nctx,
         scratch_shapes=[
             pltpu.VMEM((2, nctx * LANES, half), BF16),
@@ -426,25 +420,7 @@
         ],
         name="tails",
         compiler_params=pltpu.CompilerParams(vmem_limit_bytes=GRANT),
-    )(scal, *halves, gain, weight, message)
-
-
-def merge_kernel(message, passed, line, out):
-    rows = message.shape[0]
-    out[0:rows, :] = (message[...].astype(F32) + passed[...].astype(F32)).astype(BF16)
-    out[rows:, :] = line[...]
-
-
-def merge(message, passed, line):
-    rows, channels = message.shape
-    return pl.pallas_call(
-        merge_kernel,
-        out_shape=jax.ShapeDtypeStruct((rows + TILE, channels), BF16),
-        in_specs=[VMEM] * 3,
-        out_specs=VMEM,
-        name="merge",
-        compiler_params=pltpu.CompilerParams(vmem_limit_bytes=GRANT),
-    )(message, passed, line)
+    )(scal, *halves, gain, weight)
 
 
 def minus_expm1(x):
@@ -536,9 +512,7 @@
     by_block = pl.BlockSpec((rows, BW), lambda j: (0, j))
     row_spec = pl.BlockSpec((1, BW), lambda j: (0, j))
     gate_spec = pl.BlockSpec((1, BW, BW), lambda j: (j, 0, 0))
-    line_specs = [
-        pl.BlockSpec((TILE, channels), functools.partial(lambda at, j: (at, 0), at)) for _, at in lines
-    ]
+    line_spec = pl.BlockSpec((TILE, channels), lambda j: (0, 0))
     full = jax.ShapeDtypeStruct((rows, channels), F32)
     return pl.pallas_call(
         functools.partial(recur_kernel, len(mains), len(lines), features),
@@ -546,7 +520,7 @@
         out_shape=(full, full, jax.ShapeDtypeStruct((SUB, channels), F32)),
         in_specs=[SMEM]
         + [by_block] * len(mains)
-        + line_specs
+        + [line_spec] * len(lines)
         + [pl.BlockSpec((CONV, BW), lambda j: (0, j)), gate_spec, gate_spec]
         + [row_spec] * 3,
         out_specs=(by_block, by_block, pl.BlockSpec((SUB, BW), lambda j: (0, j))),
@@ -558,7 +532,7 @@
         ],
         name="recur",
         compiler_params=pltpu.CompilerParams(vmem_limit_bytes=GRANT),
-    )(scal, *mains, *[line for line, _ in lines], conv_w, decay_w, input_w, decay_b, input_b, codes)
+    )(scal, *mains, *lines, conv_w, decay_w, input_w, decay_b, input_b, codes)
 
 
 def local_near(
@@ -604,7 +578,7 @@
             pieces[done | flip] = swapped(pieces[done], "mp", flip)
         flip //= 2
     kv = assemble(scal, [pieces[e] for e in range(nmp)], rows, shard, nctx)
-    chunks = [0, 1] + list(range(nctx - 1, 1, -1))
+    chunks = [0] + list(range(nctx - 1, 2, -2)) + [1] + list(range(nctx - 2, 1, -2))
     gain = norm_gain.reshape(1, features)
     halves, places = [], {}
     messages, give = {}, {}
@@ -623,21 +597,17 @@
         halves += [mine, other]
         places[e] = (at, 0)
         messages[e], give[e] = project(scal, mine, other, gain, lru_weight, 1, shard)
-    tail_lines = tails(
-        scal, halves, [places[e] for e in range(nctx)], gain, lru_weight, messages[1], 1
-    )
-    mains, lines = [messages[0]], []
-    lines.append((tail_lines[0], 0))
-    got = swapped(tail_lines[1], "ctx", 1)
-    mains.append(got)
-    lines.append((got, rows // TILE))
-    for flip in range(nctx - 1, 1, -2):
-        passed = swapped(messages[flip], "ctx", 1)
-        lines.append((swapped(tail_lines[flip], "ctx", flip), 0))
-        both = merge(messages[flip - 1], passed, tail_lines[flip - 1])
-        got = swapped(both, "ctx", flip - 1)
-        mains.append(got)
-        lines.append((got, rows // TILE))
+    lines = list(tails(scal, halves, [places[e] for e in range(nctx)], gain, lru_weight, rows))
+    mains = [messages[0]]
+    for flip in range(nctx - 1, 0, -1):
+        if flip % 2 and flip > 1:
+            passed = swapped(messages[flip], "ctx", 1)
+            both = messages[flip - 1].astype(F32) + passed.astype(F32)
+            messages[flip - 1] = both.astype(BF16)
+        else:
+            mains.append(swapped(messages[flip], "ctx", flip))
+    for flip in range(1, nctx):
+        lines[flip] = swapped(lines[flip], "ctx", flip)
     given = [give[0]]
     for flip in range(1, nctx):
         given.append(swapped(give[flip], "ctx", flip))

time: 139 us -> 154 us (1.11)
  starting transfers between devices: 35.9 us -> 44.4 us
  waiting for transfers between devices: 69.8 us -> 76.4 us
    ppermute x31 -> x33, starting transfers between devices: 32.8 us -> 42.5 us  [swapped(): return lax.ppermute(value, axis, [(s, s ^ flip) for s in range(count)])]
    ppermute x31 -> x33, waiting for transfers between devices: 68.5 us -> 74 us  [swapped(): return lax.ppermute(value, axis, [(s, s ^ flip) for s in range(count)])]
  transfers between devices with their start and end apart: 33 -> 35, of which waited for: 15 -> 14; matrix products, arithmetic and copies ran while one was open for 1% -> 1% of each run, Pallas kernels for 20% -> 16%
where the time goes in v6:
time: 154 us
  waiting for transfers between devices  76.4 us (50%)
  starting transfers between devices  44.4 us (29%)
  Pallas kernels  27.5 us (18%)
  local copies, waits for them, and re-layouts  2.71 us (2%)
  other arithmetic  1.91 us (1%)
    ppermute x33, waiting for transfers between devices, swapped(): return lax.ppermute(value, axis, [(s, s ^ flip) for s in range(count)])  74 us
    ppermute x33, starting transfers between devices, swapped(): return lax.ppermute(value, axis, [(s, s ^ flip) for s in range(count)])  42.5 us
    pallas_call x4, Pallas kernels, attend(): pl.pallas_call(functools.partial(attend_kernel, nctx, back, steps, shard)...  13 us
    pallas_call x4, Pallas kernels, project(): pl.pallas_call(functools.partial(project_kernel, count), out_shape=tuple(...  5.06 us
    pallas_call x1, Pallas kernels, recur(): pl.pallas_call(functools.partial(recur_kernel, len(mains), len(lines), fe...  4.93 us
  transfers between devices with their start and end apart: 35, of which 14 were waited for; matrix products, arithmetic and copies ran while one was open for 1% of the time, Pallas kernels for 16%

profile of v6, /device:TPU:0, one launch (start us, length us, event | category | flops | bytes accessed | tf_op | source)
XLA Modules:
  0.0 154.1 jit_solution(6348281176876990981)
XLA Ops:
  0.6 3.1 %collective-permute-start = (bf16[64,512]{1,0:T(8,128)(2,1)}, bf16[64,512]{1,0:T(8,128)(2,1)S(1)}, u32[]{:S(2)}, u32[]{:S(2)}) collective-permute-start(bf16[64,512]{1,0:T(8,128)(2,1)} %param.14), channel_id=1, source_target_pairs={{0,4},{4,0},{8,12},{12,8},{1,5},{5,1},{9,13},{13,9},{2,6},{6,2},{1... | collective-permute-start | bytes 196616 | tf_op jit(solution)/shard_map/ppermute | solution.py:175
  3.8 2.6 %collective-permute-start.1 = (bf16[64,512]{1,0:T(8,128)(2,1)}, bf16[64,512]{1,0:T(8,128)(2,1)S(1)}, u32[]{:S(2)}, u32[]{:S(2)}) collective-permute-start(bf16[64,512]{1,0:T(8,128)(2,1)} %param.14), channel_id=1, source_target_pairs={{0,8},{4,12},{8,0},{12,4},{1,9},{5,13},{9,1},{13,5},{2,10},{6,14},... | collective-permute-start | bytes 196616 | tf_op jit(solution)/shard_map/ppermute | solution.py:175
  6.3 0.9 constant_dynamic-update-slice_fusion.3
  7.3 4.0 %collective-permute-done.1 = bf16[64,512]{1,0:T(8,128)(2,1)S(1)} collective-permute-done((bf16[64,512]{1,0:T(8,128)(2,1)}, bf16[64,512]{1,0:T(8,128)(2,1)S(1)}, u32[]{:S(2)}, u32[]{:S(2)}) %collective-permute-start.1) | collective-permute-done | bytes 65568 | tf_op jit(solution)/shard_map/ppermute | solution.py:175
  11.3 1.4 collective-permute-done.2
  12.7 1.5 collective-permute-start.4
  14.1 1.8 %collective-permute-start.15 = (bf16[256,1024]{1,0:T(8,128)(2,1)}, bf16[256,1024]{1,0:T(8,128)(2,1)S(1)}, u32[]{:S(2)}, u32[]{:S(2)}) collective-permute-start(bf16[256,1024]{1,0:T(8,128)(2,1)} %refs_0_.1), channel_id=1, source_target_pairs={{0,12},{4,8},{8,4},{12,0},{1,13},{5,9},{9,5},{13,1},{2,14},{6,10},... | collective-permute-start | bytes 1572872 | tf_op jit(solution)/shard_map/ppermute | solution.py:175
  16.0 3.1 %collective-permute-done.4.refs_2_ = bf16[256,512]{1,0:T(8,128)(2,1)S(1)} collective-permute-done((bf16[256,512]{1,0:T(8,128)(2,1)S(1)}, bf16[256,512]{1,0:T(8,128)(2,1)S(1)}, u32[]{:S(2)}, u32[]{:S(2)}) %collective-permute-start.4) | collective-permute-done | bytes 262176 | tf_op jit(solution)/shard_map/ppermute | solution.py:175
  19.1 1.0 copy-done.2
  20.1 0.7 copy-done.8
  20.8 0.7 pack.1
  21.5 1.9 %collective-permute-start.22 = (bf16[64,1024]{1,0:T(8,128)(2,1)S(1)}, bf16[64,1024]{1,0:T(8,128)(2,1)S(1)}, u32[]{:S(2)}, u32[]{:S(2)}) collective-permute-start(bf16[64,1024]{1,0:T(8,128)(2,1)S(1)} %get-tuple-element.43), channel_id=1, source_target_pairs={{0,12},{4,8},{8,4},{12,0},{1,13},{5,9},{9,5},{13,1},{2,14},{6,10},... | collective-permute-start | bytes 393224 | tf_op jit(solution)/shard_map/ppermute | solution.py:175
  23.4 0.6 assemble.1.refs_2_
  24.0 6.8 %collective-permute-done.22.refs_1_ = bf16[64,1024]{1,0:T(8,128)(2,1)S(1)} collective-permute-done((bf16[64,1024]{1,0:T(8,128)(2,1)S(1)}, bf16[64,1024]{1,0:T(8,128)(2,1)S(1)}, u32[]{:S(2)}, u32[]{:S(2)}) %collective-permute-start.22) | collective-permute-done | bytes 131104 | tf_op jit(solution)/shard_map/ppermute | solution.py:175
  30.8 3.3 %attend.7 = (bf16[256,512]{1,0:T(8,128)(2,1)S(1)}, bf16[256,512]{1,0:T(8,128)(2,1)S(1)}) custom-call(s32[4]{0:T(128)S(1)} %get-tuple-element.30.scal, bf16[256,1024]{1,0:T(8,128)(2,1)S(1)} %collective-permute-done.15.refs_0_, bf16[64,1024]{1,0:T(8,128)(2,1)S(1)} %collective-permute-done.22.refs_1_, bf16[1024,512]{1,0:T(8,128)(2,1)S(1)} %assemble.1.refs_2_, ...), custom_call_target="tpu_custom_call" | custom-call | tf_op jit(solution)/shard_map/attend/pallas_call | solution.py:300
  34.1 0.1 collective-permute-start.23
  34.2 13.1 %collective-permute-start.9 = (bf16[256,1024]{1,0:T(8,128)(2,1)S(1)}, bf16[256,1024]{1,0:T(8,128)(2,1)S(1)}, u32[]{:S(2)}, u32[]{:S(2)}) collective-permute-start(bf16[256,1024]{1,0:T(8,128)(2,1)S(1)} %copy-done.3), channel_id=1, source_target_pairs={{0,4},{4,0},{8,12},{12,8},{1,5},{5,1},{9,13},{13,9},{2,6},{6,2},{1... | collective-permute-start | bytes 1572872 | tf_op jit(solution)/shard_map/ppermute | solution.py:175
  47.3 0.1 collective-permute-start.16
  47.4 0.6 collective-permute-start.24
  48.0 1.9 %collective-permute-start.10 = (bf16[64,1024]{1,0:T(8,128)(2,1)S(1)}, bf16[64,1024]{1,0:T(8,128)(2,1)S(1)}, u32[]{:S(2)}, u32[]{:S(2)}) collective-permute-start(bf16[64,1024]{1,0:T(8,128)(2,1)S(1)} %get-tuple-element.35), channel_id=1, source_target_pairs={{0,4},{4,0},{8,12},{12,8},{1,5},{5,1},{9,13},{13,9},{2,6},{6,2},{1... | collective-permute-start | bytes 393224 | tf_op jit(solution)/shard_map/ppermute | solution.py:175
  50.0 1.1 collective-permute-start.17
  51.1 25.6 %collective-permute-done.10.refs_1_ = bf16[64,1024]{1,0:T(8,128)(2,1)S(1)} collective-permute-done((bf16[64,1024]{1,0:T(8,128)(2,1)S(1)}, bf16[64,1024]{1,0:T(8,128)(2,1)S(1)}, u32[]{:S(2)}, u32[]{:S(2)}) %collective-permute-start.10) | collective-permute-done | bytes 131104 | tf_op jit(solution)/shard_map/ppermute | solution.py:175
  76.6 3.2 %attend.5 = (bf16[256,512]{1,0:T(8,128)(2,1)S(1)}, bf16[256,512]{1,0:T(8,128)(2,1)S(1)}) custom-call(s32[4]{0:T(128)S(1)} %get-tuple-element.30.scal, bf16[256,1024]{1,0:T(8,128)(2,1)S(1)} %collective-permute-done.9.refs_0_, bf16[64,1024]{1,0:T(8,128)(2,1)S(1)} %collective-permute-done.10.refs_1_, bf16[1024,512]{1,0:T(8,128)(2,1)S(1)} %assemble.1.refs_2_, ...), custom_call_target="tpu_custom_call" | custom-call | tf_op jit(solution)/shard_map/attend/pallas_call | solution.py:300
  79.9 0.1 collective-permute-start.11
  80.0 3.2 %attend.6 = (bf16[256,512]{1,0:T(8,128)(2,1)S(1)}, bf16[256,512]{1,0:T(8,128)(2,1)S(1)}) custom-call(s32[4]{0:T(128)S(1)} %get-tuple-element.30.scal, bf16[256,1024]{1,0:T(8,128)(2,1)S(1)} %collective-permute-done.16.refs_0_, bf16[64,1024]{1,0:T(8,128)(2,1)S(1)} %collective-permute-done.17.refs_1_, bf16[1024,512]{1,0:T(8,128)(2,1)S(1)} %assemble.1.refs_2_, ...), custom_call_target="tpu_custom_call" | custom-call | tf_op jit(solution)/shard_map/attend/pallas_call | solution.py:300
  83.2 0.6 collective-permute-start.18
  83.9 0.1 collective-permute-start.25
  84.0 0.6 collective-permute-start.12
  84.6 0.3 collective-permute-done.18
  85.1 1.2 collective-permute-start.19
  86.3 3.2 %attend.4 = (bf16[256,512]{1,0:T(8,128)(2,1)S(1)}, bf16[256,512]{1,0:T(8,128)(2,1)S(1)}) custom-call(s32[4]{0:T(128)S(1)} %get-tuple-element.30.scal, bf16[256,1024]{1,0:T(8,128)(2,1)S(1)} %copy-done.3, bf16[64,1024]{1,0:T(8,128)(2,1)S(1)} %get-tuple-element.31.refs_1_, bf16[1024,512]{1,0:T(8,128)(2,1)S(1)} %assemble.1.refs_2_, bf16[1024,1024]{1,0:T(8,128)(2,1)S(1)} %copy-done.1), custom_call_target="tpu_custom_call" | custom-call | tf_op jit(solution)/shard_map/attend/pallas_call | solution.py:300
  89.5 0.1 collective-permute-start.6
  89.6 1.3 project.7
  90.9 0.1 collective-permute-start.27
  91.0 2.3 %collective-permute-done.12 = bf16[256,512]{1,0:T(8,128)(2,1)S(1)} collective-permute-done((bf16[256,512]{1,0:T(8,128)(2,1)S(1)}, bf16[256,512]{1,0:T(8,128)(2,1)S(1)}, u32[]{:S(2)}, u32[]{:S(2)}) %collective-permute-start.12) | collective-permute-done | bytes 262176 | tf_op jit(solution)/shard_map/ppermute | solution.py:175
  93.3 0.2 add_convert_fusion.6.own.refs_4_
  93.5 0.1 collective-permute-start.13
  93.6 4.8 %collective-permute-done.19 = bf16[256,512]{1,0:T(8,128)(2,1)S(1)} collective-permute-done((bf16[256,512]{1,0:T(8,128)(2,1)S(1)}, bf16[256,512]{1,0:T(8,128)(2,1)S(1)}, u32[]{:S(2)}, u32[]{:S(2)}) %collective-permute-start.19) | collective-permute-done | bytes 262176 | tf_op jit(solution)/shard_map/ppermute | solution.py:175
  98.5 0.1 collective-permute-start.20
  98.6 0.1 add_convert_fusion.9
  98.6 0.6 collective-permute-start.7
  99.2 1.3 project.5
  100.5 0.1 collective-permute-start.29
  100.6 1.3 project.6
  101.9 3.9 %collective-permute-done.27 = bf16[256,1024]{1,0:T(8,128)(2,1)S(1)} collective-permute-done((bf16[256,1024]{1,0:T(8,128)(2,1)S(1)}, bf16[256,1024]{1,0:T(8,128)(2,1)S(1)}, u32[]{:S(2)}, u32[]{:S(2)}) %collective-permute-start.27) | collective-permute-done | bytes 524320 | tf_op jit(solution)/shard_map/ppermute | solution.py:175
  105.8 0.2 add_convert_fusion.1
  106.0 1.1 collective-permute-start.28
  107.1 0.3 collective-permute-done.7
  107.5 0.1 collective-permute-start.8
  107.6 1.5 collective-permute-done.8.other.refs_1_
  109.1 1.8 %tails.1 = (bf16[16,1024]{1,0:T(8,128)(2,1)S(1)}, bf16[16,1024]{1,0:T(8,128)(2,1)S(1)}, bf16[16,1024]{1,0:T(8,128)(2,1)S(1)}, bf16[16,1024]{1,0:T(8,128)(2,1)S(1)}) custom-call(s32[4]{0:T(128)S(1)} %get-tuple-element.30.scal, bf16[256,512]{1,0:T(8,128)(2,1)S(1)} %add_convert_fusion.8.own.refs_0_, bf16[256,512]{1,0:T(8,128)(2,1)S(1)} %collective-permute-done.8.other.refs_1_, ...), custom_call_target="tpu_custom_call" | custom-call | tf_op jit(solution)/shard_map/tails/pallas_call | solution.py:412
  111.0 1.8 %collective-permute-start.30 = (bf16[16,1024]{1,0:T(8,128)(2,1)S(1)}, bf16[16,1024]{1,0:T(8,128)(2,1)S(1)}, u32[]{:S(2)}, u32[]{:S(2)}) collective-permute-start(bf16[16,1024]{1,0:T(8,128)(2,1)S(1)} %get-tuple-element.52), channel_id=1, source_target_pairs={{0,4},{4,0},{8,12},{12,8},{1,5},{5,1},{9,13},{13,9},{2,6},{6,2},{1... | collective-permute-start | bytes 98312 | tf_op jit(solution)/shard_map/ppermute | solution.py:175
  112.8 1.4 collective-permute-start.31
  114.1 1.3 collective-permute-start.32
  115.5 11.1 %collective-permute-done.30.refs_4_ = bf16[16,1024]{1,0:T(8,128)(2,1)S(1)} collective-permute-done((bf16[16,1024]{1,0:T(8,128)(2,1)S(1)}, bf16[16,1024]{1,0:T(8,128)(2,1)S(1)}, u32[]{:S(2)}, u32[]{:S(2)}) %collective-permute-start.30) | collective-permute-done | bytes 32800 | tf_op jit(solution)/shard_map/ppermute | solution.py:175
  126.5 2.5 %collective-permute-start.26 = (bf16[64,1024]{1,0:T(8,128)(2,1)S(1)}, bf16[64,1024]{1,0:T(8,128)(2,1)S(1)}, u32[]{:S(2)}, u32[]{:S(2)}) collective-permute-start(bf16[64,1024]{1,0:T(8,128)(2,1)S(1)} %get-tuple-element.46), channel_id=1, source_target_pairs={{0,12},{4,8},{8,4},{12,0},{1,13},{5,9},{9,5},{13,1},{2,14},{6,10},... | collective-permute-start | bytes 393224 | tf_op jit(solution)/shard_map/ppermute | solution.py:175
  129.0 8.9 %collective-permute-done.31.refs_5_ = bf16[16,1024]{1,0:T(8,128)(2,1)S(1)} collective-permute-done((bf16[16,1024]{1,0:T(8,128)(2,1)S(1)}, bf16[16,1024]{1,0:T(8,128)(2,1)S(1)}, u32[]{:S(2)}, u32[]{:S(2)}) %collective-permute-start.31) | collective-permute-done | bytes 32800 | tf_op jit(solution)/shard_map/ppermute | solution.py:175
  138.0 3.1 %collective-permute-start.21 = (bf16[64,1024]{1,0:T(8,128)(2,1)S(1)}, bf16[64,1024]{1,0:T(8,128)(2,1)S(1)}, u32[]{:S(2)}, u32[]{:S(2)}) collective-permute-start(bf16[64,1024]{1,0:T(8,128)(2,1)S(1)} %get-tuple-element.42), channel_id=1, source_target_pairs={{0,8},{4,12},{8,0},{12,4},{1,9},{5,13},{9,1},{13,5},{2,10},{6,14},... | collective-permute-start | bytes 393224 | tf_op jit(solution)/shard_map/ppermute | solution.py:175
  141.0 1.3 project.4
  142.4 4.9 %recur.1 = (f32[256,1024]{1,0:T(8,128)S(1)}, f32[256,1024]{1,0:T(8,128)S(1)}, f32[8,1024]{1,0:T(8,128)S(1)}) custom-call(s32[4]{0:T(128)S(1)} %get-tuple-element.30.scal, bf16[256,1024]{1,0:T(8,128)(2,1)S(1)} %get-tuple-element.47.refs_0_, bf16[256,1024]{1,0:T(8,128)(2,1)S(1)} %collective-permute-done.28.refs_1_, ...), custom_call_target="tpu_custom_call" | custom-call | tf_op jit(solution)/shard_map/recur/pallas_call | solution.py:517
  147.4 1.9 %collective-permute-start.34 = (f32[8,1024]{1,0:T(8,128)S(1)}, f32[8,1024]{1,0:T(8,128)S(1)}, u32[]{:S(2)}, u32[]{:S(2)}) collective-permute-start(f32[8,1024]{1,0:T(8,128)S(1)} %get-tuple-element.57), channel_id=1, source_target_pairs={{0,8},{4,12},{8,0},{12,4},{1,9},{5,13},{9,1},{13,5},{2,10},{6,14},... | collective-permute-start | bytes 98312 | tf_op jit(solution)/shard_map/ppermute | solution.py:170
  149.3 1.4 join.1
  150.6 2.4 %collective-permute-done.33 = f32[8,1024]{1,0:T(8,128)S(1)} collective-permute-done((f32[8,1024]{1,0:T(8,128)S(1)}, f32[8,1024]{1,0:T(8,128)S(1)}, u32[]{:S(2)}, u32[]{:S(2)}) %collective-permute-start.33) | collective-permute-done | bytes 32800 | tf_op jit(solution)/shard_map/ppermute | solution.py:170
  153.1 1.0 add_convert_fusion
  (58 shorter events, 0.6 us)
Async XLA Ops:
  0.6 30.2 %copy-start.1 = (bf16[1024,1024]{1,0:T(8,128)(2,1)S(1)}, bf16[1024,1024]{1,0:T(8,128)(2,1)}, u32[]{:S(2)}) copy-start(bf16[1024,1024]{1,0:T(8,128)(2,1)} %refs_3_.7) | copy-start | bytes 6291460
  0.6 6.6 %collective-permute-start = (bf16[64,512]{1,0:T(8,128)(2,1)}, bf16[64,512]{1,0:T(8,128)(2,1)S(1)}, u32[]{:S(2)}, u32[]{:S(2)}) collective-permute-start(bf16[64,512]{1,0:T(8,128)(2,1)} %param.14), channel_id=1, source_target_pairs={{0,4},{4,0},{8,12},{12,8},{1,5},{5,1},{9,13},{13,9},{2,6},{6,2},{1... | collective-permute-start | bytes 196616 | tf_op jit(solution)/shard_map/ppermute | solution.py:175
  3.8 7.5 %collective-permute-start.1 = (bf16[64,512]{1,0:T(8,128)(2,1)}, bf16[64,512]{1,0:T(8,128)(2,1)S(1)}, u32[]{:S(2)}, u32[]{:S(2)}) collective-permute-start(bf16[64,512]{1,0:T(8,128)(2,1)} %param.14), channel_id=1, source_target_pairs={{0,8},{4,12},{8,0},{12,4},{1,9},{5,13},{9,1},{13,5},{2,10},{6,14},... | collective-permute-start | bytes 196616 | tf_op jit(solution)/shard_map/ppermute | solution.py:175
  6.3 6.3 %collective-permute-start.2 = (bf16[64,512]{1,0:T(8,128)(2,1)}, bf16[64,512]{1,0:T(8,128)(2,1)S(1)}, u32[]{:S(2)}, u32[]{:S(2)}) collective-permute-start(bf16[64,512]{1,0:T(8,128)(2,1)} %param.14), channel_id=1, source_target_pairs={{0,12},{4,8},{8,4},{12,0},{1,13},{5,9},{9,5},{13,1},{2,14},{6,10},... | collective-permute-start | bytes 196616 | tf_op jit(solution)/shard_map/ppermute | solution.py:175
  12.7 6.4 %collective-permute-start.4 = (bf16[256,512]{1,0:T(8,128)(2,1)S(1)}, bf16[256,512]{1,0:T(8,128)(2,1)S(1)}, u32[]{:S(2)}, u32[]{:S(2)}) collective-permute-start(bf16[256,512]{1,0:T(8,128)(2,1)S(1)} %constant_dynamic-update-slice_fusion.refs_0_), channel_id=1, source_target_pairs={{0,2},{1,3},{2,0},{3,1},{4,6},{5,7},{6,4},{7,5},{8,10},{9,11},{10,... | collective-permute-start | bytes 786440 | tf_op jit(solution)/shard_map/ppermute | solution.py:175
  14.1 16.7 %collective-permute-start.15 = (bf16[256,1024]{1,0:T(8,128)(2,1)}, bf16[256,1024]{1,0:T(8,128)(2,1)S(1)}, u32[]{:S(2)}, u32[]{:S(2)}) collective-permute-start(bf16[256,1024]{1,0:T(8,128)(2,1)} %refs_0_.1), channel_id=1, source_target_pairs={{0,12},{4,8},{8,4},{12,0},{1,13},{5,9},{9,5},{13,1},{2,14},{6,10},... | collective-permute-start | bytes 1572872 | tf_op jit(solution)/shard_map/ppermute | solution.py:175
  16.0 7.4 %collective-permute-start.3 = (bf16[256,512]{1,0:T(8,128)(2,1)S(1)}, bf16[256,512]{1,0:T(8,128)(2,1)S(1)}, u32[]{:S(2)}, u32[]{:S(2)}) collective-permute-start(bf16[256,512]{1,0:T(8,128)(2,1)S(1)} %constant_dynamic-update-slice_fusion.refs_0_), channel_id=1, source_target_pairs={{0,1},{1,0},{2,3},{3,2},{4,5},{5,4},{6,7},{7,6},{8,9},{9,8},{10,11... | collective-permute-start | bytes 786440 | tf_op jit(solution)/shard_map/ppermute | solution.py:175
  19.1 4.3 %collective-permute-start.5 = (bf16[256,512]{1,0:T(8,128)(2,1)S(1)}, bf16[256,512]{1,0:T(8,128)(2,1)S(1)}, u32[]{:S(2)}, u32[]{:S(2)}) collective-permute-start(bf16[256,512]{1,0:T(8,128)(2,1)S(1)} %collective-permute-done.4.refs_2_), channel_id=1, source_target_pairs={{0,1},{1,0},{2,3},{3,2},{4,5},{5,4},{6,7},{7,6},{8,9},{9,8},{10,11... | collective-permute-start | bytes 786440 | tf_op jit(solution)/shard_map/ppermute | solution.py:175
  19.1 1.0 copy-start.2
  20.1 0.7 copy-start.8
  21.5 9.3 %collective-permute-start.22 = (bf16[64,1024]{1,0:T(8,128)(2,1)S(1)}, bf16[64,1024]{1,0:T(8,128)(2,1)S(1)}, u32[]{:S(2)}, u32[]{:S(2)}) collective-permute-start(bf16[64,1024]{1,0:T(8,128)(2,1)S(1)} %get-tuple-element.43), channel_id=1, source_target_pairs={{0,12},{4,8},{8,4},{12,0},{1,13},{5,9},{9,5},{13,1},{2,14},{6,10},... | collective-permute-start | bytes 393224 | tf_op jit(solution)/shard_map/ppermute | solution.py:175
  24.0 10.1 %copy-start.3 = (bf16[256,1024]{1,0:T(8,128)(2,1)S(1)}, bf16[256,1024]{1,0:T(8,128)(2,1)}, u32[]{:S(2)}) copy-start(bf16[256,1024]{1,0:T(8,128)(2,1)} %refs_0_.1) | copy-start | bytes 1572868
  34.1 13.3 %collective-permute-start.23 = (bf16[256,512]{1,0:T(8,128)(2,1)S(1)}, bf16[256,512]{1,0:T(8,128)(2,1)S(1)}, u32[]{:S(2)}, u32[]{:S(2)}) collective-permute-start(bf16[256,512]{1,0:T(8,128)(2,1)S(1)} %get-tuple-element.45), channel_id=1, source_target_pairs={{0,1},{1,0},{2,3},{3,2},{4,5},{5,4},{6,7},{7,6},{8,9},{9,8},{10,11... | collective-permute-start | bytes 786440 | tf_op jit(solution)/shard_map/ppermute | solution.py:175
  34.2 42.5 %collective-permute-start.9 = (bf16[256,1024]{1,0:T(8,128)(2,1)S(1)}, bf16[256,1024]{1,0:T(8,128)(2,1)S(1)}, u32[]{:S(2)}, u32[]{:S(2)}) collective-permute-start(bf16[256,1024]{1,0:T(8,128)(2,1)S(1)} %copy-done.3), channel_id=1, source_target_pairs={{0,4},{4,0},{8,12},{12,8},{1,5},{5,1},{9,13},{13,9},{2,6},{6,2},{1... | collective-permute-start | bytes 1572872 | tf_op jit(solution)/shard_map/ppermute | solution.py:175
  47.3 32.7 %collective-permute-start.16 = (bf16[256,1024]{1,0:T(8,128)(2,1)S(1)}, bf16[256,1024]{1,0:T(8,128)(2,1)S(1)}, u32[]{:S(2)}, u32[]{:S(2)}) collective-permute-start(bf16[256,1024]{1,0:T(8,128)(2,1)S(1)} %collective-permute-done.15.refs_0_), channel_id=1, source_target_pairs={{0,4},{4,0},{8,12},{12,8},{1,5},{5,1},{9,13},{13,9},{2,6},{6,2},{1... | collective-permute-start | bytes 1572872 | tf_op jit(solution)/shard_map/ppermute | solution.py:175
  47.4 36.4 %collective-permute-start.24 = (bf16[256,512]{1,0:T(8,128)(2,1)S(1)}, bf16[256,512]{1,0:T(8,128)(2,1)S(1)}, u32[]{:S(2)}, u32[]{:S(2)}) collective-permute-start(bf16[256,512]{1,0:T(8,128)(2,1)S(1)} %add_convert_fusion.3), channel_id=1, source_target_pairs={{0,2},{1,3},{2,0},{3,1},{4,6},{5,7},{6,4},{7,5},{8,10},{9,11},{10,... | collective-permute-start | bytes 786440 | tf_op jit(solution)/shard_map/ppermute | solution.py:175
  48.0 28.6 %collective-permute-start.10 = (bf16[64,1024]{1,0:T(8,128)(2,1)S(1)}, bf16[64,1024]{1,0:T(8,128)(2,1)S(1)}, u32[]{:S(2)}, u32[]{:S(2)}) collective-permute-start(bf16[64,1024]{1,0:T(8,128)(2,1)S(1)} %get-tuple-element.35), channel_id=1, source_target_pairs={{0,4},{4,0},{8,12},{12,8},{1,5},{5,1},{9,13},{13,9},{2,6},{6,2},{1... | collective-permute-start | bytes 393224 | tf_op jit(solution)/shard_map/ppermute | solution.py:175
  50.0 30.0 %collective-permute-start.17 = (bf16[64,1024]{1,0:T(8,128)(2,1)S(1)}, bf16[64,1024]{1,0:T(8,128)(2,1)S(1)}, u32[]{:S(2)}, u32[]{:S(2)}) collective-permute-start(bf16[64,1024]{1,0:T(8,128)(2,1)S(1)} %get-tuple-element.39), channel_id=1, source_target_pairs={{0,8},{4,12},{8,0},{12,4},{1,9},{5,13},{9,1},{13,5},{2,10},{6,14},... | collective-permute-start | bytes 393224 | tf_op jit(solution)/shard_map/ppermute | solution.py:175
  79.9 4.1 %collective-permute-start.11 = (bf16[256,512]{1,0:T(8,128)(2,1)S(1)}, bf16[256,512]{1,0:T(8,128)(2,1)S(1)}, u32[]{:S(2)}, u32[]{:S(2)}) collective-permute-start(bf16[256,512]{1,0:T(8,128)(2,1)S(1)} %get-tuple-element.37), channel_id=1, source_target_pairs={{0,1},{1,0},{2,3},{3,2},{4,5},{5,4},{6,7},{7,6},{8,9},{9,8},{10,11... | collective-permute-start | bytes 786440 | tf_op jit(solution)/shard_map/ppermute | solution.py:175
  83.2 1.7 %collective-permute-start.18 = (bf16[256,512]{1,0:T(8,128)(2,1)S(1)}, bf16[256,512]{1,0:T(8,128)(2,1)S(1)}, u32[]{:S(2)}, u32[]{:S(2)}) collective-permute-start(bf16[256,512]{1,0:T(8,128)(2,1)S(1)} %get-tuple-element.41), channel_id=1, source_target_pairs={{0,1},{1,0},{2,3},{3,2},{4,5},{5,4},{6,7},{7,6},{8,9},{9,8},{10,11... | collective-permute-start | bytes 786440 | tf_op jit(solution)/shard_map/ppermute | solution.py:175
  83.9 5.7 %collective-permute-start.25 = (bf16[256,512]{1,0:T(8,128)(2,1)S(1)}, bf16[256,512]{1,0:T(8,128)(2,1)S(1)}, u32[]{:S(2)}, u32[]{:S(2)}) collective-permute-start(bf16[256,512]{1,0:T(8,128)(2,1)S(1)} %add_convert_fusion.2.own.refs_2_), channel_id=1, source_target_pairs={{0,1},{1,0},{2,3},{3,2},{4,5},{5,4},{6,7},{7,6},{8,9},{9,8},{10,11... | collective-permute-start | bytes 786440 | tf_op jit(solution)/shard_map/ppermute | solution.py:175
  84.0 9.2 %collective-permute-start.12 = (bf16[256,512]{1,0:T(8,128)(2,1)S(1)}, bf16[256,512]{1,0:T(8,128)(2,1)S(1)}, u32[]{:S(2)}, u32[]{:S(2)}) collective-permute-start(bf16[256,512]{1,0:T(8,128)(2,1)S(1)} %add_convert_fusion.7), channel_id=1, source_target_pairs={{0,2},{1,3},{2,0},{3,1},{4,6},{5,7},{6,4},{7,5},{8,10},{9,11},{10,... | collective-permute-start | bytes 786440 | tf_op jit(solution)/shard_map/ppermute | solution.py:175
  85.0 4.6 %copy-start = (bf16[1024,1024]{1,0:T(8,128)(2,1)S(1)}, bf16[1024,1024]{1,0:T(8,128)(2,1)}, u32[]{:S(2)}) copy-start(bf16[1024,1024]{1,0:T(8,128)(2,1)} %refs_9_.2) | copy-start | bytes 6291460
  85.0 4.6 %copy-start.6 = (f32[4096]{0:T(1024)S(1)}, f32[4096]{0:T(1024)}, u32[]{:S(2)}) copy-start(f32[4096]{0:T(1024)} %param.25) | copy-start | bytes 49156
  85.1 13.4 %collective-permute-start.19 = (bf16[256,512]{1,0:T(8,128)(2,1)S(1)}, bf16[256,512]{1,0:T(8,128)(2,1)S(1)}, u32[]{:S(2)}, u32[]{:S(2)}) collective-permute-start(bf16[256,512]{1,0:T(8,128)(2,1)S(1)} %add_convert_fusion.5), channel_id=1, source_target_pairs={{0,2},{1,3},{2,0},{3,1},{4,6},{5,7},{6,4},{7,5},{8,10},{9,11},{10,... | collective-permute-start | bytes 786440 | tf_op jit(solution)/shard_map/ppermute | solution.py:175
  89.5 9.0 %collective-permute-start.6 = (bf16[256,512]{1,0:T(8,128)(2,1)S(1)}, bf16[256,512]{1,0:T(8,128)(2,1)S(1)}, u32[]{:S(2)}, u32[]{:S(2)}) collective-permute-start(bf16[256,512]{1,0:T(8,128)(2,1)S(1)} %get-tuple-element.33), channel_id=1, source_target_pairs={{0,1},{1,0},{2,3},{3,2},{4,5},{5,4},{6,7},{7,6},{8,9},{9,8},{10,11... | collective-permute-start | bytes 786440 | tf_op jit(solution)/shard_map/ppermute | solution.py:175
  90.9 14.9 %collective-permute-start.27 = (bf16[256,1024]{1,0:T(8,128)(2,1)S(1)}, bf16[256,1024]{1,0:T(8,128)(2,1)S(1)}, u32[]{:S(2)}, u32[]{:S(2)}) collective-permute-start(bf16[256,1024]{1,0:T(8,128)(2,1)S(1)} %get-tuple-element.49), channel_id=1, source_target_pairs={{0,4},{4,0},{8,12},{12,8},{1,5},{5,1},{9,13},{13,9},{2,6},{6,2},{1... | collective-permute-start | bytes 1572872 | tf_op jit(solution)/shard_map/ppermute | solution.py:175
  93.5 5.7 %collective-permute-start.13 = (bf16[256,512]{1,0:T(8,128)(2,1)S(1)}, bf16[256,512]{1,0:T(8,128)(2,1)S(1)}, u32[]{:S(2)}, u32[]{:S(2)}) collective-permute-start(bf16[256,512]{1,0:T(8,128)(2,1)S(1)} %add_convert_fusion.6.own.refs_4_), channel_id=1, source_target_pairs={{0,1},{1,0},{2,3},{3,2},{4,5},{5,4},{6,7},{7,6},{8,9},{9,8},{10,11... | collective-permute-start | bytes 786440 | tf_op jit(solution)/shard_map/ppermute | solution.py:175
  98.5 2.1 %collective-permute-start.20 = (bf16[256,512]{1,0:T(8,128)(2,1)S(1)}, bf16[256,512]{1,0:T(8,128)(2,1)S(1)}, u32[]{:S(2)}, u32[]{:S(2)}) collective-permute-start(bf16[256,512]{1,0:T(8,128)(2,1)S(1)} %add_convert_fusion.4.own.refs_6_), channel_id=1, source_target_pairs={{0,1},{1,0},{2,3},{3,2},{4,5},{5,4},{6,7},{7,6},{8,9},{9,8},{10,11... | collective-permute-start | bytes 786440 | tf_op jit(solution)/shard_map/ppermute | solution.py:175
  98.6 8.8 %collective-permute-start.7 = (bf16[256,512]{1,0:T(8,128)(2,1)S(1)}, bf16[256,512]{1,0:T(8,128)(2,1)S(1)}, u32[]{:S(2)}, u32[]{:S(2)}) collective-permute-start(bf16[256,512]{1,0:T(8,128)(2,1)S(1)} %add_convert_fusion.9), channel_id=1, source_target_pairs={{0,2},{1,3},{2,0},{3,1},{4,6},{5,7},{6,4},{7,5},{8,10},{9,11},{10,... | collective-permute-start | bytes 786440 | tf_op jit(solution)/shard_map/ppermute | solution.py:175
  100.5 41.8 %collective-permute-start.29 = (bf16[256,1024]{1,0:T(8,128)(2,1)S(1)}, bf16[256,1024]{1,0:T(8,128)(2,1)S(1)}, u32[]{:S(2)}, u32[]{:S(2)}) collective-permute-start(bf16[256,1024]{1,0:T(8,128)(2,1)S(1)} %get-tuple-element.50), channel_id=1, source_target_pairs={{0,4},{4,0},{8,12},{12,8},{1,5},{5,1},{9,13},{13,9},{2,6},{6,2},{1... | collective-permute-start | bytes 1572872 | tf_op jit(solution)/shard_map/ppermute | solution.py:175
  106.0 36.3 %collective-permute-start.28 = (bf16[256,1024]{1,0:T(8,128)(2,1)S(1)}, bf16[256,1024]{1,0:T(8,128)(2,1)S(1)}, u32[]{:S(2)}, u32[]{:S(2)}) collective-permute-start(bf16[256,1024]{1,0:T(8,128)(2,1)S(1)} %add_convert_fusion.1), channel_id=1, source_target_pairs={{0,8},{4,12},{8,0},{12,4},{1,9},{5,13},{9,1},{13,5},{2,10},{6,14},... | collective-permute-start | bytes 1572872 | tf_op jit(solution)/shard_map/ppermute | solution.py:175
  107.5 1.6 %collective-permute-start.8 = (bf16[256,512]{1,0:T(8,128)(2,1)S(1)}, bf16[256,512]{1,0:T(8,128)(2,1)S(1)}, u32[]{:S(2)}, u32[]{:S(2)}) collective-permute-start(bf16[256,512]{1,0:T(8,128)(2,1)S(1)} %add_convert_fusion.8.own.refs_0_), channel_id=1, source_target_pairs={{0,1},{1,0},{2,3},{3,2},{4,5},{5,4},{6,7},{7,6},{8,9},{9,8},{10,11... | collective-permute-start | bytes 786440 | tf_op jit(solution)/shard_map/ppermute | solution.py:175
  110.9 31.4 %copy-start.4 = (bf16[4,256,256]{2,1,0:T(8,128)(2,1)S(1)}, bf16[4,256,256]{2,1,0:T(8,128)(2,1)}, u32[]{:S(2)}) copy-start(bf16[4,256,256]{2,1,0:T(8,128)(2,1)} %refs_8_.1) | copy-start | bytes 1572868
  110.9 31.4 %copy-start.5 = (bf16[4,256,256]{2,1,0:T(8,128)(2,1)S(1)}, bf16[4,256,256]{2,1,0:T(8,128)(2,1)}, u32[]{:S(2)}) copy-start(bf16[4,256,256]{2,1,0:T(8,128)(2,1)} %refs_9_.3) | copy-start | bytes 1572868
  111.0 31.4 %copy-start.7 = (f32[4,1024]{1,0:T(4,128)S(1)}, f32[4,1024]{1,0:T(4,128)}, u32[]{:S(2)}) copy-start(f32[4,1024]{1,0:T(4,128)} %refs_7_.1) | copy-start | bytes 49156
  111.0 31.4 %copy-start.9 = (f32[1024]{0:T(1024)S(1)}, f32[1024]{0:T(1024)}, u32[]{:S(2)}) copy-start(f32[1024]{0:T(1024)} %param.22) | copy-start | bytes 12292
  111.0 31.4 %copy-start.10 = (f32[1024]{0:T(1024)S(1)}, f32[1024]{0:T(1024)}, u32[]{:S(2)}) copy-start(f32[1024]{0:T(1024)} %param.23) | copy-start | bytes 12292
  111.0 31.4 %copy-start.11 = (s32[1024]{0:T(1024)S(1)}, s32[1024]{0:T(1024)}, u32[]{:S(2)}) copy-start(s32[1024]{0:T(1024)} %param.24) | copy-start | bytes 12292
  111.0 15.5 %collective-permute-start.30 = (bf16[16,1024]{1,0:T(8,128)(2,1)S(1)}, bf16[16,1024]{1,0:T(8,128)(2,1)S(1)}, u32[]{:S(2)}, u32[]{:S(2)}) collective-permute-start(bf16[16,1024]{1,0:T(8,128)(2,1)S(1)} %get-tuple-element.52), channel_id=1, source_target_pairs={{0,4},{4,0},{8,12},{12,8},{1,5},{5,1},{9,13},{13,9},{2,6},{6,2},{1... | collective-permute-start | bytes 98312 | tf_op jit(solution)/shard_map/ppermute | solution.py:175
  112.8 25.2 %collective-permute-start.31 = (bf16[16,1024]{1,0:T(8,128)(2,1)S(1)}, bf16[16,1024]{1,0:T(8,128)(2,1)S(1)}, u32[]{:S(2)}, u32[]{:S(2)}) collective-permute-start(bf16[16,1024]{1,0:T(8,128)(2,1)S(1)} %get-tuple-element.53), channel_id=1, source_target_pairs={{0,8},{4,12},{8,0},{12,4},{1,9},{5,13},{9,1},{13,5},{2,10},{6,14},... | collective-permute-start | bytes 98312 | tf_op jit(solution)/shard_map/ppermute | solution.py:175
  114.1 23.8 %collective-permute-start.32 = (bf16[16,1024]{1,0:T(8,128)(2,1)S(1)}, bf16[16,1024]{1,0:T(8,128)(2,1)S(1)}, u32[]{:S(2)}, u32[]{:S(2)}) collective-permute-start(bf16[16,1024]{1,0:T(8,128)(2,1)S(1)} %get-tuple-element.54), channel_id=1, source_target_pairs={{0,12},{4,8},{8,4},{12,0},{1,13},{5,9},{9,5},{13,1},{2,14},{6,10},... | collective-permute-start | bytes 98312 | tf_op jit(solution)/shard_map/ppermute | solution.py:175
  126.5 22.7 %collective-permute-start.26 = (bf16[64,1024]{1,0:T(8,128)(2,1)S(1)}, bf16[64,1024]{1,0:T(8,128)(2,1)S(1)}, u32[]{:S(2)}, u32[]{:S(2)}) collective-permute-start(bf16[64,1024]{1,0:T(8,128)(2,1)S(1)} %get-tuple-element.46), channel_id=1, source_target_pairs={{0,12},{4,8},{8,4},{12,0},{1,13},{5,9},{9,5},{13,1},{2,14},{6,10},... | collective-permute-start | bytes 393224 | tf_op jit(solution)/shard_map/ppermute | solution.py:175
  138.0 11.3 %collective-permute-start.14 = (bf16[64,1024]{1,0:T(8,128)(2,1)S(1)}, bf16[64,1024]{1,0:T(8,128)(2,1)S(1)}, u32[]{:S(2)}, u32[]{:S(2)}) collective-permute-start(bf16[64,1024]{1,0:T(8,128)(2,1)S(1)} %get-tuple-element.38), channel_id=1, source_target_pairs={{0,4},{4,0},{8,12},{12,8},{1,5},{5,1},{9,13},{13,9},{2,6},{6,2},{1... | collective-permute-start | bytes 393224 | tf_op jit(solution)/shard_map/ppermute | solution.py:175
  138.0 11.3 %collective-permute-start.21 = (bf16[64,1024]{1,0:T(8,128)(2,1)S(1)}, bf16[64,1024]{1,0:T(8,128)(2,1)S(1)}, u32[]{:S(2)}, u32[]{:S(2)}) collective-permute-start(bf16[64,1024]{1,0:T(8,128)(2,1)S(1)} %get-tuple-element.42), channel_id=1, source_target_pairs={{0,8},{4,12},{8,0},{12,4},{1,9},{5,13},{9,1},{13,5},{2,10},{6,14},... | collective-permute-start | bytes 393224 | tf_op jit(solution)/shard_map/ppermute | solution.py:175
  147.3 5.8 %collective-permute-start.33 = (f32[8,1024]{1,0:T(8,128)S(1)}, f32[8,1024]{1,0:T(8,128)S(1)}, u32[]{:S(2)}, u32[]{:S(2)}) collective-permute-start(f32[8,1024]{1,0:T(8,128)S(1)} %get-tuple-element.57), channel_id=1, source_target_pairs={{0,4},{4,8},{8,12},{12,0},{1,5},{5,9},{9,13},{13,1},{2,6},{6,10},{... | collective-permute-start | bytes 98312 | tf_op jit(solution)/shard_map/ppermute | solution.py:170
  147.4 5.7 %collective-permute-start.34 = (f32[8,1024]{1,0:T(8,128)S(1)}, f32[8,1024]{1,0:T(8,128)S(1)}, u32[]{:S(2)}, u32[]{:S(2)}) collective-permute-start(f32[8,1024]{1,0:T(8,128)S(1)} %get-tuple-element.57), channel_id=1, source_target_pairs={{0,8},{4,12},{8,0},{12,4},{1,9},{5,13},{9,1},{13,5},{2,10},{6,14},... | collective-permute-start | bytes 98312 | tf_op jit(solution)/shard_map/ppermute | solution.py:170

commit v7 on v6

--- a/solution.py
+++ b/solution.py
@@ -430,7 +430,7 @@
     return jnp.where(x > -0.3, -x * series, 1.0 - jnp.exp(x))
 
 
-def recur_kernel(count, nlines, features, scal, *refs):
+def recur_kernel(count, nlines, features, first, scal, *refs):
     mains, lines = refs[:count], refs[count : count + nlines]
     conv_w, decay_w, input_w, decay_b, input_b, codes = refs[count + nlines : count + nlines + 6]
     local_ref, cum_ref, last_ref, ext, keep_s, state_s, factor_s = refs[count + nlines + 6 :]
@@ -447,7 +447,7 @@
         factor = lax.rsqrt(sums * (1.0 / features) + 1e-06)
         factor_s[...] = jnp.transpose(jnp.broadcast_to(factor, (LANES, rows + LANES)))
 
-    lanes = pl.ds(pl.multiple_of(pl.program_id(0) * width, width), width)
+    lanes = pl.ds(pl.multiple_of((first + pl.program_id(0)) * width, width), width)
     main = tail = None
     for piece in mains:
         term = piece[...].astype(F32)
@@ -506,22 +506,29 @@
     last_ref[...] = jnp.where(line == 0, run_keep, run_state)
 
 
-def recur(scal, mains, lines, conv_w, decay_w, input_w, decay_b, input_b, codes, rows, features):
+def recur(scal, mains, lines, conv_w, decay_w, input_w, decay_b, input_b, codes, features, first, count):
     channels = conv_w.shape[1]
+    rows = mains[0].shape[0]
     tiles = rows // SUB
+    main_specs = [
+        pl.BlockSpec(
+            (rows, BW), functools.partial(lambda at, j: (0, at + j), first if m.shape[1] == channels else 0)
+        )
+        for m in mains
+    ]
     by_block = pl.BlockSpec((rows, BW), lambda j: (0, j))
-    row_spec = pl.BlockSpec((1, BW), lambda j: (0, j))
-    gate_spec = pl.BlockSpec((1, BW, BW), lambda j: (j, 0, 0))
+    row_spec = pl.BlockSpec((1, BW), lambda j: (0, first + j))
+    gate_spec = pl.BlockSpec((1, BW, BW), lambda j: (first + j, 0, 0))
     line_spec = pl.BlockSpec((TILE, channels), lambda j: (0, 0))
-    full = jax.ShapeDtypeStruct((rows, channels), F32)
+    full = jax.ShapeDtypeStruct((rows, count * BW), F32)
     return pl.pallas_call(
-        functools.partial(recur_kernel, len(mains), len(lines), features),
-        grid=(channels // BW,),
-        out_shape=(full, full, jax.ShapeDtypeStruct((SUB, channels), F32)),
+        functools.partial(recur_kernel, len(mains), len(lines), features, first),
+        grid=(count,),
+        out_shape=(full, full, jax.ShapeDtypeStruct((SUB, count * BW), F32)),
         in_specs=[SMEM]
-        + [by_block] * len(mains)
+        + main_specs
         + [line_spec] * len(lines)
-        + [pl.BlockSpec((CONV, BW), lambda j: (0, j)), gate_spec, gate_spec]
+        + [pl.BlockSpec((CONV, BW), lambda j: (0, first + j)), gate_spec, gate_spec]
         + [row_spec] * 3,
         out_specs=(by_block, by_block, pl.BlockSpec((SUB, BW), lambda j: (0, j))),
         scratch_shapes=[
@@ -533,6 +540,33 @@
         name="recur",
         compiler_params=pltpu.CompilerParams(vmem_limit_bytes=GRANT),
     )(scal, *mains, *lines, conv_w, decay_w, input_w, decay_b, input_b, codes)
+
+
+def finish_kernel(parts, scal, *refs):
+    states, cums, before, out = refs[:parts], refs[parts : 2 * parts], refs[2 * parts : -1], refs[-1]
+    incoming = jnp.zeros((1, out.shape[1]), F32)
+    for step in range(len(before), 0, -1):
+        piece = before[step - 1]
+        incoming = piece[0:1, :] * incoming + piece[1:2, :]
+        incoming = jnp.where(scal[0] >= step, incoming, 0.0)
+    first = 0
+    for state, cum in zip(states, cums):
+        stop = first + state.shape[1]
+        out[:, first:stop] = (state[...] + cum[...] * incoming[:, first:stop]).astype(BF16)
+        first = stop
+
+
+def finish(scal, states, cums, before):
+    rows = states[0].shape[0]
+    channels = before[0].shape[1]
+    return pl.pallas_call(
+        functools.partial(finish_kernel, len(states)),
+        out_shape=jax.ShapeDtypeStruct((rows, channels), BF16),
+        in_specs=[SMEM] + [VMEM] * (2 * len(states) + len(before)),
+        out_specs=VMEM,
+        name="finish",
+        compiler_params=pltpu.CompilerParams(vmem_limit_bytes=GRANT),
+    )(scal, *states, *cums, *before)
 
 
 def local_near(
@@ -554,8 +588,8 @@
     shard = keyvals.shape[0]
     tokens = segment_ids.shape[0]
     nctx, nmp = lax.axis_size("ctx"), lax.axis_size("mp")
-    ctx_index = lax.axis_index("ctx")
     features = residual.shape[1]
+    cols = out_weight.shape[1]
     longest = tokens // 2
     back = -(-(min(WIN, longest) - 1) // rows)
     reach = min(nctx - 1, -(-longest // rows))
@@ -598,42 +632,57 @@
         places[e] = (at, 0)
         messages[e], give[e] = project(scal, mine, other, gain, lru_weight, 1, shard)
     lines = list(tails(scal, halves, [places[e] for e in range(nctx)], gain, lru_weight, rows))
-    mains = [messages[0]]
+    blocks = lru_weight.shape[1] // BW
+    parts = 2 if blocks % 2 == 0 else 1
+    span = lru_weight.shape[1] // parts
+    mains = [[messages[0]] for _ in range(parts)]
     for flip in range(nctx - 1, 0, -1):
         if flip % 2 and flip > 1:
             passed = swapped(messages[flip], "ctx", 1)
-            both = messages[flip - 1].astype(F32) + passed.astype(F32)
-            messages[flip - 1] = both.astype(BF16)
+            merged = []
+            for part in range(parts):
+                cols = slice(part * span, (part + 1) * span)
+                both = messages[flip - 1][:, cols].astype(F32) + passed[:, cols].astype(F32)
+                merged.append(both.astype(BF16))
+            messages[flip - 1] = merged
+        elif flip > 1:
+            for part in range(parts):
+                mains[part].append(swapped(messages[flip][part], "ctx", flip))
         else:
-            mains.append(swapped(messages[flip], "ctx", flip))
+            got = swapped(messages[1], "ctx", 1)
+            for main in mains:
+                main.append(got)
     for flip in range(1, nctx):
         lines[flip] = swapped(lines[flip], "ctx", flip)
     given = [give[0]]
     for flip in range(1, nctx):
         given.append(swapped(give[flip], "ctx", flip))
-    local_state, cum_keep, last = recur(
-        scal,
-        mains,
-        lines,
-        conv_weight,
-        gate_decay_w,
-        gate_input_w,
-        gate_decay_b.reshape(1, -1),
-        gate_input_b.reshape(1, -1),
-        decay_codes.reshape(1, -1),
-        rows,
-        features,
-    )
+    states, cums, lasts = [], [], []
+    for part in range(parts):
+        state, cum, last = recur(
+            scal,
+            mains[part],
+            lines,
+            conv_weight,
+            gate_decay_w,
+            gate_input_w,
+            gate_decay_b.reshape(1, -1),
+            gate_input_b.reshape(1, -1),
+            decay_codes.reshape(1, -1),
+            features,
+            part * blocks // parts,
+            blocks // parts,
+        )
+        states.append(state)
+        cums.append(cum)
+        lasts.append(last)
+    last = jnp.concatenate(lasts, axis=1)
     before = []
     for step in range(1, reach + 1):
         before.append(rotated(last, "ctx", -step))
     resid_out = join(scal, given)
-    incoming = jnp.zeros_like(last[0])
-    for step in range(reach, 0, -1):
-        piece = before[step - 1]
-        incoming = jnp.where(ctx_index >= step, piece[0] * incoming + piece[1], 0.0)
-    states = local_state + cum_keep * incoming[None, :]
-    return (resid_out, states.astype(BF16))
+    out = finish(scal, states, cums, before)
+    return (resid_out, out)
 
 
 def local(queries, keyvals, segment_ids, residual, out_weight, *rest):

time: 154 us -> 149 us (0.968)
  waiting for transfers between devices: 76.4 us -> 64.8 us
  starting transfers between devices: 44.4 us -> 49.6 us
  Pallas kernels: 27.5 us -> 29.8 us
    ppermute x33 -> x34, waiting for transfers between devices: 74 us -> 62.8 us  [swapped(): return lax.ppermute(value, axis, [(s, s ^ flip) for s in range(count)])]
    ppermute x33 -> x34, starting transfers between devices: 42.5 us -> 46.1 us  [swapped(): return lax.ppermute(value, axis, [(s, s ^ flip) for s in range(count)])]
    ppermute x2, starting transfers between devices: 1.94 us -> 3.48 us  [rotated(): lax.ppermute(value, axis, [(s, (s - steps) % count) for s in range(count)])]
    pallas_call x1 -> x2, Pallas kernels: 4.93 us -> 5.6 us  [recur(): pl.pallas_call(functools.partial(recur_kernel, len(mains), len(lines), fe...]
  transfers between devices with their start and end apart: 35 -> 36, of which waited for: 14 -> 13; matrix products, arithmetic and copies ran while one was open for 1% -> 1% of each run, Pallas kernels for 16% -> 19%
where the time goes in v7:
time: 149 us
  waiting for transfers between devices  64.8 us (43%)
  starting transfers between devices  49.6 us (33%)
  Pallas kernels  29.8 us (20%)
  local copies, waits for them, and re-layouts  2.66 us (2%)
    ppermute x34, waiting for transfers between devices, swapped(): return lax.ppermute(value, axis, [(s, s ^ flip) for s in range(count)])  62.8 us
    ppermute x34, starting transfers between devices, swapped(): return lax.ppermute(value, axis, [(s, s ^ flip) for s in range(count)])  46.1 us
    pallas_call x4, Pallas kernels, attend(): pl.pallas_call(functools.partial(attend_kernel, nctx, back, steps, shard)...  13 us
    pallas_call x2, Pallas kernels, recur(): pl.pallas_call(functools.partial(recur_kernel, len(mains), len(lines), fe...  5.6 us
    pallas_call x4, Pallas kernels, project(): pl.pallas_call(functools.partial(project_kernel, count), out_shape=tuple(...  5.23 us
    ppermute x2, starting transfers between devices, rotated(): lax.ppermute(value, axis, [(s, (s - steps) % count) for s in range(count)])  3.48 us
  transfers between devices with their start and end apart: 36, of which 13 were waited for; matrix products, arithmetic and copies ran while one was open for 1% of the time, Pallas kernels for 19%

profile of v7, /device:TPU:0, one launch (start us, length us, event | category | flops | bytes accessed | tf_op | source)
XLA Modules:
  0.0 148.6 jit_solution(8763524338815805452)
XLA Ops:
  0.6 4.1 %collective-permute-start.1 = (bf16[64,512]{1,0:T(8,128)(2,1)}, bf16[64,512]{1,0:T(8,128)(2,1)S(1)}, u32[]{:S(2)}, u32[]{:S(2)}) collective-permute-start(bf16[64,512]{1,0:T(8,128)(2,1)} %param.14), channel_id=1, source_target_pairs={{0,8},{4,12},{8,0},{12,4},{1,9},{5,13},{9,1},{13,5},{2,10},{6,14},... | collective-permute-start | bytes 196616 | tf_op jit(solution)/shard_map/ppermute | solution.py:175
  4.8 1.6 %collective-permute-start = (bf16[64,512]{1,0:T(8,128)(2,1)}, bf16[64,512]{1,0:T(8,128)(2,1)S(1)}, u32[]{:S(2)}, u32[]{:S(2)}) collective-permute-start(bf16[64,512]{1,0:T(8,128)(2,1)} %param.14), channel_id=1, source_target_pairs={{0,4},{4,0},{8,12},{12,8},{1,5},{5,1},{9,13},{13,9},{2,6},{6,2},{1... | collective-permute-start | bytes 196616 | tf_op jit(solution)/shard_map/ppermute | solution.py:175
  6.3 3.8 %collective-permute-start.15 = (bf16[256,1024]{1,0:T(8,128)(2,1)}, bf16[256,1024]{1,0:T(8,128)(2,1)S(1)}, u32[]{:S(2)}, u32[]{:S(2)}) collective-permute-start(bf16[256,1024]{1,0:T(8,128)(2,1)} %refs_0_.1), channel_id=1, source_target_pairs={{0,12},{4,8},{8,4},{12,0},{1,13},{5,9},{9,5},{13,1},{2,14},{6,10},... | collective-permute-start | bytes 1572872 | tf_op jit(solution)/shard_map/ppermute | solution.py:175
  10.2 0.8 constant_dynamic-update-slice_fusion.3
  11.1 2.3 %collective-permute-done.2 = bf16[64,512]{1,0:T(8,128)(2,1)S(1)} collective-permute-done((bf16[64,512]{1,0:T(8,128)(2,1)}, bf16[64,512]{1,0:T(8,128)(2,1)S(1)}, u32[]{:S(2)}, u32[]{:S(2)}) %collective-permute-start.2) | collective-permute-done | bytes 65568 | tf_op jit(solution)/shard_map/ppermute | solution.py:175
  13.4 1.5 %collective-permute-start.4 = (bf16[256,512]{1,0:T(8,128)(2,1)S(1)}, bf16[256,512]{1,0:T(8,128)(2,1)S(1)}, u32[]{:S(2)}, u32[]{:S(2)}) collective-permute-start(bf16[256,512]{1,0:T(8,128)(2,1)S(1)} %constant_dynamic-update-slice_fusion.refs_0_), channel_id=1, source_target_pairs={{0,2},{1,3},{2,0},{3,1},{4,6},{5,7},{6,4},{7,5},{8,10},{9,11},{10,... | collective-permute-start | bytes 786440 | tf_op jit(solution)/shard_map/ppermute | solution.py:175
  14.9 4.9 %collective-permute-done.4.refs_2_ = bf16[256,512]{1,0:T(8,128)(2,1)S(1)} collective-permute-done((bf16[256,512]{1,0:T(8,128)(2,1)S(1)}, bf16[256,512]{1,0:T(8,128)(2,1)S(1)}, u32[]{:S(2)}, u32[]{:S(2)}) %collective-permute-start.4) | collective-permute-done | bytes 262176 | tf_op jit(solution)/shard_map/ppermute | solution.py:175
  19.8 11.4 %collective-permute-start.9 = (bf16[256,1024]{1,0:T(8,128)(2,1)}, bf16[256,1024]{1,0:T(8,128)(2,1)S(1)}, u32[]{:S(2)}, u32[]{:S(2)}) collective-permute-start(bf16[256,1024]{1,0:T(8,128)(2,1)} %refs_0_.1), channel_id=1, source_target_pairs={{0,4},{4,0},{8,12},{12,8},{1,5},{5,1},{9,13},{13,9},{2,6},{6,2},{1... | collective-permute-start | bytes 1572872 | tf_op jit(solution)/shard_map/ppermute | solution.py:175
  31.1 1.0 copy-done.4
  32.2 0.7 copy-done.11
  32.8 0.7 pack.1
  33.6 3.5 %collective-permute-start.22 = (bf16[64,1024]{1,0:T(8,128)(2,1)S(1)}, bf16[64,1024]{1,0:T(8,128)(2,1)S(1)}, u32[]{:S(2)}, u32[]{:S(2)}) collective-permute-start(bf16[64,1024]{1,0:T(8,128)(2,1)S(1)} %get-tuple-element.46), channel_id=1, source_target_pairs={{0,12},{4,8},{8,4},{12,0},{1,13},{5,9},{9,5},{13,1},{2,14},{6,10},... | collective-permute-start | bytes 393224 | tf_op jit(solution)/shard_map/ppermute | solution.py:175
  37.1 0.6 assemble.1.refs_2_
  37.7 12.6 %collective-permute-done.22.refs_1_ = bf16[64,1024]{1,0:T(8,128)(2,1)S(1)} collective-permute-done((bf16[64,1024]{1,0:T(8,128)(2,1)S(1)}, bf16[64,1024]{1,0:T(8,128)(2,1)S(1)}, u32[]{:S(2)}, u32[]{:S(2)}) %collective-permute-start.22) | collective-permute-done | bytes 131104 | tf_op jit(solution)/shard_map/ppermute | solution.py:175
  50.3 3.3 %attend.7 = (bf16[256,512]{1,0:T(8,128)(2,1)S(1)}, bf16[256,512]{1,0:T(8,128)(2,1)S(1)}) custom-call(s32[4]{0:T(128)S(1)} %get-tuple-element.33.scal, bf16[256,1024]{1,0:T(8,128)(2,1)S(1)} %collective-permute-done.15.refs_0_, bf16[64,1024]{1,0:T(8,128)(2,1)S(1)} %collective-permute-done.22.refs_1_, bf16[1024,512]{1,0:T(8,128)(2,1)S(1)} %assemble.1.refs_2_, ...), custom_call_target="tpu_custom_call" | custom-call | tf_op jit(solution)/shard_map/attend/pallas_call | solution.py:300
  53.6 0.1 collective-permute-start.23
  53.7 0.1 collective-permute-start.10
  53.8 0.9 collective-permute-start.17
  54.7 8.9 %collective-permute-done.10.refs_1_ = bf16[64,1024]{1,0:T(8,128)(2,1)S(1)} collective-permute-done((bf16[64,1024]{1,0:T(8,128)(2,1)S(1)}, bf16[64,1024]{1,0:T(8,128)(2,1)S(1)}, u32[]{:S(2)}, u32[]{:S(2)}) %collective-permute-start.10) | collective-permute-done | bytes 131104 | tf_op jit(solution)/shard_map/ppermute | solution.py:175
  63.6 3.2 %attend.5 = (bf16[256,512]{1,0:T(8,128)(2,1)S(1)}, bf16[256,512]{1,0:T(8,128)(2,1)S(1)}) custom-call(s32[4]{0:T(128)S(1)} %get-tuple-element.33.scal, bf16[256,1024]{1,0:T(8,128)(2,1)S(1)} %collective-permute-done.9.refs_0_, bf16[64,1024]{1,0:T(8,128)(2,1)S(1)} %collective-permute-done.10.refs_1_, bf16[1024,512]{1,0:T(8,128)(2,1)S(1)} %assemble.1.refs_2_, ...), custom_call_target="tpu_custom_call" | custom-call | tf_op jit(solution)/shard_map/attend/pallas_call | solution.py:300
  66.8 0.1 collective-permute-start.11
  67.0 1.6 %collective-permute-start.24 = (bf16[256,512]{1,0:T(8,128)(2,1)S(1)}, bf16[256,512]{1,0:T(8,128)(2,1)S(1)}, u32[]{:S(2)}, u32[]{:S(2)}) collective-permute-start(bf16[256,512]{1,0:T(8,128)(2,1)S(1)} %add_convert_fusion.3), channel_id=1, source_target_pairs={{0,2},{1,3},{2,0},{3,1},{4,6},{5,7},{6,4},{7,5},{8,10},{9,11},{10,... | collective-permute-start | bytes 786440 | tf_op jit(solution)/shard_map/ppermute | solution.py:175
  68.6 3.2 %attend.4 = (bf16[256,512]{1,0:T(8,128)(2,1)S(1)}, bf16[256,512]{1,0:T(8,128)(2,1)S(1)}) custom-call(s32[4]{0:T(128)S(1)} %get-tuple-element.33.scal, bf16[256,1024]{1,0:T(8,128)(2,1)S(1)} %copy-done.5, bf16[64,1024]{1,0:T(8,128)(2,1)S(1)} %get-tuple-element.34.refs_1_, bf16[1024,512]{1,0:T(8,128)(2,1)S(1)} %assemble.1.refs_2_, bf16[1024,1024]{1,0:T(8,128)(2,1)S(1)} %copy-done.1), custom_call_target="tpu_custom_call" | custom-call | tf_op jit(solution)/shard_map/attend/pallas_call | solution.py:300
  71.8 0.3 collective-permute-start.6
  72.1 3.2 %attend.6 = (bf16[256,512]{1,0:T(8,128)(2,1)S(1)}, bf16[256,512]{1,0:T(8,128)(2,1)S(1)}) custom-call(s32[4]{0:T(128)S(1)} %get-tuple-element.33.scal, bf16[256,1024]{1,0:T(8,128)(2,1)S(1)} %collective-permute-done.16.refs_0_, bf16[64,1024]{1,0:T(8,128)(2,1)S(1)} %collective-permute-done.17.refs_1_, bf16[1024,512]{1,0:T(8,128)(2,1)S(1)} %assemble.1.refs_2_, ...), custom_call_target="tpu_custom_call" | custom-call | tf_op jit(solution)/shard_map/attend/pallas_call | solution.py:300
  75.4 0.4 collective-permute-start.18
  75.8 0.6 collective-permute-start.12
  76.5 0.1 collective-permute-start.25
  76.6 0.4 collective-permute-done.18
  77.0 1.2 collective-permute-start.19
  78.2 6.9 %collective-permute-done.12 = bf16[256,512]{1,0:T(8,128)(2,1)S(1)} collective-permute-done((bf16[256,512]{1,0:T(8,128)(2,1)S(1)}, bf16[256,512]{1,0:T(8,128)(2,1)S(1)}, u32[]{:S(2)}, u32[]{:S(2)}) %collective-permute-start.12) | collective-permute-done | bytes 262176 | tf_op jit(solution)/shard_map/ppermute | solution.py:175
  85.1 0.1 collective-permute-start.13
  85.2 1.4 project.7
  86.7 0.1 collective-permute-start.27
  86.8 0.6 collective-permute-start.7
  87.4 2.5 %collective-permute-done.19 = bf16[256,512]{1,0:T(8,128)(2,1)S(1)} collective-permute-done((bf16[256,512]{1,0:T(8,128)(2,1)S(1)}, bf16[256,512]{1,0:T(8,128)(2,1)S(1)}, u32[]{:S(2)}, u32[]{:S(2)}) %collective-permute-start.19) | collective-permute-done | bytes 262176 | tf_op jit(solution)/shard_map/ppermute | solution.py:175
  90.0 0.1 collective-permute-start.20
  90.1 1.3 project.5
  91.3 0.1 collective-permute-start.29
  91.4 4.2 %collective-permute-done.7 = bf16[256,512]{1,0:T(8,128)(2,1)S(1)} collective-permute-done((bf16[256,512]{1,0:T(8,128)(2,1)S(1)}, bf16[256,512]{1,0:T(8,128)(2,1)S(1)}, u32[]{:S(2)}, u32[]{:S(2)}) %collective-permute-start.7) | collective-permute-done | bytes 262176 | tf_op jit(solution)/shard_map/ppermute | solution.py:175
  95.7 0.1 collective-permute-start.8
  95.8 1.3 project.6
  97.0 4.5 %collective-permute-done.27 = bf16[256,1024]{1,0:T(8,128)(2,1)S(1)} collective-permute-done((bf16[256,1024]{1,0:T(8,128)(2,1)S(1)}, bf16[256,1024]{1,0:T(8,128)(2,1)S(1)}, u32[]{:S(2)}, u32[]{:S(2)}) %collective-permute-start.27) | collective-permute-done | bytes 524320 | tf_op jit(solution)/shard_map/ppermute | solution.py:175
  101.5 0.1 add_convert_fusion
  101.7 2.0 %collective-permute-start.28 = (bf16[256,512]{1,0:T(8,128)(2,1)S(1)}, bf16[256,512]{1,0:T(8,128)(2,1)S(1)}, u32[]{:S(2)}, u32[]{:S(2)}) collective-permute-start(bf16[256,512]{1,0:T(8,128)(2,1)S(1)} %get-tuple-element.65), channel_id=1, source_target_pairs={{0,8},{4,12},{8,0},{12,4},{1,9},{5,13},{9,1},{13,5},{2,10},{6,14},... | collective-permute-start | bytes 786440 | tf_op jit(solution)/shard_map/ppermute | solution.py:175
  103.7 1.0 collective-permute-start.33
  104.7 1.8 %tails.1 = (bf16[16,1024]{1,0:T(8,128)(2,1)S(1)}, bf16[16,1024]{1,0:T(8,128)(2,1)S(1)}, bf16[16,1024]{1,0:T(8,128)(2,1)S(1)}, bf16[16,1024]{1,0:T(8,128)(2,1)S(1)}) custom-call(s32[4]{0:T(128)S(1)} %get-tuple-element.33.scal, bf16[256,512]{1,0:T(8,128)(2,1)S(1)} %add_convert_fusion.8.own.refs_0_, bf16[256,512]{1,0:T(8,128)(2,1)S(1)} %collective-permute-done.8.other.refs_1_, ...), custom_call_target="tpu_custom_call" | custom-call | tf_op jit(solution)/shard_map/tails/pallas_call | solution.py:412
  106.6 1.2 collective-permute-start.30
  107.8 2.8 %collective-permute-start.31 = (bf16[16,1024]{1,0:T(8,128)(2,1)S(1)}, bf16[16,1024]{1,0:T(8,128)(2,1)S(1)}, u32[]{:S(2)}, u32[]{:S(2)}) collective-permute-start(bf16[16,1024]{1,0:T(8,128)(2,1)S(1)} %get-tuple-element.56), channel_id=1, source_target_pairs={{0,8},{4,12},{8,0},{12,4},{1,9},{5,13},{9,1},{13,5},{2,10},{6,14},... | collective-permute-start | bytes 98312 | tf_op jit(solution)/shard_map/ppermute | solution.py:175
  110.6 12.0 %collective-permute-done.30.refs_4_ = bf16[16,1024]{1,0:T(8,128)(2,1)S(1)} collective-permute-done((bf16[16,1024]{1,0:T(8,128)(2,1)S(1)}, bf16[16,1024]{1,0:T(8,128)(2,1)S(1)}, u32[]{:S(2)}, u32[]{:S(2)}) %collective-permute-start.30) | collective-permute-done | bytes 32800 | tf_op jit(solution)/shard_map/ppermute | solution.py:175
  122.6 3.1 %collective-permute-start.32 = (bf16[16,1024]{1,0:T(8,128)(2,1)S(1)}, bf16[16,1024]{1,0:T(8,128)(2,1)S(1)}, u32[]{:S(2)}, u32[]{:S(2)}) collective-permute-start(bf16[16,1024]{1,0:T(8,128)(2,1)S(1)} %get-tuple-element.57), channel_id=1, source_target_pairs={{0,12},{4,8},{8,4},{12,0},{1,13},{5,9},{9,5},{13,1},{2,14},{6,10},... | collective-permute-start | bytes 98312 | tf_op jit(solution)/shard_map/ppermute | solution.py:175
  125.7 1.3 project.4
  127.0 2.4 %collective-permute-done.31.refs_5_ = bf16[16,1024]{1,0:T(8,128)(2,1)S(1)} collective-permute-done((bf16[16,1024]{1,0:T(8,128)(2,1)S(1)}, bf16[16,1024]{1,0:T(8,128)(2,1)S(1)}, u32[]{:S(2)}, u32[]{:S(2)}) %collective-permute-start.31) | collective-permute-done | bytes 32800 | tf_op jit(solution)/shard_map/ppermute | solution.py:175
  129.4 0.6 collective-permute-start.14
  130.0 2.8 %collective-permute-start.26 = (bf16[64,1024]{1,0:T(8,128)(2,1)S(1)}, bf16[64,1024]{1,0:T(8,128)(2,1)S(1)}, u32[]{:S(2)}, u32[]{:S(2)}) collective-permute-start(bf16[64,1024]{1,0:T(8,128)(2,1)S(1)} %get-tuple-element.49), channel_id=1, source_target_pairs={{0,12},{4,8},{8,4},{12,0},{1,13},{5,9},{9,5},{13,1},{2,14},{6,10},... | collective-permute-start | bytes 393224 | tf_op jit(solution)/shard_map/ppermute | solution.py:175
  132.8 0.6 collective-permute-start.21
  133.5 2.8 %recur.2 = (f32[256,512]{1,0:T(8,128)S(1)}, f32[256,512]{1,0:T(8,128)S(1)}, f32[8,512]{1,0:T(8,128)S(1)}) custom-call(s32[4]{0:T(128)S(1)} %get-tuple-element.33.scal, bf16[256,1024]{1,0:T(8,128)(2,1)S(1)} %get-tuple-element.50.refs_0_, bf16[256,512]{1,0:T(8,128)(2,1)S(1)} %collective-permute-done.28.refs_1_, ...), custom_call_target="tpu_custom_call" | custom-call | tf_op jit(solution)/shard_map/recur/pallas_call | solution.py:524
  136.3 2.8 %recur.3 = (f32[256,512]{1,0:T(8,128)S(1)}, f32[256,512]{1,0:T(8,128)S(1)}, f32[8,512]{1,0:T(8,128)S(1)}) custom-call(s32[4]{0:T(128)S(1)} %get-tuple-element.33.scal, bf16[256,1024]{1,0:T(8,128)(2,1)S(1)} %get-tuple-element.50.refs_0_, bf16[256,512]{1,0:T(8,128)(2,1)S(1)} %collective-permute-done.33.refs_1_, ...), custom_call_target="tpu_custom_call" | custom-call | tf_op jit(solution)/shard_map/recur/pallas_call | solution.py:524
  139.1 2.4 %collective-permute-start.35 = (f32[8,1024]{1,0:T(8,128)S(1)}, f32[8,1024]{1,0:T(8,128)S(1)}, u32[]{:S(2)}, u32[]{:S(2)}) collective-permute-start(f32[8,1024]{1,0:T(8,128)S(1)} %constant_dynamic-update-slice_fusion.4), channel_id=1, source_target_pairs={{0,8},{4,12},{8,0},{12,4},{1,9},{5,13},{9,1},{13,5},{2,10},{6,14},... | collective-permute-start | bytes 98312 | tf_op jit(solution)/shard_map/ppermute | solution.py:170
  141.5 1.1 collective-permute-start.34
  142.6 1.2 collective-permute-done.21.refs_2_
  143.8 1.4 join.1
  145.2 2.0 %collective-permute-done.34.refs_4_ = f32[8,1024]{1,0:T(8,128)S(1)} collective-permute-done((f32[8,1024]{1,0:T(8,128)S(1)}, f32[8,1024]{1,0:T(8,128)S(1)}, u32[]{:S(2)}, u32[]{:S(2)}) %collective-permute-start.34) | collective-permute-done | bytes 32800 | tf_op jit(solution)/shard_map/ppermute | solution.py:170
  147.2 1.5 finish.1
  (62 shorter events, 0.7 us)
Async XLA Ops:
  0.6 49.7 %copy-start.1 = (bf16[1024,1024]{1,0:T(8,128)(2,1)S(1)}, bf16[1024,1024]{1,0:T(8,128)(2,1)}, u32[]{:S(2)}) copy-start(bf16[1024,1024]{1,0:T(8,128)(2,1)} %refs_3_.7) | copy-start | bytes 6291460
  0.6 10.4 %collective-permute-start.1 = (bf16[64,512]{1,0:T(8,128)(2,1)}, bf16[64,512]{1,0:T(8,128)(2,1)S(1)}, u32[]{:S(2)}, u32[]{:S(2)}) collective-permute-start(bf16[64,512]{1,0:T(8,128)(2,1)} %param.14), channel_id=1, source_target_pairs={{0,8},{4,12},{8,0},{12,4},{1,9},{5,13},{9,1},{13,5},{2,10},{6,14},... | collective-permute-start | bytes 196616 | tf_op jit(solution)/shard_map/ppermute | solution.py:175
  4.8 6.2 %collective-permute-start = (bf16[64,512]{1,0:T(8,128)(2,1)}, bf16[64,512]{1,0:T(8,128)(2,1)S(1)}, u32[]{:S(2)}, u32[]{:S(2)}) collective-permute-start(bf16[64,512]{1,0:T(8,128)(2,1)} %param.14), channel_id=1, source_target_pairs={{0,4},{4,0},{8,12},{12,8},{1,5},{5,1},{9,13},{13,9},{2,6},{6,2},{1... | collective-permute-start | bytes 196616 | tf_op jit(solution)/shard_map/ppermute | solution.py:175
  6.3 7.0 %collective-permute-start.2 = (bf16[64,512]{1,0:T(8,128)(2,1)}, bf16[64,512]{1,0:T(8,128)(2,1)S(1)}, u32[]{:S(2)}, u32[]{:S(2)}) collective-permute-start(bf16[64,512]{1,0:T(8,128)(2,1)} %param.14), channel_id=1, source_target_pairs={{0,12},{4,8},{8,4},{12,0},{1,13},{5,9},{9,5},{13,1},{2,14},{6,10},... | collective-permute-start | bytes 196616 | tf_op jit(solution)/shard_map/ppermute | solution.py:175
  6.3 30.7 %collective-permute-start.15 = (bf16[256,1024]{1,0:T(8,128)(2,1)}, bf16[256,1024]{1,0:T(8,128)(2,1)S(1)}, u32[]{:S(2)}, u32[]{:S(2)}) collective-permute-start(bf16[256,1024]{1,0:T(8,128)(2,1)} %refs_0_.1), channel_id=1, source_target_pairs={{0,12},{4,8},{8,4},{12,0},{1,13},{5,9},{9,5},{13,1},{2,14},{6,10},... | collective-permute-start | bytes 1572872 | tf_op jit(solution)/shard_map/ppermute | solution.py:175
  13.4 6.4 %collective-permute-start.4 = (bf16[256,512]{1,0:T(8,128)(2,1)S(1)}, bf16[256,512]{1,0:T(8,128)(2,1)S(1)}, u32[]{:S(2)}, u32[]{:S(2)}) collective-permute-start(bf16[256,512]{1,0:T(8,128)(2,1)S(1)} %constant_dynamic-update-slice_fusion.refs_0_), channel_id=1, source_target_pairs={{0,2},{1,3},{2,0},{3,1},{4,6},{5,7},{6,4},{7,5},{8,10},{9,11},{10,... | collective-permute-start | bytes 786440 | tf_op jit(solution)/shard_map/ppermute | solution.py:175
  14.9 22.2 %collective-permute-start.3 = (bf16[256,512]{1,0:T(8,128)(2,1)S(1)}, bf16[256,512]{1,0:T(8,128)(2,1)S(1)}, u32[]{:S(2)}, u32[]{:S(2)}) collective-permute-start(bf16[256,512]{1,0:T(8,128)(2,1)S(1)} %constant_dynamic-update-slice_fusion.refs_0_), channel_id=1, source_target_pairs={{0,1},{1,0},{2,3},{3,2},{4,5},{5,4},{6,7},{7,6},{8,9},{9,8},{10,11... | collective-permute-start | bytes 786440 | tf_op jit(solution)/shard_map/ppermute | solution.py:175
  19.8 17.3 %collective-permute-start.5 = (bf16[256,512]{1,0:T(8,128)(2,1)S(1)}, bf16[256,512]{1,0:T(8,128)(2,1)S(1)}, u32[]{:S(2)}, u32[]{:S(2)}) collective-permute-start(bf16[256,512]{1,0:T(8,128)(2,1)S(1)} %collective-permute-done.4.refs_2_), channel_id=1, source_target_pairs={{0,1},{1,0},{2,3},{3,2},{4,5},{5,4},{6,7},{7,6},{8,9},{9,8},{10,11... | collective-permute-start | bytes 786440 | tf_op jit(solution)/shard_map/ppermute | solution.py:175
  19.8 43.8 %collective-permute-start.9 = (bf16[256,1024]{1,0:T(8,128)(2,1)}, bf16[256,1024]{1,0:T(8,128)(2,1)S(1)}, u32[]{:S(2)}, u32[]{:S(2)}) collective-permute-start(bf16[256,1024]{1,0:T(8,128)(2,1)} %refs_0_.1), channel_id=1, source_target_pairs={{0,4},{4,0},{8,12},{12,8},{1,5},{5,1},{9,13},{13,9},{2,6},{6,2},{1... | collective-permute-start | bytes 1572872 | tf_op jit(solution)/shard_map/ppermute | solution.py:175
  31.1 1.0 copy-start.4
  32.2 0.7 copy-start.11
  33.6 16.8 %collective-permute-start.22 = (bf16[64,1024]{1,0:T(8,128)(2,1)S(1)}, bf16[64,1024]{1,0:T(8,128)(2,1)S(1)}, u32[]{:S(2)}, u32[]{:S(2)}) collective-permute-start(bf16[64,1024]{1,0:T(8,128)(2,1)S(1)} %get-tuple-element.46), channel_id=1, source_target_pairs={{0,12},{4,8},{8,4},{12,0},{1,13},{5,9},{9,5},{13,1},{2,14},{6,10},... | collective-permute-start | bytes 393224 | tf_op jit(solution)/shard_map/ppermute | solution.py:175
  37.0 35.0 %collective-permute-start.16 = (bf16[256,1024]{1,0:T(8,128)(2,1)S(1)}, bf16[256,1024]{1,0:T(8,128)(2,1)S(1)}, u32[]{:S(2)}, u32[]{:S(2)}) collective-permute-start(bf16[256,1024]{1,0:T(8,128)(2,1)S(1)} %collective-permute-done.15.refs_0_), channel_id=1, source_target_pairs={{0,4},{4,0},{8,12},{12,8},{1,5},{5,1},{9,13},{13,9},{2,6},{6,2},{1... | collective-permute-start | bytes 1572872 | tf_op jit(solution)/shard_map/ppermute | solution.py:175
  53.6 13.3 %collective-permute-start.23 = (bf16[256,512]{1,0:T(8,128)(2,1)S(1)}, bf16[256,512]{1,0:T(8,128)(2,1)S(1)}, u32[]{:S(2)}, u32[]{:S(2)}) collective-permute-start(bf16[256,512]{1,0:T(8,128)(2,1)S(1)} %get-tuple-element.48), channel_id=1, source_target_pairs={{0,1},{1,0},{2,3},{3,2},{4,5},{5,4},{6,7},{7,6},{8,9},{9,8},{10,11... | collective-permute-start | bytes 786440 | tf_op jit(solution)/shard_map/ppermute | solution.py:175
  53.7 9.9 %collective-permute-start.10 = (bf16[64,1024]{1,0:T(8,128)(2,1)S(1)}, bf16[64,1024]{1,0:T(8,128)(2,1)S(1)}, u32[]{:S(2)}, u32[]{:S(2)}) collective-permute-start(bf16[64,1024]{1,0:T(8,128)(2,1)S(1)} %get-tuple-element.38), channel_id=1, source_target_pairs={{0,4},{4,0},{8,12},{12,8},{1,5},{5,1},{9,13},{13,9},{2,6},{6,2},{1... | collective-permute-start | bytes 393224 | tf_op jit(solution)/shard_map/ppermute | solution.py:175
  53.7 14.8 %copy-start.5 = (bf16[256,1024]{1,0:T(8,128)(2,1)S(1)}, bf16[256,1024]{1,0:T(8,128)(2,1)}, u32[]{:S(2)}) copy-start(bf16[256,1024]{1,0:T(8,128)(2,1)} %refs_0_.1) | copy-start | bytes 1572868
  53.8 18.3 %collective-permute-start.17 = (bf16[64,1024]{1,0:T(8,128)(2,1)S(1)}, bf16[64,1024]{1,0:T(8,128)(2,1)S(1)}, u32[]{:S(2)}, u32[]{:S(2)}) collective-permute-start(bf16[64,1024]{1,0:T(8,128)(2,1)S(1)} %get-tuple-element.42), channel_id=1, source_target_pairs={{0,8},{4,12},{8,0},{12,4},{1,9},{5,13},{9,1},{13,5},{2,10},{6,14},... | collective-permute-start | bytes 393224 | tf_op jit(solution)/shard_map/ppermute | solution.py:175
  66.8 8.9 %collective-permute-start.11 = (bf16[256,512]{1,0:T(8,128)(2,1)S(1)}, bf16[256,512]{1,0:T(8,128)(2,1)S(1)}, u32[]{:S(2)}, u32[]{:S(2)}) collective-permute-start(bf16[256,512]{1,0:T(8,128)(2,1)S(1)} %get-tuple-element.40), channel_id=1, source_target_pairs={{0,1},{1,0},{2,3},{3,2},{4,5},{5,4},{6,7},{7,6},{8,9},{9,8},{10,11... | collective-permute-start | bytes 786440 | tf_op jit(solution)/shard_map/ppermute | solution.py:175
  67.0 9.4 %collective-permute-start.24 = (bf16[256,512]{1,0:T(8,128)(2,1)S(1)}, bf16[256,512]{1,0:T(8,128)(2,1)S(1)}, u32[]{:S(2)}, u32[]{:S(2)}) collective-permute-start(bf16[256,512]{1,0:T(8,128)(2,1)S(1)} %add_convert_fusion.3), channel_id=1, source_target_pairs={{0,2},{1,3},{2,0},{3,1},{4,6},{5,7},{6,4},{7,5},{8,10},{9,11},{10,... | collective-permute-start | bytes 786440 | tf_op jit(solution)/shard_map/ppermute | solution.py:175
  71.8 15.0 %collective-permute-start.6 = (bf16[256,512]{1,0:T(8,128)(2,1)S(1)}, bf16[256,512]{1,0:T(8,128)(2,1)S(1)}, u32[]{:S(2)}, u32[]{:S(2)}) collective-permute-start(bf16[256,512]{1,0:T(8,128)(2,1)S(1)} %get-tuple-element.36), channel_id=1, source_target_pairs={{0,1},{1,0},{2,3},{3,2},{4,5},{5,4},{6,7},{7,6},{8,9},{9,8},{10,11... | collective-permute-start | bytes 786440 | tf_op jit(solution)/shard_map/ppermute | solution.py:175
  75.3 9.9 %copy-start = (bf16[1024,1024]{1,0:T(8,128)(2,1)S(1)}, bf16[1024,1024]{1,0:T(8,128)(2,1)}, u32[]{:S(2)}) copy-start(bf16[1024,1024]{1,0:T(8,128)(2,1)} %refs_9_.3) | copy-start | bytes 6291460
  75.4 9.9 %copy-start.6 = (f32[4096]{0:T(1024)S(1)}, f32[4096]{0:T(1024)}, u32[]{:S(2)}) copy-start(f32[4096]{0:T(1024)} %param.25) | copy-start | bytes 49156
  75.4 1.6 %collective-permute-start.18 = (bf16[256,512]{1,0:T(8,128)(2,1)S(1)}, bf16[256,512]{1,0:T(8,128)(2,1)S(1)}, u32[]{:S(2)}, u32[]{:S(2)}) collective-permute-start(bf16[256,512]{1,0:T(8,128)(2,1)S(1)} %get-tuple-element.44), channel_id=1, source_target_pairs={{0,1},{1,0},{2,3},{3,2},{4,5},{5,4},{6,7},{7,6},{8,9},{9,8},{10,11... | collective-permute-start | bytes 786440 | tf_op jit(solution)/shard_map/ppermute | solution.py:175
  75.8 9.2 %collective-permute-start.12 = (bf16[256,512]{1,0:T(8,128)(2,1)S(1)}, bf16[256,512]{1,0:T(8,128)(2,1)S(1)}, u32[]{:S(2)}, u32[]{:S(2)}) collective-permute-start(bf16[256,512]{1,0:T(8,128)(2,1)S(1)} %add_convert_fusion.7), channel_id=1, source_target_pairs={{0,2},{1,3},{2,0},{3,1},{4,6},{5,7},{6,4},{7,5},{8,10},{9,11},{10,... | collective-permute-start | bytes 786440 | tf_op jit(solution)/shard_map/ppermute | solution.py:175
  76.5 8.7 %collective-permute-start.25 = (bf16[256,512]{1,0:T(8,128)(2,1)S(1)}, bf16[256,512]{1,0:T(8,128)(2,1)S(1)}, u32[]{:S(2)}, u32[]{:S(2)}) collective-permute-start(bf16[256,512]{1,0:T(8,128)(2,1)S(1)} %add_convert_fusion.2.own.refs_2_), channel_id=1, source_target_pairs={{0,1},{1,0},{2,3},{3,2},{4,5},{5,4},{6,7},{7,6},{8,9},{9,8},{10,11... | collective-permute-start | bytes 786440 | tf_op jit(solution)/shard_map/ppermute | solution.py:175
  77.0 12.9 %collective-permute-start.19 = (bf16[256,512]{1,0:T(8,128)(2,1)S(1)}, bf16[256,512]{1,0:T(8,128)(2,1)S(1)}, u32[]{:S(2)}, u32[]{:S(2)}) collective-permute-start(bf16[256,512]{1,0:T(8,128)(2,1)S(1)} %add_convert_fusion.5), channel_id=1, source_target_pairs={{0,2},{1,3},{2,0},{3,1},{4,6},{5,7},{6,4},{7,5},{8,10},{9,11},{10,... | collective-permute-start | bytes 786440 | tf_op jit(solution)/shard_map/ppermute | solution.py:175
  85.1 4.9 %collective-permute-start.13 = (bf16[256,512]{1,0:T(8,128)(2,1)S(1)}, bf16[256,512]{1,0:T(8,128)(2,1)S(1)}, u32[]{:S(2)}, u32[]{:S(2)}) collective-permute-start(bf16[256,512]{1,0:T(8,128)(2,1)S(1)} %add_convert_fusion.6.own.refs_4_), channel_id=1, source_target_pairs={{0,1},{1,0},{2,3},{3,2},{4,5},{5,4},{6,7},{7,6},{8,9},{9,8},{10,11... | collective-permute-start | bytes 786440 | tf_op jit(solution)/shard_map/ppermute | solution.py:175
  86.7 14.9 %collective-permute-start.27 = (bf16[256,1024]{1,0:T(8,128)(2,1)S(1)}, bf16[256,1024]{1,0:T(8,128)(2,1)S(1)}, u32[]{:S(2)}, u32[]{:S(2)}) collective-permute-start(bf16[256,1024]{1,0:T(8,128)(2,1)S(1)} %get-tuple-element.52), channel_id=1, source_target_pairs={{0,4},{4,0},{8,12},{12,8},{1,5},{5,1},{9,13},{13,9},{2,6},{6,2},{1... | collective-permute-start | bytes 1572872 | tf_op jit(solution)/shard_map/ppermute | solution.py:175
  86.8 8.8 %collective-permute-start.7 = (bf16[256,512]{1,0:T(8,128)(2,1)S(1)}, bf16[256,512]{1,0:T(8,128)(2,1)S(1)}, u32[]{:S(2)}, u32[]{:S(2)}) collective-permute-start(bf16[256,512]{1,0:T(8,128)(2,1)S(1)} %add_convert_fusion.9), channel_id=1, source_target_pairs={{0,2},{1,3},{2,0},{3,1},{4,6},{5,7},{6,4},{7,5},{8,10},{9,11},{10,... | collective-permute-start | bytes 786440 | tf_op jit(solution)/shard_map/ppermute | solution.py:175
  90.0 5.8 %collective-permute-start.20 = (bf16[256,512]{1,0:T(8,128)(2,1)S(1)}, bf16[256,512]{1,0:T(8,128)(2,1)S(1)}, u32[]{:S(2)}, u32[]{:S(2)}) collective-permute-start(bf16[256,512]{1,0:T(8,128)(2,1)S(1)} %add_convert_fusion.4.own.refs_6_), channel_id=1, source_target_pairs={{0,1},{1,0},{2,3},{3,2},{4,5},{5,4},{6,7},{7,6},{8,9},{9,8},{10,11... | collective-permute-start | bytes 786440 | tf_op jit(solution)/shard_map/ppermute | solution.py:175
  91.3 41.4 %collective-permute-start.29 = (bf16[256,1024]{1,0:T(8,128)(2,1)S(1)}, bf16[256,1024]{1,0:T(8,128)(2,1)S(1)}, u32[]{:S(2)}, u32[]{:S(2)}) collective-permute-start(bf16[256,1024]{1,0:T(8,128)(2,1)S(1)} %get-tuple-element.53), channel_id=1, source_target_pairs={{0,4},{4,0},{8,12},{12,8},{1,5},{5,1},{9,13},{13,9},{2,6},{6,2},{1... | collective-permute-start | bytes 1572872 | tf_op jit(solution)/shard_map/ppermute | solution.py:175
  95.7 9.0 %collective-permute-start.8 = (bf16[256,512]{1,0:T(8,128)(2,1)S(1)}, bf16[256,512]{1,0:T(8,128)(2,1)S(1)}, u32[]{:S(2)}, u32[]{:S(2)}) collective-permute-start(bf16[256,512]{1,0:T(8,128)(2,1)S(1)} %add_convert_fusion.8.own.refs_0_), channel_id=1, source_target_pairs={{0,1},{1,0},{2,3},{3,2},{4,5},{5,4},{6,7},{7,6},{8,9},{9,8},{10,11... | collective-permute-start | bytes 786440 | tf_op jit(solution)/shard_map/ppermute | solution.py:175
  101.7 31.7 %collective-permute-start.28 = (bf16[256,512]{1,0:T(8,128)(2,1)S(1)}, bf16[256,512]{1,0:T(8,128)(2,1)S(1)}, u32[]{:S(2)}, u32[]{:S(2)}) collective-permute-start(bf16[256,512]{1,0:T(8,128)(2,1)S(1)} %get-tuple-element.65), channel_id=1, source_target_pairs={{0,8},{4,12},{8,0},{12,4},{1,9},{5,13},{9,1},{13,5},{2,10},{6,14},... | collective-permute-start | bytes 786440 | tf_op jit(solution)/shard_map/ppermute | solution.py:175
  103.7 32.6 %collective-permute-start.33 = (bf16[256,512]{1,0:T(8,128)(2,1)S(1)}, bf16[256,512]{1,0:T(8,128)(2,1)S(1)}, u32[]{:S(2)}, u32[]{:S(2)}) collective-permute-start(bf16[256,512]{1,0:T(8,128)(2,1)S(1)} %get-tuple-element.64), channel_id=1, source_target_pairs={{0,8},{4,12},{8,0},{12,4},{1,9},{5,13},{9,1},{13,5},{2,10},{6,14},... | collective-permute-start | bytes 786440 | tf_op jit(solution)/shard_map/ppermute | solution.py:175
  106.5 26.9 %copy-start.2 = (bf16[4,256,256]{2,1,0:T(8,128)(2,1)S(1)}, bf16[4,256,256]{2,1,0:T(8,128)(2,1)}, u32[]{:S(2)}) copy-start(bf16[4,256,256]{2,1,0:T(8,128)(2,1)} %refs_8_.3) | copy-start | bytes 1572868
  106.5 26.9 %copy-start.3 = (bf16[4,256,256]{2,1,0:T(8,128)(2,1)S(1)}, bf16[4,256,256]{2,1,0:T(8,128)(2,1)}, u32[]{:S(2)}) copy-start(bf16[4,256,256]{2,1,0:T(8,128)(2,1)} %refs_9_.5) | copy-start | bytes 1572868
  106.5 26.9 %copy-start.7 = (f32[4,1024]{1,0:T(4,128)S(1)}, f32[4,1024]{1,0:T(4,128)}, u32[]{:S(2)}) copy-start(f32[4,1024]{1,0:T(4,128)} %refs_7_.3) | copy-start | bytes 49156
  106.6 26.9 %copy-start.8 = (f32[1024]{0:T(1024)S(1)}, f32[1024]{0:T(1024)}, u32[]{:S(2)}) copy-start(f32[1024]{0:T(1024)} %param.22) | copy-start | bytes 12292
  106.6 26.9 %copy-start.9 = (f32[1024]{0:T(1024)S(1)}, f32[1024]{0:T(1024)}, u32[]{:S(2)}) copy-start(f32[1024]{0:T(1024)} %param.23) | copy-start | bytes 12292
  106.6 26.9 %copy-start.10 = (s32[1024]{0:T(1024)S(1)}, s32[1024]{0:T(1024)}, u32[]{:S(2)}) copy-start(s32[1024]{0:T(1024)} %param.24) | copy-start | bytes 12292
  106.6 16.0 %collective-permute-start.30 = (bf16[16,1024]{1,0:T(8,128)(2,1)S(1)}, bf16[16,1024]{1,0:T(8,128)(2,1)S(1)}, u32[]{:S(2)}, u32[]{:S(2)}) collective-permute-start(bf16[16,1024]{1,0:T(8,128)(2,1)S(1)} %get-tuple-element.55), channel_id=1, source_target_pairs={{0,4},{4,0},{8,12},{12,8},{1,5},{5,1},{9,13},{13,9},{2,6},{6,2},{1... | collective-permute-start | bytes 98312 | tf_op jit(solution)/shard_map/ppermute | solution.py:175
  107.8 21.6 %collective-permute-start.31 = (bf16[16,1024]{1,0:T(8,128)(2,1)S(1)}, bf16[16,1024]{1,0:T(8,128)(2,1)S(1)}, u32[]{:S(2)}, u32[]{:S(2)}) collective-permute-start(bf16[16,1024]{1,0:T(8,128)(2,1)S(1)} %get-tuple-element.56), channel_id=1, source_target_pairs={{0,8},{4,12},{8,0},{12,4},{1,9},{5,13},{9,1},{13,5},{2,10},{6,14},... | collective-permute-start | bytes 98312 | tf_op jit(solution)/shard_map/ppermute | solution.py:175
  122.6 7.3 %collective-permute-start.32 = (bf16[16,1024]{1,0:T(8,128)(2,1)S(1)}, bf16[16,1024]{1,0:T(8,128)(2,1)S(1)}, u32[]{:S(2)}, u32[]{:S(2)}) collective-permute-start(bf16[16,1024]{1,0:T(8,128)(2,1)S(1)} %get-tuple-element.57), channel_id=1, source_target_pairs={{0,12},{4,8},{8,4},{12,0},{1,13},{5,9},{9,5},{13,1},{2,14},{6,10},... | collective-permute-start | bytes 98312 | tf_op jit(solution)/shard_map/ppermute | solution.py:175
  129.4 13.2 %collective-permute-start.14 = (bf16[64,1024]{1,0:T(8,128)(2,1)S(1)}, bf16[64,1024]{1,0:T(8,128)(2,1)S(1)}, u32[]{:S(2)}, u32[]{:S(2)}) collective-permute-start(bf16[64,1024]{1,0:T(8,128)(2,1)S(1)} %get-tuple-element.41), channel_id=1, source_target_pairs={{0,4},{4,0},{8,12},{12,8},{1,5},{5,1},{9,13},{13,9},{2,6},{6,2},{1... | collective-permute-start | bytes 393224 | tf_op jit(solution)/shard_map/ppermute | solution.py:175
  130.0 12.6 %collective-permute-start.26 = (bf16[64,1024]{1,0:T(8,128)(2,1)S(1)}, bf16[64,1024]{1,0:T(8,128)(2,1)S(1)}, u32[]{:S(2)}, u32[]{:S(2)}) collective-permute-start(bf16[64,1024]{1,0:T(8,128)(2,1)S(1)} %get-tuple-element.49), channel_id=1, source_target_pairs={{0,12},{4,8},{8,4},{12,0},{1,13},{5,9},{9,5},{13,1},{2,14},{6,10},... | collective-permute-start | bytes 393224 | tf_op jit(solution)/shard_map/ppermute | solution.py:175
  132.8 11.0 %collective-permute-start.21 = (bf16[64,1024]{1,0:T(8,128)(2,1)S(1)}, bf16[64,1024]{1,0:T(8,128)(2,1)S(1)}, u32[]{:S(2)}, u32[]{:S(2)}) collective-permute-start(bf16[64,1024]{1,0:T(8,128)(2,1)S(1)} %get-tuple-element.45), channel_id=1, source_target_pairs={{0,8},{4,12},{8,0},{12,4},{1,9},{5,13},{9,1},{13,5},{2,10},{6,14},... | collective-permute-start | bytes 393224 | tf_op jit(solution)/shard_map/ppermute | solution.py:175
  139.1 6.1 %collective-permute-start.35 = (f32[8,1024]{1,0:T(8,128)S(1)}, f32[8,1024]{1,0:T(8,128)S(1)}, u32[]{:S(2)}, u32[]{:S(2)}) collective-permute-start(f32[8,1024]{1,0:T(8,128)S(1)} %constant_dynamic-update-slice_fusion.4), channel_id=1, source_target_pairs={{0,8},{4,12},{8,0},{12,4},{1,9},{5,13},{9,1},{13,5},{2,10},{6,14},... | collective-permute-start | bytes 98312 | tf_op jit(solution)/shard_map/ppermute | solution.py:170
  141.5 5.7 %collective-permute-start.34 = (f32[8,1024]{1,0:T(8,128)S(1)}, f32[8,1024]{1,0:T(8,128)S(1)}, u32[]{:S(2)}, u32[]{:S(2)}) collective-permute-start(f32[8,1024]{1,0:T(8,128)S(1)} %constant_dynamic-update-slice_fusion.4), channel_id=1, source_target_pairs={{0,4},{4,8},{8,12},{12,0},{1,5},{5,9},{9,13},{13,1},{2,6},{6,10},{... | collective-permute-start | bytes 98312 | tf_op jit(solution)/shard_map/ppermute | solution.py:170

commit v8 on v7

--- a/solution.py
+++ b/solution.py
@@ -251,17 +251,17 @@
     )(scal, *pieces)
 
 
-def attend_kernel(nctx, back, steps, shard, scal, *refs):
+def attend_kernel(nctx, back, steps, shard, count_resid, scal, *refs):
     count = len(steps)
-    q_refs, resid_refs = refs[:count], refs[count : 2 * count]
-    kv, weight, keep, send, att, acc = refs[2 * count :]
+    q_refs, resid_refs = refs[:count], refs[count : count + count_resid]
+    kv, weight, keep, send, att, acc = refs[count + count_resid :]
     rows, width = att.shape
     heads = width // HD
     half = weight.shape[1] // 2
     ctx_index, mp_index, low, high = scal[0], scal[1], scal[2], scal[3]
     side = jnp.bitwise_and(mp_index, 1)
     window = min(back + 1, nctx) * rows
-    scale = 1.0 / math.sqrt(HD)
+    scale = math.log2(math.e) / math.sqrt(HD)
     for j, step in enumerate(steps):
         block = jnp.bitwise_xor(ctx_index, step)
         first_key = pl.multiple_of(
@@ -270,16 +270,16 @@
         qpos = block * rows + lax.broadcasted_iota(jnp.int32, (rows, 1), 0)
         start = segment_start(qpos, low, high)
         kpos = first_key + lax.broadcasted_iota(jnp.int32, (1, window), 1)
-        allowed = (kpos <= qpos) & (kpos >= start) & (qpos - kpos < WIN)
+        allowed = (kpos <= qpos) & (kpos >= jnp.maximum(start, qpos - (WIN - 1)))
         for h in range(heads):
             query = q_refs[j][:, h * HD : (h + 1) * HD]
             keys = kv[pl.ds(first_key, window), :HD]
             scores = lax.dot_general(
                 query, keys, (((1,), (1,)), ((), ())), preferred_element_type=F32
             )
-            scores = jnp.where(allowed, scores * scale, -1e30)
+            scores = jnp.where(allowed, scores, -1e30)
             top = jnp.max(scores, axis=1, keepdims=True)
-            weights = jnp.exp(scores - top)
+            weights = jnp.exp2((scores - top) * scale)
             total = jnp.sum(weights, axis=1, keepdims=True)
             values = kv[pl.ds(first_key, window), HD:]
             gathered = jnp.dot(weights.astype(BF16), values, preferred_element_type=F32)
@@ -288,7 +288,8 @@
         for out, which in ((send, 1 - side), (keep, side)):
             cols = pl.ds(pl.multiple_of(which * half, half), half)
             acc[...] = jnp.dot(att[...], weight[:, cols], preferred_element_type=F32)
-            acc[own, :] += resid_refs[j][:, cols].astype(F32)
+            if count_resid:
+                acc[own, :] += resid_refs[j][:, cols].astype(F32)
             out[j * rows : (j + 1) * rows, :] = acc[...].astype(BF16)
 
 
@@ -298,14 +299,36 @@
     half = weight.shape[1] // 2
     shape = jax.ShapeDtypeStruct((count * rows, half), BF16)
     return pl.pallas_call(
-        functools.partial(attend_kernel, nctx, back, steps, shard),
+        functools.partial(attend_kernel, nctx, back, steps, shard, len(residuals)),
         out_shape=(shape, shape),
-        in_specs=[SMEM] + [VMEM] * (2 * count + 2),
+        in_specs=[SMEM] + [VMEM] * (count + len(residuals) + 2),
         out_specs=(VMEM, VMEM),
         scratch_shapes=[pltpu.VMEM((rows, width), BF16), pltpu.VMEM((rows, half), F32)],
         name="attend",
         compiler_params=pltpu.CompilerParams(vmem_limit_bytes=GRANT),
     )(scal, *queries, *residuals, kv, weight)
+
+
+def topped_kernel(shard, scal, keep, send, resid, keep_out, send_out):
+    half = keep.shape[1]
+    side = jnp.bitwise_and(scal[1], 1)
+    own = pl.ds(pl.multiple_of(scal[1] * shard, shard), shard)
+    for piece, out, which in ((send, send_out, 1 - side), (keep, keep_out, side)):
+        cols = pl.ds(pl.multiple_of(which * half, half), half)
+        out[...] = piece[...]
+        out[own, :] = (piece[own, :].astype(F32) + resid[:, cols].astype(F32)).astype(BF16)
+
+
+def topped(scal, keep, send, resid):
+    shape = jax.ShapeDtypeStruct(keep.shape, BF16)
+    return pl.pallas_call(
+        functools.partial(topped_kernel, resid.shape[0]),
+        out_shape=(shape, shape),
+        in_specs=[SMEM] + [VMEM] * 3,
+        out_specs=(VMEM, VMEM),
+        name="topped",
+        compiler_params=pltpu.CompilerParams(vmem_limit_bytes=GRANT),
+    )(scal, keep, send, resid)
 
 
 def split_weights(gain, weight, ctx_index, side):
@@ -617,9 +640,10 @@
     halves, places = [], {}
     messages, give = {}, {}
     for at, e in enumerate(chunks):
-        keep, send = attend(
-            scal, [visiting[e]], [resid_parts[e]], kv, out_weight, nctx, back, (e,), shard
-        )
+        now = [] if e in (1, nctx - 1) else [resid_parts[e]]
+        keep, send = attend(scal, [visiting[e]], now, kv, out_weight, nctx, back, (e,), shard)
+        if not now:
+            keep, send = topped(scal, keep, send, resid_parts[e])
         other = swapped(send, "mp", 1)
         mine = (keep.astype(F32) + other.astype(F32)).astype(BF16)
         flip = 2
@@ -633,20 +657,19 @@
         messages[e], give[e] = project(scal, mine, other, gain, lru_weight, 1, shard)
     lines = list(tails(scal, halves, [places[e] for e in range(nctx)], gain, lru_weight, rows))
     blocks = lru_weight.shape[1] // BW
-    parts = 2 if blocks % 2 == 0 else 1
-    span = lru_weight.shape[1] // parts
-    mains = [[messages[0]] for _ in range(parts)]
+    parts = [(0, blocks - blocks // 2), (blocks - blocks // 2, blocks // 2)] if blocks > 1 else [(0, blocks)]
+    mains = [[messages[0]] for _ in parts]
     for flip in range(nctx - 1, 0, -1):
         if flip % 2 and flip > 1:
             passed = swapped(messages[flip], "ctx", 1)
             merged = []
-            for part in range(parts):
-                cols = slice(part * span, (part + 1) * span)
+            for first, count in parts:
+                cols = slice(first * BW, (first + count) * BW)
                 both = messages[flip - 1][:, cols].astype(F32) + passed[:, cols].astype(F32)
                 merged.append(both.astype(BF16))
             messages[flip - 1] = merged
         elif flip > 1:
-            for part in range(parts):
+            for part in range(len(parts)):
                 mains[part].append(swapped(messages[flip][part], "ctx", flip))
         else:
             got = swapped(messages[1], "ctx", 1)
@@ -658,7 +681,7 @@
     for flip in range(1, nctx):
         given.append(swapped(give[flip], "ctx", flip))
     states, cums, lasts = [], [], []
-    for part in range(parts):
+    for part, (first, count) in enumerate(parts):
         state, cum, last = recur(
             scal,
             mains[part],
@@ -670,8 +693,8 @@
             gate_input_b.reshape(1, -1),
             decay_codes.reshape(1, -1),
             features,
-            part * blocks // parts,
-            blocks // parts,
+            first,
+            count,
         )
         states.append(state)
         cums.append(cum)

time: 149 us -> 146 us (0.980)
  waiting for transfers between devices: 64.8 us -> 61.2 us
    ppermute x34, waiting for transfers between devices: 62.8 us -> 59.2 us  [swapped(): return lax.ppermute(value, axis, [(s, s ^ flip) for s in range(count)])]
    pallas_call x4 -> x6, Pallas kernels: 13 us -> 13.3 us  [the longest x4 12.1 us: attend(): pl.pallas_call(functools.partial(attend_kernel, nctx, back, steps, shard,...]
  transfers between devices with their start and end apart: 36 -> 36, of which waited for: 13 -> 13; matrix products, arithmetic and copies ran while one was open for 1% -> 1% of each run, Pallas kernels for 19% -> 20%
where the time goes in v8:
time: 146 us; the launch traced here: 145 us
  waiting for transfers between devices  61.2 us (42%)
  starting transfers between devices  49.6 us (34%)
  Pallas kernels  30.1 us (21%)
  local copies, waits for them, and re-layouts  2.66 us (2%)
    ppermute x34, waiting for transfers between devices, swapped(): return lax.ppermute(value, axis, [(s, s ^ flip) for s in range(count)])  59.2 us
    ppermute x34, starting transfers between devices, swapped(): return lax.ppermute(value, axis, [(s, s ^ flip) for s in range(count)])  46.1 us
    pallas_call x4, Pallas kernels, attend(): pl.pallas_call(functools.partial(attend_kernel, nctx, back, steps, shard,...  12.1 us
    pallas_call x2, Pallas kernels, recur(): pl.pallas_call(functools.partial(recur_kernel, len(mains), len(lines), fe...  5.6 us
    pallas_call x4, Pallas kernels, project(): pl.pallas_call(functools.partial(project_kernel, count), out_shape=tuple(...  5.23 us
    ppermute x2, starting transfers between devices, rotated(): lax.ppermute(value, axis, [(s, (s - steps) % count) for s in range(count)])  3.48 us
  transfers between devices with their start and end apart: 36, of which 13 were waited for; matrix products, arithmetic and copies ran while one was open for 1% of the time, Pallas kernels for 20%

profile of v8, /device:TPU:0, one launch (start us, length us, event | category | flops | bytes accessed | tf_op | source)
XLA Modules:
  0.0 145.4 jit_solution(12722115954484984061)
XLA Ops:
  0.6 4.1 %collective-permute-start.1 = (bf16[64,512]{1,0:T(8,128)(2,1)}, bf16[64,512]{1,0:T(8,128)(2,1)S(1)}, u32[]{:S(2)}, u32[]{:S(2)}) collective-permute-start(bf16[64,512]{1,0:T(8,128)(2,1)} %param.14), channel_id=1, source_target_pairs={{0,8},{4,12},{8,0},{12,4},{1,9},{5,13},{9,1},{13,5},{2,10},{6,14},... | collective-permute-start | bytes 196616 | tf_op jit(solution)/shard_map/ppermute | solution.py:175
  4.8 1.6 %collective-permute-start = (bf16[64,512]{1,0:T(8,128)(2,1)}, bf16[64,512]{1,0:T(8,128)(2,1)S(1)}, u32[]{:S(2)}, u32[]{:S(2)}) collective-permute-start(bf16[64,512]{1,0:T(8,128)(2,1)} %param.14), channel_id=1, source_target_pairs={{0,4},{4,0},{8,12},{12,8},{1,5},{5,1},{9,13},{13,9},{2,6},{6,2},{1... | collective-permute-start | bytes 196616 | tf_op jit(solution)/shard_map/ppermute | solution.py:175
  6.3 3.8 %collective-permute-start.15 = (bf16[256,1024]{1,0:T(8,128)(2,1)}, bf16[256,1024]{1,0:T(8,128)(2,1)S(1)}, u32[]{:S(2)}, u32[]{:S(2)}) collective-permute-start(bf16[256,1024]{1,0:T(8,128)(2,1)} %refs_0_.1), channel_id=1, source_target_pairs={{0,12},{4,8},{8,4},{12,0},{1,13},{5,9},{9,5},{13,1},{2,14},{6,10},... | collective-permute-start | bytes 1572872 | tf_op jit(solution)/shard_map/ppermute | solution.py:175
  10.2 0.8 constant_dynamic-update-slice_fusion.3
  11.1 2.3 %collective-permute-done.2 = bf16[64,512]{1,0:T(8,128)(2,1)S(1)} collective-permute-done((bf16[64,512]{1,0:T(8,128)(2,1)}, bf16[64,512]{1,0:T(8,128)(2,1)S(1)}, u32[]{:S(2)}, u32[]{:S(2)}) %collective-permute-start.2) | collective-permute-done | bytes 65568 | tf_op jit(solution)/shard_map/ppermute | solution.py:175
  13.4 1.5 %collective-permute-start.4 = (bf16[256,512]{1,0:T(8,128)(2,1)S(1)}, bf16[256,512]{1,0:T(8,128)(2,1)S(1)}, u32[]{:S(2)}, u32[]{:S(2)}) collective-permute-start(bf16[256,512]{1,0:T(8,128)(2,1)S(1)} %constant_dynamic-update-slice_fusion.refs_0_), channel_id=1, source_target_pairs={{0,2},{1,3},{2,0},{3,1},{4,6},{5,7},{6,4},{7,5},{8,10},{9,11},{10,... | collective-permute-start | bytes 786440 | tf_op jit(solution)/shard_map/ppermute | solution.py:175
  14.9 4.9 %collective-permute-done.4.refs_2_ = bf16[256,512]{1,0:T(8,128)(2,1)S(1)} collective-permute-done((bf16[256,512]{1,0:T(8,128)(2,1)S(1)}, bf16[256,512]{1,0:T(8,128)(2,1)S(1)}, u32[]{:S(2)}, u32[]{:S(2)}) %collective-permute-start.4) | collective-permute-done | bytes 262176 | tf_op jit(solution)/shard_map/ppermute | solution.py:175
  19.8 11.4 %collective-permute-start.9 = (bf16[256,1024]{1,0:T(8,128)(2,1)}, bf16[256,1024]{1,0:T(8,128)(2,1)S(1)}, u32[]{:S(2)}, u32[]{:S(2)}) collective-permute-start(bf16[256,1024]{1,0:T(8,128)(2,1)} %refs_0_.1), channel_id=1, source_target_pairs={{0,4},{4,0},{8,12},{12,8},{1,5},{5,1},{9,13},{13,9},{2,6},{6,2},{1... | collective-permute-start | bytes 1572872 | tf_op jit(solution)/shard_map/ppermute | solution.py:175
  31.1 1.0 copy-done.4
  32.2 0.7 copy-done.11
  32.8 0.7 pack.1
  33.6 3.5 %collective-permute-start.22 = (bf16[64,1024]{1,0:T(8,128)(2,1)S(1)}, bf16[64,1024]{1,0:T(8,128)(2,1)S(1)}, u32[]{:S(2)}, u32[]{:S(2)}) collective-permute-start(bf16[64,1024]{1,0:T(8,128)(2,1)S(1)} %get-tuple-element.54), channel_id=1, source_target_pairs={{0,12},{4,8},{8,4},{12,0},{1,13},{5,9},{9,5},{13,1},{2,14},{6,10},... | collective-permute-start | bytes 393224 | tf_op jit(solution)/shard_map/ppermute | solution.py:175
  37.1 0.6 assemble.1.refs_2_.refs_1_
  37.7 3.0 %attend.7 = (bf16[256,512]{1,0:T(8,128)(2,1)S(1)}, bf16[256,512]{1,0:T(8,128)(2,1)S(1)}) custom-call(s32[4]{0:T(128)S(1)} %get-tuple-element.37.scal, bf16[256,1024]{1,0:T(8,128)(2,1)S(1)} %collective-permute-done.15.refs_0_, bf16[1024,512]{1,0:T(8,128)(2,1)S(1)} %assemble.1.refs_2_.refs_1_, bf16[1024,1024]{1,0:T(8,128)(2,1)S(1)} %copy-done.1), custom_call_target="tpu_custom_call" | custom-call | tf_op jit(solution)/shard_map/attend/pallas_call | solution.py:301
  40.7 9.6 %collective-permute-done.22.resid = bf16[64,1024]{1,0:T(8,128)(2,1)S(1)} collective-permute-done((bf16[64,1024]{1,0:T(8,128)(2,1)S(1)}, bf16[64,1024]{1,0:T(8,128)(2,1)S(1)}, u32[]{:S(2)}, u32[]{:S(2)}) %collective-permute-start.22) | collective-permute-done | bytes 131104 | tf_op jit(solution)/shard_map/ppermute | solution.py:175
  50.3 0.6 topped.3
  50.9 0.1 collective-permute-start.23
  51.0 0.1 collective-permute-start.10
  51.1 0.9 collective-permute-start.17
  52.1 3.0 %attend.5 = (bf16[256,512]{1,0:T(8,128)(2,1)S(1)}, bf16[256,512]{1,0:T(8,128)(2,1)S(1)}) custom-call(s32[4]{0:T(128)S(1)} %get-tuple-element.37.scal, bf16[256,1024]{1,0:T(8,128)(2,1)S(1)} %collective-permute-done.9.refs_0_, bf16[1024,512]{1,0:T(8,128)(2,1)S(1)} %assemble.1.refs_2_.refs_1_, bf16[1024,1024]{1,0:T(8,128)(2,1)S(1)} %copy-done.1), custom_call_target="tpu_custom_call" | custom-call | tf_op jit(solution)/shard_map/attend/pallas_call | solution.py:301
  55.1 8.5 %collective-permute-done.10.resid = bf16[64,1024]{1,0:T(8,128)(2,1)S(1)} collective-permute-done((bf16[64,1024]{1,0:T(8,128)(2,1)S(1)}, bf16[64,1024]{1,0:T(8,128)(2,1)S(1)}, u32[]{:S(2)}, u32[]{:S(2)}) %collective-permute-start.10) | collective-permute-done | bytes 131104 | tf_op jit(solution)/shard_map/ppermute | solution.py:175
  63.6 0.6 topped.2
  64.2 0.1 collective-permute-start.11
  64.4 1.6 %collective-permute-start.24 = (bf16[256,512]{1,0:T(8,128)(2,1)S(1)}, bf16[256,512]{1,0:T(8,128)(2,1)S(1)}, u32[]{:S(2)}, u32[]{:S(2)}) collective-permute-start(bf16[256,512]{1,0:T(8,128)(2,1)S(1)} %add_convert_fusion.3), channel_id=1, source_target_pairs={{0,2},{1,3},{2,0},{3,1},{4,6},{5,7},{6,4},{7,5},{8,10},{9,11},{10,... | collective-permute-start | bytes 786440 | tf_op jit(solution)/shard_map/ppermute | solution.py:175
  65.9 3.0 %attend.4 = (bf16[256,512]{1,0:T(8,128)(2,1)S(1)}, bf16[256,512]{1,0:T(8,128)(2,1)S(1)}) custom-call(s32[4]{0:T(128)S(1)} %get-tuple-element.37.scal, bf16[256,1024]{1,0:T(8,128)(2,1)S(1)} %copy-done.5, bf16[64,1024]{1,0:T(8,128)(2,1)S(1)} %get-tuple-element.38.refs_1_, bf16[1024,512]{1,0:T(8,128)(2,1)S(1)} %assemble.1.refs_2_.refs_1_, ...), custom_call_target="tpu_custom_call" | custom-call | tf_op jit(solution)/shard_map/attend/pallas_call | solution.py:301
  69.0 0.3 collective-permute-start.6
  69.3 3.0 %attend.6 = (bf16[256,512]{1,0:T(8,128)(2,1)S(1)}, bf16[256,512]{1,0:T(8,128)(2,1)S(1)}) custom-call(s32[4]{0:T(128)S(1)} %get-tuple-element.37.scal, bf16[256,1024]{1,0:T(8,128)(2,1)S(1)} %collective-permute-done.16.refs_0_, bf16[64,1024]{1,0:T(8,128)(2,1)S(1)} %collective-permute-done.17.refs_1_, bf16[1024,512]{1,0:T(8,128)(2,1)S(1)} %assemble.1.refs_2_.refs_1_, ...), custom_call_target="tpu_custom_call" | custom-call | tf_op jit(solution)/shard_map/attend/pallas_call | solution.py:301
  72.3 0.4 collective-permute-start.18
  72.8 0.6 collective-permute-start.12
  73.5 0.4 collective-permute-done.18
  74.0 1.2 collective-permute-start.19
  75.2 6.8 %collective-permute-done.12 = bf16[256,512]{1,0:T(8,128)(2,1)S(1)} collective-permute-done((bf16[256,512]{1,0:T(8,128)(2,1)S(1)}, bf16[256,512]{1,0:T(8,128)(2,1)S(1)}, u32[]{:S(2)}, u32[]{:S(2)}) %collective-permute-start.12) | collective-permute-done | bytes 262176 | tf_op jit(solution)/shard_map/ppermute | solution.py:175
  82.1 0.1 collective-permute-start.13
  82.2 1.3 project.7
  83.5 0.1 collective-permute-start.27
  83.6 0.6 collective-permute-start.7
  84.2 2.8 %collective-permute-done.19 = bf16[256,512]{1,0:T(8,128)(2,1)S(1)} collective-permute-done((bf16[256,512]{1,0:T(8,128)(2,1)S(1)}, bf16[256,512]{1,0:T(8,128)(2,1)S(1)}, u32[]{:S(2)}, u32[]{:S(2)}) %collective-permute-start.19) | collective-permute-done | bytes 262176 | tf_op jit(solution)/shard_map/ppermute | solution.py:175
  87.1 0.1 collective-permute-start.20
  87.1 1.5 project.5
  88.6 0.1 collective-permute-start.29
  88.7 3.8 %collective-permute-done.7 = bf16[256,512]{1,0:T(8,128)(2,1)S(1)} collective-permute-done((bf16[256,512]{1,0:T(8,128)(2,1)S(1)}, bf16[256,512]{1,0:T(8,128)(2,1)S(1)}, u32[]{:S(2)}, u32[]{:S(2)}) %collective-permute-start.7) | collective-permute-done | bytes 262176 | tf_op jit(solution)/shard_map/ppermute | solution.py:175
  92.7 1.3 project.6
  93.9 4.4 %collective-permute-done.27 = bf16[256,1024]{1,0:T(8,128)(2,1)S(1)} collective-permute-done((bf16[256,1024]{1,0:T(8,128)(2,1)S(1)}, bf16[256,1024]{1,0:T(8,128)(2,1)S(1)}, u32[]{:S(2)}, u32[]{:S(2)}) %collective-permute-start.27) | collective-permute-done | bytes 524320 | tf_op jit(solution)/shard_map/ppermute | solution.py:175
  98.3 0.1 add_convert_fusion
  98.5 2.0 %collective-permute-start.28 = (bf16[256,512]{1,0:T(8,128)(2,1)S(1)}, bf16[256,512]{1,0:T(8,128)(2,1)S(1)}, u32[]{:S(2)}, u32[]{:S(2)}) collective-permute-start(bf16[256,512]{1,0:T(8,128)(2,1)S(1)} %get-tuple-element.73), channel_id=1, source_target_pairs={{0,8},{4,12},{8,0},{12,4},{1,9},{5,13},{9,1},{13,5},{2,10},{6,14},... | collective-permute-start | bytes 786440 | tf_op jit(solution)/shard_map/ppermute | solution.py:175
  100.5 1.0 collective-permute-start.33
  101.5 1.8 %tails.1 = (bf16[16,1024]{1,0:T(8,128)(2,1)S(1)}, bf16[16,1024]{1,0:T(8,128)(2,1)S(1)}, bf16[16,1024]{1,0:T(8,128)(2,1)S(1)}, bf16[16,1024]{1,0:T(8,128)(2,1)S(1)}) custom-call(s32[4]{0:T(128)S(1)} %get-tuple-element.37.scal, bf16[256,512]{1,0:T(8,128)(2,1)S(1)} %add_convert_fusion.8.own.refs_0_, bf16[256,512]{1,0:T(8,128)(2,1)S(1)} %collective-permute-done.8.other.refs_1_, ...), custom_call_target="tpu_custom_call" | custom-call | tf_op jit(solution)/shard_map/tails/pallas_call | solution.py:435
  103.4 1.2 collective-permute-start.30
  104.6 2.8 %collective-permute-start.31 = (bf16[16,1024]{1,0:T(8,128)(2,1)S(1)}, bf16[16,1024]{1,0:T(8,128)(2,1)S(1)}, u32[]{:S(2)}, u32[]{:S(2)}) collective-permute-start(bf16[16,1024]{1,0:T(8,128)(2,1)S(1)} %get-tuple-element.64), channel_id=1, source_target_pairs={{0,8},{4,12},{8,0},{12,4},{1,9},{5,13},{9,1},{13,5},{2,10},{6,14},... | collective-permute-start | bytes 98312 | tf_op jit(solution)/shard_map/ppermute | solution.py:175
  107.4 12.0 %collective-permute-done.30.refs_4_ = bf16[16,1024]{1,0:T(8,128)(2,1)S(1)} collective-permute-done((bf16[16,1024]{1,0:T(8,128)(2,1)S(1)}, bf16[16,1024]{1,0:T(8,128)(2,1)S(1)}, u32[]{:S(2)}, u32[]{:S(2)}) %collective-permute-start.30) | collective-permute-done | bytes 32800 | tf_op jit(solution)/shard_map/ppermute | solution.py:175
  119.4 3.1 %collective-permute-start.32 = (bf16[16,1024]{1,0:T(8,128)(2,1)S(1)}, bf16[16,1024]{1,0:T(8,128)(2,1)S(1)}, u32[]{:S(2)}, u32[]{:S(2)}) collective-permute-start(bf16[16,1024]{1,0:T(8,128)(2,1)S(1)} %get-tuple-element.65), channel_id=1, source_target_pairs={{0,12},{4,8},{8,4},{12,0},{1,13},{5,9},{9,5},{13,1},{2,14},{6,10},... | collective-permute-start | bytes 98312 | tf_op jit(solution)/shard_map/ppermute | solution.py:175
  122.5 1.3 project.4
  123.8 2.4 %collective-permute-done.31.refs_5_ = bf16[16,1024]{1,0:T(8,128)(2,1)S(1)} collective-permute-done((bf16[16,1024]{1,0:T(8,128)(2,1)S(1)}, bf16[16,1024]{1,0:T(8,128)(2,1)S(1)}, u32[]{:S(2)}, u32[]{:S(2)}) %collective-permute-start.31) | collective-permute-done | bytes 32800 | tf_op jit(solution)/shard_map/ppermute | solution.py:175
  126.2 0.6 collective-permute-start.14
  126.7 2.8 %collective-permute-start.26 = (bf16[64,1024]{1,0:T(8,128)(2,1)S(1)}, bf16[64,1024]{1,0:T(8,128)(2,1)S(1)}, u32[]{:S(2)}, u32[]{:S(2)}) collective-permute-start(bf16[64,1024]{1,0:T(8,128)(2,1)S(1)} %get-tuple-element.57), channel_id=1, source_target_pairs={{0,12},{4,8},{8,4},{12,0},{1,13},{5,9},{9,5},{13,1},{2,14},{6,10},... | collective-permute-start | bytes 393224 | tf_op jit(solution)/shard_map/ppermute | solution.py:175
  129.6 0.6 collective-permute-start.21
  130.2 2.8 %recur.2 = (f32[256,512]{1,0:T(8,128)S(1)}, f32[256,512]{1,0:T(8,128)S(1)}, f32[8,512]{1,0:T(8,128)S(1)}) custom-call(s32[4]{0:T(128)S(1)} %get-tuple-element.37.scal, bf16[256,1024]{1,0:T(8,128)(2,1)S(1)} %get-tuple-element.58.refs_0_, bf16[256,512]{1,0:T(8,128)(2,1)S(1)} %collective-permute-done.28.refs_1_, ...), custom_call_target="tpu_custom_call" | custom-call | tf_op jit(solution)/shard_map/recur/pallas_call | solution.py:547
  133.1 2.8 %recur.3 = (f32[256,512]{1,0:T(8,128)S(1)}, f32[256,512]{1,0:T(8,128)S(1)}, f32[8,512]{1,0:T(8,128)S(1)}) custom-call(s32[4]{0:T(128)S(1)} %get-tuple-element.37.scal, bf16[256,1024]{1,0:T(8,128)(2,1)S(1)} %get-tuple-element.58.refs_0_, bf16[256,512]{1,0:T(8,128)(2,1)S(1)} %collective-permute-done.33.refs_1_, ...), custom_call_target="tpu_custom_call" | custom-call | tf_op jit(solution)/shard_map/recur/pallas_call | solution.py:547
  135.9 2.4 %collective-permute-start.35 = (f32[8,1024]{1,0:T(8,128)S(1)}, f32[8,1024]{1,0:T(8,128)S(1)}, u32[]{:S(2)}, u32[]{:S(2)}) collective-permute-start(f32[8,1024]{1,0:T(8,128)S(1)} %constant_dynamic-update-slice_fusion.4), channel_id=1, source_target_pairs={{0,8},{4,12},{8,0},{12,4},{1,9},{5,13},{9,1},{13,5},{2,10},{6,14},... | collective-permute-start | bytes 98312 | tf_op jit(solution)/shard_map/ppermute | solution.py:170
  138.2 1.1 collective-permute-start.34
  139.4 1.2 collective-permute-done.21.refs_2_
  140.6 1.4 join.1
  142.0 2.0 %collective-permute-done.34.refs_4_ = f32[8,1024]{1,0:T(8,128)S(1)} collective-permute-done((f32[8,1024]{1,0:T(8,128)S(1)}, f32[8,1024]{1,0:T(8,128)S(1)}, u32[]{:S(2)}, u32[]{:S(2)}) %collective-permute-start.34) | collective-permute-done | bytes 32800 | tf_op jit(solution)/shard_map/ppermute | solution.py:170
  144.0 1.5 %finish.1 = bf16[256,1024]{1,0:T(8,128)(2,1)} custom-call(s32[4]{0:T(128)S(1)} %get-tuple-element.37.scal, f32[256,512]{1,0:T(8,128)S(1)} %get-tuple-element.66.refs_0_, f32[256,512]{1,0:T(8,128)S(1)} %get-tuple-element.67.refs_1_, f32[256,512]{1,0:T(8,128)S(1)} %get-tuple-element.68.refs_2_, f32[256,512]{1,0:T(8,128)S(1)} %get-tuple-element.69.refs_3_, ...), custom_call_target="tpu_custom_call" | custom-call | tf_op jit(solution)/shard_map/finish/pallas_call | solution.py:585
  (64 shorter events, 0.8 us)
Async XLA Ops:
  0.6 37.1 %copy-start.1 = (bf16[1024,1024]{1,0:T(8,128)(2,1)S(1)}, bf16[1024,1024]{1,0:T(8,128)(2,1)}, u32[]{:S(2)}) copy-start(bf16[1024,1024]{1,0:T(8,128)(2,1)} %refs_2_.3) | copy-start | bytes 6291460
  0.6 10.4 %collective-permute-start.1 = (bf16[64,512]{1,0:T(8,128)(2,1)}, bf16[64,512]{1,0:T(8,128)(2,1)S(1)}, u32[]{:S(2)}, u32[]{:S(2)}) collective-permute-start(bf16[64,512]{1,0:T(8,128)(2,1)} %param.14), channel_id=1, source_target_pairs={{0,8},{4,12},{8,0},{12,4},{1,9},{5,13},{9,1},{13,5},{2,10},{6,14},... | collective-permute-start | bytes 196616 | tf_op jit(solution)/shard_map/ppermute | solution.py:175
  4.8 6.2 %collective-permute-start = (bf16[64,512]{1,0:T(8,128)(2,1)}, bf16[64,512]{1,0:T(8,128)(2,1)S(1)}, u32[]{:S(2)}, u32[]{:S(2)}) collective-permute-start(bf16[64,512]{1,0:T(8,128)(2,1)} %param.14), channel_id=1, source_target_pairs={{0,4},{4,0},{8,12},{12,8},{1,5},{5,1},{9,13},{13,9},{2,6},{6,2},{1... | collective-permute-start | bytes 196616 | tf_op jit(solution)/shard_map/ppermute | solution.py:175
  6.3 7.0 %collective-permute-start.2 = (bf16[64,512]{1,0:T(8,128)(2,1)}, bf16[64,512]{1,0:T(8,128)(2,1)S(1)}, u32[]{:S(2)}, u32[]{:S(2)}) collective-permute-start(bf16[64,512]{1,0:T(8,128)(2,1)} %param.14), channel_id=1, source_target_pairs={{0,12},{4,8},{8,4},{12,0},{1,13},{5,9},{9,5},{13,1},{2,14},{6,10},... | collective-permute-start | bytes 196616 | tf_op jit(solution)/shard_map/ppermute | solution.py:175
  6.3 30.7 %collective-permute-start.15 = (bf16[256,1024]{1,0:T(8,128)(2,1)}, bf16[256,1024]{1,0:T(8,128)(2,1)S(1)}, u32[]{:S(2)}, u32[]{:S(2)}) collective-permute-start(bf16[256,1024]{1,0:T(8,128)(2,1)} %refs_0_.1), channel_id=1, source_target_pairs={{0,12},{4,8},{8,4},{12,0},{1,13},{5,9},{9,5},{13,1},{2,14},{6,10},... | collective-permute-start | bytes 1572872 | tf_op jit(solution)/shard_map/ppermute | solution.py:175
  13.4 6.4 %collective-permute-start.4 = (bf16[256,512]{1,0:T(8,128)(2,1)S(1)}, bf16[256,512]{1,0:T(8,128)(2,1)S(1)}, u32[]{:S(2)}, u32[]{:S(2)}) collective-permute-start(bf16[256,512]{1,0:T(8,128)(2,1)S(1)} %constant_dynamic-update-slice_fusion.refs_0_), channel_id=1, source_target_pairs={{0,2},{1,3},{2,0},{3,1},{4,6},{5,7},{6,4},{7,5},{8,10},{9,11},{10,... | collective-permute-start | bytes 786440 | tf_op jit(solution)/shard_map/ppermute | solution.py:175
  14.9 22.2 %collective-permute-start.3 = (bf16[256,512]{1,0:T(8,128)(2,1)S(1)}, bf16[256,512]{1,0:T(8,128)(2,1)S(1)}, u32[]{:S(2)}, u32[]{:S(2)}) collective-permute-start(bf16[256,512]{1,0:T(8,128)(2,1)S(1)} %constant_dynamic-update-slice_fusion.refs_0_), channel_id=1, source_target_pairs={{0,1},{1,0},{2,3},{3,2},{4,5},{5,4},{6,7},{7,6},{8,9},{9,8},{10,11... | collective-permute-start | bytes 786440 | tf_op jit(solution)/shard_map/ppermute | solution.py:175
  19.8 17.3 %collective-permute-start.5 = (bf16[256,512]{1,0:T(8,128)(2,1)S(1)}, bf16[256,512]{1,0:T(8,128)(2,1)S(1)}, u32[]{:S(2)}, u32[]{:S(2)}) collective-permute-start(bf16[256,512]{1,0:T(8,128)(2,1)S(1)} %collective-permute-done.4.refs_2_), channel_id=1, source_target_pairs={{0,1},{1,0},{2,3},{3,2},{4,5},{5,4},{6,7},{7,6},{8,9},{9,8},{10,11... | collective-permute-start | bytes 786440 | tf_op jit(solution)/shard_map/ppermute | solution.py:175
  19.8 32.3 %collective-permute-start.9 = (bf16[256,1024]{1,0:T(8,128)(2,1)}, bf16[256,1024]{1,0:T(8,128)(2,1)S(1)}, u32[]{:S(2)}, u32[]{:S(2)}) collective-permute-start(bf16[256,1024]{1,0:T(8,128)(2,1)} %refs_0_.1), channel_id=1, source_target_pairs={{0,4},{4,0},{8,12},{12,8},{1,5},{5,1},{9,13},{13,9},{2,6},{6,2},{1... | collective-permute-start | bytes 1572872 | tf_op jit(solution)/shard_map/ppermute | solution.py:175
  31.1 1.0 copy-start.4
  32.2 0.7 copy-start.11
  33.6 16.8 %collective-permute-start.22 = (bf16[64,1024]{1,0:T(8,128)(2,1)S(1)}, bf16[64,1024]{1,0:T(8,128)(2,1)S(1)}, u32[]{:S(2)}, u32[]{:S(2)}) collective-permute-start(bf16[64,1024]{1,0:T(8,128)(2,1)S(1)} %get-tuple-element.54), channel_id=1, source_target_pairs={{0,12},{4,8},{8,4},{12,0},{1,13},{5,9},{9,5},{13,1},{2,14},{6,10},... | collective-permute-start | bytes 393224 | tf_op jit(solution)/shard_map/ppermute | solution.py:175
  37.0 32.2 %collective-permute-start.16 = (bf16[256,1024]{1,0:T(8,128)(2,1)S(1)}, bf16[256,1024]{1,0:T(8,128)(2,1)S(1)}, u32[]{:S(2)}, u32[]{:S(2)}) collective-permute-start(bf16[256,1024]{1,0:T(8,128)(2,1)S(1)} %collective-permute-done.15.refs_0_), channel_id=1, source_target_pairs={{0,4},{4,0},{8,12},{12,8},{1,5},{5,1},{9,13},{13,9},{2,6},{6,2},{1... | collective-permute-start | bytes 1572872 | tf_op jit(solution)/shard_map/ppermute | solution.py:175
  50.9 13.3 %collective-permute-start.23 = (bf16[256,512]{1,0:T(8,128)(2,1)S(1)}, bf16[256,512]{1,0:T(8,128)(2,1)S(1)}, u32[]{:S(2)}, u32[]{:S(2)}) collective-permute-start(bf16[256,512]{1,0:T(8,128)(2,1)S(1)} %get-tuple-element.56), channel_id=1, source_target_pairs={{0,1},{1,0},{2,3},{3,2},{4,5},{5,4},{6,7},{7,6},{8,9},{9,8},{10,11... | collective-permute-start | bytes 786440 | tf_op jit(solution)/shard_map/ppermute | solution.py:175
  51.0 12.6 %collective-permute-start.10 = (bf16[64,1024]{1,0:T(8,128)(2,1)S(1)}, bf16[64,1024]{1,0:T(8,128)(2,1)S(1)}, u32[]{:S(2)}, u32[]{:S(2)}) collective-permute-start(bf16[64,1024]{1,0:T(8,128)(2,1)S(1)} %get-tuple-element.44), channel_id=1, source_target_pairs={{0,4},{4,0},{8,12},{12,8},{1,5},{5,1},{9,13},{13,9},{2,6},{6,2},{1... | collective-permute-start | bytes 393224 | tf_op jit(solution)/shard_map/ppermute | solution.py:175
  51.1 14.8 %copy-start.5 = (bf16[256,1024]{1,0:T(8,128)(2,1)S(1)}, bf16[256,1024]{1,0:T(8,128)(2,1)}, u32[]{:S(2)}) copy-start(bf16[256,1024]{1,0:T(8,128)(2,1)} %refs_0_.1) | copy-start | bytes 1572868
  51.1 18.1 %collective-permute-start.17 = (bf16[64,1024]{1,0:T(8,128)(2,1)S(1)}, bf16[64,1024]{1,0:T(8,128)(2,1)S(1)}, u32[]{:S(2)}, u32[]{:S(2)}) collective-permute-start(bf16[64,1024]{1,0:T(8,128)(2,1)S(1)} %get-tuple-element.48), channel_id=1, source_target_pairs={{0,8},{4,12},{8,0},{12,4},{1,9},{5,13},{9,1},{13,5},{2,10},{6,14},... | collective-permute-start | bytes 393224 | tf_op jit(solution)/shard_map/ppermute | solution.py:175
  64.2 8.5 %collective-permute-start.11 = (bf16[256,512]{1,0:T(8,128)(2,1)S(1)}, bf16[256,512]{1,0:T(8,128)(2,1)S(1)}, u32[]{:S(2)}, u32[]{:S(2)}) collective-permute-start(bf16[256,512]{1,0:T(8,128)(2,1)S(1)} %get-tuple-element.46), channel_id=1, source_target_pairs={{0,1},{1,0},{2,3},{3,2},{4,5},{5,4},{6,7},{7,6},{8,9},{9,8},{10,11... | collective-permute-start | bytes 786440 | tf_op jit(solution)/shard_map/ppermute | solution.py:175
  64.4 9.0 %collective-permute-start.24 = (bf16[256,512]{1,0:T(8,128)(2,1)S(1)}, bf16[256,512]{1,0:T(8,128)(2,1)S(1)}, u32[]{:S(2)}, u32[]{:S(2)}) collective-permute-start(bf16[256,512]{1,0:T(8,128)(2,1)S(1)} %add_convert_fusion.3), channel_id=1, source_target_pairs={{0,2},{1,3},{2,0},{3,1},{4,6},{5,7},{6,4},{7,5},{8,10},{9,11},{10,... | collective-permute-start | bytes 786440 | tf_op jit(solution)/shard_map/ppermute | solution.py:175
  69.0 14.6 %collective-permute-start.6 = (bf16[256,512]{1,0:T(8,128)(2,1)S(1)}, bf16[256,512]{1,0:T(8,128)(2,1)S(1)}, u32[]{:S(2)}, u32[]{:S(2)}) collective-permute-start(bf16[256,512]{1,0:T(8,128)(2,1)S(1)} %get-tuple-element.40), channel_id=1, source_target_pairs={{0,1},{1,0},{2,3},{3,2},{4,5},{5,4},{6,7},{7,6},{8,9},{9,8},{10,11... | collective-permute-start | bytes 786440 | tf_op jit(solution)/shard_map/ppermute | solution.py:175
  72.3 9.9 %copy-start = (bf16[1024,1024]{1,0:T(8,128)(2,1)S(1)}, bf16[1024,1024]{1,0:T(8,128)(2,1)}, u32[]{:S(2)}) copy-start(bf16[1024,1024]{1,0:T(8,128)(2,1)} %refs_9_.3) | copy-start | bytes 6291460
  72.3 9.9 %copy-start.6 = (f32[4096]{0:T(1024)S(1)}, f32[4096]{0:T(1024)}, u32[]{:S(2)}) copy-start(f32[4096]{0:T(1024)} %param.25) | copy-start | bytes 49156
  72.3 1.6 %collective-permute-start.18 = (bf16[256,512]{1,0:T(8,128)(2,1)S(1)}, bf16[256,512]{1,0:T(8,128)(2,1)S(1)}, u32[]{:S(2)}, u32[]{:S(2)}) collective-permute-start(bf16[256,512]{1,0:T(8,128)(2,1)S(1)} %get-tuple-element.50), channel_id=1, source_target_pairs={{0,1},{1,0},{2,3},{3,2},{4,5},{5,4},{6,7},{7,6},{8,9},{9,8},{10,11... | collective-permute-start | bytes 786440 | tf_op jit(solution)/shard_map/ppermute | solution.py:175
  72.8 9.2 %collective-permute-start.12 = (bf16[256,512]{1,0:T(8,128)(2,1)S(1)}, bf16[256,512]{1,0:T(8,128)(2,1)S(1)}, u32[]{:S(2)}, u32[]{:S(2)}) collective-permute-start(bf16[256,512]{1,0:T(8,128)(2,1)S(1)} %add_convert_fusion.7), channel_id=1, source_target_pairs={{0,2},{1,3},{2,0},{3,1},{4,6},{5,7},{6,4},{7,5},{8,10},{9,11},{10,... | collective-permute-start | bytes 786440 | tf_op jit(solution)/shard_map/ppermute | solution.py:175
  73.4 8.7 %collective-permute-start.25 = (bf16[256,512]{1,0:T(8,128)(2,1)S(1)}, bf16[256,512]{1,0:T(8,128)(2,1)S(1)}, u32[]{:S(2)}, u32[]{:S(2)}) collective-permute-start(bf16[256,512]{1,0:T(8,128)(2,1)S(1)} %add_convert_fusion.2.own.refs_2_), channel_id=1, source_target_pairs={{0,1},{1,0},{2,3},{3,2},{4,5},{5,4},{6,7},{7,6},{8,9},{9,8},{10,11... | collective-permute-start | bytes 786440 | tf_op jit(solution)/shard_map/ppermute | solution.py:175
  74.0 13.0 %collective-permute-start.19 = (bf16[256,512]{1,0:T(8,128)(2,1)S(1)}, bf16[256,512]{1,0:T(8,128)(2,1)S(1)}, u32[]{:S(2)}, u32[]{:S(2)}) collective-permute-start(bf16[256,512]{1,0:T(8,128)(2,1)S(1)} %add_convert_fusion.5), channel_id=1, source_target_pairs={{0,2},{1,3},{2,0},{3,1},{4,6},{5,7},{6,4},{7,5},{8,10},{9,11},{10,... | collective-permute-start | bytes 786440 | tf_op jit(solution)/shard_map/ppermute | solution.py:175
  82.1 5.1 %collective-permute-start.13 = (bf16[256,512]{1,0:T(8,128)(2,1)S(1)}, bf16[256,512]{1,0:T(8,128)(2,1)S(1)}, u32[]{:S(2)}, u32[]{:S(2)}) collective-permute-start(bf16[256,512]{1,0:T(8,128)(2,1)S(1)} %add_convert_fusion.6.own.refs_4_), channel_id=1, source_target_pairs={{0,1},{1,0},{2,3},{3,2},{4,5},{5,4},{6,7},{7,6},{8,9},{9,8},{10,11... | collective-permute-start | bytes 786440 | tf_op jit(solution)/shard_map/ppermute | solution.py:175
  83.5 14.9 %collective-permute-start.27 = (bf16[256,1024]{1,0:T(8,128)(2,1)S(1)}, bf16[256,1024]{1,0:T(8,128)(2,1)S(1)}, u32[]{:S(2)}, u32[]{:S(2)}) collective-permute-start(bf16[256,1024]{1,0:T(8,128)(2,1)S(1)} %get-tuple-element.60), channel_id=1, source_target_pairs={{0,4},{4,0},{8,12},{12,8},{1,5},{5,1},{9,13},{13,9},{2,6},{6,2},{1... | collective-permute-start | bytes 1572872 | tf_op jit(solution)/shard_map/ppermute | solution.py:175
  83.6 8.9 %collective-permute-start.7 = (bf16[256,512]{1,0:T(8,128)(2,1)S(1)}, bf16[256,512]{1,0:T(8,128)(2,1)S(1)}, u32[]{:S(2)}, u32[]{:S(2)}) collective-permute-start(bf16[256,512]{1,0:T(8,128)(2,1)S(1)} %add_convert_fusion.9), channel_id=1, source_target_pairs={{0,2},{1,3},{2,0},{3,1},{4,6},{5,7},{6,4},{7,5},{8,10},{9,11},{10,... | collective-permute-start | bytes 786440 | tf_op jit(solution)/shard_map/ppermute | solution.py:175
  87.1 5.6 %collective-permute-start.20 = (bf16[256,512]{1,0:T(8,128)(2,1)S(1)}, bf16[256,512]{1,0:T(8,128)(2,1)S(1)}, u32[]{:S(2)}, u32[]{:S(2)}) collective-permute-start(bf16[256,512]{1,0:T(8,128)(2,1)S(1)} %add_convert_fusion.4.own.refs_6_), channel_id=1, source_target_pairs={{0,1},{1,0},{2,3},{3,2},{4,5},{5,4},{6,7},{7,6},{8,9},{9,8},{10,11... | collective-permute-start | bytes 786440 | tf_op jit(solution)/shard_map/ppermute | solution.py:175
  88.6 41.0 %collective-permute-start.29 = (bf16[256,1024]{1,0:T(8,128)(2,1)S(1)}, bf16[256,1024]{1,0:T(8,128)(2,1)S(1)}, u32[]{:S(2)}, u32[]{:S(2)}) collective-permute-start(bf16[256,1024]{1,0:T(8,128)(2,1)S(1)} %get-tuple-element.61), channel_id=1, source_target_pairs={{0,4},{4,0},{8,12},{12,8},{1,5},{5,1},{9,13},{13,9},{2,6},{6,2},{1... | collective-permute-start | bytes 1572872 | tf_op jit(solution)/shard_map/ppermute | solution.py:175
  92.6 8.9 %collective-permute-start.8 = (bf16[256,512]{1,0:T(8,128)(2,1)S(1)}, bf16[256,512]{1,0:T(8,128)(2,1)S(1)}, u32[]{:S(2)}, u32[]{:S(2)}) collective-permute-start(bf16[256,512]{1,0:T(8,128)(2,1)S(1)} %add_convert_fusion.8.own.refs_0_), channel_id=1, source_target_pairs={{0,1},{1,0},{2,3},{3,2},{4,5},{5,4},{6,7},{7,6},{8,9},{9,8},{10,11... | collective-permute-start | bytes 786440 | tf_op jit(solution)/shard_map/ppermute | solution.py:175
  98.5 31.7 %collective-permute-start.28 = (bf16[256,512]{1,0:T(8,128)(2,1)S(1)}, bf16[256,512]{1,0:T(8,128)(2,1)S(1)}, u32[]{:S(2)}, u32[]{:S(2)}) collective-permute-start(bf16[256,512]{1,0:T(8,128)(2,1)S(1)} %get-tuple-element.73), channel_id=1, source_target_pairs={{0,8},{4,12},{8,0},{12,4},{1,9},{5,13},{9,1},{13,5},{2,10},{6,14},... | collective-permute-start | bytes 786440 | tf_op jit(solution)/shard_map/ppermute | solution.py:175
  100.5 32.6 %collective-permute-start.33 = (bf16[256,512]{1,0:T(8,128)(2,1)S(1)}, bf16[256,512]{1,0:T(8,128)(2,1)S(1)}, u32[]{:S(2)}, u32[]{:S(2)}) collective-permute-start(bf16[256,512]{1,0:T(8,128)(2,1)S(1)} %get-tuple-element.72), channel_id=1, source_target_pairs={{0,8},{4,12},{8,0},{12,4},{1,9},{5,13},{9,1},{13,5},{2,10},{6,14},... | collective-permute-start | bytes 786440 | tf_op jit(solution)/shard_map/ppermute | solution.py:175
  103.3 26.9 %copy-start.2 = (bf16[4,256,256]{2,1,0:T(8,128)(2,1)S(1)}, bf16[4,256,256]{2,1,0:T(8,128)(2,1)}, u32[]{:S(2)}) copy-start(bf16[4,256,256]{2,1,0:T(8,128)(2,1)} %refs_8_.3) | copy-start | bytes 1572868
  103.3 26.9 %copy-start.3 = (bf16[4,256,256]{2,1,0:T(8,128)(2,1)S(1)}, bf16[4,256,256]{2,1,0:T(8,128)(2,1)}, u32[]{:S(2)}) copy-start(bf16[4,256,256]{2,1,0:T(8,128)(2,1)} %refs_9_.5) | copy-start | bytes 1572868
  103.3 26.9 %copy-start.7 = (f32[4,1024]{1,0:T(4,128)S(1)}, f32[4,1024]{1,0:T(4,128)}, u32[]{:S(2)}) copy-start(f32[4,1024]{1,0:T(4,128)} %refs_7_.3) | copy-start | bytes 49156
  103.3 26.9 %copy-start.8 = (f32[1024]{0:T(1024)S(1)}, f32[1024]{0:T(1024)}, u32[]{:S(2)}) copy-start(f32[1024]{0:T(1024)} %param.22) | copy-start | bytes 12292
  103.4 26.9 %copy-start.9 = (f32[1024]{0:T(1024)S(1)}, f32[1024]{0:T(1024)}, u32[]{:S(2)}) copy-start(f32[1024]{0:T(1024)} %param.23) | copy-start | bytes 12292
  103.4 26.9 %copy-start.10 = (s32[1024]{0:T(1024)S(1)}, s32[1024]{0:T(1024)}, u32[]{:S(2)}) copy-start(s32[1024]{0:T(1024)} %param.24) | copy-start | bytes 12292
  103.4 16.0 %collective-permute-start.30 = (bf16[16,1024]{1,0:T(8,128)(2,1)S(1)}, bf16[16,1024]{1,0:T(8,128)(2,1)S(1)}, u32[]{:S(2)}, u32[]{:S(2)}) collective-permute-start(bf16[16,1024]{1,0:T(8,128)(2,1)S(1)} %get-tuple-element.63), channel_id=1, source_target_pairs={{0,4},{4,0},{8,12},{12,8},{1,5},{5,1},{9,13},{13,9},{2,6},{6,2},{1... | collective-permute-start | bytes 98312 | tf_op jit(solution)/shard_map/ppermute | solution.py:175
  104.6 21.6 %collective-permute-start.31 = (bf16[16,1024]{1,0:T(8,128)(2,1)S(1)}, bf16[16,1024]{1,0:T(8,128)(2,1)S(1)}, u32[]{:S(2)}, u32[]{:S(2)}) collective-permute-start(bf16[16,1024]{1,0:T(8,128)(2,1)S(1)} %get-tuple-element.64), channel_id=1, source_target_pairs={{0,8},{4,12},{8,0},{12,4},{1,9},{5,13},{9,1},{13,5},{2,10},{6,14},... | collective-permute-start | bytes 98312 | tf_op jit(solution)/shard_map/ppermute | solution.py:175
  119.4 7.3 %collective-permute-start.32 = (bf16[16,1024]{1,0:T(8,128)(2,1)S(1)}, bf16[16,1024]{1,0:T(8,128)(2,1)S(1)}, u32[]{:S(2)}, u32[]{:S(2)}) collective-permute-start(bf16[16,1024]{1,0:T(8,128)(2,1)S(1)} %get-tuple-element.65), channel_id=1, source_target_pairs={{0,12},{4,8},{8,4},{12,0},{1,13},{5,9},{9,5},{13,1},{2,14},{6,10},... | collective-permute-start | bytes 98312 | tf_op jit(solution)/shard_map/ppermute | solution.py:175
  126.2 13.2 %collective-permute-start.14 = (bf16[64,1024]{1,0:T(8,128)(2,1)S(1)}, bf16[64,1024]{1,0:T(8,128)(2,1)S(1)}, u32[]{:S(2)}, u32[]{:S(2)}) collective-permute-start(bf16[64,1024]{1,0:T(8,128)(2,1)S(1)} %get-tuple-element.47), channel_id=1, source_target_pairs={{0,4},{4,0},{8,12},{12,8},{1,5},{5,1},{9,13},{13,9},{2,6},{6,2},{1... | collective-permute-start | bytes 393224 | tf_op jit(solution)/shard_map/ppermute | solution.py:175
  126.7 12.6 %collective-permute-start.26 = (bf16[64,1024]{1,0:T(8,128)(2,1)S(1)}, bf16[64,1024]{1,0:T(8,128)(2,1)S(1)}, u32[]{:S(2)}, u32[]{:S(2)}) collective-permute-start(bf16[64,1024]{1,0:T(8,128)(2,1)S(1)} %get-tuple-element.57), channel_id=1, source_target_pairs={{0,12},{4,8},{8,4},{12,0},{1,13},{5,9},{9,5},{13,1},{2,14},{6,10},... | collective-permute-start | bytes 393224 | tf_op jit(solution)/shard_map/ppermute | solution.py:175
  129.6 11.0 %collective-permute-start.21 = (bf16[64,1024]{1,0:T(8,128)(2,1)S(1)}, bf16[64,1024]{1,0:T(8,128)(2,1)S(1)}, u32[]{:S(2)}, u32[]{:S(2)}) collective-permute-start(bf16[64,1024]{1,0:T(8,128)(2,1)S(1)} %get-tuple-element.51), channel_id=1, source_target_pairs={{0,8},{4,12},{8,0},{12,4},{1,9},{5,13},{9,1},{13,5},{2,10},{6,14},... | collective-permute-start | bytes 393224 | tf_op jit(solution)/shard_map/ppermute | solution.py:175
  135.9 6.1 %collective-permute-start.35 = (f32[8,1024]{1,0:T(8,128)S(1)}, f32[8,1024]{1,0:T(8,128)S(1)}, u32[]{:S(2)}, u32[]{:S(2)}) collective-permute-start(f32[8,1024]{1,0:T(8,128)S(1)} %constant_dynamic-update-slice_fusion.4), channel_id=1, source_target_pairs={{0,8},{4,12},{8,0},{12,4},{1,9},{5,13},{9,1},{13,5},{2,10},{6,14},... | collective-permute-start | bytes 98312 | tf_op jit(solution)/shard_map/ppermute | solution.py:170
  138.2 5.7 %collective-permute-start.34 = (f32[8,1024]{1,0:T(8,128)S(1)}, f32[8,1024]{1,0:T(8,128)S(1)}, u32[]{:S(2)}, u32[]{:S(2)}) collective-permute-start(f32[8,1024]{1,0:T(8,128)S(1)} %constant_dynamic-update-slice_fusion.4), channel_id=1, source_target_pairs={{0,4},{4,8},{8,12},{12,0},{1,5},{5,9},{9,13},{13,1},{2,6},{6,10},{... | collective-permute-start | bytes 98312 | tf_op jit(solution)/shard_map/ppermute | solution.py:170
